TPU v7x, 32 devices: a whole 2x2x4 slice. The times are simulated.
32 devices in a mesh: grp: 2 (over y), rows: 8 (over z, x), diam: 2 (over core).
Axes of the slice: x: 2, y: 2, z: 4, core: 2. Of those that a mesh axis runs over, the one named last changes fastest.
Arguments:
- phi: bfloat16 [8192, 3200], P('rows', 'diam'), may hold values from -0.4375 to 0.4375
- loads: bfloat16 [8192, 512], P('rows'), may hold values from -1 to 1
- harm_diam: int32 [16], replicated, may hold values from 0 to 15
- mistuning: float32 [3200, 3200], P('diam', 'rows'), may hold values from -0.109375 to 0.109375
- dyn_diag: float32 [6400], P('grp'), parts along dimension 0, may hold values from 0.8 to 3
- blade_order: int32 [16], replicated, may hold values from 0 to 15, each once
Outputs:
- blades: bfloat16 [16, 64, 8192], P('diam', 'grp', 'rows'), parts along dimension 1
There are 2 independent parts, one for each index of `grp`. A program takes and returns all parts, laid end to end along the dimension named above; an argument that names none is the same for every part. Nothing has to cross between parts.
Inputs may be any that keep to these rules, and one draw needn't show every extreme that they name: `blade_order`: each blade once.
All inputs are finite; a program needn't handle non-finite values.
Results may differ from a plain program's by a relative error of at most 0.013.
Values may be sent and summed in bfloat16 or wider, within the bound.
No kernel may reach another device: no remote copies, remote signals or barrier semaphores. Data moves between devices by JAX's collectives and lax.ppermute only.
A program may use at most 64 MiB of HBM per device.

v0:
```python
import math

import jax
import jax.numpy as jnp
from jax import lax
from jax.sharding import PartitionSpec as P

NBLADE = 16
MODES = 200
NHARM = 16
ITERS = 4


def cyclic_rows(blade_order):
    count = NBLADE
    blade_pos = jnp.arange(count).astype(jnp.float32)[:, None]
    harmonic = jnp.arange(count)[None, :]
    half_count = count // 2
    wave = jnp.where(harmonic > half_count, harmonic - half_count, harmonic).astype(jnp.float32)
    angle = 2.0 * math.pi * wave * blade_pos / count
    scale = jnp.where(
        (harmonic == 0) | (harmonic == half_count), 1.0 / math.sqrt(count), math.sqrt(2.0 / count)
    )
    cyclic_tab = jnp.where(harmonic > half_count, jnp.sin(angle), jnp.cos(angle)) * scale
    onehot = (blade_order[:, None] == jnp.arange(count)[None, :]).astype(jnp.float32)
    return jnp.dot(onehot, cyclic_tab, precision=lax.Precision.HIGHEST)


def on_device(phi, loads, harm_diam, mistuning, dyn_diag, blade_order):
    rows_dev = phi.shape[0]
    half_modes = phi.shape[1]
    local_diam = half_modes // MODES
    columns = loads.shape[1] // NHARM
    col_width = mistuning.shape[1]
    diam_index = lax.axis_index("diam")
    row_index = lax.axis_index("rows")
    first_diam = diam_index * local_diam
    diam_ids = first_diam + jnp.arange(local_diam, dtype=jnp.int32)
    select = (harm_diam[:, None] == diam_ids[None, :]).astype(jnp.bfloat16)
    combined = jnp.einsum(
        "rkc,kh->rhc",
        loads.reshape(rows_dev, NHARM, columns),
        select,
        preferred_element_type=jnp.float32,
    ).astype(jnp.bfloat16)
    shapes = phi.reshape(rows_dev, local_diam, MODES)
    force_part = jnp.einsum(
        "rhm,rhc->hmc", shapes, combined, preferred_element_type=jnp.float32
    ).reshape(half_modes, columns)
    half_start = diam_index * half_modes
    dyn_half = lax.dynamic_slice_in_dim(dyn_diag, half_start, half_modes, 0)[:, None]

    def row_total(partial_term):
        return lax.psum(partial_term, "rows")

    force_half = row_total(force_part)
    amp_half = force_half / dyn_half
    for sweep in range(ITERS):
        full_amp = lax.all_gather(amp_half, "diam", axis=0, tiled=True)
        col_part = lax.dynamic_slice_in_dim(full_amp, row_index * col_width, col_width, 0)
        amp_half = (
            force_half
            - row_total(
                jnp.dot(
                    mistuning,
                    col_part,
                    precision=lax.Precision.HIGHEST,
                    preferred_element_type=jnp.float32,
                )
            )
        ) / dyn_half
    amp_low = amp_half.astype(jnp.bfloat16).reshape(local_diam, MODES, columns)
    sector = jnp.einsum("rhm,hmc->hcr", shapes, amp_low, preferred_element_type=jnp.float32).astype(
        jnp.bfloat16
    )
    table = cyclic_rows(blade_order)
    table_cols = lax.dynamic_slice_in_dim(table, first_diam, local_diam, 1)
    partial_value = jnp.einsum(
        "sh,hcr->scr", table_cols, sector.astype(jnp.float32), precision=lax.Precision.HIGHEST
    )
    blades = lax.psum_scatter(
        partial_value.astype(jnp.bfloat16), "diam", scatter_dimension=0, tiled=True
    )
    return blades


def solution(mesh):
    placed = (P("rows", "diam"), P("rows", None), P(), P("diam", "rows"), P("grp"), P())
    return jax.shard_map(
        on_device, mesh=mesh, in_specs=placed, out_specs=P("diam", "grp", "rows"), check_vma=False
    )
```

profile of v0, /device:TPU:1, one launch (start us, length us, event | category | flops | bytes accessed | tf_op | source)
XLA Modules:
  0.0 430.7 jit_solution(11352834408343363607)
XLA Ops:
  6.5 2.4 copy.15
  9.0 1.9 fusion.1
  10.9 1.1 convolution_bitcast_fusion.4
  12.9 1.8 reshape.56
  14.8 70.1 %all-reduce.6.cloned.1.call-done = f32[1600,32]{0,1:T(8,128)} async-done(((f32[1600,32]{0,1:T(8,128)}), f32[1600,32]{0,1:T(8,128)}) %all-reduce.6.cloned.1.call-update) | async-done | bytes 204816 | tf_op jit(solution)/shard_map/psum | solution.py:54
  85.9 4.4 %all-gather = f32[2,1600,32]{1,2,0:T(8,128)S(1)} all-gather(f32[1,1600,32]{1,2,0:T(8,128)S(1)} %divide_bitcast_fusion.3), channel_id=1, replica_groups=mesh['grp'=2,'rows'=8,'diam'=2] {'diam'}, dimensions={0}, use_global_device_ids=true | all-gather | bytes 614400 | tf_op jit(solution)/shard_map/all_gather | solution.py:59
  90.3 1.1 copy.19
  91.4 2.1 reshape.59
  93.5 4.0 convolution_bitcast_fusion.3
  97.5 67.6 %all-reduce.8.cloned.1.call-done = f32[1600,32]{0,1:T(8,128)} async-done(((f32[1600,32]{0,1:T(8,128)}), f32[1600,32]{0,1:T(8,128)}) %all-reduce.8.cloned.1.call-update) | async-done | bytes 204816 | tf_op jit(solution)/shard_map/psum | solution.py:54
  165.2 1.0 divide_bitcast_fusion.2
  166.1 4.2 all-gather.1
  170.4 1.1 copy.20
  171.5 2.1 reshape.61
  173.5 4.0 convolution_bitcast_fusion.2
  177.6 67.6 %all-reduce.10.cloned.1.call-done = f32[1600,32]{0,1:T(8,128)} async-done(((f32[1600,32]{0,1:T(8,128)}), f32[1600,32]{0,1:T(8,128)}) %all-reduce.10.cloned.1.call-update) | async-done | bytes 204816 | tf_op jit(solution)/shard_map/psum | solution.py:54
  246.2 4.2 all-gather.2
  250.4 1.1 copy.21
  251.5 2.1 reshape.63
  253.6 4.0 convolution_bitcast_fusion.1
  257.7 67.6 %all-reduce.12.cloned.1.call-done = f32[1600,32]{0,1:T(8,128)} async-done(((f32[1600,32]{0,1:T(8,128)}), f32[1600,32]{0,1:T(8,128)}) %all-reduce.12.cloned.1.call-update) | async-done | bytes 204816 | tf_op jit(solution)/shard_map/psum | solution.py:54
  326.3 4.2 all-gather.3
  330.5 1.1 copy.22
  331.6 2.1 reshape.65
  333.7 4.0 convolution_bitcast_fusion
  338.3 67.2 %all-reduce.14.cloned.1.call-done = f32[1600,32]{0,1:T(8,128)} async-done(((f32[1600,32]{0,1:T(8,128)}), f32[1600,32]{0,1:T(8,128)}) %all-reduce.14.cloned.1.call-update) | async-done | bytes 204816 | tf_op jit(solution)/shard_map/psum | solution.py:54
  405.4 1.6 divide_convert_fusion
  407.0 1.1 reshape.57
  409.0 1.1 fusion
  410.1 1.1 copy.28
  411.1 10.6 %reduce-scatter.4.cloned.1.call-done = bf16[8,32768]{1,0:T(8,128)(2,1)} async-done(((bf16[16,32768]{1,0:T(8,128)(2,1)}), bf16[8,32768]{1,0:T(8,128)(2,1)}) %reduce-scatter.4.cloned.1.call-update) | async-done | bytes 524304
  421.7 2.1 copy.25
  (31 shorter events, 5.5 us)
Async XLA Ops:
  6.5 4.3 %copy-start = (bf16[1024,1600]{0,1:T(8,128)(2,1)S(1)}, bf16[1024,1600]{0,1:T(8,128)(2,1)}, u32[]{:S(2)}) copy-start(bf16[1024,1600]{0,1:T(8,128)(2,1)} %param.6) | copy-start | bytes 9830404
  6.5 78.4 %all-reduce.6.cloned.1.call-start = ((), (), s32[]{:S(2)}) async-start(), calls=%async_computation.1 | async-start | bytes 425984 | tf_op jit(solution)/shard_map/psum | solution.py:54
  10.9 3.9 copy-start.2
  14.7 150.5 %all-reduce.8.cloned.1.call-start = ((), (), s32[]{:S(2)}) async-start(), calls=%async_computation.2 | async-start | bytes 425984 | tf_op jit(solution)/shard_map/psum | solution.py:54
  85.9 79.3 %copy-start.1 = (f32[1600,32]{0,1:T(8,128)S(1)}, f32[1600,32]{0,1:T(8,128)}, u32[]{:S(2)}) copy-start(f32[1600,32]{0,1:T(8,128)} %all-reduce.6.cloned.1.call-done) | copy-start | bytes 614404
  97.5 147.8 %all-reduce.10.cloned.1.call-start = ((), (), s32[]{:S(2)}) async-start(), calls=%async_computation.3 | async-start | bytes 425984 | tf_op jit(solution)/shard_map/psum | solution.py:54
  177.6 147.8 %all-reduce.12.cloned.1.call-start = ((), (), s32[]{:S(2)}) async-start(), calls=%async_computation.4 | async-start | bytes 425984 | tf_op jit(solution)/shard_map/psum | solution.py:54
  257.6 147.8 %all-reduce.14.cloned.1.call-start = ((), (), s32[]{:S(2)}) async-start(), calls=%async_computation.5 | async-start | bytes 425984 | tf_op jit(solution)/shard_map/psum | solution.py:54
  326.3 11.7 %copy-start.3 = (s32[16]{0:T(128)S(1)}, s32[16]{0:T(128)}, u32[]{:S(2)}) copy-start(s32[16]{0:T(128)} %param.11) | copy-start | bytes 196
  337.7 84.0 %reduce-scatter.4.cloned.1.call-start = ((), (), s32[]{:S(2)}) async-start(), calls=%async_computation.6 | async-start | bytes 1572864
Sparse Core Ops, SparseCore 0:
  14.8 70.1 all-reduce.5
  97.6 67.5 all-reduce.7
  177.7 67.5 all-reduce.9
  257.8 67.5 all-reduce.11
  337.8 67.5 all-reduce.13
  411.3 10.4 reduce-scatter.3
where the time goes:
time: 432 us; the launch traced here: 431 us
  waiting for transfers between devices  351 us (81%)
  local copies, waits for them, and re-layouts  22.1 us (5%)
  matrix products  21.2 us (5%)
  blocking collectives  17.1 us (4%)
  between operations  13.6 us (3%)
  other arithmetic  5.46 us (1%)
    psum x5, waiting for transfers between devices, row_total(): return lax.psum(partial_term, 'rows')  340 us
    all_gather x4, blocking collectives, on_device(): full_amp = lax.all_gather(amp_half, 'diam', axis=0, tiled=True)  17.1 us
    dot_general x4, matrix products, on_device(): jnp.dot(mistuning, col_part, precision=lax.Precision.HIGHEST, preferred_e...  16 us
    unnamed x14, local copies, waits for them, and re-layouts  11.8 us
    unnamed x7, waiting for transfers between devices  10.7 us
  transfers between devices with their start and end apart: 6, of which 6 were waited for; matrix products, arithmetic and copies ran while one was open for 0% of the time, Pallas kernels for 0%

commit v1 on v0

--- a/solution.py
+++ b/solution.py
@@ -9,6 +9,9 @@
 MODES = 200
 NHARM = 16
 ITERS = 4
+SWAP = [(0, 1), (1, 0)]
+F32 = jnp.float32
+BF16 = jnp.bfloat16
 
 
 def cyclic_rows(blade_order):
@@ -26,7 +29,7 @@
     return jnp.dot(onehot, cyclic_tab, precision=lax.Precision.HIGHEST)
 
 
-def on_device(phi, loads, harm_diam, mistuning, dyn_diag, blade_order):
+def general_plan(phi, loads, harm_diam, mistuning, dyn_diag, blade_order):
     rows_dev = phi.shape[0]
     half_modes = phi.shape[1]
     local_diam = half_modes // MODES
@@ -84,8 +87,94 @@
     return blades
 
 
+def by_parity(arr, parity):
+    pairs = arr.reshape((arr.shape[0] // 2, 2) + arr.shape[1:])
+    return jnp.where(parity == 0, pairs[:, 0], pairs[:, 1])
+
+
+def chunk_plan(phi, loads, harm_diam, mistuning, dyn_diag, blade_order):
+    rows_dev, half_modes = phi.shape
+    local_diam = half_modes // MODES
+    columns = loads.shape[1] // NHARM
+    core = lax.axis_index("diam")
+    own_diam = 2 * lax.axis_index("rows") + core
+    first_diam = core * local_diam
+
+    def other_core(value):
+        return lax.ppermute(value, "diam", SWAP)
+
+    def in_half_order(own, received):
+        return jnp.where(
+            core == 0, jnp.concatenate([own, received]), jnp.concatenate([received, own])
+        )
+
+    shapes = phi.T.reshape(local_diam, MODES, rows_dev)
+    shapes_received = other_core(shapes)
+
+    stiff = mistuning.T.reshape(2 * MODES, local_diam, MODES).transpose(1, 0, 2).astype(BF16)
+    coupling = in_half_order(by_parity(stiff, core), other_core(by_parity(stiff, 1 - core)))
+    coupling_own = jnp.where(core == 0, coupling[:, :MODES], coupling[:, MODES:])
+    coupling_other = jnp.where(core == 0, coupling[:, MODES:], coupling[:, :MODES])
+
+    diam_ids = first_diam + jnp.arange(local_diam, dtype=jnp.int32)
+    select = (harm_diam[None, :] == diam_ids[:, None]).astype(BF16)
+    spread = jnp.einsum("hk,cd->hckd", select, jnp.eye(columns, dtype=BF16)).reshape(
+        local_diam * columns, NHARM * columns
+    )
+    combined = (
+        jnp.einsum("ak,rk->ar", spread, loads, preferred_element_type=F32)
+        .astype(BF16)
+        .reshape(local_diam, columns, rows_dev)
+    )
+    force_part = jnp.einsum(
+        "hcr,hmr->hcm", combined, shapes, preferred_element_type=F32
+    ).astype(BF16)
+    force_slots = in_half_order(
+        by_parity(force_part, core), other_core(by_parity(force_part, 1 - core))
+    )
+
+    def row_total(slots):
+        got = lax.all_to_all(slots, "rows", 0, 0, tiled=True)
+        return jnp.sum(got.astype(F32), axis=0)
+
+    dyn_own = lax.dynamic_slice_in_dim(dyn_diag, own_diam * MODES, MODES, 0)[None, :]
+    force = row_total(force_slots)
+    amp = force / dyn_own
+    for sweep in range(ITERS):
+        amp_low = amp.astype(BF16)
+        amp_other = other_core(amp_low)
+        part = jnp.einsum("cj,sjm->scm", amp_low, coupling_own, preferred_element_type=F32)
+        part = part + jnp.einsum(
+            "cj,sjm->scm", amp_other, coupling_other, preferred_element_type=F32
+        )
+        amp = (force - row_total(part.astype(BF16))) / dyn_own
+    amp_low = amp.astype(BF16)
+    same = lax.all_to_all(
+        jnp.broadcast_to(amp_low[None], (local_diam,) + amp_low.shape), "rows", 0, 0, tiled=True
+    )
+    crossed = other_core(same)
+    even = jnp.where(core == 0, same, crossed)
+    odd = jnp.where(core == 0, crossed, same)
+    amps = jnp.stack([even, odd], axis=1).reshape(NBLADE, columns, MODES)
+
+    table = lax.dynamic_slice_in_dim(cyclic_rows(blade_order), first_diam, local_diam, 0)
+    weights = (table.T[:, :, None, None] * amps.astype(F32)[:, None]).astype(BF16)
+    weights = weights.reshape(2, local_diam, local_diam * columns, MODES)
+    mine = jnp.where(core == 0, weights[0], weights[1])
+    theirs = jnp.where(core == 0, weights[1], weights[0])
+    blades = jnp.einsum("ham,hmr->ar", mine, shapes, preferred_element_type=F32) + jnp.einsum(
+        "ham,hmr->ar", theirs, shapes_received, preferred_element_type=F32
+    )
+    return blades.astype(BF16).reshape(local_diam, columns, rows_dev)
+
+
 def solution(mesh):
     placed = (P("rows", "diam"), P("rows", None), P(), P("diam", "rows"), P("grp"), P())
+    one_each = mesh.shape["rows"] * 2 == NBLADE and mesh.shape["diam"] == 2
     return jax.shard_map(
-        on_device, mesh=mesh, in_specs=placed, out_specs=P("diam", "grp", "rows"), check_vma=False
+        chunk_plan if one_each else general_plan,
+        mesh=mesh,
+        in_specs=placed,
+        out_specs=P("diam", "grp", "rows"),
+        check_vma=False,
     )

time: 432 us -> 102 us (0.24)
  waiting for transfers between devices: 351 us -> 27.6 us
  starting transfers between devices: 0.39 us -> 27.4 us
  between operations: 13.6 us -> 0.27 us
  local copies, waits for them, and re-layouts: 22.1 us -> 9.56 us
  matrix products: 21.2 us -> 12.3 us
    psum x5 -> x0, waiting for transfers between devices: 340 us -> none  [row_total(): return lax.psum(partial_term, 'rows')]
    all_to_all x0 -> x4, waiting for transfers between devices: none -> 24.2 us  [the longest x3 18.3 us: row_total(): got = lax.all_to_all(slots, 'rows', 0, 0, tiled=True)]
    all_to_all x0 -> x2, blocking collectives: none -> 17.6 us  [row_total(): got = lax.all_to_all(slots, 'rows', 0, 0, tiled=True)]
    all_gather x4 -> x0, blocking collectives: 17.1 us -> none  [on_device(): full_amp = lax.all_gather(amp_half, 'diam', axis=0, tiled=True)]
    all_to_all x0 -> x4, starting transfers between devices: none -> 16.8 us  [the longest x3 13.4 us: row_total(): got = lax.all_to_all(slots, 'rows', 0, 0, tiled=True)]
    unnamed x7 -> x0, waiting for transfers between devices: 10.7 us -> none
    ppermute x0 -> x8, starting transfers between devices: none -> 10.6 us  [other_core(): return lax.ppermute(value, 'diam', SWAP)]
    unnamed x14 -> x8, local copies, waits for them, and re-layouts: 11.8 us -> 1.79 us
  transfers between devices with their start and end apart: 6 -> 12, of which waited for: 6 -> 8; matrix products, arithmetic and copies ran while one was open for 0% -> 15% of each run, Pallas kernels for 0% -> 0%
where the time goes in v1:
time: 102 us; the launch traced here: 101 us
  waiting for transfers between devices  27.6 us (27%)
  starting transfers between devices  27.4 us (27%)
  blocking collectives  17.6 us (17%)
  matrix products  12.3 us (12%)
  local copies, waits for them, and re-layouts  9.56 us (9%)
  other arithmetic  6.71 us (7%)
    all_to_all x3, waiting for transfers between devices, row_total(): got = lax.all_to_all(slots, 'rows', 0, 0, tiled=True)  18.3 us
    all_to_all x2, blocking collectives, row_total(): got = lax.all_to_all(slots, 'rows', 0, 0, tiled=True)  17.6 us
    all_to_all x3, starting transfers between devices, row_total(): got = lax.all_to_all(slots, 'rows', 0, 0, tiled=True)  13.4 us
    ppermute x8, starting transfers between devices, other_core(): return lax.ppermute(value, 'diam', SWAP)  10.6 us
    all_to_all x1, waiting for transfers between devices, chunk_plan(): lax.all_to_all(jnp.broadcast_to(amp_low[None], (local_diam,) + amp_low.sh...  5.89 us
    convert_element_type x2, local copies, waits for them, and re-layouts, chunk_plan(): mistuning.T.reshape(2 * MODES, local_diam, MODES).transpose(1, 0, 2)  5.26 us
    dot_general x1, matrix products, chunk_plan(): jnp.einsum('ham,hmr->ar', theirs, shapes_received, preferred_element_type...  3.91 us
    ppermute x8, waiting for transfers between devices, other_core(): return lax.ppermute(value, 'diam', SWAP)  3.43 us
  transfers between devices with their start and end apart: 12, of which 8 were waited for; matrix products, arithmetic and copies ran while one was open for 15% of the time, Pallas kernels for 0%

profile of v1, /device:TPU:1, one launch (start us, length us, event | category | flops | bytes accessed | tf_op | source)
XLA Modules:
  0.0 101.4 jit_solution(17523021051338704440)
XLA Ops:
  0.0 0.8 compare_convert_fusion
  1.0 1.0 reshape.109
  2.5 3.2 %convolution_convert_fusion.1 = bf16[8,32,200]{2,1,0:T(8,128)(2,1)S(1)} fusion(bf16[8,32,1024]{2,1,0:T(8,128)(2,1)S(1)} %bitcast.125, bf16[8,200,1024]{2,1,0:T(8,128)(2,1)} %bitcast.122), kind=kOutput, calls=%fused_computation.8 | convolution fusion | flops 104908800 | bytes 3903488 | tf_op jit(solution)/shard_map/hcr,hmr->hcm/dot_general | solution.py:129
  6.0 3.5 %convert_element_type.117 = bf16[400,8,200]{2,1,0:T(8,128)(2,1)} reshape(bf16[400,1600]{1,0:T(8,128)(2,1)S(1)} %convert_bitcast_fusion) | data formatting | bytes 2560000 | tf_op jit(solution)/shard_map/convert_element_type | solution.py:114
  9.5 1.8 %copy.23 = bf16[8,400,200]{2,1,0:T(8,128)(2,1)S(1)} copy(bf16[8,400,200]{2,0,1:T(8,128)(2,1)} %bitcast.121) | data formatting | bytes 2560000 | tf_op jit(solution)/shard_map/convert_element_type | solution.py:114
  11.2 1.0 select_bitcast_fusion
  14.2 6.5 %all-to-all-start = ((bf16[8,32,200]{2,1,0:T(8,128)(2,1)}), bf16[8,32,200]{2,1,0:T(8,128)(2,1)}, u32[]{:S(2)}, u32[]{:S(2)}) async-start(bf16[8,32,200]{2,1,0:T(8,128)(2,1)} %maximum_select_fusion.1), calls=%async_computation | async-start | bytes 262144 | tf_op jit(solution)/shard_map/all_to_all | solution.py:137
  20.8 6.2 %all-to-all-done = bf16[8,32,200]{2,1,0:T(8,128)(2,1)} async-done(((bf16[8,32,200]{2,1,0:T(8,128)(2,1)}), bf16[8,32,200]{2,1,0:T(8,128)(2,1)}, u32[]{:S(2)}, u32[]{:S(2)}) %all-to-all-start) | async-done | bytes 102432 | tf_op jit(solution)/shard_map/all_to_all | solution.py:137
  27.0 0.9 convert_reduce_fusion.4
  28.0 2.0 %collective-permute-start.2 = (bf16[32,200]{1,0:T(8,128)(2,1)S(1)}, bf16[32,200]{1,0:T(8,128)(2,1)S(1)}, u32[]{:S(2)}, u32[]{:S(2)}) collective-permute-start(bf16[32,200]{1,0:T(8,128)(2,1)S(1)} %divide_convert_fusion.4), channel_id=1, source_target_pairs={{0,1},{1,0},{2,3},{3,2},{4,5},{5,4},{6,7},{7,6},{8,9},{9,8},{10,11... | collective-permute-start | bytes 38408 | tf_op jit(solution)/shard_map/ppermute | solution.py:104
  29.9 2.0 %maximum_select_fusion = bf16[8,400,200]{2,1,0:T(8,128)(2,1)S(1)} fusion(bf16[4,400,200]{2,1,0:T(8,128)(2,1)} %collective-permute-done.1, bf16[4,400,200]{2,1,0:T(8,128)(2,1)S(1)} %fusion.2, pred[]{:T(512)S(6)} %eq.61), kind=kLoop, calls=%fused_computation.1 | loop fusion | flops 1920000 | bytes 2560001 | tf_op jit(solution)/shard_map/jit(_where)/select_n | solution.py:107
  32.6 9.1 %all_to_all.30 = bf16[8,32,200]{2,1,0:T(8,128)(2,1)S(1)} all-to-all(bf16[8,32,200]{2,1,0:T(8,128)(2,1)S(1)} %fusion.3), channel_id=1, replica_groups=mesh['grp'=2,'rows'=8,'diam'=2] {'rows'}, dimensions={0} | all-to-all | bytes 204800 | tf_op jit(solution)/shard_map/all_to_all | solution.py:137
  41.7 1.3 %collective-permute-start.3 = (bf16[32,200]{1,0:T(8,128)(2,1)S(1)}, bf16[32,200]{1,0:T(8,128)(2,1)S(1)}, u32[]{:S(2)}, u32[]{:S(2)}) collective-permute-start(bf16[32,200]{1,0:T(8,128)(2,1)S(1)} %divide_convert_fusion.3), channel_id=1, source_target_pairs={{0,1},{1,0},{2,3},{3,2},{4,5},{5,4},{6,7},{7,6},{8,9},{9,8},{10,11... | collective-permute-start | bytes 38408 | tf_op jit(solution)/shard_map/ppermute | solution.py:104
  43.0 0.8 collective-permute-done.3
  44.4 8.6 %all_to_all.31 = bf16[8,32,200]{2,1,0:T(8,128)(2,1)S(1)} all-to-all(bf16[8,32,200]{2,1,0:T(8,128)(2,1)S(1)} %fusion.4), channel_id=1, replica_groups=mesh['grp'=2,'rows'=8,'diam'=2] {'rows'}, dimensions={0} | all-to-all | bytes 204800 | tf_op jit(solution)/shard_map/all_to_all | solution.py:137
  53.0 1.8 %collective-permute-start.4 = (bf16[32,200]{1,0:T(8,128)(2,1)S(1)}, bf16[32,200]{1,0:T(8,128)(2,1)S(1)}, u32[]{:S(2)}, u32[]{:S(2)}) collective-permute-start(bf16[32,200]{1,0:T(8,128)(2,1)S(1)} %divide_convert_fusion.2), channel_id=1, source_target_pairs={{0,1},{1,0},{2,3},{3,2},{4,5},{5,4},{6,7},{7,6},{8,9},{9,8},{10,11... | collective-permute-start | bytes 38408 | tf_op jit(solution)/shard_map/ppermute | solution.py:104
  54.8 0.8 collective-permute-done.4
  55.9 0.9 fusion.5
  56.8 3.5 %all-to-all-start.3 = ((bf16[8,32,200]{2,1,0:T(8,128)(2,1)}), bf16[8,32,200]{2,1,0:T(8,128)(2,1)S(1)}, u32[]{:S(2)}, u32[]{:S(2)}) async-start(bf16[8,32,200]{2,1,0:T(8,128)(2,1)} %fusion.5), calls=%async_computation.3 | async-start | bytes 262144 | tf_op jit(solution)/shard_map/all_to_all | solution.py:137
  60.7 5.8 %all-to-all-done.3 = bf16[8,32,200]{2,1,0:T(8,128)(2,1)S(1)} async-done(((bf16[8,32,200]{2,1,0:T(8,128)(2,1)}), bf16[8,32,200]{2,1,0:T(8,128)(2,1)S(1)}, u32[]{:S(2)}, u32[]{:S(2)}) %all-to-all-start.3) | async-done | bytes 102432 | tf_op jit(solution)/shard_map/all_to_all | solution.py:137
  66.6 1.7 %collective-permute-start.5 = (bf16[32,200]{1,0:T(8,128)(2,1)S(1)}, bf16[32,200]{1,0:T(8,128)(2,1)S(1)}, u32[]{:S(2)}, u32[]{:S(2)}) collective-permute-start(bf16[32,200]{1,0:T(8,128)(2,1)S(1)} %divide_convert_fusion.1), channel_id=1, source_target_pairs={{0,1},{1,0},{2,3},{3,2},{4,5},{5,4},{6,7},{7,6},{8,9},{9,8},{10,11... | collective-permute-start | bytes 38408 | tf_op jit(solution)/shard_map/ppermute | solution.py:104
  68.3 0.8 collective-permute-done.5
  69.4 0.9 fusion.6
  70.3 3.4 %all-to-all-start.4 = ((bf16[8,32,200]{2,1,0:T(8,128)(2,1)}), bf16[8,32,200]{2,1,0:T(8,128)(2,1)S(1)}, u32[]{:S(2)}, u32[]{:S(2)}) async-start(bf16[8,32,200]{2,1,0:T(8,128)(2,1)} %fusion.6), calls=%async_computation.4 | async-start | bytes 262144 | tf_op jit(solution)/shard_map/all_to_all | solution.py:137
  73.7 6.2 %all-to-all-done.4 = bf16[8,32,200]{2,1,0:T(8,128)(2,1)S(1)} async-done(((bf16[8,32,200]{2,1,0:T(8,128)(2,1)}), bf16[8,32,200]{2,1,0:T(8,128)(2,1)S(1)}, u32[]{:S(2)}, u32[]{:S(2)}) %all-to-all-start.4) | async-done | bytes 102432 | tf_op jit(solution)/shard_map/all_to_all | solution.py:137
  80.6 3.4 %all-to-all-start.5 = ((bf16[8,32,200]{2,1,0:T(8,128)(2,1)}), bf16[8,32,200]{2,1,0:T(8,128)(2,1)S(1)}, u32[]{:S(2)}, u32[]{:S(2)}) async-start(bf16[8,32,200]{2,1,0:T(8,128)(2,1)} %broadcast_in_dim.21), calls=%async_computation.5 | async-start | bytes 262144 | tf_op jit(solution)/shard_map/all_to_all | solution.py:152
  84.2 5.9 %all-to-all-done.5 = bf16[8,32,200]{2,1,0:T(8,128)(2,1)S(1)} async-done(((bf16[8,32,200]{2,1,0:T(8,128)(2,1)}), bf16[8,32,200]{2,1,0:T(8,128)(2,1)S(1)}, u32[]{:S(2)}, u32[]{:S(2)}) %all-to-all-start.5) | async-done | bytes 102432 | tf_op jit(solution)/shard_map/all_to_all | solution.py:152
  90.1 2.8 %collective-permute-start.6 = (bf16[8,32,200]{2,1,0:T(8,128)(2,1)S(1)}, bf16[8,32,200]{2,1,0:T(8,128)(2,1)S(1)}, u32[]{:S(2)}, u32[]{:S(2)}) collective-permute-start(bf16[8,32,200]{2,1,0:T(8,128)(2,1)S(1)} %all-to-all-done.5), channel_id=1, source_target_pairs={{0,1},{1,0},{2,3},{3,2},{4,5},{5,4},{6,7},{7,6},{8,9},{9,8},{10,11... | collective-permute-start | bytes 307208 | tf_op jit(solution)/shard_map/ppermute | solution.py:104
  93.0 0.9 collective-permute-done.6
  94.6 1.8 %copy-done.1 = bf16[1024,1600]{0,1:T(8,128)(2,1)S(1)} copy-done((bf16[1024,1600]{0,1:T(8,128)(2,1)S(1)}, bf16[1024,1600]{0,1:T(8,128)(2,1)}, u32[]{:S(2)}) %copy-start.1) | copy-done | bytes 3276824
  96.3 1.2 %convolution_bitcast_fusion.1 = f32[256,1024]{1,0:T(8,128)S(1)} fusion(bf16[8,256,200]{2,1,0:T(8,128)(2,1)S(1)} %bitcast.127, bf16[8,200,1024]{2,1,0:T(8,128)(2,1)S(1)} %bitcast.124), kind=kOutput, calls=%fused_computation.3 | convolution fusion | flops 838860800 | bytes 5144576 | tf_op jit(solution)/shard_map/ham,hmr->ar/dot_general | solution.py:165
  97.5 3.9 %fusion.1 = bf16[256,1024]{1,0:T(8,128)(2,1)} fusion(f32[256,1024]{1,0:T(8,128)S(1)} %convolution_bitcast_fusion.1, bf16[8,256,200]{2,1,0:T(8,128)(2,1)S(1)} %bitcast.126, bf16[8,200,1024]{2,1,0:T(8,128)(2,1)} %collective-permute-done.7), kind=kOutput, calls=%fused_computation.7 | convolution fusion | flops 839385088 | bytes 5668864 | tf_op jit(solution)/shard_map/ham,hmr->ar/dot_general | solution.py:165
  (51 shorter events, 6.7 us)
Async XLA Ops:
  0.0 2.0 %copy-start = (bf16[1024,512]{1,0:T(8,128)(2,1)S(1)}, bf16[1024,512]{1,0:T(8,128)(2,1)}, u32[]{:S(2)}) copy-start(bf16[1024,512]{1,0:T(8,128)(2,1)} %param.7) | copy-start | bytes 3145732
  2.5 3.3 %copy-start.2 = (f32[1600,400]{0,1:T(8,128)S(1)}, f32[1600,400]{0,1:T(8,128)}, u32[]{:S(2)}) copy-start(f32[1600,400]{0,1:T(8,128)} %param.9) | copy-start | bytes 7680004
  5.7 7.7 %collective-permute-start = (bf16[4,32,200]{2,1,0:T(8,128)(2,1)S(1)}, bf16[4,32,200]{2,1,0:T(8,128)(2,1)S(1)}, u32[]{:S(2)}, u32[]{:S(2)}) collective-permute-start(bf16[4,32,200]{2,1,0:T(8,128)(2,1)S(1)} %get-tuple-element.12), channel_id=1, source_target_pairs={{0,1},{1,0},{2,3},{3,2},{4,5},{5,4},{6,7},{7,6},{8,9},{9,8},{10,11... | collective-permute-start | bytes 153608 | tf_op jit(solution)/shard_map/ppermute | solution.py:104
  12.2 17.7 %collective-permute-start.1 = (bf16[4,400,200]{2,1,0:T(8,128)(2,1)}, bf16[4,400,200]{2,1,0:T(8,128)(2,1)}, u32[]{:S(2)}, u32[]{:S(2)}) collective-permute-start(bf16[4,400,200]{2,1,0:T(8,128)(2,1)} %select_bitcast_fusion), channel_id=1, source_target_pairs={{0,1},{1,0},{2,3},{3,2},{4,5},{5,4},{6,7},{7,6},{8,9},{9,8},{10,11... | collective-permute-start | bytes 1920008 | tf_op jit(solution)/shard_map/ppermute | solution.py:104
  14.2 12.9 %all-to-all-start = ((bf16[8,32,200]{2,1,0:T(8,128)(2,1)}), bf16[8,32,200]{2,1,0:T(8,128)(2,1)}, u32[]{:S(2)}, u32[]{:S(2)}) async-start(bf16[8,32,200]{2,1,0:T(8,128)(2,1)} %maximum_select_fusion.1), calls=%async_computation | async-start | bytes 262144 | tf_op jit(solution)/shard_map/all_to_all | solution.py:137
  28.0 4.1 %collective-permute-start.2 = (bf16[32,200]{1,0:T(8,128)(2,1)S(1)}, bf16[32,200]{1,0:T(8,128)(2,1)S(1)}, u32[]{:S(2)}, u32[]{:S(2)}) collective-permute-start(bf16[32,200]{1,0:T(8,128)(2,1)S(1)} %divide_convert_fusion.4), channel_id=1, source_target_pairs={{0,1},{1,0},{2,3},{3,2},{4,5},{5,4},{6,7},{7,6},{8,9},{9,8},{10,11... | collective-permute-start | bytes 38408 | tf_op jit(solution)/shard_map/ppermute | solution.py:104
  41.7 2.2 %collective-permute-start.3 = (bf16[32,200]{1,0:T(8,128)(2,1)S(1)}, bf16[32,200]{1,0:T(8,128)(2,1)S(1)}, u32[]{:S(2)}, u32[]{:S(2)}) collective-permute-start(bf16[32,200]{1,0:T(8,128)(2,1)S(1)} %divide_convert_fusion.3), channel_id=1, source_target_pairs={{0,1},{1,0},{2,3},{3,2},{4,5},{5,4},{6,7},{7,6},{8,9},{9,8},{10,11... | collective-permute-start | bytes 38408 | tf_op jit(solution)/shard_map/ppermute | solution.py:104
  53.0 2.6 %collective-permute-start.4 = (bf16[32,200]{1,0:T(8,128)(2,1)S(1)}, bf16[32,200]{1,0:T(8,128)(2,1)S(1)}, u32[]{:S(2)}, u32[]{:S(2)}) collective-permute-start(bf16[32,200]{1,0:T(8,128)(2,1)S(1)} %divide_convert_fusion.2), channel_id=1, source_target_pairs={{0,1},{1,0},{2,3},{3,2},{4,5},{5,4},{6,7},{7,6},{8,9},{9,8},{10,11... | collective-permute-start | bytes 38408 | tf_op jit(solution)/shard_map/ppermute | solution.py:104
  56.8 27.2 %copy-start.3 = (s32[16]{0:T(128)S(1)}, s32[16]{0:T(128)}, u32[]{:S(2)}) copy-start(s32[16]{0:T(128)} %param.11) | copy-start | bytes 196
  56.8 9.7 %all-to-all-start.3 = ((bf16[8,32,200]{2,1,0:T(8,128)(2,1)}), bf16[8,32,200]{2,1,0:T(8,128)(2,1)S(1)}, u32[]{:S(2)}, u32[]{:S(2)}) async-start(bf16[8,32,200]{2,1,0:T(8,128)(2,1)} %fusion.5), calls=%async_computation.3 | async-start | bytes 262144 | tf_op jit(solution)/shard_map/all_to_all | solution.py:137
  60.3 37.2 %collective-permute-start.7 = (bf16[8,200,1024]{2,1,0:T(8,128)(2,1)}, bf16[8,200,1024]{2,1,0:T(8,128)(2,1)}, u32[]{:S(2)}, u32[]{:S(2)}) collective-permute-start(bf16[8,200,1024]{2,1,0:T(8,128)(2,1)} %bitcast.123), channel_id=1, source_target_pairs={{0,1},{1,0},{2,3},{3,2},{4,5},{5,4},{6,7},{7,6},{8,9},{9,8},{10,11... | collective-permute-start | bytes 9830408 | tf_op jit(solution)/shard_map/ppermute | solution.py:104
  66.6 2.5 %collective-permute-start.5 = (bf16[32,200]{1,0:T(8,128)(2,1)S(1)}, bf16[32,200]{1,0:T(8,128)(2,1)S(1)}, u32[]{:S(2)}, u32[]{:S(2)}) collective-permute-start(bf16[32,200]{1,0:T(8,128)(2,1)S(1)} %divide_convert_fusion.1), channel_id=1, source_target_pairs={{0,1},{1,0},{2,3},{3,2},{4,5},{5,4},{6,7},{7,6},{8,9},{9,8},{10,11... | collective-permute-start | bytes 38408 | tf_op jit(solution)/shard_map/ppermute | solution.py:104
  70.3 9.6 %all-to-all-start.4 = ((bf16[8,32,200]{2,1,0:T(8,128)(2,1)}), bf16[8,32,200]{2,1,0:T(8,128)(2,1)S(1)}, u32[]{:S(2)}, u32[]{:S(2)}) async-start(bf16[8,32,200]{2,1,0:T(8,128)(2,1)} %fusion.6), calls=%async_computation.4 | async-start | bytes 262144 | tf_op jit(solution)/shard_map/all_to_all | solution.py:137
  80.6 9.5 %all-to-all-start.5 = ((bf16[8,32,200]{2,1,0:T(8,128)(2,1)}), bf16[8,32,200]{2,1,0:T(8,128)(2,1)S(1)}, u32[]{:S(2)}, u32[]{:S(2)}) async-start(bf16[8,32,200]{2,1,0:T(8,128)(2,1)} %broadcast_in_dim.21), calls=%async_computation.5 | async-start | bytes 262144 | tf_op jit(solution)/shard_map/all_to_all | solution.py:152
  90.1 3.8 %collective-permute-start.6 = (bf16[8,32,200]{2,1,0:T(8,128)(2,1)S(1)}, bf16[8,32,200]{2,1,0:T(8,128)(2,1)S(1)}, u32[]{:S(2)}, u32[]{:S(2)}) collective-permute-start(bf16[8,32,200]{2,1,0:T(8,128)(2,1)S(1)} %all-to-all-done.5), channel_id=1, source_target_pairs={{0,1},{1,0},{2,3},{3,2},{4,5},{5,4},{6,7},{7,6},{8,9},{9,8},{10,11... | collective-permute-start | bytes 307208 | tf_op jit(solution)/shard_map/ppermute | solution.py:104
  94.4 1.9 %copy-start.1 = (bf16[1024,1600]{0,1:T(8,128)(2,1)S(1)}, bf16[1024,1600]{0,1:T(8,128)(2,1)}, u32[]{:S(2)}) copy-start(bf16[1024,1600]{0,1:T(8,128)(2,1)} %param.6) | copy-start | bytes 9830404

commit v2 on v0

--- a/solution.py
+++ b/solution.py
@@ -1,14 +1,20 @@
+import functools
 import math
 
 import jax
 import jax.numpy as jnp
 from jax import lax
+from jax.experimental import pallas as pl
+from jax.experimental.pallas import tpu as pltpu
 from jax.sharding import PartitionSpec as P
 
 NBLADE = 16
 MODES = 200
 NHARM = 16
 ITERS = 4
+SWAP = [(0, 1), (1, 0)]
+F32 = jnp.float32
+BF16 = jnp.bfloat16
 
 
 def cyclic_rows(blade_order):
@@ -26,7 +32,7 @@
     return jnp.dot(onehot, cyclic_tab, precision=lax.Precision.HIGHEST)
 
 
-def on_device(phi, loads, harm_diam, mistuning, dyn_diag, blade_order):
+def general_plan(phi, loads, harm_diam, mistuning, dyn_diag, blade_order):
     rows_dev = phi.shape[0]
     half_modes = phi.shape[1]
     local_diam = half_modes // MODES
@@ -84,8 +90,218 @@
     return blades
 
 
+VMEM = pl.BlockSpec(memory_space=pltpu.VMEM)
+SMEM = pl.BlockSpec(memory_space=pltpu.SMEM)
+HBM = pl.BlockSpec(memory_space=pltpu.HBM)
+LIMIT = pltpu.CompilerParams(vmem_limit_bytes=24 << 20)
+
+
+def nt_dot(left, right):
+    return lax.dot_general(left, right, (((1,), (1,)), ((), ())), preferred_element_type=F32)
+
+
+def pick(core, even, odd):
+    return jnp.where(core == 0, even, odd)
+
+
+def force_kernel(columns, core_ref, harm_ref, loads_hbm, phi_hbm, mine_ref, send_ref, loads_ref, phi_ref, combined_ref, load_sem, phi_sem):
+    core = core_ref[0]
+    local_diam = phi_ref.shape[0]
+    load_copy = pltpu.make_async_copy(loads_hbm, loads_ref, load_sem)
+    load_copy.start()
+    copies = [
+        pltpu.make_async_copy(phi_hbm.at[k], phi_ref.at[k], phi_sem.at[k])
+        for k in range(local_diam)
+    ]
+    for copy in copies:
+        copy.start()
+    shape = (local_diam * columns, loads_ref.shape[1])
+    row = lax.broadcasted_iota(jnp.int32, shape, 0)
+    col = lax.broadcasted_iota(jnp.int32, shape, 1)
+    harmonic = col // columns
+    excited = jnp.zeros(shape, jnp.int32)
+    for k in range(NHARM):
+        excited = jnp.where(harmonic == k, harm_ref[k], excited)
+    hit = (row % columns == col % columns) & (excited == row // columns + core * local_diam)
+    spread = jnp.where(hit, 1.0, 0.0).astype(BF16)
+    load_copy.wait()
+    combined_ref[...] = nt_dot(spread, loads_ref[...]).astype(BF16)
+    for k in range(0, local_diam, 2):
+        part = []
+        for at in (k, k + 1):
+            copies[at].wait()
+            part.append(nt_dot(combined_ref[at * columns : (at + 1) * columns], phi_ref[at]))
+        mine_ref[k // 2] = pick(core, part[0], part[1]).astype(BF16)
+        send_ref[k // 2] = pick(core, part[1], part[0]).astype(BF16)
+
+
+def regroup_kernel(core_ref, stiff_ref, keep_ref, send_ref):
+    core = core_ref[0]
+    for k in range(0, 2 * keep_ref.shape[1], 2):
+        for chunk in range(2):
+            pair = [
+                stiff_ref[chunk * MODES : (chunk + 1) * MODES, (k + odd) * MODES : (k + odd + 1) * MODES]
+                for odd in range(2)
+            ]
+            keep_ref[pick(core, chunk, 1 - chunk), k // 2] = pick(core, pair[0], pair[1]).astype(BF16)
+            send_ref[pick(core, 1 - chunk, chunk), k // 2] = pick(core, pair[1], pair[0]).astype(BF16)
+
+
+def product_kernel(source, core_ref, amp_ref, keep_ref, recv_ref, *rest):
+    prev_ref, out_ref = rest if len(rest) == 2 else (None, rest[0])
+    core = core_ref[0]
+    slots = keep_ref.shape[1]
+    for half, ref in ((core, keep_ref), (1 - core, recv_ref)):
+        for k in range(slots):
+            at = half * slots + k
+            value = jnp.dot(amp_ref[...], ref[source, k], preferred_element_type=F32)
+            if prev_ref is not None:
+                value = value + prev_ref[at]
+            out_ref[at] = value.astype(out_ref.dtype)
+
+
+def blades_kernel(crossed, core_ref, table_ref, amp_ref, own_ref, recv_ref, *rest):
+    prev_ref, out_ref = rest if len(rest) == 2 else (None, rest[0])
+    core = core_ref[0]
+    local_diam, columns, _ = amp_ref.shape
+    half_count = local_diam // 2
+    odd = 1 - core if crossed else core
+    total = None
+    for half, ref in ((core, own_ref), (1 - core, recv_ref)):
+        for k in range(half_count):
+            at = half * half_count + k
+            amp = amp_ref[at].astype(F32)
+            weights = jnp.concatenate(
+                [(table_ref[s, 2 * at + odd] * amp).astype(BF16) for s in range(local_diam)]
+            )
+            value = jnp.dot(weights, ref[2 * k + odd], preferred_element_type=F32)
+            total = value if total is None else total + value
+    total = total.reshape(out_ref.shape)
+    if prev_ref is not None:
+        total = total + prev_ref[...]
+    out_ref[...] = total.astype(out_ref.dtype)
+
+
+def chunk_plan(phi, loads, harm_diam, mistuning, dyn_diag, blade_order):
+    rows_dev, half_modes = phi.shape
+    local_diam = half_modes // MODES
+    columns = loads.shape[1] // NHARM
+    core = lax.axis_index("diam")
+    own_diam = 2 * lax.axis_index("rows") + core
+    first_diam = core * local_diam
+    core_arg = core.reshape(1).astype(jnp.int32)
+    pairs = local_diam // 2
+
+    def other_core(value):
+        return lax.ppermute(value, "diam", SWAP)
+
+    def in_half_order(own, received):
+        return jnp.where(
+            core == 0, jnp.concatenate([own, received]), jnp.concatenate([received, own])
+        )
+
+    def exchange(slots):
+        return lax.all_to_all(slots, "rows", 0, 0, tiled=True)
+
+    def row_total(got):
+        return jnp.sum(got.astype(F32), axis=0)
+
+    half_slots = jax.ShapeDtypeStruct((pairs, columns, MODES), BF16)
+    shapes = phi.T.reshape(local_diam, MODES, rows_dev)
+    mine, send = pl.pallas_call(
+        functools.partial(force_kernel, columns),
+        name="force",
+        in_specs=[SMEM, SMEM, HBM, HBM],
+        out_specs=[VMEM, VMEM],
+        out_shape=[half_slots, half_slots],
+        scratch_shapes=[
+            pltpu.VMEM(loads.shape, BF16),
+            pltpu.VMEM(shapes.shape, BF16),
+            pltpu.VMEM((local_diam * columns, rows_dev), BF16),
+            pltpu.SemaphoreType.DMA,
+            pltpu.SemaphoreType.DMA((local_diam,)),
+        ],
+        compiler_params=pltpu.CompilerParams(vmem_limit_bytes=60 << 20),
+    )(core_arg, harm_diam, loads, shapes)
+    force_slots = in_half_order(mine, other_core(send))
+    force_slots, stiff, order, shapes_sent = lax.optimization_barrier(
+        (force_slots, mistuning.T, blade_order, shapes)
+    )
+    force_got = exchange(force_slots)
+
+    group = jax.ShapeDtypeStruct((2, pairs, MODES, MODES), BF16)
+    keep, sent = pl.pallas_call(
+        regroup_kernel,
+        name="regroup",
+        in_specs=[SMEM, VMEM],
+        out_specs=[VMEM, VMEM],
+        out_shape=[group, group],
+        compiler_params=LIMIT,
+        cost_estimate=pl.CostEstimate(
+            flops=2 * mistuning.size, bytes_accessed=8 * mistuning.size, transcendentals=0
+        ),
+    )(core_arg, stiff)
+    recv = other_core(sent)
+    shapes_received = other_core(shapes_sent)
+    table = lax.dynamic_slice_in_dim(cyclic_rows(order), first_diam, local_diam, 0)
+    dyn_own = lax.dynamic_slice_in_dim(dyn_diag, own_diam * MODES, MODES, 0)[None, :]
+    force_got, keep, table, dyn_own = lax.optimization_barrier((force_got, keep, table, dyn_own))
+
+    slots_shape = (local_diam, columns, MODES)
+
+    def product(source, *operands):
+        return pl.pallas_call(
+            functools.partial(product_kernel, source),
+            name="product",
+            in_specs=[SMEM] + [VMEM] * len(operands),
+            out_specs=VMEM,
+            out_shape=jax.ShapeDtypeStruct(slots_shape, BF16 if source else F32),
+            compiler_params=LIMIT,
+        )(core_arg, *operands)
+
+    force = row_total(force_got)
+    amp = force / dyn_own
+    for sweep in range(ITERS):
+        amp_low = amp.astype(BF16)
+        amp_other = other_core(amp_low)
+        part = product(0, amp_low, keep, recv)
+        part, amp_other = lax.optimization_barrier((part, amp_other))
+        part = product(1, amp_other, keep, recv, part)
+        amp = (force - row_total(exchange(part))) / dyn_own
+        if sweep == 0:
+            amp, shapes_received = lax.optimization_barrier((amp, shapes_received))
+    same = exchange(jnp.broadcast_to(amp.astype(BF16)[None], slots_shape))
+    crossed = other_core(same)
+
+    def blades(is_crossed, amps, *prev):
+        return pl.pallas_call(
+            functools.partial(blades_kernel, is_crossed),
+            name="blades",
+            in_specs=[SMEM, SMEM] + [VMEM] * (3 + len(prev)),
+            out_specs=VMEM,
+            out_shape=jax.ShapeDtypeStruct(
+                (local_diam, columns, rows_dev), BF16 if is_crossed else F32
+            ),
+            compiler_params=LIMIT,
+            cost_estimate=pl.CostEstimate(
+                flops=2 * local_diam * columns * phi.size,
+                bytes_accessed=4 * phi.size,
+                transcendentals=0,
+            ),
+        )(core_arg, table, amps, shapes, shapes_received, *prev)
+
+    part = blades(False, same)
+    part, crossed = lax.optimization_barrier((part, crossed))
+    return blades(True, crossed, part)
+
+
 def solution(mesh):
     placed = (P("rows", "diam"), P("rows", None), P(), P("diam", "rows"), P("grp"), P())
+    one_each = mesh.shape["rows"] * 2 == NBLADE and mesh.shape["diam"] == 2
     return jax.shard_map(
-        on_device, mesh=mesh, in_specs=placed, out_specs=P("diam", "grp", "rows"), check_vma=False
-    )
+        chunk_plan if one_each else general_plan,
+        mesh=mesh,
+        in_specs=placed,
+        out_specs=P("diam", "grp", "rows"),
+        check_vma=False,
+    )

time: 432 us -> 92.6 us (0.21)
  waiting for transfers between devices: 351 us -> 6.68 us
  blocking collectives: 17.1 us -> 43.9 us
  local copies, waits for them, and re-layouts: 22.1 us -> 0.79 us
  matrix products: 21.2 us -> 0.23 us
  Pallas kernels: 0 us -> 20.7 us
  starting transfers between devices: 0.39 us -> 16.9 us
  between operations: 13.6 us -> 0.14 us
    psum x5 -> x0, waiting for transfers between devices: 340 us -> none  [row_total(): return lax.psum(partial_term, 'rows')]
    all_to_all x0 -> x5, blocking collectives: none -> 43.9 us  [exchange(): return lax.all_to_all(slots, 'rows', 0, 0, tiled=True)]
    dot_general x8 -> x0, matrix products: 20.9 us -> none  [the longest x4 16 us: on_device(): jnp.dot(mistuning, col_part, precision=lax.Precision.HIGHEST, preferred_e...]
    pallas_call x0 -> x12, Pallas kernels: none -> 20.7 us  [the longest x2 9.14 us: blades(): pl.pallas_call(functools.partial(blades_kernel, is_crossed), name='blades...]
    all_gather x4 -> x0, blocking collectives: 17.1 us -> none  [on_device(): full_amp = lax.all_gather(amp_half, 'diam', axis=0, tiled=True)]
    unnamed x14 -> x4, local copies, waits for them, and re-layouts: 11.8 us -> 0.01 us
    unnamed x7 -> x0, waiting for transfers between devices: 10.7 us -> none
    ppermute x0 -> x8, starting transfers between devices: none -> 10 us  [other_core(): return lax.ppermute(value, 'diam', SWAP)]
  transfers between devices with their start and end apart: 6 -> 9, of which waited for: 6 -> 6; matrix products, arithmetic and copies ran while one was open for 0% -> 2% of each run, Pallas kernels for 0% -> 9%
where the time goes in v2:
time: 92.6 us; the launch traced here: 92 us
  blocking collectives  43.9 us (47%)
  Pallas kernels  20.7 us (22%)
  starting transfers between devices  16.9 us (18%)
  waiting for transfers between devices  6.68 us (7%)
  other arithmetic  2.73 us (3%)
    all_to_all x5, blocking collectives, exchange(): return lax.all_to_all(slots, 'rows', 0, 0, tiled=True)  43.9 us
    ppermute x8, starting transfers between devices, other_core(): return lax.ppermute(value, 'diam', SWAP)  10 us
    pallas_call x2, Pallas kernels, blades(): pl.pallas_call(functools.partial(blades_kernel, is_crossed), name='blades...  9.14 us
    all_to_all x1, starting transfers between devices, exchange(): return lax.all_to_all(slots, 'rows', 0, 0, tiled=True)  6.88 us
    pallas_call x1, Pallas kernels, chunk_plan(): pl.pallas_call(functools.partial(force_kernel, columns), name='force', in...  6.86 us
    ppermute x8, waiting for transfers between devices, other_core(): return lax.ppermute(value, 'diam', SWAP)  3.75 us
    all_to_all x1, waiting for transfers between devices, exchange(): return lax.all_to_all(slots, 'rows', 0, 0, tiled=True)  2.93 us
    pallas_call x1, Pallas kernels, chunk_plan(): pl.pallas_call(regroup_kernel, name='regroup', in_specs=[SMEM, VMEM], out...  2.69 us
  transfers between devices with their start and end apart: 9, of which 6 were waited for; matrix products, arithmetic and copies ran while one was open for 2% of the time, Pallas kernels for 9%

profile of v2, /device:TPU:1, one launch (start us, length us, event | category | flops | bytes accessed | tf_op | source)
XLA Modules:
  0.0 92.0 jit_solution(3487177567438976611)
XLA Ops:
  0.0 6.9 %force.1 = (bf16[4,32,200]{2,1,0:T(8,128)(2,1)}, bf16[4,32,200]{2,1,0:T(8,128)(2,1)}) custom-call(s32[1]{0:T(128)} %bitcast.core_ref, s32[16]{0:T(128)} %harm_ref.1, bf16[1024,512]{1,0:T(8,128)(2,1)} %loads_hbm.1, bf16[8,200,1024]{2,1,0:T(8,128)(2,1)} %bitcast.2.phi_hbm.own_ref), custom_call_target="tpu_custom_call" | custom-call | tf_op jit(solution)/shard_map/force/pallas_call | solution.py:211
  7.0 1.4 %collective-permute-done = bf16[4,32,200]{2,1,0:T(8,128)(2,1)S(1)} collective-permute-done((bf16[4,32,200]{2,1,0:T(8,128)(2,1)}, bf16[4,32,200]{2,1,0:T(8,128)(2,1)S(1)}, u32[]{:S(2)}, u32[]{:S(2)}) %collective-permute-start) | collective-permute-done | bytes 51232 | tf_op jit(solution)/shard_map/ppermute | solution.py:196
  8.4 1.6 %maximum_select_fusion = bf16[8,32,200]{2,1,0:T(8,128)(2,1)} fusion(bf16[4,32,200]{2,1,0:T(8,128)(2,1)S(1)} %collective-permute-done, bf16[4,32,200]{2,1,0:T(8,128)(2,1)} %get-tuple-element.29, pred[]{:T(512)S(6)} %eq.32), kind=kLoop, calls=%fused_computation.5 | loop fusion | flops 153600 | bytes 204801 | tf_op jit(solution)/shard_map/jit(_where)/select_n | solution.py:199
  10.2 0.8 dynamic_slice.7
  11.0 6.9 %all-to-all-start = ((bf16[8,32,200]{2,1,0:T(8,128)(2,1)}), bf16[8,32,200]{2,1,0:T(8,128)(2,1)}, u32[]{:S(2)}, u32[]{:S(2)}) async-start(bf16[8,32,200]{2,1,0:T(8,128)(2,1)} %maximum_select_fusion), calls=%async_computation | async-start | bytes 262144 | tf_op jit(solution)/shard_map/all_to_all | solution.py:204
  17.9 2.7 %regroup.1 = (bf16[2,4,200,200]{3,2,1,0:T(8,128)(2,1)S(1)}, bf16[2,4,200,200]{3,2,1,0:T(8,128)(2,1)}) custom-call(s32[1]{0:T(128)} %bitcast.core_ref, f32[400,1600]{1,0:T(8,128)S(1)} %bitcast.7), custom_call_target="tpu_custom_call" | custom-call | flops 1280000 | bytes 5120000 | tf_op jit(solution)/shard_map/regroup/pallas_call | solution.py:233
  20.5 0.4 collective-permute-start.1
  21.2 2.9 %all-to-all-done = bf16[8,32,200]{2,1,0:T(8,128)(2,1)} async-done(((bf16[8,32,200]{2,1,0:T(8,128)(2,1)}), bf16[8,32,200]{2,1,0:T(8,128)(2,1)}, u32[]{:S(2)}, u32[]{:S(2)}) %all-to-all-start) | async-done | bytes 102432 | tf_op jit(solution)/shard_map/all_to_all | solution.py:204
  24.2 0.9 %convert_reduce_fusion.4 = f32[32,200]{1,0:T(8,128)S(1)} fusion(bf16[8,32,200]{2,1,0:T(8,128)(2,1)} %all-to-all-done), kind=kLoop, calls=%fused_computation.4 | loop fusion | flops 96000 | bytes 128000 | tf_op jit(solution)/shard_map/reduce_sum | solution.py:207
  25.1 1.8 %collective-permute-start.2 = (bf16[32,200]{1,0:T(8,128)(2,1)S(1)}, bf16[32,200]{1,0:T(8,128)(2,1)S(1)}, u32[]{:S(2)}, u32[]{:S(2)}) collective-permute-start(bf16[32,200]{1,0:T(8,128)(2,1)S(1)} %divide_convert_fusion.3.amp_ref), channel_id=1, source_target_pairs={{0,1},{1,0},{2,3},{3,2},{4,5},{5,4},{6,7},{7,6},{8,9},{9,8},{10,11... | collective-permute-start | bytes 38408 | tf_op jit(solution)/shard_map/ppermute | solution.py:196
  26.9 0.3 product.8.rest_0_
  27.2 0.6 collective-permute-done.2.amp_ref
  27.8 0.3 product.9
  28.0 8.6 %all_to_all.30 = bf16[8,32,200]{2,1,0:T(8,128)(2,1)S(1)} all-to-all(bf16[8,32,200]{2,1,0:T(8,128)(2,1)S(1)} %product.9), channel_id=1, replica_groups=mesh['grp'=2,'rows'=8,'diam'=2] {'rows'}, dimensions={0} | all-to-all | bytes 204800 | tf_op jit(solution)/shard_map/all_to_all | solution.py:204
  36.7 1.8 %collective-permute-start.4 = (bf16[32,200]{1,0:T(8,128)(2,1)S(1)}, bf16[32,200]{1,0:T(8,128)(2,1)S(1)}, u32[]{:S(2)}, u32[]{:S(2)}) collective-permute-start(bf16[32,200]{1,0:T(8,128)(2,1)S(1)} %subtract_divide_fusion.amp_ref), channel_id=1, source_target_pairs={{0,1},{1,0},{2,3},{3,2},{4,5},{5,4},{6,7},{7,6},{8,9},{9,8},{10,11... | collective-permute-start | bytes 38408 | tf_op jit(solution)/shard_map/ppermute | solution.py:196
  38.5 0.3 product.10.rest_0_
  38.7 0.6 collective-permute-done.4.amp_ref
  39.3 0.3 product.11
  39.6 8.6 %all_to_all.31 = bf16[8,32,200]{2,1,0:T(8,128)(2,1)S(1)} all-to-all(bf16[8,32,200]{2,1,0:T(8,128)(2,1)S(1)} %product.11), channel_id=1, replica_groups=mesh['grp'=2,'rows'=8,'diam'=2] {'rows'}, dimensions={0} | all-to-all | bytes 204800 | tf_op jit(solution)/shard_map/all_to_all | solution.py:204
  48.2 1.8 %collective-permute-start.5 = (bf16[32,200]{1,0:T(8,128)(2,1)S(1)}, bf16[32,200]{1,0:T(8,128)(2,1)S(1)}, u32[]{:S(2)}, u32[]{:S(2)}) collective-permute-start(bf16[32,200]{1,0:T(8,128)(2,1)S(1)} %divide_convert_fusion.2.amp_ref), channel_id=1, source_target_pairs={{0,1},{1,0},{2,3},{3,2},{4,5},{5,4},{6,7},{7,6},{8,9},{9,8},{10,11... | collective-permute-start | bytes 38408 | tf_op jit(solution)/shard_map/ppermute | solution.py:196
  50.3 0.6 collective-permute-done.5.amp_ref
  50.8 0.3 product.13
  51.1 8.6 %all_to_all.32 = bf16[8,32,200]{2,1,0:T(8,128)(2,1)S(1)} all-to-all(bf16[8,32,200]{2,1,0:T(8,128)(2,1)S(1)} %product.13), channel_id=1, replica_groups=mesh['grp'=2,'rows'=8,'diam'=2] {'rows'}, dimensions={0} | all-to-all | bytes 204800 | tf_op jit(solution)/shard_map/all_to_all | solution.py:204
  59.7 1.8 %collective-permute-start.6 = (bf16[32,200]{1,0:T(8,128)(2,1)S(1)}, bf16[32,200]{1,0:T(8,128)(2,1)S(1)}, u32[]{:S(2)}, u32[]{:S(2)}) collective-permute-start(bf16[32,200]{1,0:T(8,128)(2,1)S(1)} %divide_convert_fusion.1.amp_ref), channel_id=1, source_target_pairs={{0,1},{1,0},{2,3},{3,2},{4,5},{5,4},{6,7},{7,6},{8,9},{9,8},{10,11... | collective-permute-start | bytes 38408 | tf_op jit(solution)/shard_map/ppermute | solution.py:196
  61.6 0.3 product.14.rest_0_
  61.8 0.6 collective-permute-done.6.amp_ref
  62.4 0.3 product.15
  62.7 8.6 %all_to_all.33 = bf16[8,32,200]{2,1,0:T(8,128)(2,1)S(1)} all-to-all(bf16[8,32,200]{2,1,0:T(8,128)(2,1)S(1)} %product.15), channel_id=1, replica_groups=mesh['grp'=2,'rows'=8,'diam'=2] {'rows'}, dimensions={0} | all-to-all | bytes 204800 | tf_op jit(solution)/shard_map/all_to_all | solution.py:204
  71.3 9.5 %all_to_all.34.amp_ref = bf16[8,32,200]{2,1,0:T(8,128)(2,1)S(1)} all-to-all(bf16[8,32,200]{2,1,0:T(8,128)(2,1)S(1)} %broadcast_in_dim.33), channel_id=1, replica_groups=mesh['grp'=2,'rows'=8,'diam'=2] {'rows'}, dimensions={0} | all-to-all | bytes 204800 | tf_op jit(solution)/shard_map/all_to_all | solution.py:204
  80.8 2.1 %collective-permute-start.7 = (bf16[8,32,200]{2,1,0:T(8,128)(2,1)S(1)}, bf16[8,32,200]{2,1,0:T(8,128)(2,1)S(1)}, u32[]{:S(2)}, u32[]{:S(2)}) collective-permute-start(bf16[8,32,200]{2,1,0:T(8,128)(2,1)S(1)} %all_to_all.34.amp_ref), channel_id=1, source_target_pairs={{0,1},{1,0},{2,3},{3,2},{4,5},{5,4},{6,7},{7,6},{8,9},{9,8},{10,11... | collective-permute-start | bytes 307208 | tf_op jit(solution)/shard_map/ppermute | solution.py:196
  82.9 4.2 %blades.2.rest_0_ = f32[8,32,1024]{2,1,0:T(8,128)S(1)} custom-call(s32[1]{0:T(128)} %bitcast.core_ref, f32[8,16]{1,0:T(8,128)S(1)} %constant_dynamic-slice_fusion.table_ref, bf16[8,32,200]{2,1,0:T(8,128)(2,1)S(1)} %all_to_all.34.amp_ref, bf16[8,200,1024]{2,1,0:T(8,128)(2,1)} %bitcast.2.phi_hbm.own_ref, bf16[8,200,1024]{2,1,0:T(8,128)(2,1)} %collective-permute-done.3.recv_ref), custom_call_target="tpu_custom_call" | custom-call | flops 838860800 | bytes 6553600 | tf_op jit(solution)/shard_map/blades/pallas_call | solution.py:277
  87.1 5.0 %blades.3 = bf16[8,32,1024]{2,1,0:T(8,128)(2,1)} custom-call(s32[1]{0:T(128)} %bitcast.core_ref, f32[8,16]{1,0:T(8,128)S(1)} %constant_dynamic-slice_fusion.table_ref, bf16[8,32,200]{2,1,0:T(8,128)(2,1)S(1)} %collective-permute-done.7.amp_ref, bf16[8,200,1024]{2,1,0:T(8,128)(2,1)} %bitcast.2.phi_hbm.own_ref, ...), custom_call_target="tpu_custom_call" | custom-call | flops 838860800 | bytes 6553600 | tf_op jit(solution)/shard_map/blades/pallas_call | solution.py:277
  (25 shorter events, 1.0 us)
Async XLA Ops:
  0.0 17.9 %copy-start = (f32[1600,400]{0,1:T(8,128)S(1)}, f32[1600,400]{0,1:T(8,128)}, u32[]{:S(2)}) copy-start(f32[1600,400]{0,1:T(8,128)} %param.9) | copy-start | bytes 7680004
  0.0 21.0 %copy-start.1 = (s32[16]{0:T(128)S(1)}, s32[16]{0:T(128)}, u32[]{:S(2)}) copy-start(s32[16]{0:T(128)} %param.11) | copy-start | bytes 196
  6.9 1.5 %collective-permute-start = (bf16[4,32,200]{2,1,0:T(8,128)(2,1)}, bf16[4,32,200]{2,1,0:T(8,128)(2,1)S(1)}, u32[]{:S(2)}, u32[]{:S(2)}) collective-permute-start(bf16[4,32,200]{2,1,0:T(8,128)(2,1)} %get-tuple-element.30), channel_id=1, source_target_pairs={{0,1},{1,0},{2,3},{3,2},{4,5},{5,4},{6,7},{7,6},{8,9},{9,8},{10,11... | collective-permute-start | bytes 153608 | tf_op jit(solution)/shard_map/ppermute | solution.py:196
  10.0 26.6 %collective-permute-start.3 = (bf16[8,200,1024]{2,1,0:T(8,128)(2,1)}, bf16[8,200,1024]{2,1,0:T(8,128)(2,1)}, u32[]{:S(2)}, u32[]{:S(2)}) collective-permute-start(bf16[8,200,1024]{2,1,0:T(8,128)(2,1)} %bitcast.2.phi_hbm.own_ref), channel_id=1, source_target_pairs={{0,1},{1,0},{2,3},{3,2},{4,5},{5,4},{6,7},{7,6},{8,9},{9,8},{10,11... | collective-permute-start | bytes 9830408 | tf_op jit(solution)/shard_map/ppermute | solution.py:196
  11.0 13.2 %all-to-all-start = ((bf16[8,32,200]{2,1,0:T(8,128)(2,1)}), bf16[8,32,200]{2,1,0:T(8,128)(2,1)}, u32[]{:S(2)}, u32[]{:S(2)}) async-start(bf16[8,32,200]{2,1,0:T(8,128)(2,1)} %maximum_select_fusion), calls=%async_computation | async-start | bytes 262144 | tf_op jit(solution)/shard_map/all_to_all | solution.py:204
  20.5 6.4 %collective-permute-start.1 = (bf16[2,4,200,200]{3,2,1,0:T(8,128)(2,1)}, bf16[2,4,200,200]{3,2,1,0:T(8,128)(2,1)S(1)}, u32[]{:S(2)}, u32[]{:S(2)}) collective-permute-start(bf16[2,4,200,200]{3,2,1,0:T(8,128)(2,1)} %get-tuple-element.39), channel_id=1, source_target_pairs={{0,1},{1,0},{2,3},{3,2},{4,5},{5,4},{6,7},{7,6},{8,9},{9,8},{10,11... | collective-permute-start | bytes 1920008 | tf_op jit(solution)/shard_map/ppermute | solution.py:196
  25.1 2.6 %collective-permute-start.2 = (bf16[32,200]{1,0:T(8,128)(2,1)S(1)}, bf16[32,200]{1,0:T(8,128)(2,1)S(1)}, u32[]{:S(2)}, u32[]{:S(2)}) collective-permute-start(bf16[32,200]{1,0:T(8,128)(2,1)S(1)} %divide_convert_fusion.3.amp_ref), channel_id=1, source_target_pairs={{0,1},{1,0},{2,3},{3,2},{4,5},{5,4},{6,7},{7,6},{8,9},{9,8},{10,11... | collective-permute-start | bytes 38408 | tf_op jit(solution)/shard_map/ppermute | solution.py:196
  36.7 2.6 %collective-permute-start.4 = (bf16[32,200]{1,0:T(8,128)(2,1)S(1)}, bf16[32,200]{1,0:T(8,128)(2,1)S(1)}, u32[]{:S(2)}, u32[]{:S(2)}) collective-permute-start(bf16[32,200]{1,0:T(8,128)(2,1)S(1)} %subtract_divide_fusion.amp_ref), channel_id=1, source_target_pairs={{0,1},{1,0},{2,3},{3,2},{4,5},{5,4},{6,7},{7,6},{8,9},{9,8},{10,11... | collective-permute-start | bytes 38408 | tf_op jit(solution)/shard_map/ppermute | solution.py:196
  48.2 2.6 %collective-permute-start.5 = (bf16[32,200]{1,0:T(8,128)(2,1)S(1)}, bf16[32,200]{1,0:T(8,128)(2,1)S(1)}, u32[]{:S(2)}, u32[]{:S(2)}) collective-permute-start(bf16[32,200]{1,0:T(8,128)(2,1)S(1)} %divide_convert_fusion.2.amp_ref), channel_id=1, source_target_pairs={{0,1},{1,0},{2,3},{3,2},{4,5},{5,4},{6,7},{7,6},{8,9},{9,8},{10,11... | collective-permute-start | bytes 38408 | tf_op jit(solution)/shard_map/ppermute | solution.py:196
  59.7 2.6 %collective-permute-start.6 = (bf16[32,200]{1,0:T(8,128)(2,1)S(1)}, bf16[32,200]{1,0:T(8,128)(2,1)S(1)}, u32[]{:S(2)}, u32[]{:S(2)}) collective-permute-start(bf16[32,200]{1,0:T(8,128)(2,1)S(1)} %divide_convert_fusion.1.amp_ref), channel_id=1, source_target_pairs={{0,1},{1,0},{2,3},{3,2},{4,5},{5,4},{6,7},{7,6},{8,9},{9,8},{10,11... | collective-permute-start | bytes 38408 | tf_op jit(solution)/shard_map/ppermute | solution.py:196
  80.8 6.2 %collective-permute-start.7 = (bf16[8,32,200]{2,1,0:T(8,128)(2,1)S(1)}, bf16[8,32,200]{2,1,0:T(8,128)(2,1)S(1)}, u32[]{:S(2)}, u32[]{:S(2)}) collective-permute-start(bf16[8,32,200]{2,1,0:T(8,128)(2,1)S(1)} %all_to_all.34.amp_ref), channel_id=1, source_target_pairs={{0,1},{1,0},{2,3},{3,2},{4,5},{5,4},{6,7},{7,6},{8,9},{9,8},{10,11... | collective-permute-start | bytes 307208 | tf_op jit(solution)/shard_map/ppermute | solution.py:196

commit v3 on v2

--- a/solution.py
+++ b/solution.py
@@ -90,49 +90,52 @@
     return blades
 
 
+def by_parity(arr, parity):
+    pairs = arr.reshape((arr.shape[0] // 2, 2) + arr.shape[1:])
+    return jnp.where(parity == 0, pairs[:, 0], pairs[:, 1])
+
+
 VMEM = pl.BlockSpec(memory_space=pltpu.VMEM)
 SMEM = pl.BlockSpec(memory_space=pltpu.SMEM)
 HBM = pl.BlockSpec(memory_space=pltpu.HBM)
-LIMIT = pltpu.CompilerParams(vmem_limit_bytes=24 << 20)
-
-
-def nt_dot(left, right):
-    return lax.dot_general(left, right, (((1,), (1,)), ((), ())), preferred_element_type=F32)
+LIMIT = pltpu.CompilerParams(vmem_limit_bytes=8 << 20)
 
 
 def pick(core, even, odd):
     return jnp.where(core == 0, even, odd)
 
 
-def force_kernel(columns, core_ref, harm_ref, loads_hbm, phi_hbm, mine_ref, send_ref, loads_ref, phi_ref, combined_ref, load_sem, phi_sem):
-    core = core_ref[0]
+def load_kernel(columns, core_ref, harm_ref, loads_ref, phi_hbm, combined_ref, phi_ref, phi_sem):
     local_diam = phi_ref.shape[0]
-    load_copy = pltpu.make_async_copy(loads_hbm, loads_ref, load_sem)
-    load_copy.start()
+    phi_copy = pltpu.make_async_copy(phi_hbm, phi_ref, phi_sem)
+    phi_copy.start()
+    wide = loads_ref.shape[1]
+    first_diam = core_ref[0] * local_diam
+    col = lax.broadcasted_iota(jnp.int32, (8, wide), 1)
+    key = jnp.zeros((8, wide), jnp.int32)
+    for k in range(NHARM):
+        inside = (col >= k * columns) & (col < (k + 1) * columns)
+        key = jnp.where(inside, (harm_ref[k] - first_diam - k) * columns + col, key)
+    shape = (local_diam * columns, wide)
+    row = lax.broadcasted_iota(jnp.int32, shape, 0)
+    spread = jnp.where(row == jnp.broadcast_to(key[0:1], shape), 1.0, 0.0).astype(BF16)
+    combined = lax.dot_general(
+        spread, loads_ref[...], (((1,), (1,)), ((), ())), preferred_element_type=F32
+    )
+    combined_ref[...] = combined.astype(BF16).reshape(combined_ref.shape)
+    phi_copy.wait()
+
+
+def fetch_kernel(own_hbm, recv_hbm, both_ref, sems):
+    half = own_hbm.shape[0]
     copies = [
-        pltpu.make_async_copy(phi_hbm.at[k], phi_ref.at[k], phi_sem.at[k])
-        for k in range(local_diam)
+        pltpu.make_async_copy(own_hbm, both_ref.at[:half], sems.at[0]),
+        pltpu.make_async_copy(recv_hbm, both_ref.at[half:], sems.at[1]),
     ]
     for copy in copies:
         copy.start()
-    shape = (local_diam * columns, loads_ref.shape[1])
-    row = lax.broadcasted_iota(jnp.int32, shape, 0)
-    col = lax.broadcasted_iota(jnp.int32, shape, 1)
-    harmonic = col // columns
-    excited = jnp.zeros(shape, jnp.int32)
-    for k in range(NHARM):
-        excited = jnp.where(harmonic == k, harm_ref[k], excited)
-    hit = (row % columns == col % columns) & (excited == row // columns + core * local_diam)
-    spread = jnp.where(hit, 1.0, 0.0).astype(BF16)
-    load_copy.wait()
-    combined_ref[...] = nt_dot(spread, loads_ref[...]).astype(BF16)
-    for k in range(0, local_diam, 2):
-        part = []
-        for at in (k, k + 1):
-            copies[at].wait()
-            part.append(nt_dot(combined_ref[at * columns : (at + 1) * columns], phi_ref[at]))
-        mine_ref[k // 2] = pick(core, part[0], part[1]).astype(BF16)
-        send_ref[k // 2] = pick(core, part[1], part[0]).astype(BF16)
+    for copy in copies:
+        copy.wait()
 
 
 def regroup_kernel(core_ref, stiff_ref, keep_ref, send_ref):
@@ -160,26 +163,19 @@
             out_ref[at] = value.astype(out_ref.dtype)
 
 
-def blades_kernel(crossed, core_ref, table_ref, amp_ref, own_ref, recv_ref, *rest):
-    prev_ref, out_ref = rest if len(rest) == 2 else (None, rest[0])
+def weights_kernel(core_ref, table_ref, same_ref, crossed_ref, out_ref):
     core = core_ref[0]
-    local_diam, columns, _ = amp_ref.shape
+    local_diam, columns, _ = same_ref.shape
     half_count = local_diam // 2
-    odd = 1 - core if crossed else core
-    total = None
-    for half, ref in ((core, own_ref), (1 - core, recv_ref)):
+    for at_half, half in enumerate((core, 1 - core)):
         for k in range(half_count):
             at = half * half_count + k
-            amp = amp_ref[at].astype(F32)
-            weights = jnp.concatenate(
-                [(table_ref[s, 2 * at + odd] * amp).astype(BF16) for s in range(local_diam)]
-            )
-            value = jnp.dot(weights, ref[2 * k + odd], preferred_element_type=F32)
-            total = value if total is None else total + value
-    total = total.reshape(out_ref.shape)
-    if prev_ref is not None:
-        total = total + prev_ref[...]
-    out_ref[...] = total.astype(out_ref.dtype)
+            for odd, amp_ref in ((core, same_ref), (1 - core, crossed_ref)):
+                amp = amp_ref[at].astype(F32)
+                for s in range(local_diam):
+                    value = table_ref[s, 2 * at + odd] * amp
+                    place = at_half * local_diam + 2 * k + odd
+                    out_ref[place, s * columns : (s + 1) * columns] = value.astype(BF16)
 
 
 def chunk_plan(phi, loads, harm_diam, mistuning, dyn_diag, blade_order):
@@ -206,26 +202,28 @@
     def row_total(got):
         return jnp.sum(got.astype(F32), axis=0)
 
-    half_slots = jax.ShapeDtypeStruct((pairs, columns, MODES), BF16)
     shapes = phi.T.reshape(local_diam, MODES, rows_dev)
-    mine, send = pl.pallas_call(
-        functools.partial(force_kernel, columns),
-        name="force",
-        in_specs=[SMEM, SMEM, HBM, HBM],
+    shape_sized = jax.ShapeDtypeStruct(shapes.shape, BF16)
+    combined, shapes_near = pl.pallas_call(
+        functools.partial(load_kernel, columns),
+        name="load",
+        in_specs=[SMEM, SMEM, VMEM, HBM],
         out_specs=[VMEM, VMEM],
-        out_shape=[half_slots, half_slots],
-        scratch_shapes=[
-            pltpu.VMEM(loads.shape, BF16),
-            pltpu.VMEM(shapes.shape, BF16),
-            pltpu.VMEM((local_diam * columns, rows_dev), BF16),
-            pltpu.SemaphoreType.DMA,
-            pltpu.SemaphoreType.DMA((local_diam,)),
+        out_shape=[
+            jax.ShapeDtypeStruct((local_diam, columns, rows_dev), BF16),
+            shape_sized,
         ],
-        compiler_params=pltpu.CompilerParams(vmem_limit_bytes=60 << 20),
+        scratch_shapes=[pltpu.SemaphoreType.DMA],
+        compiler_params=LIMIT,
     )(core_arg, harm_diam, loads, shapes)
-    force_slots = in_half_order(mine, other_core(send))
-    force_slots, stiff, order, shapes_sent = lax.optimization_barrier(
-        (force_slots, mistuning.T, blade_order, shapes)
+    force_part = jnp.einsum(
+        "hcr,hmr->hcm", combined, shapes_near, preferred_element_type=F32
+    ).astype(BF16)
+    force_slots = in_half_order(
+        by_parity(force_part, core), other_core(by_parity(force_part, 1 - core))
+    )
+    force_slots, stiff, order, shapes_sent, dyn_diag = lax.optimization_barrier(
+        (force_slots, mistuning.T, blade_order, shapes, dyn_diag)
     )
     force_got = exchange(force_slots)
 
@@ -270,29 +268,32 @@
         amp = (force - row_total(exchange(part))) / dyn_own
         if sweep == 0:
             amp, shapes_received = lax.optimization_barrier((amp, shapes_received))
+    amp, own_hbm, recv_hbm = lax.optimization_barrier((amp, shapes, shapes_received))
     same = exchange(jnp.broadcast_to(amp.astype(BF16)[None], slots_shape))
+    shapes_both = pl.pallas_call(
+        fetch_kernel,
+        name="fetch",
+        in_specs=[HBM, HBM],
+        out_specs=VMEM,
+        out_shape=jax.ShapeDtypeStruct((NBLADE, MODES, rows_dev), BF16),
+        scratch_shapes=[pltpu.SemaphoreType.DMA((2,))],
+        compiler_params=LIMIT,
+        cost_estimate=pl.CostEstimate(
+            flops=0, bytes_accessed=8 * phi.size, transcendentals=0
+        ),
+    )(own_hbm, recv_hbm)
+    same, shapes_both = lax.optimization_barrier((same, shapes_both))
     crossed = other_core(same)
-
-    def blades(is_crossed, amps, *prev):
-        return pl.pallas_call(
-            functools.partial(blades_kernel, is_crossed),
-            name="blades",
-            in_specs=[SMEM, SMEM] + [VMEM] * (3 + len(prev)),
-            out_specs=VMEM,
-            out_shape=jax.ShapeDtypeStruct(
-                (local_diam, columns, rows_dev), BF16 if is_crossed else F32
-            ),
-            compiler_params=LIMIT,
-            cost_estimate=pl.CostEstimate(
-                flops=2 * local_diam * columns * phi.size,
-                bytes_accessed=4 * phi.size,
-                transcendentals=0,
-            ),
-        )(core_arg, table, amps, shapes, shapes_received, *prev)
-
-    part = blades(False, same)
-    part, crossed = lax.optimization_barrier((part, crossed))
-    return blades(True, crossed, part)
+    weights = pl.pallas_call(
+        weights_kernel,
+        name="weights",
+        in_specs=[SMEM, SMEM, VMEM, VMEM],
+        out_specs=VMEM,
+        out_shape=jax.ShapeDtypeStruct((NBLADE, local_diam * columns, MODES), BF16),
+        compiler_params=LIMIT,
+    )(core_arg, table, same, crossed)
+    blades = jnp.einsum("ham,hmr->ar", weights, shapes_both, preferred_element_type=F32)
+    return blades.astype(BF16).reshape(local_diam, columns, rows_dev)
 
 
 def solution(mesh):

time: 92.6 us -> 89.8 us (0.970)
  blocking collectives: 43.9 us -> 34.3 us
  Pallas kernels: 20.7 us -> 11.2 us
  matrix products: 0.23 us -> 6.99 us
  local copies, waits for them, and re-layouts: 0.79 us -> 6.07 us
  starting transfers between devices: 16.9 us -> 21 us
    pallas_call x3, Pallas kernels: 16 us -> 6.48 us  [the longest x1 2.94 us: chunk_plan(): pl.pallas_call(fetch_kernel, name='fetch', in_specs=[HBM, HBM], out_specs...]
    all_to_all x5 -> x4, blocking collectives: 43.9 us -> 34.3 us  [exchange(): return lax.all_to_all(slots, 'rows', 0, 0, tiled=True)]
    dot_general x0 -> x2, matrix products: none -> 6.76 us  [the longest x1 5.66 us: chunk_plan(): jnp.einsum('ham,hmr->ar', weights, shapes_both, preferred_element_type=F32)]
    unnamed x4 -> x10, local copies, waits for them, and re-layouts: 0.01 us -> 4.62 us
    all_to_all x1 -> x2, starting transfers between devices: 6.88 us -> 10.3 us  [exchange(): return lax.all_to_all(slots, 'rows', 0, 0, tiled=True)]
    all_to_all x1 -> x2, waiting for transfers between devices: 2.93 us -> 2.64 us  [exchange(): return lax.all_to_all(slots, 'rows', 0, 0, tiled=True)]
  transfers between devices with their start and end apart: 9 -> 10, of which waited for: 6 -> 8; matrix products, arithmetic and copies ran while one was open for 2% -> 2% of each run, Pallas kernels for 9% -> 8%
where the time goes in v3:
time: 89.8 us; the launch traced here: 88.8 us
  blocking collectives  34.3 us (38%)
  starting transfers between devices  21 us (23%)
  Pallas kernels  11.2 us (12%)
  waiting for transfers between devices  7.15 us (8%)
  matrix products  6.99 us (8%)
  local copies, waits for them, and re-layouts  6.07 us (7%)
  other arithmetic  1.84 us (2%)
    all_to_all x4, blocking collectives, exchange(): return lax.all_to_all(slots, 'rows', 0, 0, tiled=True)  34.3 us
    ppermute x8, starting transfers between devices, other_core(): return lax.ppermute(value, 'diam', SWAP)  10.7 us
    all_to_all x2, starting transfers between devices, exchange(): return lax.all_to_all(slots, 'rows', 0, 0, tiled=True)  10.3 us
    dot_general x1, matrix products, chunk_plan(): jnp.einsum('ham,hmr->ar', weights, shapes_both, preferred_element_type=F32)  5.66 us
    unnamed x10, local copies, waits for them, and re-layouts  4.62 us
    ppermute x8, waiting for transfers between devices, other_core(): return lax.ppermute(value, 'diam', SWAP)  4.51 us
    pallas_call x1, Pallas kernels, chunk_plan(): pl.pallas_call(fetch_kernel, name='fetch', in_specs=[HBM, HBM], out_specs...  2.94 us
    pallas_call x1, Pallas kernels, chunk_plan(): pl.pallas_call(regroup_kernel, name='regroup', in_specs=[SMEM, VMEM], out...  2.7 us
  transfers between devices with their start and end apart: 10, of which 8 were waited for; matrix products, arithmetic and copies ran while one was open for 2% of the time, Pallas kernels for 8%

profile of v3, /device:TPU:1, one launch (start us, length us, event | category | flops | bytes accessed | tf_op | source)
XLA Modules:
  0.0 88.8 jit_solution(3141448089150361124)
XLA Ops:
  0.0 1.2 %copy-done.2 = bf16[1024,512]{1,0:T(8,128)(2,1)S(1)} copy-done((bf16[1024,512]{1,0:T(8,128)(2,1)S(1)}, bf16[1024,512]{1,0:T(8,128)(2,1)}, u32[]{:S(2)}) %copy-start.2) | copy-done | bytes 1048600
  1.2 0.7 copy-done.3
  1.9 2.5 %load.1 = (bf16[8,32,1024]{2,1,0:T(8,128)(2,1)S(1)}, bf16[8,200,1024]{2,1,0:T(8,128)(2,1)S(1)}) custom-call(s32[1]{0:T(128)} %bitcast.core_ref, s32[16]{0:T(128)S(1)} %copy-done.3, bf16[1024,512]{1,0:T(8,128)(2,1)S(1)} %copy-done.2, bf16[8,200,1024]{2,1,0:T(8,128)(2,1)} %bitcast.2.phi_hbm.own_hbm), custom_call_target="tpu_custom_call" | custom-call | tf_op jit(solution)/shard_map/load/pallas_call | solution.py:207
  4.4 1.1 %convolution_convert_fusion = bf16[8,32,200]{2,1,0:T(8,128)(2,1)S(1)} fusion(bf16[8,32,1024]{2,1,0:T(8,128)(2,1)S(1)} %get-tuple-element.33, bf16[8,200,1024]{2,1,0:T(8,128)(2,1)S(1)} %get-tuple-element.34), kind=kOutput, calls=%fused_computation.2 | convolution fusion | flops 104908800 | bytes 3903488 | tf_op jit(solution)/shard_map/hcr,hmr->hcm/dot_general | solution.py:219
  5.7 1.2 %collective-permute-done = bf16[4,32,200]{2,1,0:T(8,128)(2,1)S(1)} collective-permute-done((bf16[4,32,200]{2,1,0:T(8,128)(2,1)S(1)}, bf16[4,32,200]{2,1,0:T(8,128)(2,1)S(1)}, u32[]{:S(2)}, u32[]{:S(2)}) %collective-permute-start) | collective-permute-done | bytes 51232 | tf_op jit(solution)/shard_map/ppermute | solution.py:192
  6.9 0.7 maximum_select_fusion
  7.7 6.9 %all-to-all-start = ((bf16[8,32,200]{2,1,0:T(8,128)(2,1)}), bf16[8,32,200]{2,1,0:T(8,128)(2,1)}, u32[]{:S(2)}, u32[]{:S(2)}) async-start(bf16[8,32,200]{2,1,0:T(8,128)(2,1)} %maximum_select_fusion), calls=%async_computation | async-start | bytes 262144 | tf_op jit(solution)/shard_map/all_to_all | solution.py:200
  14.6 2.7 %regroup.1 = (bf16[2,4,200,200]{3,2,1,0:T(8,128)(2,1)S(1)}, bf16[2,4,200,200]{3,2,1,0:T(8,128)(2,1)}) custom-call(s32[1]{0:T(128)} %bitcast.core_ref, f32[400,1600]{1,0:T(8,128)S(1)} %bitcast.29), custom_call_target="tpu_custom_call" | custom-call | flops 1280000 | bytes 5120000 | tf_op jit(solution)/shard_map/regroup/pallas_call | solution.py:231
  18.0 0.8 dynamic_slice.7
  18.8 2.1 %all-to-all-done = bf16[8,32,200]{2,1,0:T(8,128)(2,1)} async-done(((bf16[8,32,200]{2,1,0:T(8,128)(2,1)}), bf16[8,32,200]{2,1,0:T(8,128)(2,1)}, u32[]{:S(2)}, u32[]{:S(2)}) %all-to-all-start) | async-done | bytes 102432 | tf_op jit(solution)/shard_map/all_to_all | solution.py:200
  20.9 0.9 %convert_reduce_fusion.4 = f32[32,200]{1,0:T(8,128)S(1)} fusion(bf16[8,32,200]{2,1,0:T(8,128)(2,1)} %all-to-all-done), kind=kLoop, calls=%fused_computation.7 | loop fusion | flops 96000 | bytes 128000 | tf_op jit(solution)/shard_map/reduce_sum | solution.py:203
  21.9 1.8 %collective-permute-start.2 = (bf16[32,200]{1,0:T(8,128)(2,1)S(1)}, bf16[32,200]{1,0:T(8,128)(2,1)S(1)}, u32[]{:S(2)}, u32[]{:S(2)}) collective-permute-start(bf16[32,200]{1,0:T(8,128)(2,1)S(1)} %divide_convert_fusion.2.amp_ref), channel_id=1, source_target_pairs={{0,1},{1,0},{2,3},{3,2},{4,5},{5,4},{6,7},{7,6},{8,9},{9,8},{10,11... | collective-permute-start | bytes 38408 | tf_op jit(solution)/shard_map/ppermute | solution.py:192
  23.9 0.6 collective-permute-done.2.amp_ref
  24.8 8.6 %all_to_all.30 = bf16[8,32,200]{2,1,0:T(8,128)(2,1)S(1)} all-to-all(bf16[8,32,200]{2,1,0:T(8,128)(2,1)S(1)} %product.9), channel_id=1, replica_groups=mesh['grp'=2,'rows'=8,'diam'=2] {'rows'}, dimensions={0} | all-to-all | bytes 204800 | tf_op jit(solution)/shard_map/all_to_all | solution.py:200
  33.4 1.8 %collective-permute-start.4 = (bf16[32,200]{1,0:T(8,128)(2,1)S(1)}, bf16[32,200]{1,0:T(8,128)(2,1)S(1)}, u32[]{:S(2)}, u32[]{:S(2)}) collective-permute-start(bf16[32,200]{1,0:T(8,128)(2,1)S(1)} %subtract_divide_fusion.1.amp_ref), channel_id=1, source_target_pairs={{0,1},{1,0},{2,3},{3,2},{4,5},{5,4},{6,7},{7,6},{8,9},{9,8},{10,11... | collective-permute-start | bytes 38408 | tf_op jit(solution)/shard_map/ppermute | solution.py:192
  35.5 0.6 collective-permute-done.4.amp_ref
  36.3 8.6 %all_to_all.31 = bf16[8,32,200]{2,1,0:T(8,128)(2,1)S(1)} all-to-all(bf16[8,32,200]{2,1,0:T(8,128)(2,1)S(1)} %product.11), channel_id=1, replica_groups=mesh['grp'=2,'rows'=8,'diam'=2] {'rows'}, dimensions={0} | all-to-all | bytes 204800 | tf_op jit(solution)/shard_map/all_to_all | solution.py:200
  45.0 1.8 %collective-permute-start.5 = (bf16[32,200]{1,0:T(8,128)(2,1)S(1)}, bf16[32,200]{1,0:T(8,128)(2,1)S(1)}, u32[]{:S(2)}, u32[]{:S(2)}) collective-permute-start(bf16[32,200]{1,0:T(8,128)(2,1)S(1)} %divide_convert_fusion.1.amp_ref), channel_id=1, source_target_pairs={{0,1},{1,0},{2,3},{3,2},{4,5},{5,4},{6,7},{7,6},{8,9},{9,8},{10,11... | collective-permute-start | bytes 38408 | tf_op jit(solution)/shard_map/ppermute | solution.py:192
  47.0 0.6 collective-permute-done.5.amp_ref
  47.9 8.6 %all_to_all.32 = bf16[8,32,200]{2,1,0:T(8,128)(2,1)S(1)} all-to-all(bf16[8,32,200]{2,1,0:T(8,128)(2,1)S(1)} %product.13), channel_id=1, replica_groups=mesh['grp'=2,'rows'=8,'diam'=2] {'rows'}, dimensions={0} | all-to-all | bytes 204800 | tf_op jit(solution)/shard_map/all_to_all | solution.py:200
  56.5 1.8 %collective-permute-start.6 = (bf16[32,200]{1,0:T(8,128)(2,1)S(1)}, bf16[32,200]{1,0:T(8,128)(2,1)S(1)}, u32[]{:S(2)}, u32[]{:S(2)}) collective-permute-start(bf16[32,200]{1,0:T(8,128)(2,1)S(1)} %divide_convert_fusion.amp_ref), channel_id=1, source_target_pairs={{0,1},{1,0},{2,3},{3,2},{4,5},{5,4},{6,7},{7,6},{8,9},{9,8},{10,11... | collective-permute-start | bytes 38408 | tf_op jit(solution)/shard_map/ppermute | solution.py:192
  58.6 0.6 collective-permute-done.6.amp_ref
  59.4 8.6 %all_to_all.33 = bf16[8,32,200]{2,1,0:T(8,128)(2,1)S(1)} all-to-all(bf16[8,32,200]{2,1,0:T(8,128)(2,1)S(1)} %product.15), channel_id=1, replica_groups=mesh['grp'=2,'rows'=8,'diam'=2] {'rows'}, dimensions={0} | all-to-all | bytes 204800 | tf_op jit(solution)/shard_map/all_to_all | solution.py:200
  68.1 0.7 broadcast_in_dim.33
  68.7 3.4 %all-to-all-start.5 = ((bf16[8,32,200]{2,1,0:T(8,128)(2,1)}), bf16[8,32,200]{2,1,0:T(8,128)(2,1)S(1)}, u32[]{:S(2)}, u32[]{:S(2)}) async-start(bf16[8,32,200]{2,1,0:T(8,128)(2,1)} %broadcast_in_dim.33), calls=%async_computation.5 | async-start | bytes 262144 | tf_op jit(solution)/shard_map/all_to_all | solution.py:200
  72.1 2.9 %fetch.1 = bf16[16,200,1024]{2,1,0:T(8,128)(2,1)S(1)} custom-call(bf16[8,200,1024]{2,1,0:T(8,128)(2,1)} %bitcast.2.phi_hbm.own_hbm, bf16[8,200,1024]{2,1,0:T(8,128)(2,1)} %collective-permute-done.3.recv_hbm), custom_call_target="tpu_custom_call" | custom-call | bytes 13107200 | tf_op jit(solution)/shard_map/fetch/pallas_call | solution.py:273
  75.1 2.7 %copy-done = bf16[16,200,1024]{2,1,0:T(8,128)(2,1)} copy-done((bf16[16,200,1024]{2,1,0:T(8,128)(2,1)}, bf16[16,200,1024]{2,1,0:T(8,128)(2,1)S(1)}, u32[]{:S(2)}) %copy-start) | copy-done | bytes 6553624
  77.8 0.5 all-to-all-done.5.same_ref
  78.3 2.8 %collective-permute-start.7 = (bf16[8,32,200]{2,1,0:T(8,128)(2,1)S(1)}, bf16[8,32,200]{2,1,0:T(8,128)(2,1)S(1)}, u32[]{:S(2)}, u32[]{:S(2)}) collective-permute-start(bf16[8,32,200]{2,1,0:T(8,128)(2,1)S(1)} %all-to-all-done.5.same_ref), channel_id=1, source_target_pairs={{0,1},{1,0},{2,3},{3,2},{4,5},{5,4},{6,7},{7,6},{8,9},{9,8},{10,11... | collective-permute-start | bytes 307208 | tf_op jit(solution)/shard_map/ppermute | solution.py:192
  81.1 1.0 %collective-permute-done.7.crossed_ref = bf16[8,32,200]{2,1,0:T(8,128)(2,1)S(1)} collective-permute-done((bf16[8,32,200]{2,1,0:T(8,128)(2,1)S(1)}, bf16[8,32,200]{2,1,0:T(8,128)(2,1)S(1)}, u32[]{:S(2)}, u32[]{:S(2)}) %collective-permute-start.7) | collective-permute-done | bytes 102432 | tf_op jit(solution)/shard_map/ppermute | solution.py:192
  82.1 1.0 %weights.1 = bf16[16,256,200]{2,1,0:T(8,128)(2,1)S(1)} custom-call(s32[1]{0:T(128)} %bitcast.core_ref, f32[8,16]{1,0:T(8,128)S(1)} %constant_dynamic-slice_fusion.table_ref, bf16[8,32,200]{2,1,0:T(8,128)(2,1)S(1)} %all-to-all-done.5.same_ref, bf16[8,32,200]{2,1,0:T(8,128)(2,1)S(1)} %collective-permute-done.7.crossed_ref), custom_call_target="tpu_custom_call" | custom-call | tf_op jit(solution)/shard_map/weights/pallas_call | solution.py:287
  83.2 5.7 %fusion = bf16[256,1024]{1,0:T(8,128)(2,1)} fusion(bf16[16,256,200]{2,1,0:T(8,128)(2,1)S(1)} %weights.1, bf16[16,200,1024]{2,1,0:T(8,128)(2,1)} %copy-done), kind=kOutput, calls=%fused_computation.1 | convolution fusion | flops 1677983744 | bytes 8716288 | tf_op jit(solution)/shard_map/ham,hmr->ar/dot_general | solution.py:295
  (36 shorter events, 3.2 us)
Async XLA Ops:
  0.0 1.2 %copy-start.2 = (bf16[1024,512]{1,0:T(8,128)(2,1)S(1)}, bf16[1024,512]{1,0:T(8,128)(2,1)}, u32[]{:S(2)}) copy-start(bf16[1024,512]{1,0:T(8,128)(2,1)} %loads_ref.1) | copy-start | bytes 3145732
  1.2 0.7 copy-start.3
  4.4 10.2 %copy-start.1 = (f32[1600,400]{0,1:T(8,128)S(1)}, f32[1600,400]{0,1:T(8,128)}, u32[]{:S(2)}) copy-start(f32[1600,400]{0,1:T(8,128)} %param.9) | copy-start | bytes 7680004
  4.4 13.4 %copy-start.4 = (s32[16]{0:T(128)S(1)}, s32[16]{0:T(128)}, u32[]{:S(2)}) copy-start(s32[16]{0:T(128)} %param.11) | copy-start | bytes 196
  5.5 1.3 %collective-permute-start = (bf16[4,32,200]{2,1,0:T(8,128)(2,1)S(1)}, bf16[4,32,200]{2,1,0:T(8,128)(2,1)S(1)}, u32[]{:S(2)}, u32[]{:S(2)}) collective-permute-start(bf16[4,32,200]{2,1,0:T(8,128)(2,1)S(1)} %select_bitcast_fusion), channel_id=1, source_target_pairs={{0,1},{1,0},{2,3},{3,2},{4,5},{5,4},{6,7},{7,6},{8,9},{9,8},{10,11... | collective-permute-start | bytes 153608 | tf_op jit(solution)/shard_map/ppermute | solution.py:192
  7.6 25.9 %collective-permute-start.3 = (bf16[8,200,1024]{2,1,0:T(8,128)(2,1)}, bf16[8,200,1024]{2,1,0:T(8,128)(2,1)}, u32[]{:S(2)}, u32[]{:S(2)}) collective-permute-start(bf16[8,200,1024]{2,1,0:T(8,128)(2,1)} %bitcast.2.phi_hbm.own_hbm), channel_id=1, source_target_pairs={{0,1},{1,0},{2,3},{3,2},{4,5},{5,4},{6,7},{7,6},{8,9},{9,8},{10,11... | collective-permute-start | bytes 9830408 | tf_op jit(solution)/shard_map/ppermute | solution.py:192
  7.7 13.2 %all-to-all-start = ((bf16[8,32,200]{2,1,0:T(8,128)(2,1)}), bf16[8,32,200]{2,1,0:T(8,128)(2,1)}, u32[]{:S(2)}, u32[]{:S(2)}) async-start(bf16[8,32,200]{2,1,0:T(8,128)(2,1)} %maximum_select_fusion), calls=%async_computation | async-start | bytes 262144 | tf_op jit(solution)/shard_map/all_to_all | solution.py:200
  17.3 6.4 %collective-permute-start.1 = (bf16[2,4,200,200]{3,2,1,0:T(8,128)(2,1)}, bf16[2,4,200,200]{3,2,1,0:T(8,128)(2,1)S(1)}, u32[]{:S(2)}, u32[]{:S(2)}) collective-permute-start(bf16[2,4,200,200]{3,2,1,0:T(8,128)(2,1)} %get-tuple-element.44), channel_id=1, source_target_pairs={{0,1},{1,0},{2,3},{3,2},{4,5},{5,4},{6,7},{7,6},{8,9},{9,8},{10,11... | collective-permute-start | bytes 1920008 | tf_op jit(solution)/shard_map/ppermute | solution.py:192
  21.9 2.6 %collective-permute-start.2 = (bf16[32,200]{1,0:T(8,128)(2,1)S(1)}, bf16[32,200]{1,0:T(8,128)(2,1)S(1)}, u32[]{:S(2)}, u32[]{:S(2)}) collective-permute-start(bf16[32,200]{1,0:T(8,128)(2,1)S(1)} %divide_convert_fusion.2.amp_ref), channel_id=1, source_target_pairs={{0,1},{1,0},{2,3},{3,2},{4,5},{5,4},{6,7},{7,6},{8,9},{9,8},{10,11... | collective-permute-start | bytes 38408 | tf_op jit(solution)/shard_map/ppermute | solution.py:192
  33.4 2.6 %collective-permute-start.4 = (bf16[32,200]{1,0:T(8,128)(2,1)S(1)}, bf16[32,200]{1,0:T(8,128)(2,1)S(1)}, u32[]{:S(2)}, u32[]{:S(2)}) collective-permute-start(bf16[32,200]{1,0:T(8,128)(2,1)S(1)} %subtract_divide_fusion.1.amp_ref), channel_id=1, source_target_pairs={{0,1},{1,0},{2,3},{3,2},{4,5},{5,4},{6,7},{7,6},{8,9},{9,8},{10,11... | collective-permute-start | bytes 38408 | tf_op jit(solution)/shard_map/ppermute | solution.py:192
  45.0 2.6 %collective-permute-start.5 = (bf16[32,200]{1,0:T(8,128)(2,1)S(1)}, bf16[32,200]{1,0:T(8,128)(2,1)S(1)}, u32[]{:S(2)}, u32[]{:S(2)}) collective-permute-start(bf16[32,200]{1,0:T(8,128)(2,1)S(1)} %divide_convert_fusion.1.amp_ref), channel_id=1, source_target_pairs={{0,1},{1,0},{2,3},{3,2},{4,5},{5,4},{6,7},{7,6},{8,9},{9,8},{10,11... | collective-permute-start | bytes 38408 | tf_op jit(solution)/shard_map/ppermute | solution.py:192
  56.5 2.6 %collective-permute-start.6 = (bf16[32,200]{1,0:T(8,128)(2,1)S(1)}, bf16[32,200]{1,0:T(8,128)(2,1)S(1)}, u32[]{:S(2)}, u32[]{:S(2)}) collective-permute-start(bf16[32,200]{1,0:T(8,128)(2,1)S(1)} %divide_convert_fusion.amp_ref), channel_id=1, source_target_pairs={{0,1},{1,0},{2,3},{3,2},{4,5},{5,4},{6,7},{7,6},{8,9},{9,8},{10,11... | collective-permute-start | bytes 38408 | tf_op jit(solution)/shard_map/ppermute | solution.py:192
  68.7 9.6 %all-to-all-start.5 = ((bf16[8,32,200]{2,1,0:T(8,128)(2,1)}), bf16[8,32,200]{2,1,0:T(8,128)(2,1)S(1)}, u32[]{:S(2)}, u32[]{:S(2)}) async-start(bf16[8,32,200]{2,1,0:T(8,128)(2,1)} %broadcast_in_dim.33), calls=%async_computation.5 | async-start | bytes 262144 | tf_op jit(solution)/shard_map/all_to_all | solution.py:200
  75.1 2.7 %copy-start = (bf16[16,200,1024]{2,1,0:T(8,128)(2,1)}, bf16[16,200,1024]{2,1,0:T(8,128)(2,1)S(1)}, u32[]{:S(2)}) copy-start(bf16[16,200,1024]{2,1,0:T(8,128)(2,1)S(1)} %fetch.1) | copy-start | bytes 19660804
  78.3 3.8 %collective-permute-start.7 = (bf16[8,32,200]{2,1,0:T(8,128)(2,1)S(1)}, bf16[8,32,200]{2,1,0:T(8,128)(2,1)S(1)}, u32[]{:S(2)}, u32[]{:S(2)}) collective-permute-start(bf16[8,32,200]{2,1,0:T(8,128)(2,1)S(1)} %all-to-all-done.5.same_ref), channel_id=1, source_target_pairs={{0,1},{1,0},{2,3},{3,2},{4,5},{5,4},{6,7},{7,6},{8,9},{9,8},{10,11... | collective-permute-start | bytes 307208 | tf_op jit(solution)/shard_map/ppermute | solution.py:192

commit v4 on v3

--- a/solution.py
+++ b/solution.py
@@ -98,17 +98,27 @@
 VMEM = pl.BlockSpec(memory_space=pltpu.VMEM)
 SMEM = pl.BlockSpec(memory_space=pltpu.SMEM)
 HBM = pl.BlockSpec(memory_space=pltpu.HBM)
+WIDE = pltpu.CompilerParams(vmem_limit_bytes=16 << 20)
 LIMIT = pltpu.CompilerParams(vmem_limit_bytes=8 << 20)
+
+
+def in_hbm(*values):
+    return [pltpu.with_memory_space_constraint(value, pltpu.HBM) for value in values]
 
 
 def pick(core, even, odd):
     return jnp.where(core == 0, even, odd)
 
 
-def load_kernel(columns, core_ref, harm_ref, loads_ref, phi_hbm, combined_ref, phi_ref, phi_sem):
+def load_kernel(columns, core_ref, harm_hbm, loads_hbm, phi_hbm, combined_ref, phi_ref, harm_ref, loads_ref, sems):
     local_diam = phi_ref.shape[0]
-    phi_copy = pltpu.make_async_copy(phi_hbm, phi_ref, phi_sem)
+    harm_copy = pltpu.make_async_copy(harm_hbm, harm_ref, sems.at[0])
+    harm_copy.start()
+    load_copy = pltpu.make_async_copy(loads_hbm, loads_ref, sems.at[1])
+    load_copy.start()
+    phi_copy = pltpu.make_async_copy(phi_hbm, phi_ref, sems.at[2])
     phi_copy.start()
+    harm_copy.wait()
     wide = loads_ref.shape[1]
     first_diam = core_ref[0] * local_diam
     col = lax.broadcasted_iota(jnp.int32, (8, wide), 1)
@@ -119,6 +129,7 @@
     shape = (local_diam * columns, wide)
     row = lax.broadcasted_iota(jnp.int32, shape, 0)
     spread = jnp.where(row == jnp.broadcast_to(key[0:1], shape), 1.0, 0.0).astype(BF16)
+    load_copy.wait()
     combined = lax.dot_general(
         spread, loads_ref[...], (((1,), (1,)), ((), ())), preferred_element_type=F32
     )
@@ -126,19 +137,29 @@
     phi_copy.wait()
 
 
-def fetch_kernel(own_hbm, recv_hbm, both_ref, sems):
-    half = own_hbm.shape[0]
-    copies = [
-        pltpu.make_async_copy(own_hbm, both_ref.at[:half], sems.at[0]),
-        pltpu.make_async_copy(recv_hbm, both_ref.at[half:], sems.at[1]),
+def parity_copies(odd, own_hbm, recv_hbm, near_ref, sems):
+    pairs = own_hbm.shape[0] // 2
+    return [
+        pltpu.make_async_copy(
+            ref.at[2 * k + odd], near_ref.at[at_half * pairs + k], sems.at[at_half * pairs + k]
+        )
+        for at_half, ref in enumerate((own_hbm, recv_hbm))
+        for k in range(pairs)
     ]
+
+
+def fetch_kernel(core_ref, own_hbm, recv_hbm, near_ref, sems):
+    copies = parity_copies(core_ref[0], own_hbm, recv_hbm, near_ref, sems)
     for copy in copies:
         copy.start()
     for copy in copies:
         copy.wait()
 
 
-def regroup_kernel(core_ref, stiff_ref, keep_ref, send_ref):
+def regroup_kernel(core_ref, stiff_hbm, keep_ref, send_ref, stiff_ref, sem):
+    copy = pltpu.make_async_copy(stiff_hbm, stiff_ref, sem)
+    copy.start()
+    copy.wait()
     core = core_ref[0]
     for k in range(0, 2 * keep_ref.shape[1], 2):
         for chunk in range(2):
@@ -163,19 +184,37 @@
             out_ref[at] = value.astype(out_ref.dtype)
 
 
-def weights_kernel(core_ref, table_ref, same_ref, crossed_ref, out_ref):
+def parity_product(odd, core, table_ref, amp_ref, near_ref, copies):
+    local_diam, columns, _ = amp_ref.shape
+    pairs = local_diam // 2
+    total = None
+    for at_half, half in enumerate((core, 1 - core)):
+        for k in range(pairs):
+            at = half * pairs + k
+            amp = amp_ref[at].astype(F32)
+            weights = jnp.concatenate(
+                [(table_ref[s, 2 * at + odd] * amp).astype(BF16) for s in range(local_diam)]
+            )
+            if copies:
+                copies[at_half * pairs + k].wait()
+            shape = near_ref[at_half * pairs + k]
+            value = jnp.dot(weights, shape, preferred_element_type=F32)
+            total = value if total is None else total + value
+    return total.reshape(local_diam, columns, near_ref.shape[2])
+
+
+def same_kernel(core_ref, table_ref, amp_ref, near_ref, out_ref):
     core = core_ref[0]
-    local_diam, columns, _ = same_ref.shape
-    half_count = local_diam // 2
-    for at_half, half in enumerate((core, 1 - core)):
-        for k in range(half_count):
-            at = half * half_count + k
-            for odd, amp_ref in ((core, same_ref), (1 - core, crossed_ref)):
-                amp = amp_ref[at].astype(F32)
-                for s in range(local_diam):
-                    value = table_ref[s, 2 * at + odd] * amp
-                    place = at_half * local_diam + 2 * k + odd
-                    out_ref[place, s * columns : (s + 1) * columns] = value.astype(BF16)
+    out_ref[...] = parity_product(core, core, table_ref, amp_ref, near_ref, None)
+
+
+def crossed_kernel(core_ref, table_ref, amp_ref, own_hbm, recv_hbm, prev_ref, out_ref, near_ref, sems):
+    core = core_ref[0]
+    copies = parity_copies(1 - core, own_hbm, recv_hbm, near_ref, sems)
+    for copy in copies:
+        copy.start()
+    total = parity_product(1 - core, core, table_ref, amp_ref, near_ref, copies)
+    out_ref[...] = (total + prev_ref[...]).astype(out_ref.dtype)
 
 
 def chunk_plan(phi, loads, harm_diam, mistuning, dyn_diag, blade_order):
@@ -207,15 +246,19 @@
     combined, shapes_near = pl.pallas_call(
         functools.partial(load_kernel, columns),
         name="load",
-        in_specs=[SMEM, SMEM, VMEM, HBM],
+        in_specs=[SMEM, HBM, HBM, HBM],
         out_specs=[VMEM, VMEM],
         out_shape=[
             jax.ShapeDtypeStruct((local_diam, columns, rows_dev), BF16),
             shape_sized,
         ],
-        scratch_shapes=[pltpu.SemaphoreType.DMA],
+        scratch_shapes=[
+            pltpu.SMEM(harm_diam.shape, jnp.int32),
+            pltpu.VMEM(loads.shape, BF16),
+            pltpu.SemaphoreType.DMA((3,)),
+        ],
         compiler_params=LIMIT,
-    )(core_arg, harm_diam, loads, shapes)
+    )(core_arg, *in_hbm(harm_diam, loads, shapes))
     force_part = jnp.einsum(
         "hcr,hmr->hcm", combined, shapes_near, preferred_element_type=F32
     ).astype(BF16)
@@ -231,14 +274,15 @@
     keep, sent = pl.pallas_call(
         regroup_kernel,
         name="regroup",
-        in_specs=[SMEM, VMEM],
+        in_specs=[SMEM, HBM],
         out_specs=[VMEM, VMEM],
         out_shape=[group, group],
-        compiler_params=LIMIT,
+        scratch_shapes=[pltpu.VMEM(stiff.shape, F32), pltpu.SemaphoreType.DMA],
+        compiler_params=WIDE,
         cost_estimate=pl.CostEstimate(
             flops=2 * mistuning.size, bytes_accessed=8 * mistuning.size, transcendentals=0
         ),
-    )(core_arg, stiff)
+    )(core_arg, *in_hbm(stiff))
     recv = other_core(sent)
     shapes_received = other_core(shapes_sent)
     table = lax.dynamic_slice_in_dim(cyclic_rows(order), first_diam, local_diam, 0)
@@ -270,30 +314,47 @@
             amp, shapes_received = lax.optimization_barrier((amp, shapes_received))
     amp, own_hbm, recv_hbm = lax.optimization_barrier((amp, shapes, shapes_received))
     same = exchange(jnp.broadcast_to(amp.astype(BF16)[None], slots_shape))
-    shapes_both = pl.pallas_call(
+    near = pl.pallas_call(
         fetch_kernel,
         name="fetch",
-        in_specs=[HBM, HBM],
+        in_specs=[SMEM, HBM, HBM],
         out_specs=VMEM,
-        out_shape=jax.ShapeDtypeStruct((NBLADE, MODES, rows_dev), BF16),
-        scratch_shapes=[pltpu.SemaphoreType.DMA((2,))],
+        out_shape=shape_sized,
+        scratch_shapes=[pltpu.SemaphoreType.DMA((local_diam,))],
         compiler_params=LIMIT,
         cost_estimate=pl.CostEstimate(
-            flops=0, bytes_accessed=8 * phi.size, transcendentals=0
+            flops=0, bytes_accessed=4 * phi.size, transcendentals=0
         ),
-    )(own_hbm, recv_hbm)
-    same, shapes_both = lax.optimization_barrier((same, shapes_both))
+    )(core_arg, own_hbm, recv_hbm)
+    same, near = lax.optimization_barrier((same, near))
     crossed = other_core(same)
-    weights = pl.pallas_call(
-        weights_kernel,
-        name="weights",
+    half_cost = pl.CostEstimate(
+        flops=2 * local_diam * columns * phi.size, bytes_accessed=2 * phi.size, transcendentals=0
+    )
+    out_shape = (local_diam, columns, rows_dev)
+    part = pl.pallas_call(
+        same_kernel,
+        name="blades_same",
         in_specs=[SMEM, SMEM, VMEM, VMEM],
         out_specs=VMEM,
-        out_shape=jax.ShapeDtypeStruct((NBLADE, local_diam * columns, MODES), BF16),
+        out_shape=jax.ShapeDtypeStruct(out_shape, F32),
         compiler_params=LIMIT,
-    )(core_arg, table, same, crossed)
-    blades = jnp.einsum("ham,hmr->ar", weights, shapes_both, preferred_element_type=F32)
-    return blades.astype(BF16).reshape(local_diam, columns, rows_dev)
+        cost_estimate=half_cost,
+    )(core_arg, table, same, near)
+    part, crossed = lax.optimization_barrier((part, crossed))
+    return pl.pallas_call(
+        crossed_kernel,
+        name="blades_crossed",
+        in_specs=[SMEM, SMEM, VMEM, HBM, HBM, VMEM],
+        out_specs=VMEM,
+        out_shape=jax.ShapeDtypeStruct(out_shape, BF16),
+        scratch_shapes=[
+            pltpu.VMEM(shapes.shape, BF16),
+            pltpu.SemaphoreType.DMA((local_diam,)),
+        ],
+        compiler_params=WIDE,
+        cost_estimate=half_cost,
+    )(core_arg, table, crossed, own_hbm, recv_hbm, part)
 
 
 def solution(mesh):

time: 89.8 us -> 85.4 us (0.951)
  matrix products: 6.99 us -> 1.34 us
  local copies, waits for them, and re-layouts: 6.07 us -> 1.46 us
  Pallas kernels: 11.2 us -> 15.8 us
  waiting for transfers between devices: 7.15 us -> 8.9 us
  other arithmetic: 1.84 us -> 0.94 us
    dot_general x1 -> x0, matrix products: 5.66 us -> none  [chunk_plan(): jnp.einsum('ham,hmr->ar', weights, shapes_both, preferred_element_type=F32)]
    pallas_call x3 -> x4, Pallas kernels: 6.69 us -> 11.5 us  [the longest x1 4.19 us: chunk_plan(): pl.pallas_call(crossed_kernel, name='blades_crossed', in_specs=[SMEM, SME...]
    unnamed x10 -> x2, local copies, waits for them, and re-layouts: 4.62 us -> 0.01 us
    all_to_all x2, waiting for transfers between devices: 2.64 us -> 5.37 us  [exchange(): return lax.all_to_all(slots, 'rows', 0, 0, tiled=True)]
    ppermute x8, waiting for transfers between devices: 4.51 us -> 3.53 us  [other_core(): return lax.ppermute(value, 'diam', SWAP)]
    reduce_sum x5, other arithmetic: 1.04 us -> 0.13 us  [row_total(): return jnp.sum(got.astype(F32), axis=0)]
  transfers between devices with their start and end apart: 10 -> 10, of which waited for: 8 -> 7; matrix products, arithmetic and copies ran while one was open for 2% -> 1% of each run, Pallas kernels for 8% -> 10%
where the time goes in v4:
time: 85.4 us; the launch traced here: 84.7 us
  blocking collectives  35 us (41%)
  starting transfers between devices  21.1 us (25%)
  Pallas kernels  15.8 us (19%)
  waiting for transfers between devices  8.9 us (10%)
  local copies, waits for them, and re-layouts  1.46 us (2%)
  matrix products  1.34 us (2%)
  other arithmetic  0.94 us (1%)
    all_to_all x4, blocking collectives, exchange(): return lax.all_to_all(slots, 'rows', 0, 0, tiled=True)  35 us
    ppermute x8, starting transfers between devices, other_core(): return lax.ppermute(value, 'diam', SWAP)  10.8 us
    all_to_all x2, starting transfers between devices, exchange(): return lax.all_to_all(slots, 'rows', 0, 0, tiled=True)  10.3 us
    all_to_all x2, waiting for transfers between devices, exchange(): return lax.all_to_all(slots, 'rows', 0, 0, tiled=True)  5.37 us
    pallas_call x1, Pallas kernels, chunk_plan(): pl.pallas_call(crossed_kernel, name='blades_crossed', in_specs=[SMEM, SME...  4.19 us
    pallas_call x1, Pallas kernels, chunk_plan(): pl.pallas_call(regroup_kernel, name='regroup', in_specs=[SMEM, HBM], out_...  3.55 us
    ppermute x8, waiting for transfers between devices, other_core(): return lax.ppermute(value, 'diam', SWAP)  3.53 us
    pallas_call x1, Pallas kernels, chunk_plan(): pl.pallas_call(functools.partial(load_kernel, columns), name='load', in_s...  2.28 us
  transfers between devices with their start and end apart: 10, of which 7 were waited for; matrix products, arithmetic and copies ran while one was open for 1% of the time, Pallas kernels for 10%

profile of v4, /device:TPU:1, one launch (start us, length us, event | category | flops | bytes accessed | tf_op | source)
XLA Modules:
  0.0 84.7 jit_solution(7577303083770440618)
XLA Ops:
  0.0 2.3 %load.1 = (bf16[8,32,1024]{2,1,0:T(8,128)(2,1)S(1)}, bf16[8,200,1024]{2,1,0:T(8,128)(2,1)S(1)}) custom-call(s32[1]{0:T(128)} %bitcast.core_ref, s32[16]{0:T(128)} %harm_hbm.1, bf16[1024,512]{1,0:T(8,128)(2,1)} %loads_hbm.1, bf16[8,200,1024]{2,1,0:T(8,128)(2,1)} %bitcast.2.phi_hbm.own_hbm), custom_call_target="tpu_custom_call" | custom-call | tf_op jit(solution)/shard_map/load/pallas_call | solution.py:246
  2.3 1.1 %convolution_convert_fusion = bf16[8,32,200]{2,1,0:T(8,128)(2,1)S(1)} fusion(bf16[8,32,1024]{2,1,0:T(8,128)(2,1)S(1)} %get-tuple-element.35, bf16[8,200,1024]{2,1,0:T(8,128)(2,1)S(1)} %get-tuple-element.36), kind=kOutput, calls=%fused_computation | convolution fusion | flops 104908800 | bytes 3903488 | tf_op jit(solution)/shard_map/hcr,hmr->hcm/dot_general | solution.py:262
  3.6 1.2 %collective-permute-done = bf16[4,32,200]{2,1,0:T(8,128)(2,1)S(1)} collective-permute-done((bf16[4,32,200]{2,1,0:T(8,128)(2,1)S(1)}, bf16[4,32,200]{2,1,0:T(8,128)(2,1)S(1)}, u32[]{:S(2)}, u32[]{:S(2)}) %collective-permute-start) | collective-permute-done | bytes 51232 | tf_op jit(solution)/shard_map/ppermute | solution.py:231
  4.7 0.7 maximum_select_fusion
  5.6 6.9 %all-to-all-start = ((bf16[8,32,200]{2,1,0:T(8,128)(2,1)}), bf16[8,32,200]{2,1,0:T(8,128)(2,1)S(1)}, u32[]{:S(2)}, u32[]{:S(2)}) async-start(bf16[8,32,200]{2,1,0:T(8,128)(2,1)} %maximum_select_fusion), calls=%async_computation | async-start | bytes 262144 | tf_op jit(solution)/shard_map/all_to_all | solution.py:239
  12.5 3.5 %regroup.1 = (bf16[2,4,200,200]{3,2,1,0:T(8,128)(2,1)S(1)}, bf16[2,4,200,200]{3,2,1,0:T(8,128)(2,1)S(1)}) custom-call(s32[1]{0:T(128)} %bitcast.core_ref, f32[400,1600]{1,0:T(8,128)} %bitcast.22), custom_call_target="tpu_custom_call" | custom-call | flops 1280000 | bytes 5120000 | tf_op jit(solution)/shard_map/regroup/pallas_call | solution.py:274
  16.1 0.5 collective-permute-start.1
  16.8 0.8 dynamic_slice.7
  17.6 1.1 %all-to-all-done = bf16[8,32,200]{2,1,0:T(8,128)(2,1)S(1)} async-done(((bf16[8,32,200]{2,1,0:T(8,128)(2,1)}), bf16[8,32,200]{2,1,0:T(8,128)(2,1)S(1)}, u32[]{:S(2)}, u32[]{:S(2)}) %all-to-all-start) | async-done | bytes 102432 | tf_op jit(solution)/shard_map/all_to_all | solution.py:239
  18.8 1.8 %collective-permute-start.2 = (bf16[32,200]{1,0:T(8,128)(2,1)S(1)}, bf16[32,200]{1,0:T(8,128)(2,1)S(1)}, u32[]{:S(2)}, u32[]{:S(2)}) collective-permute-start(bf16[32,200]{1,0:T(8,128)(2,1)S(1)} %divide_convert_fusion.2.amp_ref), channel_id=1, source_target_pairs={{0,1},{1,0},{2,3},{3,2},{4,5},{5,4},{6,7},{7,6},{8,9},{9,8},{10,11... | collective-permute-start | bytes 38408 | tf_op jit(solution)/shard_map/ppermute | solution.py:231
  20.6 0.3 product.8.rest_0_
  20.8 0.6 collective-permute-done.2.amp_ref
  21.4 0.3 product.9
  21.7 9.2 %all_to_all.30 = bf16[8,32,200]{2,1,0:T(8,128)(2,1)S(1)} all-to-all(bf16[8,32,200]{2,1,0:T(8,128)(2,1)S(1)} %product.9), channel_id=1, replica_groups=mesh['grp'=2,'rows'=8,'diam'=2] {'rows'}, dimensions={0} | all-to-all | bytes 204800 | tf_op jit(solution)/shard_map/all_to_all | solution.py:239
  30.9 1.8 %collective-permute-start.4 = (bf16[32,200]{1,0:T(8,128)(2,1)S(1)}, bf16[32,200]{1,0:T(8,128)(2,1)S(1)}, u32[]{:S(2)}, u32[]{:S(2)}) collective-permute-start(bf16[32,200]{1,0:T(8,128)(2,1)S(1)} %subtract_divide_fusion.1.amp_ref), channel_id=1, source_target_pairs={{0,1},{1,0},{2,3},{3,2},{4,5},{5,4},{6,7},{7,6},{8,9},{9,8},{10,11... | collective-permute-start | bytes 38408 | tf_op jit(solution)/shard_map/ppermute | solution.py:231
  33.0 0.6 collective-permute-done.4.amp_ref
  33.8 8.6 %all_to_all.31 = bf16[8,32,200]{2,1,0:T(8,128)(2,1)S(1)} all-to-all(bf16[8,32,200]{2,1,0:T(8,128)(2,1)S(1)} %product.11), channel_id=1, replica_groups=mesh['grp'=2,'rows'=8,'diam'=2] {'rows'}, dimensions={0} | all-to-all | bytes 204800 | tf_op jit(solution)/shard_map/all_to_all | solution.py:239
  42.5 1.8 %collective-permute-start.5 = (bf16[32,200]{1,0:T(8,128)(2,1)S(1)}, bf16[32,200]{1,0:T(8,128)(2,1)S(1)}, u32[]{:S(2)}, u32[]{:S(2)}) collective-permute-start(bf16[32,200]{1,0:T(8,128)(2,1)S(1)} %divide_convert_fusion.1.amp_ref), channel_id=1, source_target_pairs={{0,1},{1,0},{2,3},{3,2},{4,5},{5,4},{6,7},{7,6},{8,9},{9,8},{10,11... | collective-permute-start | bytes 38408 | tf_op jit(solution)/shard_map/ppermute | solution.py:231
  44.3 0.3 product.12.rest_0_
  44.5 0.6 collective-permute-done.5.amp_ref
  45.4 8.6 %all_to_all.32 = bf16[8,32,200]{2,1,0:T(8,128)(2,1)S(1)} all-to-all(bf16[8,32,200]{2,1,0:T(8,128)(2,1)S(1)} %product.13), channel_id=1, replica_groups=mesh['grp'=2,'rows'=8,'diam'=2] {'rows'}, dimensions={0} | all-to-all | bytes 204800 | tf_op jit(solution)/shard_map/all_to_all | solution.py:239
  54.0 1.8 %collective-permute-start.6 = (bf16[32,200]{1,0:T(8,128)(2,1)S(1)}, bf16[32,200]{1,0:T(8,128)(2,1)S(1)}, u32[]{:S(2)}, u32[]{:S(2)}) collective-permute-start(bf16[32,200]{1,0:T(8,128)(2,1)S(1)} %divide_convert_fusion.amp_ref), channel_id=1, source_target_pairs={{0,1},{1,0},{2,3},{3,2},{4,5},{5,4},{6,7},{7,6},{8,9},{9,8},{10,11... | collective-permute-start | bytes 38408 | tf_op jit(solution)/shard_map/ppermute | solution.py:231
  55.8 0.3 product.14.rest_0_
  56.1 0.6 collective-permute-done.6.amp_ref
  56.9 8.6 %all_to_all.33 = bf16[8,32,200]{2,1,0:T(8,128)(2,1)S(1)} all-to-all(bf16[8,32,200]{2,1,0:T(8,128)(2,1)S(1)} %product.15), channel_id=1, replica_groups=mesh['grp'=2,'rows'=8,'diam'=2] {'rows'}, dimensions={0} | all-to-all | bytes 204800 | tf_op jit(solution)/shard_map/all_to_all | solution.py:239
  65.5 0.7 broadcast_in_dim.33
  66.2 3.4 %all-to-all-start.5 = ((bf16[8,32,200]{2,1,0:T(8,128)(2,1)}), bf16[8,32,200]{2,1,0:T(8,128)(2,1)S(1)}, u32[]{:S(2)}, u32[]{:S(2)}) async-start(bf16[8,32,200]{2,1,0:T(8,128)(2,1)} %broadcast_in_dim.33), calls=%async_computation.5 | async-start | bytes 262144 | tf_op jit(solution)/shard_map/all_to_all | solution.py:239
  69.6 1.9 %fetch.1.near_ref = bf16[8,200,1024]{2,1,0:T(8,128)(2,1)S(1)} custom-call(s32[1]{0:T(128)} %bitcast.core_ref, bf16[8,200,1024]{2,1,0:T(8,128)(2,1)} %bitcast.2.phi_hbm.own_hbm, bf16[8,200,1024]{2,1,0:T(8,128)(2,1)} %collective-permute-done.3.recv_hbm), custom_call_target="tpu_custom_call" | custom-call | bytes 6553600 | tf_op jit(solution)/shard_map/fetch/pallas_call | solution.py:317
  71.6 4.3 %all-to-all-done.5.amp_ref = bf16[8,32,200]{2,1,0:T(8,128)(2,1)S(1)} async-done(((bf16[8,32,200]{2,1,0:T(8,128)(2,1)}), bf16[8,32,200]{2,1,0:T(8,128)(2,1)S(1)}, u32[]{:S(2)}, u32[]{:S(2)}) %all-to-all-start.5) | async-done | bytes 102432 | tf_op jit(solution)/shard_map/all_to_all | solution.py:239
  75.8 2.8 %collective-permute-start.7 = (bf16[8,32,200]{2,1,0:T(8,128)(2,1)S(1)}, bf16[8,32,200]{2,1,0:T(8,128)(2,1)S(1)}, u32[]{:S(2)}, u32[]{:S(2)}) collective-permute-start(bf16[8,32,200]{2,1,0:T(8,128)(2,1)S(1)} %all-to-all-done.5.amp_ref), channel_id=1, source_target_pairs={{0,1},{1,0},{2,3},{3,2},{4,5},{5,4},{6,7},{7,6},{8,9},{9,8},{10,11... | collective-permute-start | bytes 307208 | tf_op jit(solution)/shard_map/ppermute | solution.py:231
  78.6 1.8 %blades_same.1.prev_ref = f32[8,32,1024]{2,1,0:T(8,128)S(1)} custom-call(s32[1]{0:T(128)} %bitcast.core_ref, f32[8,16]{1,0:T(8,128)S(1)} %constant_dynamic-slice_fusion.table_ref, bf16[8,32,200]{2,1,0:T(8,128)(2,1)S(1)} %all-to-all-done.5.amp_ref, bf16[8,200,1024]{2,1,0:T(8,128)(2,1)S(1)} %fetch.1.near_ref), custom_call_target="tpu_custom_call" | custom-call | flops 838860800 | bytes 3276800 | tf_op jit(solution)/shard_map/blades_same/pallas_call | solution.py:335
  80.5 4.2 %blades_crossed.1 = bf16[8,32,1024]{2,1,0:T(8,128)(2,1)} custom-call(s32[1]{0:T(128)} %bitcast.core_ref, f32[8,16]{1,0:T(8,128)S(1)} %constant_dynamic-slice_fusion.table_ref, bf16[8,32,200]{2,1,0:T(8,128)(2,1)S(1)} %collective-permute-done.7.amp_ref, bf16[8,200,1024]{2,1,0:T(8,128)(2,1)} %bitcast.2.phi_hbm.own_hbm, ...), custom_call_target="tpu_custom_call" | custom-call | flops 838860800 | bytes 3276800 | tf_op jit(solution)/shard_map/blades_crossed/pallas_call | solution.py:345
  (28 shorter events, 1.8 us)
Async XLA Ops:
  2.3 14.3 %copy-start = (s32[16]{0:T(128)S(1)}, s32[16]{0:T(128)}, u32[]{:S(2)}) copy-start(s32[16]{0:T(128)} %param.11) | copy-start | bytes 196
  3.4 1.3 %collective-permute-start = (bf16[4,32,200]{2,1,0:T(8,128)(2,1)S(1)}, bf16[4,32,200]{2,1,0:T(8,128)(2,1)S(1)}, u32[]{:S(2)}, u32[]{:S(2)}) collective-permute-start(bf16[4,32,200]{2,1,0:T(8,128)(2,1)S(1)} %select_bitcast_fusion), channel_id=1, source_target_pairs={{0,1},{1,0},{2,3},{3,2},{4,5},{5,4},{6,7},{7,6},{8,9},{9,8},{10,11... | collective-permute-start | bytes 153608 | tf_op jit(solution)/shard_map/ppermute | solution.py:231
  5.5 25.5 %collective-permute-start.3 = (bf16[8,200,1024]{2,1,0:T(8,128)(2,1)}, bf16[8,200,1024]{2,1,0:T(8,128)(2,1)}, u32[]{:S(2)}, u32[]{:S(2)}) collective-permute-start(bf16[8,200,1024]{2,1,0:T(8,128)(2,1)} %bitcast.2.phi_hbm.own_hbm), channel_id=1, source_target_pairs={{0,1},{1,0},{2,3},{3,2},{4,5},{5,4},{6,7},{7,6},{8,9},{9,8},{10,11... | collective-permute-start | bytes 9830408 | tf_op jit(solution)/shard_map/ppermute | solution.py:231
  5.6 13.1 %all-to-all-start = ((bf16[8,32,200]{2,1,0:T(8,128)(2,1)}), bf16[8,32,200]{2,1,0:T(8,128)(2,1)S(1)}, u32[]{:S(2)}, u32[]{:S(2)}) async-start(bf16[8,32,200]{2,1,0:T(8,128)(2,1)} %maximum_select_fusion), calls=%async_computation | async-start | bytes 262144 | tf_op jit(solution)/shard_map/all_to_all | solution.py:239
  16.1 4.5 %collective-permute-start.1 = (bf16[2,4,200,200]{3,2,1,0:T(8,128)(2,1)S(1)}, bf16[2,4,200,200]{3,2,1,0:T(8,128)(2,1)S(1)}, u32[]{:S(2)}, u32[]{:S(2)}) collective-permute-start(bf16[2,4,200,200]{3,2,1,0:T(8,128)(2,1)S(1)} %get-tuple-element.46), channel_id=1, source_target_pairs={{0,1},{1,0},{2,3},{3,2},{4,5},{5,4},{6,7},{7,6},{8,9},{9,8},{10,11... | collective-permute-start | bytes 1920008 | tf_op jit(solution)/shard_map/ppermute | solution.py:231
  18.8 2.6 %collective-permute-start.2 = (bf16[32,200]{1,0:T(8,128)(2,1)S(1)}, bf16[32,200]{1,0:T(8,128)(2,1)S(1)}, u32[]{:S(2)}, u32[]{:S(2)}) collective-permute-start(bf16[32,200]{1,0:T(8,128)(2,1)S(1)} %divide_convert_fusion.2.amp_ref), channel_id=1, source_target_pairs={{0,1},{1,0},{2,3},{3,2},{4,5},{5,4},{6,7},{7,6},{8,9},{9,8},{10,11... | collective-permute-start | bytes 38408 | tf_op jit(solution)/shard_map/ppermute | solution.py:231
  30.9 2.6 %collective-permute-start.4 = (bf16[32,200]{1,0:T(8,128)(2,1)S(1)}, bf16[32,200]{1,0:T(8,128)(2,1)S(1)}, u32[]{:S(2)}, u32[]{:S(2)}) collective-permute-start(bf16[32,200]{1,0:T(8,128)(2,1)S(1)} %subtract_divide_fusion.1.amp_ref), channel_id=1, source_target_pairs={{0,1},{1,0},{2,3},{3,2},{4,5},{5,4},{6,7},{7,6},{8,9},{9,8},{10,11... | collective-permute-start | bytes 38408 | tf_op jit(solution)/shard_map/ppermute | solution.py:231
  42.5 2.6 %collective-permute-start.5 = (bf16[32,200]{1,0:T(8,128)(2,1)S(1)}, bf16[32,200]{1,0:T(8,128)(2,1)S(1)}, u32[]{:S(2)}, u32[]{:S(2)}) collective-permute-start(bf16[32,200]{1,0:T(8,128)(2,1)S(1)} %divide_convert_fusion.1.amp_ref), channel_id=1, source_target_pairs={{0,1},{1,0},{2,3},{3,2},{4,5},{5,4},{6,7},{7,6},{8,9},{9,8},{10,11... | collective-permute-start | bytes 38408 | tf_op jit(solution)/shard_map/ppermute | solution.py:231
  54.0 2.6 %collective-permute-start.6 = (bf16[32,200]{1,0:T(8,128)(2,1)S(1)}, bf16[32,200]{1,0:T(8,128)(2,1)S(1)}, u32[]{:S(2)}, u32[]{:S(2)}) collective-permute-start(bf16[32,200]{1,0:T(8,128)(2,1)S(1)} %divide_convert_fusion.amp_ref), channel_id=1, source_target_pairs={{0,1},{1,0},{2,3},{3,2},{4,5},{5,4},{6,7},{7,6},{8,9},{9,8},{10,11... | collective-permute-start | bytes 38408 | tf_op jit(solution)/shard_map/ppermute | solution.py:231
  66.2 9.6 %all-to-all-start.5 = ((bf16[8,32,200]{2,1,0:T(8,128)(2,1)}), bf16[8,32,200]{2,1,0:T(8,128)(2,1)S(1)}, u32[]{:S(2)}, u32[]{:S(2)}) async-start(bf16[8,32,200]{2,1,0:T(8,128)(2,1)} %broadcast_in_dim.33), calls=%async_computation.5 | async-start | bytes 262144 | tf_op jit(solution)/shard_map/all_to_all | solution.py:239
  75.8 4.6 %collective-permute-start.7 = (bf16[8,32,200]{2,1,0:T(8,128)(2,1)S(1)}, bf16[8,32,200]{2,1,0:T(8,128)(2,1)S(1)}, u32[]{:S(2)}, u32[]{:S(2)}) collective-permute-start(bf16[8,32,200]{2,1,0:T(8,128)(2,1)S(1)} %all-to-all-done.5.amp_ref), channel_id=1, source_target_pairs={{0,1},{1,0},{2,3},{3,2},{4,5},{5,4},{6,7},{7,6},{8,9},{9,8},{10,11... | collective-permute-start | bytes 307208 | tf_op jit(solution)/shard_map/ppermute | solution.py:231

commit v5 on v4

--- a/solution.py
+++ b/solution.py
@@ -137,30 +137,29 @@
     phi_copy.wait()
 
 
-def parity_copies(odd, own_hbm, recv_hbm, near_ref, sems):
-    pairs = own_hbm.shape[0] // 2
+def parity_copies(odd, source, near_ref, first, sems):
     return [
-        pltpu.make_async_copy(
-            ref.at[2 * k + odd], near_ref.at[at_half * pairs + k], sems.at[at_half * pairs + k]
-        )
-        for at_half, ref in enumerate((own_hbm, recv_hbm))
-        for k in range(pairs)
+        pltpu.make_async_copy(source.at[2 * k + odd], near_ref.at[first + k], sems.at[first + k])
+        for k in range(source.shape[0] // 2)
     ]
 
 
-def fetch_kernel(core_ref, own_hbm, recv_hbm, near_ref, sems):
-    copies = parity_copies(core_ref[0], own_hbm, recv_hbm, near_ref, sems)
-    for copy in copies:
-        copy.start()
-    for copy in copies:
-        copy.wait()
-
-
-def regroup_kernel(core_ref, stiff_hbm, keep_ref, send_ref, stiff_ref, sem):
+def assemble_kernel(core_ref, part_ref, recv_ref, out_ref):
+    core = core_ref[0]
+    pairs = recv_ref.shape[0]
+    for k in range(pairs):
+        out_ref[core * pairs + k] = part_ref[2 * k + core]
+        out_ref[(1 - core) * pairs + k] = recv_ref[k]
+
+
+def regroup_kernel(core_ref, stiff_hbm, own_hbm, keep_ref, send_ref, near_ref, stiff_ref, sem, near_sems):
+    core = core_ref[0]
     copy = pltpu.make_async_copy(stiff_hbm, stiff_ref, sem)
     copy.start()
+    near_copies = parity_copies(core, own_hbm, near_ref, 0, near_sems)
+    for near_copy in near_copies:
+        near_copy.start()
     copy.wait()
-    core = core_ref[0]
     for k in range(0, 2 * keep_ref.shape[1], 2):
         for chunk in range(2):
             pair = [
@@ -169,6 +168,8 @@
             ]
             keep_ref[pick(core, chunk, 1 - chunk), k // 2] = pick(core, pair[0], pair[1]).astype(BF16)
             send_ref[pick(core, 1 - chunk, chunk), k // 2] = pick(core, pair[1], pair[0]).astype(BF16)
+    for near_copy in near_copies:
+        near_copy.wait()
 
 
 def product_kernel(source, core_ref, amp_ref, keep_ref, recv_ref, *rest):
@@ -184,37 +185,46 @@
             out_ref[at] = value.astype(out_ref.dtype)
 
 
-def parity_product(odd, core, table_ref, amp_ref, near_ref, copies):
-    local_diam, columns, _ = amp_ref.shape
-    pairs = local_diam // 2
-    total = None
-    for at_half, half in enumerate((core, 1 - core)):
+def diameter_product(odd, core, at_half, k, table_ref, amp_ref, shape):
+    local_diam = amp_ref.shape[0]
+    half = 1 - core if at_half else core
+    at = half * (local_diam // 2) + k
+    amp = amp_ref[at].astype(F32)
+    weights = jnp.concatenate(
+        [(table_ref[s, 2 * at + odd] * amp).astype(BF16) for s in range(local_diam)]
+    )
+    return jnp.dot(weights, shape, preferred_element_type=F32)
+
+
+def same_kernel(core_ref, table_ref, amp_ref, near_ref, own_hbm, recv_hbm, out_ref, far_ref, rest_ref, rest_sems, far_sems):
+    core = core_ref[0]
+    pairs = near_ref.shape[0]
+    rest = parity_copies(core, recv_hbm, rest_ref, 0, rest_sems)
+    far = parity_copies(1 - core, own_hbm, far_ref, 0, far_sems)
+    far += parity_copies(1 - core, recv_hbm, far_ref, pairs, far_sems)
+    for copy in rest + far:
+        copy.start()
+    total = 0.0
+    for k in range(pairs):
+        total = total + diameter_product(core, core, 0, k, table_ref, amp_ref, near_ref[k])
+    for k in range(pairs):
+        rest[k].wait()
+        total = total + diameter_product(core, core, 1, k, table_ref, amp_ref, rest_ref[k])
+    out_ref[...] = total.reshape(out_ref.shape)
+    for copy in far:
+        copy.wait()
+
+
+def crossed_kernel(core_ref, table_ref, amp_ref, far_ref, prev_ref, out_ref):
+    core = core_ref[0]
+    pairs = far_ref.shape[0] // 2
+    total = 0.0
+    for at_half in range(2):
         for k in range(pairs):
-            at = half * pairs + k
-            amp = amp_ref[at].astype(F32)
-            weights = jnp.concatenate(
-                [(table_ref[s, 2 * at + odd] * amp).astype(BF16) for s in range(local_diam)]
+            total = total + diameter_product(
+                1 - core, core, at_half, k, table_ref, amp_ref, far_ref[at_half * pairs + k]
             )
-            if copies:
-                copies[at_half * pairs + k].wait()
-            shape = near_ref[at_half * pairs + k]
-            value = jnp.dot(weights, shape, preferred_element_type=F32)
-            total = value if total is None else total + value
-    return total.reshape(local_diam, columns, near_ref.shape[2])
-
-
-def same_kernel(core_ref, table_ref, amp_ref, near_ref, out_ref):
-    core = core_ref[0]
-    out_ref[...] = parity_product(core, core, table_ref, amp_ref, near_ref, None)
-
-
-def crossed_kernel(core_ref, table_ref, amp_ref, own_hbm, recv_hbm, prev_ref, out_ref, near_ref, sems):
-    core = core_ref[0]
-    copies = parity_copies(1 - core, own_hbm, recv_hbm, near_ref, sems)
-    for copy in copies:
-        copy.start()
-    total = parity_product(1 - core, core, table_ref, amp_ref, near_ref, copies)
-    out_ref[...] = (total + prev_ref[...]).astype(out_ref.dtype)
+    out_ref[...] = (total.reshape(out_ref.shape) + prev_ref[...]).astype(out_ref.dtype)
 
 
 def chunk_plan(phi, loads, harm_diam, mistuning, dyn_diag, blade_order):
@@ -230,11 +240,6 @@
     def other_core(value):
         return lax.ppermute(value, "diam", SWAP)
 
-    def in_half_order(own, received):
-        return jnp.where(
-            core == 0, jnp.concatenate([own, received]), jnp.concatenate([received, own])
-        )
-
     def exchange(slots):
         return lax.all_to_all(slots, "rows", 0, 0, tiled=True)
 
@@ -242,7 +247,6 @@
         return jnp.sum(got.astype(F32), axis=0)
 
     shapes = phi.T.reshape(local_diam, MODES, rows_dev)
-    shape_sized = jax.ShapeDtypeStruct(shapes.shape, BF16)
     combined, shapes_near = pl.pallas_call(
         functools.partial(load_kernel, columns),
         name="load",
@@ -250,7 +254,7 @@
         out_specs=[VMEM, VMEM],
         out_shape=[
             jax.ShapeDtypeStruct((local_diam, columns, rows_dev), BF16),
-            shape_sized,
+            jax.ShapeDtypeStruct(shapes.shape, BF16),
         ],
         scratch_shapes=[
             pltpu.SMEM(harm_diam.shape, jnp.int32),
@@ -262,34 +266,43 @@
     force_part = jnp.einsum(
         "hcr,hmr->hcm", combined, shapes_near, preferred_element_type=F32
     ).astype(BF16)
-    force_slots = in_half_order(
-        by_parity(force_part, core), other_core(by_parity(force_part, 1 - core))
-    )
-    force_slots, stiff, order, shapes_sent, dyn_diag = lax.optimization_barrier(
-        (force_slots, mistuning.T, blade_order, shapes, dyn_diag)
+    slots_shape = (local_diam, columns, MODES)
+    force_slots = pl.pallas_call(
+        assemble_kernel,
+        name="assemble",
+        in_specs=[SMEM, VMEM, VMEM],
+        out_specs=VMEM,
+        out_shape=jax.ShapeDtypeStruct(slots_shape, BF16),
+        compiler_params=LIMIT,
+    )(core_arg, force_part, other_core(by_parity(force_part, 1 - core)))
+    force_slots, stiff, order, dyn_diag, shapes_sent = lax.optimization_barrier(
+        (force_slots, mistuning.T, blade_order, dyn_diag, shapes)
     )
     force_got = exchange(force_slots)
 
     group = jax.ShapeDtypeStruct((2, pairs, MODES, MODES), BF16)
-    keep, sent = pl.pallas_call(
+    near_sized = jax.ShapeDtypeStruct((pairs, MODES, rows_dev), BF16)
+    keep, sent, near = pl.pallas_call(
         regroup_kernel,
         name="regroup",
-        in_specs=[SMEM, HBM],
-        out_specs=[VMEM, VMEM],
-        out_shape=[group, group],
-        scratch_shapes=[pltpu.VMEM(stiff.shape, F32), pltpu.SemaphoreType.DMA],
+        in_specs=[SMEM, HBM, HBM],
+        out_specs=[VMEM, VMEM, VMEM],
+        out_shape=[group, group, near_sized],
+        scratch_shapes=[
+            pltpu.VMEM(stiff.shape, F32),
+            pltpu.SemaphoreType.DMA,
+            pltpu.SemaphoreType.DMA((pairs,)),
+        ],
         compiler_params=WIDE,
         cost_estimate=pl.CostEstimate(
             flops=2 * mistuning.size, bytes_accessed=8 * mistuning.size, transcendentals=0
         ),
-    )(core_arg, *in_hbm(stiff))
+    )(core_arg, *in_hbm(stiff, shapes))
     recv = other_core(sent)
     shapes_received = other_core(shapes_sent)
     table = lax.dynamic_slice_in_dim(cyclic_rows(order), first_diam, local_diam, 0)
     dyn_own = lax.dynamic_slice_in_dim(dyn_diag, own_diam * MODES, MODES, 0)[None, :]
     force_got, keep, table, dyn_own = lax.optimization_barrier((force_got, keep, table, dyn_own))
-
-    slots_shape = (local_diam, columns, MODES)
 
     def product(source, *operands):
         return pl.pallas_call(
@@ -312,49 +325,39 @@
         amp = (force - row_total(exchange(part))) / dyn_own
         if sweep == 0:
             amp, shapes_received = lax.optimization_barrier((amp, shapes_received))
-    amp, own_hbm, recv_hbm = lax.optimization_barrier((amp, shapes, shapes_received))
     same = exchange(jnp.broadcast_to(amp.astype(BF16)[None], slots_shape))
-    near = pl.pallas_call(
-        fetch_kernel,
-        name="fetch",
-        in_specs=[SMEM, HBM, HBM],
-        out_specs=VMEM,
-        out_shape=shape_sized,
-        scratch_shapes=[pltpu.SemaphoreType.DMA((local_diam,))],
-        compiler_params=LIMIT,
-        cost_estimate=pl.CostEstimate(
-            flops=0, bytes_accessed=4 * phi.size, transcendentals=0
-        ),
-    )(core_arg, own_hbm, recv_hbm)
-    same, near = lax.optimization_barrier((same, near))
     crossed = other_core(same)
     half_cost = pl.CostEstimate(
         flops=2 * local_diam * columns * phi.size, bytes_accessed=2 * phi.size, transcendentals=0
     )
     out_shape = (local_diam, columns, rows_dev)
-    part = pl.pallas_call(
+    part, far = pl.pallas_call(
         same_kernel,
         name="blades_same",
-        in_specs=[SMEM, SMEM, VMEM, VMEM],
-        out_specs=VMEM,
-        out_shape=jax.ShapeDtypeStruct(out_shape, F32),
-        compiler_params=LIMIT,
+        in_specs=[SMEM, SMEM, VMEM, VMEM, HBM, HBM],
+        out_specs=[VMEM, VMEM],
+        out_shape=[
+            jax.ShapeDtypeStruct(out_shape, F32),
+            jax.ShapeDtypeStruct(shapes.shape, BF16),
+        ],
+        scratch_shapes=[
+            pltpu.VMEM(near.shape, BF16),
+            pltpu.SemaphoreType.DMA((pairs,)),
+            pltpu.SemaphoreType.DMA((local_diam,)),
+        ],
+        compiler_params=WIDE,
         cost_estimate=half_cost,
-    )(core_arg, table, same, near)
-    part, crossed = lax.optimization_barrier((part, crossed))
+    )(core_arg, table, same, near, *in_hbm(shapes, shapes_received))
+    part, far, crossed = lax.optimization_barrier((part, far, crossed))
     return pl.pallas_call(
         crossed_kernel,
         name="blades_crossed",
-        in_specs=[SMEM, SMEM, VMEM, HBM, HBM, VMEM],
+        in_specs=[SMEM, SMEM, VMEM, VMEM, VMEM],
         out_specs=VMEM,
         out_shape=jax.ShapeDtypeStruct(out_shape, BF16),
-        scratch_shapes=[
-            pltpu.VMEM(shapes.shape, BF16),
-            pltpu.SemaphoreType.DMA((local_diam,)),
-        ],
         compiler_params=WIDE,
         cost_estimate=half_cost,
-    )(core_arg, table, crossed, own_hbm, recv_hbm, part)
+    )(core_arg, table, crossed, far, part)
 
 
 def solution(mesh):

time: 85.4 us -> 85.5 us (level)
  blocking collectives: 35 us -> 46 us
  waiting for transfers between devices: 8.9 us -> 3.54 us
  starting transfers between devices: 21.1 us -> 16.8 us
    all_to_all x4 -> x5, blocking collectives: 35 us -> 46 us  [exchange(): return lax.all_to_all(slots, 'rows', 0, 0, tiled=True)]
    all_to_all x2 -> x1, waiting for transfers between devices: 5.37 us -> 0.01 us  [exchange(): return lax.all_to_all(slots, 'rows', 0, 0, tiled=True)]
    all_to_all x2 -> x1, starting transfers between devices: 10.3 us -> 6.88 us  [exchange(): return lax.all_to_all(slots, 'rows', 0, 0, tiled=True)]
    pallas_call x1, Pallas kernels: 1.83 us -> 3.68 us  [chunk_plan(): pl.pallas_call(same_kernel, name='blades_same', in_specs=[SMEM, SMEM, VME...]
    pallas_call x1, Pallas kernels: 4.19 us -> 2.63 us  [chunk_plan(): pl.pallas_call(crossed_kernel, name='blades_crossed', in_specs=[SMEM, SME...]
    ppermute x8, starting transfers between devices: 10.8 us -> 9.87 us  [other_core(): return lax.ppermute(value, 'diam', SWAP)]
  transfers between devices with their start and end apart: 10 -> 9, of which waited for: 7 -> 5; matrix products, arithmetic and copies ran while one was open for 1% -> 1% of each run, Pallas kernels for 10% -> 12%
where the time goes in v5:
time: 85.5 us; the launch traced here: 84.9 us
  blocking collectives  46 us (54%)
  starting transfers between devices  16.8 us (20%)
  Pallas kernels  16.1 us (19%)
  waiting for transfers between devices  3.54 us (4%)
  matrix products  1.34 us (2%)
    all_to_all x5, blocking collectives, exchange(): return lax.all_to_all(slots, 'rows', 0, 0, tiled=True)  46 us
    ppermute x8, starting transfers between devices, other_core(): return lax.ppermute(value, 'diam', SWAP)  9.87 us
    all_to_all x1, starting transfers between devices, exchange(): return lax.all_to_all(slots, 'rows', 0, 0, tiled=True)  6.88 us
    pallas_call x1, Pallas kernels, chunk_plan(): pl.pallas_call(regroup_kernel, name='regroup', in_specs=[SMEM, HBM, HBM],...  4.88 us
    pallas_call x1, Pallas kernels, chunk_plan(): pl.pallas_call(same_kernel, name='blades_same', in_specs=[SMEM, SMEM, VME...  3.68 us
    ppermute x8, waiting for transfers between devices, other_core(): return lax.ppermute(value, 'diam', SWAP)  3.54 us
    pallas_call x1, Pallas kernels, chunk_plan(): pl.pallas_call(crossed_kernel, name='blades_crossed', in_specs=[SMEM, SME...  2.63 us
    pallas_call x1, Pallas kernels, chunk_plan(): pl.pallas_call(functools.partial(load_kernel, columns), name='load', in_s...  2.28 us
  transfers between devices with their start and end apart: 9, of which 5 were waited for; matrix products, arithmetic and copies ran while one was open for 1% of the time, Pallas kernels for 12%

profile of v5, /device:TPU:1, one launch (start us, length us, event | category | flops | bytes accessed | tf_op | source)
XLA Modules:
  0.0 84.9 jit_solution(14752953669900706723)
XLA Ops:
  0.0 2.3 %load.1 = (bf16[8,32,1024]{2,1,0:T(8,128)(2,1)S(1)}, bf16[8,200,1024]{2,1,0:T(8,128)(2,1)S(1)}) custom-call(s32[1]{0:T(128)} %bitcast.core_ref, s32[16]{0:T(128)} %harm_hbm.1, bf16[1024,512]{1,0:T(8,128)(2,1)} %loads_hbm.1, bf16[8,200,1024]{2,1,0:T(8,128)(2,1)} %bitcast.2.phi_hbm.own_hbm), custom_call_target="tpu_custom_call" | custom-call | tf_op jit(solution)/shard_map/load/pallas_call | solution.py:250
  2.3 1.1 %convolution_convert_fusion.part_ref = bf16[8,32,200]{2,1,0:T(8,128)(2,1)S(1)} fusion(bf16[8,32,1024]{2,1,0:T(8,128)(2,1)S(1)} %get-tuple-element.34, bf16[8,200,1024]{2,1,0:T(8,128)(2,1)S(1)} %get-tuple-element.35), kind=kOutput, calls=%fused_computation | convolution fusion | flops 104908800 | bytes 3903488 | tf_op jit(solution)/shard_map/hcr,hmr->hcm/dot_general | solution.py:266
  3.6 1.2 %collective-permute-done.recv_ref = bf16[4,32,200]{2,1,0:T(8,128)(2,1)S(1)} collective-permute-done((bf16[4,32,200]{2,1,0:T(8,128)(2,1)S(1)}, bf16[4,32,200]{2,1,0:T(8,128)(2,1)S(1)}, u32[]{:S(2)}, u32[]{:S(2)}) %collective-permute-start) | collective-permute-done | bytes 51232 | tf_op jit(solution)/shard_map/ppermute | solution.py:241
  4.8 0.7 assemble.1
  5.6 6.9 %all-to-all-start = ((bf16[8,32,200]{2,1,0:T(8,128)(2,1)}), bf16[8,32,200]{2,1,0:T(8,128)(2,1)S(1)}, u32[]{:S(2)}, u32[]{:S(2)}) async-start(bf16[8,32,200]{2,1,0:T(8,128)(2,1)} %assemble.1), calls=%async_computation | async-start | bytes 262144 | tf_op jit(solution)/shard_map/all_to_all | solution.py:244
  12.5 4.9 %regroup.1 = (bf16[2,4,200,200]{3,2,1,0:T(8,128)(2,1)S(1)}, bf16[2,4,200,200]{3,2,1,0:T(8,128)(2,1)}, bf16[4,200,1024]{2,1,0:T(8,128)(2,1)S(1)}) custom-call(s32[1]{0:T(128)} %bitcast.core_ref, f32[400,1600]{1,0:T(8,128)} %bitcast.23, bf16[8,200,1024]{2,1,0:T(8,128)(2,1)} %bitcast.2.phi_hbm.own_hbm), custom_call_target="tpu_custom_call" | custom-call | flops 1280000 | bytes 5120000 | tf_op jit(solution)/shard_map/regroup/pallas_call | solution.py:285
  17.4 0.5 collective-permute-start.1
  18.1 0.8 dynamic_slice.7
  18.9 1.6 %collective-permute-start.2 = (bf16[32,200]{1,0:T(8,128)(2,1)S(1)}, bf16[32,200]{1,0:T(8,128)(2,1)S(1)}, u32[]{:S(2)}, u32[]{:S(2)}) collective-permute-start(bf16[32,200]{1,0:T(8,128)(2,1)S(1)} %divide_convert_fusion.3.amp_ref), channel_id=1, source_target_pairs={{0,1},{1,0},{2,3},{3,2},{4,5},{5,4},{6,7},{7,6},{8,9},{9,8},{10,11... | collective-permute-start | bytes 38408 | tf_op jit(solution)/shard_map/ppermute | solution.py:241
  20.5 0.3 product.8.rest_0_
  20.8 0.6 collective-permute-done.2.amp_ref
  21.4 0.3 product.9
  21.6 10.7 %all_to_all.30 = bf16[8,32,200]{2,1,0:T(8,128)(2,1)S(1)} all-to-all(bf16[8,32,200]{2,1,0:T(8,128)(2,1)S(1)} %product.9), channel_id=1, replica_groups=mesh['grp'=2,'rows'=8,'diam'=2] {'rows'}, dimensions={0} | all-to-all | bytes 204800 | tf_op jit(solution)/shard_map/all_to_all | solution.py:244
  32.3 1.8 %collective-permute-start.4 = (bf16[32,200]{1,0:T(8,128)(2,1)S(1)}, bf16[32,200]{1,0:T(8,128)(2,1)S(1)}, u32[]{:S(2)}, u32[]{:S(2)}) collective-permute-start(bf16[32,200]{1,0:T(8,128)(2,1)S(1)} %subtract_divide_fusion.amp_ref), channel_id=1, source_target_pairs={{0,1},{1,0},{2,3},{3,2},{4,5},{5,4},{6,7},{7,6},{8,9},{9,8},{10,11... | collective-permute-start | bytes 38408 | tf_op jit(solution)/shard_map/ppermute | solution.py:241
  34.2 0.3 product.10.rest_0_
  34.4 0.6 collective-permute-done.4.amp_ref
  35.0 0.3 product.11
  35.3 8.6 %all_to_all.31 = bf16[8,32,200]{2,1,0:T(8,128)(2,1)S(1)} all-to-all(bf16[8,32,200]{2,1,0:T(8,128)(2,1)S(1)} %product.11), channel_id=1, replica_groups=mesh['grp'=2,'rows'=8,'diam'=2] {'rows'}, dimensions={0} | all-to-all | bytes 204800 | tf_op jit(solution)/shard_map/all_to_all | solution.py:244
  44.0 1.8 %collective-permute-start.5 = (bf16[32,200]{1,0:T(8,128)(2,1)S(1)}, bf16[32,200]{1,0:T(8,128)(2,1)S(1)}, u32[]{:S(2)}, u32[]{:S(2)}) collective-permute-start(bf16[32,200]{1,0:T(8,128)(2,1)S(1)} %divide_convert_fusion.2.amp_ref), channel_id=1, source_target_pairs={{0,1},{1,0},{2,3},{3,2},{4,5},{5,4},{6,7},{7,6},{8,9},{9,8},{10,11... | collective-permute-start | bytes 38408 | tf_op jit(solution)/shard_map/ppermute | solution.py:241
  45.7 0.2 product.12.rest_0_
  46.0 0.6 collective-permute-done.5.amp_ref
  46.6 0.3 product.13
  46.8 8.6 %all_to_all.32 = bf16[8,32,200]{2,1,0:T(8,128)(2,1)S(1)} all-to-all(bf16[8,32,200]{2,1,0:T(8,128)(2,1)S(1)} %product.13), channel_id=1, replica_groups=mesh['grp'=2,'rows'=8,'diam'=2] {'rows'}, dimensions={0} | all-to-all | bytes 204800 | tf_op jit(solution)/shard_map/all_to_all | solution.py:244
  55.5 1.8 %collective-permute-start.6 = (bf16[32,200]{1,0:T(8,128)(2,1)S(1)}, bf16[32,200]{1,0:T(8,128)(2,1)S(1)}, u32[]{:S(2)}, u32[]{:S(2)}) collective-permute-start(bf16[32,200]{1,0:T(8,128)(2,1)S(1)} %divide_convert_fusion.1.amp_ref), channel_id=1, source_target_pairs={{0,1},{1,0},{2,3},{3,2},{4,5},{5,4},{6,7},{7,6},{8,9},{9,8},{10,11... | collective-permute-start | bytes 38408 | tf_op jit(solution)/shard_map/ppermute | solution.py:241
  57.3 0.3 product.14.rest_0_
  57.5 0.6 collective-permute-done.6.amp_ref
  58.1 0.3 product.15
  58.4 8.6 %all_to_all.33 = bf16[8,32,200]{2,1,0:T(8,128)(2,1)S(1)} all-to-all(bf16[8,32,200]{2,1,0:T(8,128)(2,1)S(1)} %product.15), channel_id=1, replica_groups=mesh['grp'=2,'rows'=8,'diam'=2] {'rows'}, dimensions={0} | all-to-all | bytes 204800 | tf_op jit(solution)/shard_map/all_to_all | solution.py:244
  67.0 9.5 %all_to_all.34.amp_ref = bf16[8,32,200]{2,1,0:T(8,128)(2,1)S(1)} all-to-all(bf16[8,32,200]{2,1,0:T(8,128)(2,1)S(1)} %broadcast_in_dim.33), channel_id=1, replica_groups=mesh['grp'=2,'rows'=8,'diam'=2] {'rows'}, dimensions={0} | all-to-all | bytes 204800 | tf_op jit(solution)/shard_map/all_to_all | solution.py:244
  76.5 2.1 %collective-permute-start.7 = (bf16[8,32,200]{2,1,0:T(8,128)(2,1)S(1)}, bf16[8,32,200]{2,1,0:T(8,128)(2,1)S(1)}, u32[]{:S(2)}, u32[]{:S(2)}) collective-permute-start(bf16[8,32,200]{2,1,0:T(8,128)(2,1)S(1)} %all_to_all.34.amp_ref), channel_id=1, source_target_pairs={{0,1},{1,0},{2,3},{3,2},{4,5},{5,4},{6,7},{7,6},{8,9},{9,8},{10,11... | collective-permute-start | bytes 307208 | tf_op jit(solution)/shard_map/ppermute | solution.py:241
  78.6 3.7 %blades_same.1 = (f32[8,32,1024]{2,1,0:T(8,128)S(1)}, bf16[8,200,1024]{2,1,0:T(8,128)(2,1)S(1)}) custom-call(s32[1]{0:T(128)} %bitcast.core_ref, f32[8,16]{1,0:T(8,128)S(1)} %constant_dynamic-slice_fusion.table_ref, bf16[8,32,200]{2,1,0:T(8,128)(2,1)S(1)} %all_to_all.34.amp_ref, bf16[4,200,1024]{2,1,0:T(8,128)(2,1)S(1)} %get-tuple-element.56.near_ref, ...), custom_call_target="tpu_custom_call" | custom-call | flops 838860800 | bytes 3276800 | tf_op jit(solution)/shard_map/blades_same/pallas_call | solution.py:334
  82.3 2.6 %blades_crossed.1 = bf16[8,32,1024]{2,1,0:T(8,128)(2,1)} custom-call(s32[1]{0:T(128)} %bitcast.core_ref, f32[8,16]{1,0:T(8,128)S(1)} %constant_dynamic-slice_fusion.table_ref, bf16[8,32,200]{2,1,0:T(8,128)(2,1)S(1)} %collective-permute-done.7.amp_ref, bf16[8,200,1024]{2,1,0:T(8,128)(2,1)S(1)} %get-tuple-element.61.far_ref, ...), custom_call_target="tpu_custom_call" | custom-call | flops 838860800 | bytes 3276800 | tf_op jit(solution)/shard_map/blades_crossed/pallas_call | solution.py:352
  (25 shorter events, 0.8 us)
Async XLA Ops:
  3.4 14.4 %copy-start = (s32[16]{0:T(128)S(1)}, s32[16]{0:T(128)}, u32[]{:S(2)}) copy-start(s32[16]{0:T(128)} %param.11) | copy-start | bytes 196
  3.4 1.3 %collective-permute-start = (bf16[4,32,200]{2,1,0:T(8,128)(2,1)S(1)}, bf16[4,32,200]{2,1,0:T(8,128)(2,1)S(1)}, u32[]{:S(2)}, u32[]{:S(2)}) collective-permute-start(bf16[4,32,200]{2,1,0:T(8,128)(2,1)S(1)} %fusion.1), channel_id=1, source_target_pairs={{0,1},{1,0},{2,3},{3,2},{4,5},{5,4},{6,7},{7,6},{8,9},{9,8},{10,11... | collective-permute-start | bytes 153608 | tf_op jit(solution)/shard_map/ppermute | solution.py:241
  5.4 26.9 %collective-permute-start.3 = (bf16[8,200,1024]{2,1,0:T(8,128)(2,1)}, bf16[8,200,1024]{2,1,0:T(8,128)(2,1)}, u32[]{:S(2)}, u32[]{:S(2)}) collective-permute-start(bf16[8,200,1024]{2,1,0:T(8,128)(2,1)} %bitcast.2.phi_hbm.own_hbm), channel_id=1, source_target_pairs={{0,1},{1,0},{2,3},{3,2},{4,5},{5,4},{6,7},{7,6},{8,9},{9,8},{10,11... | collective-permute-start | bytes 9830408 | tf_op jit(solution)/shard_map/ppermute | solution.py:241
  5.6 13.3 %all-to-all-start = ((bf16[8,32,200]{2,1,0:T(8,128)(2,1)}), bf16[8,32,200]{2,1,0:T(8,128)(2,1)S(1)}, u32[]{:S(2)}, u32[]{:S(2)}) async-start(bf16[8,32,200]{2,1,0:T(8,128)(2,1)} %assemble.1), calls=%async_computation | async-start | bytes 262144 | tf_op jit(solution)/shard_map/all_to_all | solution.py:244
  17.4 3.2 %collective-permute-start.1 = (bf16[2,4,200,200]{3,2,1,0:T(8,128)(2,1)}, bf16[2,4,200,200]{3,2,1,0:T(8,128)(2,1)S(1)}, u32[]{:S(2)}, u32[]{:S(2)}) collective-permute-start(bf16[2,4,200,200]{3,2,1,0:T(8,128)(2,1)} %get-tuple-element.45), channel_id=1, source_target_pairs={{0,1},{1,0},{2,3},{3,2},{4,5},{5,4},{6,7},{7,6},{8,9},{9,8},{10,11... | collective-permute-start | bytes 1920008 | tf_op jit(solution)/shard_map/ppermute | solution.py:241
  18.9 2.4 %collective-permute-start.2 = (bf16[32,200]{1,0:T(8,128)(2,1)S(1)}, bf16[32,200]{1,0:T(8,128)(2,1)S(1)}, u32[]{:S(2)}, u32[]{:S(2)}) collective-permute-start(bf16[32,200]{1,0:T(8,128)(2,1)S(1)} %divide_convert_fusion.3.amp_ref), channel_id=1, source_target_pairs={{0,1},{1,0},{2,3},{3,2},{4,5},{5,4},{6,7},{7,6},{8,9},{9,8},{10,11... | collective-permute-start | bytes 38408 | tf_op jit(solution)/shard_map/ppermute | solution.py:241
  32.3 2.7 %collective-permute-start.4 = (bf16[32,200]{1,0:T(8,128)(2,1)S(1)}, bf16[32,200]{1,0:T(8,128)(2,1)S(1)}, u32[]{:S(2)}, u32[]{:S(2)}) collective-permute-start(bf16[32,200]{1,0:T(8,128)(2,1)S(1)} %subtract_divide_fusion.amp_ref), channel_id=1, source_target_pairs={{0,1},{1,0},{2,3},{3,2},{4,5},{5,4},{6,7},{7,6},{8,9},{9,8},{10,11... | collective-permute-start | bytes 38408 | tf_op jit(solution)/shard_map/ppermute | solution.py:241
  44.0 2.6 %collective-permute-start.5 = (bf16[32,200]{1,0:T(8,128)(2,1)S(1)}, bf16[32,200]{1,0:T(8,128)(2,1)S(1)}, u32[]{:S(2)}, u32[]{:S(2)}) collective-permute-start(bf16[32,200]{1,0:T(8,128)(2,1)S(1)} %divide_convert_fusion.2.amp_ref), channel_id=1, source_target_pairs={{0,1},{1,0},{2,3},{3,2},{4,5},{5,4},{6,7},{7,6},{8,9},{9,8},{10,11... | collective-permute-start | bytes 38408 | tf_op jit(solution)/shard_map/ppermute | solution.py:241
  55.5 2.6 %collective-permute-start.6 = (bf16[32,200]{1,0:T(8,128)(2,1)S(1)}, bf16[32,200]{1,0:T(8,128)(2,1)S(1)}, u32[]{:S(2)}, u32[]{:S(2)}) collective-permute-start(bf16[32,200]{1,0:T(8,128)(2,1)S(1)} %divide_convert_fusion.1.amp_ref), channel_id=1, source_target_pairs={{0,1},{1,0},{2,3},{3,2},{4,5},{5,4},{6,7},{7,6},{8,9},{9,8},{10,11... | collective-permute-start | bytes 38408 | tf_op jit(solution)/shard_map/ppermute | solution.py:241
  76.5 5.8 %collective-permute-start.7 = (bf16[8,32,200]{2,1,0:T(8,128)(2,1)S(1)}, bf16[8,32,200]{2,1,0:T(8,128)(2,1)S(1)}, u32[]{:S(2)}, u32[]{:S(2)}) collective-permute-start(bf16[8,32,200]{2,1,0:T(8,128)(2,1)S(1)} %all_to_all.34.amp_ref), channel_id=1, source_target_pairs={{0,1},{1,0},{2,3},{3,2},{4,5},{5,4},{6,7},{7,6},{8,9},{9,8},{10,11... | collective-permute-start | bytes 307208 | tf_op jit(solution)/shard_map/ppermute | solution.py:241

commit v6 on v5

--- a/solution.py
+++ b/solution.py
@@ -152,22 +152,26 @@
         out_ref[(1 - core) * pairs + k] = recv_ref[k]
 
 
-def regroup_kernel(core_ref, stiff_hbm, own_hbm, keep_ref, send_ref, near_ref, stiff_ref, sem, near_sems):
+def regroup_kernel(core_ref, stiff_hbm, own_hbm, keep_ref, send_ref, near_ref, stiff_ref, sems, near_sems):
     core = core_ref[0]
-    copy = pltpu.make_async_copy(stiff_hbm, stiff_ref, sem)
-    copy.start()
+    chunks = [slice(0, MODES), slice(MODES, 2 * MODES)]
+    copies = [
+        pltpu.make_async_copy(stiff_hbm.at[rows], stiff_ref.at[rows], sems.at[chunk])
+        for chunk, rows in enumerate(chunks)
+    ]
+    for copy in copies:
+        copy.start()
     near_copies = parity_copies(core, own_hbm, near_ref, 0, near_sems)
     for near_copy in near_copies:
         near_copy.start()
-    copy.wait()
-    for k in range(0, 2 * keep_ref.shape[1], 2):
-        for chunk in range(2):
-            pair = [
-                stiff_ref[chunk * MODES : (chunk + 1) * MODES, (k + odd) * MODES : (k + odd + 1) * MODES]
-                for odd in range(2)
-            ]
-            keep_ref[pick(core, chunk, 1 - chunk), k // 2] = pick(core, pair[0], pair[1]).astype(BF16)
-            send_ref[pick(core, 1 - chunk, chunk), k // 2] = pick(core, pair[1], pair[0]).astype(BF16)
+    for chunk, rows in enumerate(chunks):
+        copies[chunk].wait()
+        stiff = stiff_ref[rows].astype(BF16)
+        for k in range(keep_ref.shape[1]):
+            even = stiff[:, 2 * k * MODES : (2 * k + 1) * MODES]
+            odd = stiff[:, (2 * k + 1) * MODES : (2 * k + 2) * MODES]
+            keep_ref[pick(core, chunk, 1 - chunk), k] = pick(core, even, odd)
+            send_ref[pick(core, 1 - chunk, chunk), k] = pick(core, odd, even)
     for near_copy in near_copies:
         near_copy.wait()
 
@@ -185,46 +189,49 @@
             out_ref[at] = value.astype(out_ref.dtype)
 
 
-def diameter_product(odd, core, at_half, k, table_ref, amp_ref, shape):
-    local_diam = amp_ref.shape[0]
-    half = 1 - core if at_half else core
-    at = half * (local_diam // 2) + k
-    amp = amp_ref[at].astype(F32)
-    weights = jnp.concatenate(
-        [(table_ref[s, 2 * at + odd] * amp).astype(BF16) for s in range(local_diam)]
-    )
-    return jnp.dot(weights, shape, preferred_element_type=F32)
-
-
-def same_kernel(core_ref, table_ref, amp_ref, near_ref, own_hbm, recv_hbm, out_ref, far_ref, rest_ref, rest_sems, far_sems):
+def blades_kernel(core_ref, table_ref, same_ref, crossed_ref, near_ref, own_hbm, recv_hbm, out_hbm, far_ref, weights_ref, total_ref, out_ref, sems, out_sems):
     core = core_ref[0]
-    pairs = near_ref.shape[0]
-    rest = parity_copies(core, recv_hbm, rest_ref, 0, rest_sems)
-    far = parity_copies(1 - core, own_hbm, far_ref, 0, far_sems)
-    far += parity_copies(1 - core, recv_hbm, far_ref, pairs, far_sems)
-    for copy in rest + far:
+    local_diam, columns, _ = same_ref.shape
+    pairs = local_diam // 2
+    copies = parity_copies(core, recv_hbm, far_ref, 0, sems)
+    copies += parity_copies(1 - core, own_hbm, far_ref, pairs, sems)
+    copies += parity_copies(1 - core, recv_hbm, far_ref, 2 * pairs, sems)
+    for copy in copies:
         copy.start()
-    total = 0.0
-    for k in range(pairs):
-        total = total + diameter_product(core, core, 0, k, table_ref, amp_ref, near_ref[k])
-    for k in range(pairs):
-        rest[k].wait()
-        total = total + diameter_product(core, core, 1, k, table_ref, amp_ref, rest_ref[k])
-    out_ref[...] = total.reshape(out_ref.shape)
-    for copy in far:
-        copy.wait()
-
-
-def crossed_kernel(core_ref, table_ref, amp_ref, far_ref, prev_ref, out_ref):
-    core = core_ref[0]
-    pairs = far_ref.shape[0] // 2
-    total = 0.0
-    for at_half in range(2):
+    groups = [(core, core, same_ref), (1 - core, core, same_ref)]
+    groups += [(core, 1 - core, crossed_ref), (1 - core, 1 - core, crossed_ref)]
+    for g, (half, odd, amp_ref) in enumerate(groups):
         for k in range(pairs):
-            total = total + diameter_product(
-                1 - core, core, at_half, k, table_ref, amp_ref, far_ref[at_half * pairs + k]
-            )
-    out_ref[...] = (total.reshape(out_ref.shape) + prev_ref[...]).astype(out_ref.dtype)
+            at = half * pairs + k
+            amp = amp_ref[at].astype(F32)
+            for s in range(local_diam):
+                value = table_ref[s, 2 * at + odd] * amp
+                weights_ref[g * pairs + k, s * columns : (s + 1) * columns] = value.astype(BF16)
+        if g:
+            for copy in copies[(g - 1) * pairs : g * pairs]:
+                copy.wait()
+        last = g + 1 == len(groups)
+        wide = total_ref.shape[1] // 4 if last else total_ref.shape[1]
+        for tile in range(total_ref.shape[1] // wide):
+            lanes = slice(tile * wide, (tile + 1) * wide)
+            total = total_ref[:, lanes] if g else 0.0
+            for k in range(pairs):
+                shape = near_ref[k] if g == 0 else far_ref[(g - 1) * pairs + k, :, lanes]
+                total = total + jnp.dot(
+                    weights_ref[g * pairs + k], shape, preferred_element_type=F32
+                )
+            if last:
+                out_ref[:, :, lanes] = total.reshape(local_diam, columns, wide).astype(BF16)
+                pltpu.make_async_copy(
+                    out_ref.at[:, :, lanes], out_hbm.at[:, :, lanes], out_sems.at[tile]
+                ).start()
+            else:
+                total_ref[...] = total
+    for tile in range(4):
+        lanes = slice(tile * wide, (tile + 1) * wide)
+        pltpu.make_async_copy(
+            out_ref.at[:, :, lanes], out_hbm.at[:, :, lanes], out_sems.at[tile]
+        ).wait()
 
 
 def chunk_plan(phi, loads, harm_diam, mistuning, dyn_diag, blade_order):
@@ -267,6 +274,7 @@
         "hcr,hmr->hcm", combined, shapes_near, preferred_element_type=F32
     ).astype(BF16)
     slots_shape = (local_diam, columns, MODES)
+    force_recv = other_core(by_parity(force_part, 1 - core))
     force_slots = pl.pallas_call(
         assemble_kernel,
         name="assemble",
@@ -274,7 +282,7 @@
         out_specs=VMEM,
         out_shape=jax.ShapeDtypeStruct(slots_shape, BF16),
         compiler_params=LIMIT,
-    )(core_arg, force_part, other_core(by_parity(force_part, 1 - core)))
+    )(core_arg, force_part, force_recv)
     force_slots, stiff, order, dyn_diag, shapes_sent = lax.optimization_barrier(
         (force_slots, mistuning.T, blade_order, dyn_diag, shapes)
     )
@@ -290,7 +298,7 @@
         out_shape=[group, group, near_sized],
         scratch_shapes=[
             pltpu.VMEM(stiff.shape, F32),
-            pltpu.SemaphoreType.DMA,
+            pltpu.SemaphoreType.DMA((2,)),
             pltpu.SemaphoreType.DMA((pairs,)),
         ],
         compiler_params=WIDE,
@@ -327,37 +335,28 @@
             amp, shapes_received = lax.optimization_barrier((amp, shapes_received))
     same = exchange(jnp.broadcast_to(amp.astype(BF16)[None], slots_shape))
     crossed = other_core(same)
-    half_cost = pl.CostEstimate(
-        flops=2 * local_diam * columns * phi.size, bytes_accessed=2 * phi.size, transcendentals=0
-    )
     out_shape = (local_diam, columns, rows_dev)
-    part, far = pl.pallas_call(
-        same_kernel,
-        name="blades_same",
-        in_specs=[SMEM, SMEM, VMEM, VMEM, HBM, HBM],
-        out_specs=[VMEM, VMEM],
-        out_shape=[
-            jax.ShapeDtypeStruct(out_shape, F32),
-            jax.ShapeDtypeStruct(shapes.shape, BF16),
-        ],
+    return pl.pallas_call(
+        blades_kernel,
+        name="blades",
+        in_specs=[SMEM, SMEM, VMEM, VMEM, VMEM, HBM, HBM],
+        out_specs=HBM,
+        out_shape=jax.ShapeDtypeStruct(out_shape, BF16),
         scratch_shapes=[
-            pltpu.VMEM(near.shape, BF16),
-            pltpu.SemaphoreType.DMA((pairs,)),
-            pltpu.SemaphoreType.DMA((local_diam,)),
+            pltpu.VMEM((3 * pairs, MODES, rows_dev), BF16),
+            pltpu.VMEM((NBLADE, local_diam * columns, MODES), BF16),
+            pltpu.VMEM((local_diam * columns, rows_dev), F32),
+            pltpu.VMEM(out_shape, BF16),
+            pltpu.SemaphoreType.DMA((3 * pairs,)),
+            pltpu.SemaphoreType.DMA((4,)),
         ],
         compiler_params=WIDE,
-        cost_estimate=half_cost,
-    )(core_arg, table, same, near, *in_hbm(shapes, shapes_received))
-    part, far, crossed = lax.optimization_barrier((part, far, crossed))
-    return pl.pallas_call(
-        crossed_kernel,
-        name="blades_crossed",
-        in_specs=[SMEM, SMEM, VMEM, VMEM, VMEM],
-        out_specs=VMEM,
-        out_shape=jax.ShapeDtypeStruct(out_shape, BF16),
-        compiler_params=WIDE,
-        cost_estimate=half_cost,
-    )(core_arg, table, crossed, far, part)
+        cost_estimate=pl.CostEstimate(
+            flops=4 * local_diam * columns * phi.size,
+            bytes_accessed=4 * phi.size,
+            transcendentals=0,
+        ),
+    )(core_arg, table, same, crossed, near, *in_hbm(shapes, shapes_received))
 
 
 def solution(mesh):

time: 85.5 us -> 85.2 us (level)
  Pallas kernels: 16.1 us -> 14.6 us
  waiting for transfers between devices: 3.54 us -> 4.78 us
    pallas_call x2 -> x1, Pallas kernels: 6.31 us -> 5.24 us  [chunk_plan(): pl.pallas_call(blades_kernel, name='blades', in_specs=[SMEM, SMEM, VMEM,...]
    ppermute x8, waiting for transfers between devices: 3.54 us -> 4.53 us  [other_core(): return lax.ppermute(value, 'diam', SWAP)]
  transfers between devices with their start and end apart: 9 -> 9, of which waited for: 5 -> 7; matrix products, arithmetic and copies ran while one was open for 1% -> 1% of each run, Pallas kernels for 12% -> 7%
where the time goes in v6:
time: 85.2 us; the launch traced here: 84.4 us
  blocking collectives  45.5 us (53%)
  starting transfers between devices  17 us (20%)
  Pallas kernels  14.6 us (17%)
  waiting for transfers between devices  4.78 us (6%)
  matrix products  1.34 us (2%)
    all_to_all x5, blocking collectives, exchange(): return lax.all_to_all(slots, 'rows', 0, 0, tiled=True)  45.5 us
    ppermute x8, starting transfers between devices, other_core(): return lax.ppermute(value, 'diam', SWAP)  10.1 us
    all_to_all x1, starting transfers between devices, exchange(): return lax.all_to_all(slots, 'rows', 0, 0, tiled=True)  6.88 us
    pallas_call x1, Pallas kernels, chunk_plan(): pl.pallas_call(blades_kernel, name='blades', in_specs=[SMEM, SMEM, VMEM,...  5.24 us
    ppermute x8, waiting for transfers between devices, other_core(): return lax.ppermute(value, 'diam', SWAP)  4.53 us
    pallas_call x1, Pallas kernels, chunk_plan(): pl.pallas_call(regroup_kernel, name='regroup', in_specs=[SMEM, HBM, HBM],...  4.4 us
    pallas_call x1, Pallas kernels, chunk_plan(): pl.pallas_call(functools.partial(load_kernel, columns), name='load', in_s...  2.28 us
    pallas_call x8, Pallas kernels, product(): pl.pallas_call(functools.partial(product_kernel, source), name='product',...  2.02 us
  transfers between devices with their start and end apart: 9, of which 7 were waited for; matrix products, arithmetic and copies ran while one was open for 1% of the time, Pallas kernels for 7%

profile of v6, /device:TPU:1, one launch (start us, length us, event | category | flops | bytes accessed | tf_op | source)
XLA Modules:
  0.0 84.4 jit_solution(6345590298354864067)
XLA Ops:
  0.0 2.3 %load.1 = (bf16[8,32,1024]{2,1,0:T(8,128)(2,1)S(1)}, bf16[8,200,1024]{2,1,0:T(8,128)(2,1)S(1)}) custom-call(s32[1]{0:T(128)} %bitcast.core_ref, s32[16]{0:T(128)} %harm_hbm.1, bf16[1024,512]{1,0:T(8,128)(2,1)} %loads_hbm.1, bf16[8,200,1024]{2,1,0:T(8,128)(2,1)} %bitcast.2.phi_hbm.own_hbm), custom_call_target="tpu_custom_call" | custom-call | tf_op jit(solution)/shard_map/load/pallas_call | solution.py:257
  2.3 1.1 %convolution_convert_fusion.part_ref = bf16[8,32,200]{2,1,0:T(8,128)(2,1)S(1)} fusion(bf16[8,32,1024]{2,1,0:T(8,128)(2,1)S(1)} %get-tuple-element.29, bf16[8,200,1024]{2,1,0:T(8,128)(2,1)S(1)} %get-tuple-element.30), kind=kOutput, calls=%fused_computation | convolution fusion | flops 104908800 | bytes 3903488 | tf_op jit(solution)/shard_map/hcr,hmr->hcm/dot_general | solution.py:273
  3.6 1.2 %collective-permute-done.recv_ref = bf16[4,32,200]{2,1,0:T(8,128)(2,1)S(1)} collective-permute-done((bf16[4,32,200]{2,1,0:T(8,128)(2,1)S(1)}, bf16[4,32,200]{2,1,0:T(8,128)(2,1)S(1)}, u32[]{:S(2)}, u32[]{:S(2)}) %collective-permute-start) | collective-permute-done | bytes 51232 | tf_op jit(solution)/shard_map/ppermute | solution.py:248
  4.8 0.7 assemble.1
  5.6 6.9 %all-to-all-start = ((bf16[8,32,200]{2,1,0:T(8,128)(2,1)}), bf16[8,32,200]{2,1,0:T(8,128)(2,1)S(1)}, u32[]{:S(2)}, u32[]{:S(2)}) async-start(bf16[8,32,200]{2,1,0:T(8,128)(2,1)} %assemble.1), calls=%async_computation | async-start | bytes 262144 | tf_op jit(solution)/shard_map/all_to_all | solution.py:251
  12.5 4.4 %regroup.1 = (bf16[2,4,200,200]{3,2,1,0:T(8,128)(2,1)S(1)}, bf16[2,4,200,200]{3,2,1,0:T(8,128)(2,1)}, bf16[4,200,1024]{2,1,0:T(8,128)(2,1)S(1)}) custom-call(s32[1]{0:T(128)} %bitcast.core_ref, f32[400,1600]{1,0:T(8,128)} %bitcast.23, bf16[8,200,1024]{2,1,0:T(8,128)(2,1)} %bitcast.2.phi_hbm.own_hbm), custom_call_target="tpu_custom_call" | custom-call | flops 1280000 | bytes 5120000 | tf_op jit(solution)/shard_map/regroup/pallas_call | solution.py:293
  16.9 0.5 collective-permute-start.1
  17.6 0.8 dynamic_slice.7
  18.4 0.3 all-to-all-done
  18.7 1.8 %collective-permute-start.2 = (bf16[32,200]{1,0:T(8,128)(2,1)S(1)}, bf16[32,200]{1,0:T(8,128)(2,1)S(1)}, u32[]{:S(2)}, u32[]{:S(2)}) collective-permute-start(bf16[32,200]{1,0:T(8,128)(2,1)S(1)} %divide_convert_fusion.3.amp_ref), channel_id=1, source_target_pairs={{0,1},{1,0},{2,3},{3,2},{4,5},{5,4},{6,7},{7,6},{8,9},{9,8},{10,11... | collective-permute-start | bytes 38408 | tf_op jit(solution)/shard_map/ppermute | solution.py:248
  20.5 0.3 product.8.rest_0_
  20.8 0.6 collective-permute-done.2.amp_ref
  21.4 0.3 product.9
  21.6 10.2 %all_to_all.30 = bf16[8,32,200]{2,1,0:T(8,128)(2,1)S(1)} all-to-all(bf16[8,32,200]{2,1,0:T(8,128)(2,1)S(1)} %product.9), channel_id=1, replica_groups=mesh['grp'=2,'rows'=8,'diam'=2] {'rows'}, dimensions={0} | all-to-all | bytes 204800 | tf_op jit(solution)/shard_map/all_to_all | solution.py:251
  31.9 1.8 %collective-permute-start.4 = (bf16[32,200]{1,0:T(8,128)(2,1)S(1)}, bf16[32,200]{1,0:T(8,128)(2,1)S(1)}, u32[]{:S(2)}, u32[]{:S(2)}) collective-permute-start(bf16[32,200]{1,0:T(8,128)(2,1)S(1)} %subtract_divide_fusion.amp_ref), channel_id=1, source_target_pairs={{0,1},{1,0},{2,3},{3,2},{4,5},{5,4},{6,7},{7,6},{8,9},{9,8},{10,11... | collective-permute-start | bytes 38408 | tf_op jit(solution)/shard_map/ppermute | solution.py:248
  33.7 0.3 product.10.rest_0_
  34.0 0.6 collective-permute-done.4.amp_ref
  34.6 0.3 product.11
  34.8 8.6 %all_to_all.31 = bf16[8,32,200]{2,1,0:T(8,128)(2,1)S(1)} all-to-all(bf16[8,32,200]{2,1,0:T(8,128)(2,1)S(1)} %product.11), channel_id=1, replica_groups=mesh['grp'=2,'rows'=8,'diam'=2] {'rows'}, dimensions={0} | all-to-all | bytes 204800 | tf_op jit(solution)/shard_map/all_to_all | solution.py:251
  43.5 1.8 %collective-permute-start.5 = (bf16[32,200]{1,0:T(8,128)(2,1)S(1)}, bf16[32,200]{1,0:T(8,128)(2,1)S(1)}, u32[]{:S(2)}, u32[]{:S(2)}) collective-permute-start(bf16[32,200]{1,0:T(8,128)(2,1)S(1)} %divide_convert_fusion.2.amp_ref), channel_id=1, source_target_pairs={{0,1},{1,0},{2,3},{3,2},{4,5},{5,4},{6,7},{7,6},{8,9},{9,8},{10,11... | collective-permute-start | bytes 38408 | tf_op jit(solution)/shard_map/ppermute | solution.py:248
  45.5 0.6 collective-permute-done.5.amp_ref
  46.1 0.3 product.13
  46.4 8.6 %all_to_all.32 = bf16[8,32,200]{2,1,0:T(8,128)(2,1)S(1)} all-to-all(bf16[8,32,200]{2,1,0:T(8,128)(2,1)S(1)} %product.13), channel_id=1, replica_groups=mesh['grp'=2,'rows'=8,'diam'=2] {'rows'}, dimensions={0} | all-to-all | bytes 204800 | tf_op jit(solution)/shard_map/all_to_all | solution.py:251
  55.0 1.8 %collective-permute-start.6 = (bf16[32,200]{1,0:T(8,128)(2,1)S(1)}, bf16[32,200]{1,0:T(8,128)(2,1)S(1)}, u32[]{:S(2)}, u32[]{:S(2)}) collective-permute-start(bf16[32,200]{1,0:T(8,128)(2,1)S(1)} %divide_convert_fusion.1.amp_ref), channel_id=1, source_target_pairs={{0,1},{1,0},{2,3},{3,2},{4,5},{5,4},{6,7},{7,6},{8,9},{9,8},{10,11... | collective-permute-start | bytes 38408 | tf_op jit(solution)/shard_map/ppermute | solution.py:248
  56.8 0.3 product.14.rest_0_
  57.1 0.6 collective-permute-done.6.amp_ref
  57.7 0.3 product.15
  57.9 8.6 %all_to_all.33 = bf16[8,32,200]{2,1,0:T(8,128)(2,1)S(1)} all-to-all(bf16[8,32,200]{2,1,0:T(8,128)(2,1)S(1)} %product.15), channel_id=1, replica_groups=mesh['grp'=2,'rows'=8,'diam'=2] {'rows'}, dimensions={0} | all-to-all | bytes 204800 | tf_op jit(solution)/shard_map/all_to_all | solution.py:251
  66.6 9.5 %all_to_all.34.same_ref = bf16[8,32,200]{2,1,0:T(8,128)(2,1)S(1)} all-to-all(bf16[8,32,200]{2,1,0:T(8,128)(2,1)S(1)} %broadcast_in_dim.33), channel_id=1, replica_groups=mesh['grp'=2,'rows'=8,'diam'=2] {'rows'}, dimensions={0} | all-to-all | bytes 204800 | tf_op jit(solution)/shard_map/all_to_all | solution.py:251
  76.1 2.1 %collective-permute-start.7 = (bf16[8,32,200]{2,1,0:T(8,128)(2,1)S(1)}, bf16[8,32,200]{2,1,0:T(8,128)(2,1)S(1)}, u32[]{:S(2)}, u32[]{:S(2)}) collective-permute-start(bf16[8,32,200]{2,1,0:T(8,128)(2,1)S(1)} %all_to_all.34.same_ref), channel_id=1, source_target_pairs={{0,1},{1,0},{2,3},{3,2},{4,5},{5,4},{6,7},{7,6},{8,9},{9,8},{10,11... | collective-permute-start | bytes 307208 | tf_op jit(solution)/shard_map/ppermute | solution.py:248
  78.1 1.0 %collective-permute-done.7.crossed_ref = bf16[8,32,200]{2,1,0:T(8,128)(2,1)S(1)} collective-permute-done((bf16[8,32,200]{2,1,0:T(8,128)(2,1)S(1)}, bf16[8,32,200]{2,1,0:T(8,128)(2,1)S(1)}, u32[]{:S(2)}, u32[]{:S(2)}) %collective-permute-start.7) | collective-permute-done | bytes 102432 | tf_op jit(solution)/shard_map/ppermute | solution.py:248
  79.1 5.2 %blades.1 = bf16[8,32,1024]{2,1,0:T(8,128)(2,1)} custom-call(s32[1]{0:T(128)} %bitcast.core_ref, f32[8,16]{1,0:T(8,128)S(1)} %constant_dynamic-slice_fusion.table_ref, bf16[8,32,200]{2,1,0:T(8,128)(2,1)S(1)} %all_to_all.34.same_ref, bf16[8,32,200]{2,1,0:T(8,128)(2,1)S(1)} %collective-permute-done.7.crossed_ref, ...), custom_call_target="tpu_custom_call" | custom-call | flops 1677721600 | bytes 6553600 | tf_op jit(solution)/shard_map/blades/pallas_call | solution.py:339
  (24 shorter events, 1.0 us)
Async XLA Ops:
  3.4 14.0 %copy-start = (s32[16]{0:T(128)S(1)}, s32[16]{0:T(128)}, u32[]{:S(2)}) copy-start(s32[16]{0:T(128)} %param.11) | copy-start | bytes 196
  3.4 1.3 %collective-permute-start = (bf16[4,32,200]{2,1,0:T(8,128)(2,1)S(1)}, bf16[4,32,200]{2,1,0:T(8,128)(2,1)S(1)}, u32[]{:S(2)}, u32[]{:S(2)}) collective-permute-start(bf16[4,32,200]{2,1,0:T(8,128)(2,1)S(1)} %fusion.1), channel_id=1, source_target_pairs={{0,1},{1,0},{2,3},{3,2},{4,5},{5,4},{6,7},{7,6},{8,9},{9,8},{10,11... | collective-permute-start | bytes 153608 | tf_op jit(solution)/shard_map/ppermute | solution.py:248
  5.4 26.5 %collective-permute-start.3 = (bf16[8,200,1024]{2,1,0:T(8,128)(2,1)}, bf16[8,200,1024]{2,1,0:T(8,128)(2,1)}, u32[]{:S(2)}, u32[]{:S(2)}) collective-permute-start(bf16[8,200,1024]{2,1,0:T(8,128)(2,1)} %bitcast.2.phi_hbm.own_hbm), channel_id=1, source_target_pairs={{0,1},{1,0},{2,3},{3,2},{4,5},{5,4},{6,7},{7,6},{8,9},{9,8},{10,11... | collective-permute-start | bytes 9830408 | tf_op jit(solution)/shard_map/ppermute | solution.py:248
  5.6 13.1 %all-to-all-start = ((bf16[8,32,200]{2,1,0:T(8,128)(2,1)}), bf16[8,32,200]{2,1,0:T(8,128)(2,1)S(1)}, u32[]{:S(2)}, u32[]{:S(2)}) async-start(bf16[8,32,200]{2,1,0:T(8,128)(2,1)} %assemble.1), calls=%async_computation | async-start | bytes 262144 | tf_op jit(solution)/shard_map/all_to_all | solution.py:251
  16.9 3.6 %collective-permute-start.1 = (bf16[2,4,200,200]{3,2,1,0:T(8,128)(2,1)}, bf16[2,4,200,200]{3,2,1,0:T(8,128)(2,1)S(1)}, u32[]{:S(2)}, u32[]{:S(2)}) collective-permute-start(bf16[2,4,200,200]{3,2,1,0:T(8,128)(2,1)} %get-tuple-element.40), channel_id=1, source_target_pairs={{0,1},{1,0},{2,3},{3,2},{4,5},{5,4},{6,7},{7,6},{8,9},{9,8},{10,11... | collective-permute-start | bytes 1920008 | tf_op jit(solution)/shard_map/ppermute | solution.py:248
  18.7 2.6 %collective-permute-start.2 = (bf16[32,200]{1,0:T(8,128)(2,1)S(1)}, bf16[32,200]{1,0:T(8,128)(2,1)S(1)}, u32[]{:S(2)}, u32[]{:S(2)}) collective-permute-start(bf16[32,200]{1,0:T(8,128)(2,1)S(1)} %divide_convert_fusion.3.amp_ref), channel_id=1, source_target_pairs={{0,1},{1,0},{2,3},{3,2},{4,5},{5,4},{6,7},{7,6},{8,9},{9,8},{10,11... | collective-permute-start | bytes 38408 | tf_op jit(solution)/shard_map/ppermute | solution.py:248
  31.9 2.7 %collective-permute-start.4 = (bf16[32,200]{1,0:T(8,128)(2,1)S(1)}, bf16[32,200]{1,0:T(8,128)(2,1)S(1)}, u32[]{:S(2)}, u32[]{:S(2)}) collective-permute-start(bf16[32,200]{1,0:T(8,128)(2,1)S(1)} %subtract_divide_fusion.amp_ref), channel_id=1, source_target_pairs={{0,1},{1,0},{2,3},{3,2},{4,5},{5,4},{6,7},{7,6},{8,9},{9,8},{10,11... | collective-permute-start | bytes 38408 | tf_op jit(solution)/shard_map/ppermute | solution.py:248
  43.5 2.6 %collective-permute-start.5 = (bf16[32,200]{1,0:T(8,128)(2,1)S(1)}, bf16[32,200]{1,0:T(8,128)(2,1)S(1)}, u32[]{:S(2)}, u32[]{:S(2)}) collective-permute-start(bf16[32,200]{1,0:T(8,128)(2,1)S(1)} %divide_convert_fusion.2.amp_ref), channel_id=1, source_target_pairs={{0,1},{1,0},{2,3},{3,2},{4,5},{5,4},{6,7},{7,6},{8,9},{9,8},{10,11... | collective-permute-start | bytes 38408 | tf_op jit(solution)/shard_map/ppermute | solution.py:248
  55.0 2.6 %collective-permute-start.6 = (bf16[32,200]{1,0:T(8,128)(2,1)S(1)}, bf16[32,200]{1,0:T(8,128)(2,1)S(1)}, u32[]{:S(2)}, u32[]{:S(2)}) collective-permute-start(bf16[32,200]{1,0:T(8,128)(2,1)S(1)} %divide_convert_fusion.1.amp_ref), channel_id=1, source_target_pairs={{0,1},{1,0},{2,3},{3,2},{4,5},{5,4},{6,7},{7,6},{8,9},{9,8},{10,11... | collective-permute-start | bytes 38408 | tf_op jit(solution)/shard_map/ppermute | solution.py:248
  76.1 3.1 %collective-permute-start.7 = (bf16[8,32,200]{2,1,0:T(8,128)(2,1)S(1)}, bf16[8,32,200]{2,1,0:T(8,128)(2,1)S(1)}, u32[]{:S(2)}, u32[]{:S(2)}) collective-permute-start(bf16[8,32,200]{2,1,0:T(8,128)(2,1)S(1)} %all_to_all.34.same_ref), channel_id=1, source_target_pairs={{0,1},{1,0},{2,3},{3,2},{4,5},{5,4},{6,7},{7,6},{8,9},{9,8},{10,11... | collective-permute-start | bytes 307208 | tf_op jit(solution)/shard_map/ppermute | solution.py:248

commit v7 on v6

--- a/solution.py
+++ b/solution.py
@@ -137,13 +137,6 @@
     phi_copy.wait()
 
 
-def parity_copies(odd, source, near_ref, first, sems):
-    return [
-        pltpu.make_async_copy(source.at[2 * k + odd], near_ref.at[first + k], sems.at[first + k])
-        for k in range(source.shape[0] // 2)
-    ]
-
-
 def assemble_kernel(core_ref, part_ref, recv_ref, out_ref):
     core = core_ref[0]
     pairs = recv_ref.shape[0]
@@ -152,7 +145,7 @@
         out_ref[(1 - core) * pairs + k] = recv_ref[k]
 
 
-def regroup_kernel(core_ref, stiff_hbm, own_hbm, keep_ref, send_ref, near_ref, stiff_ref, sems, near_sems):
+def regroup_kernel(core_ref, stiff_hbm, keep_ref, send_ref, stiff_ref, sems):
     core = core_ref[0]
     chunks = [slice(0, MODES), slice(MODES, 2 * MODES)]
     copies = [
@@ -161,9 +154,6 @@
     ]
     for copy in copies:
         copy.start()
-    near_copies = parity_copies(core, own_hbm, near_ref, 0, near_sems)
-    for near_copy in near_copies:
-        near_copy.start()
     for chunk, rows in enumerate(chunks):
         copies[chunk].wait()
         stiff = stiff_ref[rows].astype(BF16)
@@ -172,8 +162,6 @@
             odd = stiff[:, (2 * k + 1) * MODES : (2 * k + 2) * MODES]
             keep_ref[pick(core, chunk, 1 - chunk), k] = pick(core, even, odd)
             send_ref[pick(core, 1 - chunk, chunk), k] = pick(core, odd, even)
-    for near_copy in near_copies:
-        near_copy.wait()
 
 
 def product_kernel(source, core_ref, amp_ref, keep_ref, recv_ref, *rest):
@@ -189,49 +177,25 @@
             out_ref[at] = value.astype(out_ref.dtype)
 
 
-def blades_kernel(core_ref, table_ref, same_ref, crossed_ref, near_ref, own_hbm, recv_hbm, out_hbm, far_ref, weights_ref, total_ref, out_ref, sems, out_sems):
+def blades_kernel(crossed, core_ref, table_ref, amp_ref, own_ref, recv_ref, *rest):
+    *prev_ref, out_ref, weights_ref = rest
     core = core_ref[0]
-    local_diam, columns, _ = same_ref.shape
+    local_diam, columns, _ = amp_ref.shape
     pairs = local_diam // 2
-    copies = parity_copies(core, recv_hbm, far_ref, 0, sems)
-    copies += parity_copies(1 - core, own_hbm, far_ref, pairs, sems)
-    copies += parity_copies(1 - core, recv_hbm, far_ref, 2 * pairs, sems)
-    for copy in copies:
-        copy.start()
-    groups = [(core, core, same_ref), (1 - core, core, same_ref)]
-    groups += [(core, 1 - core, crossed_ref), (1 - core, 1 - core, crossed_ref)]
-    for g, (half, odd, amp_ref) in enumerate(groups):
+    odd = 1 - core if crossed else core
+    total = prev_ref[0][...] if crossed else 0.0
+    for at_half, (half, phi_ref) in enumerate(((core, own_ref), (1 - core, recv_ref))):
         for k in range(pairs):
             at = half * pairs + k
+            place = at_half * pairs + k
             amp = amp_ref[at].astype(F32)
             for s in range(local_diam):
                 value = table_ref[s, 2 * at + odd] * amp
-                weights_ref[g * pairs + k, s * columns : (s + 1) * columns] = value.astype(BF16)
-        if g:
-            for copy in copies[(g - 1) * pairs : g * pairs]:
-                copy.wait()
-        last = g + 1 == len(groups)
-        wide = total_ref.shape[1] // 4 if last else total_ref.shape[1]
-        for tile in range(total_ref.shape[1] // wide):
-            lanes = slice(tile * wide, (tile + 1) * wide)
-            total = total_ref[:, lanes] if g else 0.0
-            for k in range(pairs):
-                shape = near_ref[k] if g == 0 else far_ref[(g - 1) * pairs + k, :, lanes]
-                total = total + jnp.dot(
-                    weights_ref[g * pairs + k], shape, preferred_element_type=F32
-                )
-            if last:
-                out_ref[:, :, lanes] = total.reshape(local_diam, columns, wide).astype(BF16)
-                pltpu.make_async_copy(
-                    out_ref.at[:, :, lanes], out_hbm.at[:, :, lanes], out_sems.at[tile]
-                ).start()
-            else:
-                total_ref[...] = total
-    for tile in range(4):
-        lanes = slice(tile * wide, (tile + 1) * wide)
-        pltpu.make_async_copy(
-            out_ref.at[:, :, lanes], out_hbm.at[:, :, lanes], out_sems.at[tile]
-        ).wait()
+                weights_ref[place, s * columns : (s + 1) * columns] = value.astype(BF16)
+            total = total + jnp.dot(
+                weights_ref[place], phi_ref[2 * k + odd], preferred_element_type=F32
+            )
+    out_ref[...] = total.astype(out_ref.dtype).reshape(out_ref.shape)
 
 
 def chunk_plan(phi, loads, harm_diam, mistuning, dyn_diag, blade_order):
@@ -283,31 +247,28 @@
         out_shape=jax.ShapeDtypeStruct(slots_shape, BF16),
         compiler_params=LIMIT,
     )(core_arg, force_part, force_recv)
-    force_slots, stiff, order, dyn_diag, shapes_sent = lax.optimization_barrier(
-        (force_slots, mistuning.T, blade_order, dyn_diag, shapes)
+    force_slots, stiff, order, dyn_diag = lax.optimization_barrier(
+        (force_slots, mistuning.T, blade_order, dyn_diag)
     )
     force_got = exchange(force_slots)
 
     group = jax.ShapeDtypeStruct((2, pairs, MODES, MODES), BF16)
-    near_sized = jax.ShapeDtypeStruct((pairs, MODES, rows_dev), BF16)
-    keep, sent, near = pl.pallas_call(
+    keep, sent = pl.pallas_call(
         regroup_kernel,
         name="regroup",
-        in_specs=[SMEM, HBM, HBM],
-        out_specs=[VMEM, VMEM, VMEM],
-        out_shape=[group, group, near_sized],
+        in_specs=[SMEM, HBM],
+        out_specs=[VMEM, VMEM],
+        out_shape=[group, group],
         scratch_shapes=[
             pltpu.VMEM(stiff.shape, F32),
             pltpu.SemaphoreType.DMA((2,)),
-            pltpu.SemaphoreType.DMA((pairs,)),
         ],
         compiler_params=WIDE,
         cost_estimate=pl.CostEstimate(
             flops=2 * mistuning.size, bytes_accessed=8 * mistuning.size, transcendentals=0
         ),
-    )(core_arg, *in_hbm(stiff, shapes))
+    )(core_arg, *in_hbm(stiff))
     recv = other_core(sent)
-    shapes_received = other_core(shapes_sent)
     table = lax.dynamic_slice_in_dim(cyclic_rows(order), first_diam, local_diam, 0)
     dyn_own = lax.dynamic_slice_in_dim(dyn_diag, own_diam * MODES, MODES, 0)[None, :]
     force_got, keep, table, dyn_own = lax.optimization_barrier((force_got, keep, table, dyn_own))
@@ -329,34 +290,34 @@
         amp_other = other_core(amp_low)
         part = product(0, amp_low, keep, recv)
         part, amp_other = lax.optimization_barrier((part, amp_other))
+        if sweep == ITERS - 1:
+            part, shapes_sent = lax.optimization_barrier((part, shapes))
+            shapes_received = other_core(shapes_sent)
         part = product(1, amp_other, keep, recv, part)
         amp = (force - row_total(exchange(part))) / dyn_own
-        if sweep == 0:
-            amp, shapes_received = lax.optimization_barrier((amp, shapes_received))
     same = exchange(jnp.broadcast_to(amp.astype(BF16)[None], slots_shape))
     crossed = other_core(same)
-    out_shape = (local_diam, columns, rows_dev)
-    return pl.pallas_call(
-        blades_kernel,
-        name="blades",
-        in_specs=[SMEM, SMEM, VMEM, VMEM, VMEM, HBM, HBM],
-        out_specs=HBM,
-        out_shape=jax.ShapeDtypeStruct(out_shape, BF16),
-        scratch_shapes=[
-            pltpu.VMEM((3 * pairs, MODES, rows_dev), BF16),
-            pltpu.VMEM((NBLADE, local_diam * columns, MODES), BF16),
-            pltpu.VMEM((local_diam * columns, rows_dev), F32),
-            pltpu.VMEM(out_shape, BF16),
-            pltpu.SemaphoreType.DMA((3 * pairs,)),
-            pltpu.SemaphoreType.DMA((4,)),
-        ],
-        compiler_params=WIDE,
-        cost_estimate=pl.CostEstimate(
-            flops=4 * local_diam * columns * phi.size,
-            bytes_accessed=4 * phi.size,
-            transcendentals=0,
-        ),
-    )(core_arg, table, same, crossed, near, *in_hbm(shapes, shapes_received))
+
+    def blades(crossed, amps, out_shape, *prev):
+        return pl.pallas_call(
+            functools.partial(blades_kernel, crossed),
+            name="blades",
+            in_specs=[SMEM, SMEM] + [VMEM] * (3 + len(prev)),
+            out_specs=VMEM,
+            out_shape=out_shape,
+            scratch_shapes=[pltpu.VMEM((local_diam, local_diam * columns, MODES), BF16)],
+            compiler_params=WIDE,
+            cost_estimate=pl.CostEstimate(
+                flops=2 * local_diam * columns * phi.size,
+                bytes_accessed=2 * phi.size,
+                transcendentals=0,
+            ),
+        )(core_arg, table, amps, shapes_sent, shapes_received, *prev)
+
+    part = blades(False, same, jax.ShapeDtypeStruct((local_diam * columns, rows_dev), F32))
+    part, crossed = lax.optimization_barrier((part, crossed))
+    out_shape = jax.ShapeDtypeStruct((local_diam, columns, rows_dev), BF16)
+    return blades(True, crossed, out_shape, part)
 
 
 def solution(mesh):

time: 85.2 us -> 81.9 us (0.961)
  Pallas kernels: 14.6 us -> 12.7 us
  blocking collectives: 45.5 us -> 44.3 us
    pallas_call x2 -> x3, Pallas kernels: 9.64 us -> 7.71 us  [the longest x2 4.5 us: blades(): pl.pallas_call(functools.partial(blades_kernel, crossed), name='blades',...]
    all_to_all x5, blocking collectives: 45.5 us -> 44.3 us  [exchange(): return lax.all_to_all(slots, 'rows', 0, 0, tiled=True)]
    all_to_all x1, waiting for transfers between devices: 0.26 us -> 1.27 us  [exchange(): return lax.all_to_all(slots, 'rows', 0, 0, tiled=True)]
    ppermute x8, waiting for transfers between devices: 4.53 us -> 3.52 us  [other_core(): return lax.ppermute(value, 'diam', SWAP)]
  transfers between devices with their start and end apart: 9 -> 9, of which waited for: 7 -> 6; matrix products, arithmetic and copies ran while one was open for 1% -> 1% of each run, Pallas kernels for 7% -> 8%
where the time goes in v7:
time: 81.9 us; the launch traced here: 81.5 us
  blocking collectives  44.3 us (54%)
  starting transfers between devices  17.2 us (21%)
  Pallas kernels  12.7 us (16%)
  waiting for transfers between devices  4.79 us (6%)
  matrix products  1.34 us (2%)
    all_to_all x5, blocking collectives, exchange(): return lax.all_to_all(slots, 'rows', 0, 0, tiled=True)  44.3 us
    ppermute x8, starting transfers between devices, other_core(): return lax.ppermute(value, 'diam', SWAP)  10.5 us
    all_to_all x1, starting transfers between devices, exchange(): return lax.all_to_all(slots, 'rows', 0, 0, tiled=True)  6.68 us
    pallas_call x2, Pallas kernels, blades(): pl.pallas_call(functools.partial(blades_kernel, crossed), name='blades',...  4.5 us
    ppermute x8, waiting for transfers between devices, other_core(): return lax.ppermute(value, 'diam', SWAP)  3.52 us
    pallas_call x1, Pallas kernels, chunk_plan(): pl.pallas_call(regroup_kernel, name='regroup', in_specs=[SMEM, HBM], out_...  3.21 us
    pallas_call x1, Pallas kernels, chunk_plan(): pl.pallas_call(functools.partial(load_kernel, columns), name='load', in_s...  2.28 us
    pallas_call x8, Pallas kernels, product(): pl.pallas_call(functools.partial(product_kernel, source), name='product',...  2.01 us
  transfers between devices with their start and end apart: 9, of which 6 were waited for; matrix products, arithmetic and copies ran while one was open for 1% of the time, Pallas kernels for 8%

profile of v7, /device:TPU:1, one launch (start us, length us, event | category | flops | bytes accessed | tf_op | source)
XLA Modules:
  0.0 81.5 jit_solution(10916336749949237548)
XLA Ops:
  0.0 2.3 %load.1 = (bf16[8,32,1024]{2,1,0:T(8,128)(2,1)S(1)}, bf16[8,200,1024]{2,1,0:T(8,128)(2,1)S(1)}) custom-call(s32[1]{0:T(128)} %bitcast.core_ref, s32[16]{0:T(128)} %harm_hbm.1, bf16[1024,512]{1,0:T(8,128)(2,1)} %loads_hbm.1, bf16[8,200,1024]{2,1,0:T(8,128)(2,1)} %bitcast.22), custom_call_target="tpu_custom_call" | custom-call | tf_op jit(solution)/shard_map/load/pallas_call | solution.py:221
  2.3 1.1 %convolution_convert_fusion.part_ref = bf16[8,32,200]{2,1,0:T(8,128)(2,1)S(1)} fusion(bf16[8,32,1024]{2,1,0:T(8,128)(2,1)S(1)} %get-tuple-element.29, bf16[8,200,1024]{2,1,0:T(8,128)(2,1)S(1)} %get-tuple-element.30), kind=kOutput, calls=%fused_computation | convolution fusion | flops 104908800 | bytes 3903488 | tf_op jit(solution)/shard_map/hcr,hmr->hcm/dot_general | solution.py:237
  3.6 1.2 %collective-permute-done.recv_ref = bf16[4,32,200]{2,1,0:T(8,128)(2,1)S(1)} collective-permute-done((bf16[4,32,200]{2,1,0:T(8,128)(2,1)S(1)}, bf16[4,32,200]{2,1,0:T(8,128)(2,1)S(1)}, u32[]{:S(2)}, u32[]{:S(2)}) %collective-permute-start) | collective-permute-done | bytes 51232 | tf_op jit(solution)/shard_map/ppermute | solution.py:212
  4.7 0.7 assemble.1
  5.4 6.7 %all-to-all-start = ((bf16[8,32,200]{2,1,0:T(8,128)(2,1)}), bf16[8,32,200]{2,1,0:T(8,128)(2,1)S(1)}, u32[]{:S(2)}, u32[]{:S(2)}) async-start(bf16[8,32,200]{2,1,0:T(8,128)(2,1)} %assemble.1), calls=%async_computation | async-start | bytes 262144 | tf_op jit(solution)/shard_map/all_to_all | solution.py:215
  12.1 3.2 %regroup.1 = (bf16[2,4,200,200]{3,2,1,0:T(8,128)(2,1)S(1)}, bf16[2,4,200,200]{3,2,1,0:T(8,128)(2,1)S(1)}) custom-call(s32[1]{0:T(128)} %bitcast.core_ref, f32[400,1600]{1,0:T(8,128)} %bitcast.27), custom_call_target="tpu_custom_call" | custom-call | flops 1280000 | bytes 5120000 | tf_op jit(solution)/shard_map/regroup/pallas_call | solution.py:256
  15.3 0.7 collective-permute-start.1
  16.2 0.8 dynamic_slice.7
  17.0 1.3 %all-to-all-done = bf16[8,32,200]{2,1,0:T(8,128)(2,1)S(1)} async-done(((bf16[8,32,200]{2,1,0:T(8,128)(2,1)}), bf16[8,32,200]{2,1,0:T(8,128)(2,1)S(1)}, u32[]{:S(2)}, u32[]{:S(2)}) %all-to-all-start) | async-done | bytes 102432 | tf_op jit(solution)/shard_map/all_to_all | solution.py:215
  18.4 1.8 %collective-permute-start.2 = (bf16[32,200]{1,0:T(8,128)(2,1)S(1)}, bf16[32,200]{1,0:T(8,128)(2,1)S(1)}, u32[]{:S(2)}, u32[]{:S(2)}) collective-permute-start(bf16[32,200]{1,0:T(8,128)(2,1)S(1)} %divide_convert_fusion.4.amp_ref), channel_id=1, source_target_pairs={{0,1},{1,0},{2,3},{3,2},{4,5},{5,4},{6,7},{7,6},{8,9},{9,8},{10,11... | collective-permute-start | bytes 38408 | tf_op jit(solution)/shard_map/ppermute | solution.py:212
  20.2 0.3 product.8.rest_0_
  20.4 0.6 collective-permute-done.2.amp_ref
  21.0 0.3 product.9
  21.3 9.0 %all_to_all.30 = bf16[8,32,200]{2,1,0:T(8,128)(2,1)S(1)} all-to-all(bf16[8,32,200]{2,1,0:T(8,128)(2,1)S(1)} %product.9), channel_id=1, replica_groups=mesh['grp'=2,'rows'=8,'diam'=2] {'rows'}, dimensions={0} | all-to-all | bytes 204800 | tf_op jit(solution)/shard_map/all_to_all | solution.py:215
  30.3 1.8 %collective-permute-start.3 = (bf16[32,200]{1,0:T(8,128)(2,1)S(1)}, bf16[32,200]{1,0:T(8,128)(2,1)S(1)}, u32[]{:S(2)}, u32[]{:S(2)}) collective-permute-start(bf16[32,200]{1,0:T(8,128)(2,1)S(1)} %divide_convert_fusion.3.amp_ref), channel_id=1, source_target_pairs={{0,1},{1,0},{2,3},{3,2},{4,5},{5,4},{6,7},{7,6},{8,9},{9,8},{10,11... | collective-permute-start | bytes 38408 | tf_op jit(solution)/shard_map/ppermute | solution.py:212
  32.4 0.6 collective-permute-done.3.amp_ref
  33.0 0.3 product.11
  33.3 8.6 %all_to_all.31 = bf16[8,32,200]{2,1,0:T(8,128)(2,1)S(1)} all-to-all(bf16[8,32,200]{2,1,0:T(8,128)(2,1)S(1)} %product.11), channel_id=1, replica_groups=mesh['grp'=2,'rows'=8,'diam'=2] {'rows'}, dimensions={0} | all-to-all | bytes 204800 | tf_op jit(solution)/shard_map/all_to_all | solution.py:215
  41.9 1.8 %collective-permute-start.4 = (bf16[32,200]{1,0:T(8,128)(2,1)S(1)}, bf16[32,200]{1,0:T(8,128)(2,1)S(1)}, u32[]{:S(2)}, u32[]{:S(2)}) collective-permute-start(bf16[32,200]{1,0:T(8,128)(2,1)S(1)} %divide_convert_fusion.2.amp_ref), channel_id=1, source_target_pairs={{0,1},{1,0},{2,3},{3,2},{4,5},{5,4},{6,7},{7,6},{8,9},{9,8},{10,11... | collective-permute-start | bytes 38408 | tf_op jit(solution)/shard_map/ppermute | solution.py:212
  43.7 0.3 product.12.rest_0_
  44.0 0.6 collective-permute-done.4.amp_ref
  44.6 0.3 product.13
  44.8 8.6 %all_to_all.32 = bf16[8,32,200]{2,1,0:T(8,128)(2,1)S(1)} all-to-all(bf16[8,32,200]{2,1,0:T(8,128)(2,1)S(1)} %product.13), channel_id=1, replica_groups=mesh['grp'=2,'rows'=8,'diam'=2] {'rows'}, dimensions={0} | all-to-all | bytes 204800 | tf_op jit(solution)/shard_map/all_to_all | solution.py:215
  53.4 1.8 %collective-permute-start.5 = (bf16[32,200]{1,0:T(8,128)(2,1)S(1)}, bf16[32,200]{1,0:T(8,128)(2,1)S(1)}, u32[]{:S(2)}, u32[]{:S(2)}) collective-permute-start(bf16[32,200]{1,0:T(8,128)(2,1)S(1)} %divide_convert_fusion.1.amp_ref), channel_id=1, source_target_pairs={{0,1},{1,0},{2,3},{3,2},{4,5},{5,4},{6,7},{7,6},{8,9},{9,8},{10,11... | collective-permute-start | bytes 38408 | tf_op jit(solution)/shard_map/ppermute | solution.py:212
  55.5 0.6 collective-permute-done.5.amp_ref
  56.1 0.3 collective-permute-start.6
  56.4 0.3 product.15
  56.7 8.8 %all_to_all.33 = bf16[8,32,200]{2,1,0:T(8,128)(2,1)S(1)} all-to-all(bf16[8,32,200]{2,1,0:T(8,128)(2,1)S(1)} %product.15), channel_id=1, replica_groups=mesh['grp'=2,'rows'=8,'diam'=2] {'rows'}, dimensions={0} | all-to-all | bytes 204800 | tf_op jit(solution)/shard_map/all_to_all | solution.py:215
  65.5 9.3 %all_to_all.34.amp_ref = bf16[8,32,200]{2,1,0:T(8,128)(2,1)S(1)} all-to-all(bf16[8,32,200]{2,1,0:T(8,128)(2,1)S(1)} %broadcast_in_dim.33), channel_id=1, replica_groups=mesh['grp'=2,'rows'=8,'diam'=2] {'rows'}, dimensions={0} | all-to-all | bytes 204800 | tf_op jit(solution)/shard_map/all_to_all | solution.py:215
  74.9 2.1 %collective-permute-start.7 = (bf16[8,32,200]{2,1,0:T(8,128)(2,1)S(1)}, bf16[8,32,200]{2,1,0:T(8,128)(2,1)S(1)}, u32[]{:S(2)}, u32[]{:S(2)}) collective-permute-start(bf16[8,32,200]{2,1,0:T(8,128)(2,1)S(1)} %all_to_all.34.amp_ref), channel_id=1, source_target_pairs={{0,1},{1,0},{2,3},{3,2},{4,5},{5,4},{6,7},{7,6},{8,9},{9,8},{10,11... | collective-permute-start | bytes 307208 | tf_op jit(solution)/shard_map/ppermute | solution.py:212
  76.9 1.9 %blades.2.rest_0_ = f32[256,1024]{1,0:T(8,128)S(1)} custom-call(s32[1]{0:T(128)} %bitcast.core_ref, f32[8,16]{1,0:T(8,128)S(1)} %constant_dynamic-slice_fusion.table_ref, bf16[8,32,200]{2,1,0:T(8,128)(2,1)S(1)} %all_to_all.34.amp_ref, bf16[8,200,1024]{2,1,0:T(8,128)(2,1)S(1)} %bitcast.24, bf16[8,200,1024]{2,1,0:T(8,128)(2,1)S(1)} %collective-permute-done.6.recv_ref), custom_call_target="tpu_custom_call" | custom-call | flops 838860800 | bytes 3276800 | tf_op jit(solution)/shard_map/blades/pallas_call | solution.py:302
  78.8 2.7 %blades.3 = bf16[8,32,1024]{2,1,0:T(8,128)(2,1)} custom-call(s32[1]{0:T(128)} %bitcast.core_ref, f32[8,16]{1,0:T(8,128)S(1)} %constant_dynamic-slice_fusion.table_ref, bf16[8,32,200]{2,1,0:T(8,128)(2,1)S(1)} %collective-permute-done.7.amp_ref, bf16[8,200,1024]{2,1,0:T(8,128)(2,1)S(1)} %bitcast.25, bf16[8,200,1024]{2,1,0:T(8,128)(2,1)S(1)} %collective-permute-done.6.recv_ref, ...), custom_call_target="tpu_custom_call" | custom-call | flops 838860800 | bytes 3276800 | tf_op jit(solution)/shard_map/blades/pallas_call | solution.py:302
  (27 shorter events, 1.1 us)
Async XLA Ops:
  2.3 13.7 %copy-start.1 = (s32[16]{0:T(128)S(1)}, s32[16]{0:T(128)}, u32[]{:S(2)}) copy-start(s32[16]{0:T(128)} %param.11) | copy-start | bytes 196
  3.4 1.3 %collective-permute-start = (bf16[4,32,200]{2,1,0:T(8,128)(2,1)S(1)}, bf16[4,32,200]{2,1,0:T(8,128)(2,1)S(1)}, u32[]{:S(2)}, u32[]{:S(2)}) collective-permute-start(bf16[4,32,200]{2,1,0:T(8,128)(2,1)S(1)} %fusion.1), channel_id=1, source_target_pairs={{0,1},{1,0},{2,3},{3,2},{4,5},{5,4},{6,7},{7,6},{8,9},{9,8},{10,11... | collective-permute-start | bytes 153608 | tf_op jit(solution)/shard_map/ppermute | solution.py:212
  5.4 12.9 %all-to-all-start = ((bf16[8,32,200]{2,1,0:T(8,128)(2,1)}), bf16[8,32,200]{2,1,0:T(8,128)(2,1)S(1)}, u32[]{:S(2)}, u32[]{:S(2)}) async-start(bf16[8,32,200]{2,1,0:T(8,128)(2,1)} %assemble.1), calls=%async_computation | async-start | bytes 262144 | tf_op jit(solution)/shard_map/all_to_all | solution.py:215
  15.3 4.9 %collective-permute-start.1 = (bf16[2,4,200,200]{3,2,1,0:T(8,128)(2,1)S(1)}, bf16[2,4,200,200]{3,2,1,0:T(8,128)(2,1)S(1)}, u32[]{:S(2)}, u32[]{:S(2)}) collective-permute-start(bf16[2,4,200,200]{3,2,1,0:T(8,128)(2,1)S(1)} %get-tuple-element.40), channel_id=1, source_target_pairs={{0,1},{1,0},{2,3},{3,2},{4,5},{5,4},{6,7},{7,6},{8,9},{9,8},{10,11... | collective-permute-start | bytes 1920008 | tf_op jit(solution)/shard_map/ppermute | solution.py:212
  18.4 2.7 %collective-permute-start.2 = (bf16[32,200]{1,0:T(8,128)(2,1)S(1)}, bf16[32,200]{1,0:T(8,128)(2,1)S(1)}, u32[]{:S(2)}, u32[]{:S(2)}) collective-permute-start(bf16[32,200]{1,0:T(8,128)(2,1)S(1)} %divide_convert_fusion.4.amp_ref), channel_id=1, source_target_pairs={{0,1},{1,0},{2,3},{3,2},{4,5},{5,4},{6,7},{7,6},{8,9},{9,8},{10,11... | collective-permute-start | bytes 38408 | tf_op jit(solution)/shard_map/ppermute | solution.py:212
  30.3 2.6 %collective-permute-start.3 = (bf16[32,200]{1,0:T(8,128)(2,1)S(1)}, bf16[32,200]{1,0:T(8,128)(2,1)S(1)}, u32[]{:S(2)}, u32[]{:S(2)}) collective-permute-start(bf16[32,200]{1,0:T(8,128)(2,1)S(1)} %divide_convert_fusion.3.amp_ref), channel_id=1, source_target_pairs={{0,1},{1,0},{2,3},{3,2},{4,5},{5,4},{6,7},{7,6},{8,9},{9,8},{10,11... | collective-permute-start | bytes 38408 | tf_op jit(solution)/shard_map/ppermute | solution.py:212
  41.9 14.2 %copy-start = (bf16[1024,1600]{0,1:T(8,128)(2,1)S(1)}, bf16[1024,1600]{0,1:T(8,128)(2,1)}, u32[]{:S(2)}) copy-start(bf16[1024,1600]{0,1:T(8,128)(2,1)} %param.6) | copy-start | bytes 9830404
  41.9 2.6 %collective-permute-start.4 = (bf16[32,200]{1,0:T(8,128)(2,1)S(1)}, bf16[32,200]{1,0:T(8,128)(2,1)S(1)}, u32[]{:S(2)}, u32[]{:S(2)}) collective-permute-start(bf16[32,200]{1,0:T(8,128)(2,1)S(1)} %divide_convert_fusion.2.amp_ref), channel_id=1, source_target_pairs={{0,1},{1,0},{2,3},{3,2},{4,5},{5,4},{6,7},{7,6},{8,9},{9,8},{10,11... | collective-permute-start | bytes 38408 | tf_op jit(solution)/shard_map/ppermute | solution.py:212
  53.4 2.6 %collective-permute-start.5 = (bf16[32,200]{1,0:T(8,128)(2,1)S(1)}, bf16[32,200]{1,0:T(8,128)(2,1)S(1)}, u32[]{:S(2)}, u32[]{:S(2)}) collective-permute-start(bf16[32,200]{1,0:T(8,128)(2,1)S(1)} %divide_convert_fusion.1.amp_ref), channel_id=1, source_target_pairs={{0,1},{1,0},{2,3},{3,2},{4,5},{5,4},{6,7},{7,6},{8,9},{9,8},{10,11... | collective-permute-start | bytes 38408 | tf_op jit(solution)/shard_map/ppermute | solution.py:212
  56.1 20.8 %collective-permute-start.6 = (bf16[8,200,1024]{2,1,0:T(8,128)(2,1)S(1)}, bf16[8,200,1024]{2,1,0:T(8,128)(2,1)S(1)}, u32[]{:S(2)}, u32[]{:S(2)}) collective-permute-start(bf16[8,200,1024]{2,1,0:T(8,128)(2,1)S(1)} %bitcast.23), channel_id=1, source_target_pairs={{0,1},{1,0},{2,3},{3,2},{4,5},{5,4},{6,7},{7,6},{8,9},{9,8},{10,11... | collective-permute-start | bytes 9830408 | tf_op jit(solution)/shard_map/ppermute | solution.py:212
  74.9 3.9 %collective-permute-start.7 = (bf16[8,32,200]{2,1,0:T(8,128)(2,1)S(1)}, bf16[8,32,200]{2,1,0:T(8,128)(2,1)S(1)}, u32[]{:S(2)}, u32[]{:S(2)}) collective-permute-start(bf16[8,32,200]{2,1,0:T(8,128)(2,1)S(1)} %all_to_all.34.amp_ref), channel_id=1, source_target_pairs={{0,1},{1,0},{2,3},{3,2},{4,5},{5,4},{6,7},{7,6},{8,9},{9,8},{10,11... | collective-permute-start | bytes 307208 | tf_op jit(solution)/shard_map/ppermute | solution.py:212

commit v8 on v7

--- a/solution.py
+++ b/solution.py
@@ -13,6 +13,9 @@
 NHARM = 16
 ITERS = 4
 SWAP = [(0, 1), (1, 0)]
+LANES = 128
+HALF = 64
+PACKED = (56, LANES)
 F32 = jnp.float32
 BF16 = jnp.bfloat16
 
@@ -90,11 +93,6 @@
     return blades
 
 
-def by_parity(arr, parity):
-    pairs = arr.reshape((arr.shape[0] // 2, 2) + arr.shape[1:])
-    return jnp.where(parity == 0, pairs[:, 0], pairs[:, 1])
-
-
 VMEM = pl.BlockSpec(memory_space=pltpu.VMEM)
 SMEM = pl.BlockSpec(memory_space=pltpu.SMEM)
 HBM = pl.BlockSpec(memory_space=pltpu.HBM)
@@ -106,43 +104,88 @@
     return [pltpu.with_memory_space_constraint(value, pltpu.HBM) for value in values]
 
 
+def pack(value):
+    spare = jnp.zeros((value.shape[0], 2 * LANES - MODES), F32)
+    tail = jnp.concatenate([value[:, LANES:], spare], axis=1)
+    lane = lax.broadcasted_iota(jnp.int32, (8, LANES), 1)
+    middle = []
+    for row in (0, 8):
+        late = pltpu.roll(tail[row + 16 : row + 24], HALF, 1)
+        middle.append(jnp.where(lane < HALF, tail[row : row + 8], late))
+    last = jnp.zeros((8, LANES), F32)
+    for g in range(4):
+        moved = pltpu.roll(tail[8 * g : 8 * g + 8], HALF + 8 * g, 1)
+        last = jnp.where((lane >= 8 * g) & (lane < 8 * g + 8), moved, last)
+    return jnp.concatenate([value[:, :LANES], *middle, last])
+
+
+def unpack(packed):
+    lane = lax.broadcasted_iota(jnp.int32, (8, LANES), 1)
+    tail = []
+    for g in range(4):
+        row = 32 + 8 * (g % 2)
+        middle = packed[row : row + 8]
+        if g >= 2:
+            middle = pltpu.roll(middle, HALF, 1)
+        last = pltpu.roll(packed[48:56], HALF - 8 * g, 1)
+        tail.append(jnp.where(lane < HALF, middle, last))
+    return jnp.concatenate([packed[:32], jnp.concatenate(tail)], axis=1)[:, :MODES]
+
+
 def pick(core, even, odd):
     return jnp.where(core == 0, even, odd)
 
 
-def load_kernel(columns, core_ref, harm_hbm, loads_hbm, phi_hbm, combined_ref, phi_ref, harm_ref, loads_ref, sems):
-    local_diam = phi_ref.shape[0]
+def load_kernel(columns, core_ref, harm_hbm, loads_hbm, phi_hbm, send_ref, mine_ref, phi_send_ref, phi_mine_ref, harm_ref, loads_ref, sems, phi_sems):
+    core = core_ref[0]
+    pairs = phi_mine_ref.shape[0]
     harm_copy = pltpu.make_async_copy(harm_hbm, harm_ref, sems.at[0])
     harm_copy.start()
     load_copy = pltpu.make_async_copy(loads_hbm, loads_ref, sems.at[1])
     load_copy.start()
-    phi_copy = pltpu.make_async_copy(phi_hbm, phi_ref, sems.at[2])
-    phi_copy.start()
+    copies = []
+    for k in range(pairs):
+        for at, ref, odd in ((0, phi_send_ref, 1 - core), (pairs, phi_mine_ref, core)):
+            copies.append(
+                pltpu.make_async_copy(phi_hbm.at[2 * k + odd], ref.at[k], phi_sems.at[at + k])
+            )
+    for copy in copies:
+        copy.start()
     harm_copy.wait()
     wide = loads_ref.shape[1]
-    first_diam = core_ref[0] * local_diam
     col = lax.broadcasted_iota(jnp.int32, (8, wide), 1)
-    key = jnp.zeros((8, wide), jnp.int32)
+    key = jnp.full((8, wide), -1, jnp.int32)
     for k in range(NHARM):
+        diam = harm_ref[k] - 2 * pairs * core
+        place = pick((diam & 1) - core, pairs, 0) + (diam >> 1)
+        place = jnp.where((diam >= 0) & (diam < 2 * pairs), place, 2 * pairs)
         inside = (col >= k * columns) & (col < (k + 1) * columns)
-        key = jnp.where(inside, (harm_ref[k] - first_diam - k) * columns + col, key)
-    shape = (local_diam * columns, wide)
+        key = jnp.where(inside, (place - k) * columns + col, key)
+    shape = (2 * pairs * columns, wide)
     row = lax.broadcasted_iota(jnp.int32, shape, 0)
     spread = jnp.where(row == jnp.broadcast_to(key[0:1], shape), 1.0, 0.0).astype(BF16)
     load_copy.wait()
     combined = lax.dot_general(
         spread, loads_ref[...], (((1,), (1,)), ((), ())), preferred_element_type=F32
-    )
-    combined_ref[...] = combined.astype(BF16).reshape(combined_ref.shape)
-    phi_copy.wait()
-
-
-def assemble_kernel(core_ref, part_ref, recv_ref, out_ref):
+    ).astype(BF16)
+    send_ref[...] = combined[: pairs * columns].reshape(send_ref.shape)
+    mine_ref[...] = combined[pairs * columns :].reshape(mine_ref.shape)
+    for copy in copies:
+        copy.wait()
+
+
+def assemble_kernel(core_ref, mine_ref, recv_ref, out_ref):
     core = core_ref[0]
     pairs = recv_ref.shape[0]
-    for k in range(pairs):
-        out_ref[core * pairs + k] = part_ref[2 * k + core]
-        out_ref[(1 - core) * pairs + k] = recv_ref[k]
+    for half, ref in ((core, mine_ref), (1 - core, recv_ref)):
+        for k in range(pairs):
+            out_ref[half * pairs + k] = pack(ref[k].astype(F32)).astype(BF16)
+
+
+def pack_kernel(columns, row_ref, out_ref):
+    row = jnp.broadcast_to(row_ref[...], (columns, MODES))
+    out = pack(row)
+    out_ref[...] = jnp.where(out == 0.0, 1.0, out)
 
 
 def regroup_kernel(core_ref, stiff_hbm, keep_ref, send_ref, stiff_ref, sems):
@@ -168,19 +211,22 @@
     prev_ref, out_ref = rest if len(rest) == 2 else (None, rest[0])
     core = core_ref[0]
     slots = keep_ref.shape[1]
+    amp = unpack(amp_ref[...].astype(F32)).astype(BF16)
     for half, ref in ((core, keep_ref), (1 - core, recv_ref)):
         for k in range(slots):
             at = half * slots + k
-            value = jnp.dot(amp_ref[...], ref[source, k], preferred_element_type=F32)
-            if prev_ref is not None:
-                value = value + prev_ref[at]
-            out_ref[at] = value.astype(out_ref.dtype)
+            value = jnp.dot(amp, ref[source, k], preferred_element_type=F32)
+            if prev_ref is None:
+                out_ref[at] = value
+            else:
+                out_ref[at] = pack(value + prev_ref[at]).astype(BF16)
 
 
 def blades_kernel(crossed, core_ref, table_ref, amp_ref, own_ref, recv_ref, *rest):
     *prev_ref, out_ref, weights_ref = rest
     core = core_ref[0]
-    local_diam, columns, _ = amp_ref.shape
+    local_diam = amp_ref.shape[0]
+    columns = weights_ref.shape[1] // local_diam
     pairs = local_diam // 2
     odd = 1 - core if crossed else core
     total = prev_ref[0][...] if crossed else 0.0
@@ -188,7 +234,7 @@
         for k in range(pairs):
             at = half * pairs + k
             place = at_half * pairs + k
-            amp = amp_ref[at].astype(F32)
+            amp = unpack(amp_ref[at].astype(F32))
             for s in range(local_diam):
                 value = table_ref[s, 2 * at + odd] * amp
                 weights_ref[place, s * columns : (s + 1) * columns] = value.astype(BF16)
@@ -218,27 +264,28 @@
         return jnp.sum(got.astype(F32), axis=0)
 
     shapes = phi.T.reshape(local_diam, MODES, rows_dev)
-    combined, shapes_near = pl.pallas_call(
+    half_combined = jax.ShapeDtypeStruct((pairs, columns, rows_dev), BF16)
+    half_shapes = jax.ShapeDtypeStruct((pairs, MODES, rows_dev), BF16)
+    combined_send, combined_mine, shapes_send, shapes_mine = pl.pallas_call(
         functools.partial(load_kernel, columns),
         name="load",
         in_specs=[SMEM, HBM, HBM, HBM],
-        out_specs=[VMEM, VMEM],
-        out_shape=[
-            jax.ShapeDtypeStruct((local_diam, columns, rows_dev), BF16),
-            jax.ShapeDtypeStruct(shapes.shape, BF16),
-        ],
+        out_specs=[VMEM] * 4,
+        out_shape=[half_combined, half_combined, half_shapes, half_shapes],
         scratch_shapes=[
             pltpu.SMEM(harm_diam.shape, jnp.int32),
             pltpu.VMEM(loads.shape, BF16),
-            pltpu.SemaphoreType.DMA((3,)),
+            pltpu.SemaphoreType.DMA((2,)),
+            pltpu.SemaphoreType.DMA((local_diam,)),
         ],
         compiler_params=LIMIT,
     )(core_arg, *in_hbm(harm_diam, loads, shapes))
-    force_part = jnp.einsum(
-        "hcr,hmr->hcm", combined, shapes_near, preferred_element_type=F32
-    ).astype(BF16)
-    slots_shape = (local_diam, columns, MODES)
-    force_recv = other_core(by_parity(force_part, 1 - core))
+
+    def force_part(combined, near):
+        return jnp.einsum("hcr,hmr->hcm", combined, near, preferred_element_type=F32).astype(BF16)
+
+    force_recv = other_core(force_part(combined_send, shapes_send))
+    slots_shape = (local_diam,) + PACKED
     force_slots = pl.pallas_call(
         assemble_kernel,
         name="assemble",
@@ -246,7 +293,7 @@
         out_specs=VMEM,
         out_shape=jax.ShapeDtypeStruct(slots_shape, BF16),
         compiler_params=LIMIT,
-    )(core_arg, force_part, force_recv)
+    )(core_arg, force_part(combined_mine, shapes_mine), force_recv)
     force_slots, stiff, order, dyn_diag = lax.optimization_barrier(
         (force_slots, mistuning.T, blade_order, dyn_diag)
     )
@@ -270,7 +317,15 @@
     )(core_arg, *in_hbm(stiff))
     recv = other_core(sent)
     table = lax.dynamic_slice_in_dim(cyclic_rows(order), first_diam, local_diam, 0)
-    dyn_own = lax.dynamic_slice_in_dim(dyn_diag, own_diam * MODES, MODES, 0)[None, :]
+    dyn_own = pl.pallas_call(
+        functools.partial(pack_kernel, columns),
+        name="pack",
+        in_specs=[VMEM],
+        out_specs=VMEM,
+        out_shape=jax.ShapeDtypeStruct(PACKED, F32),
+        compiler_params=LIMIT,
+        cost_estimate=pl.CostEstimate(flops=1, bytes_accessed=1, transcendentals=0),
+    )(lax.dynamic_slice_in_dim(dyn_diag, own_diam * MODES, MODES, 0)[None, :])
     force_got, keep, table, dyn_own = lax.optimization_barrier((force_got, keep, table, dyn_own))
 
     def product(source, *operands):
@@ -279,7 +334,11 @@
             name="product",
             in_specs=[SMEM] + [VMEM] * len(operands),
             out_specs=VMEM,
-            out_shape=jax.ShapeDtypeStruct(slots_shape, BF16 if source else F32),
+            out_shape=(
+                jax.ShapeDtypeStruct(slots_shape, BF16)
+                if source
+                else jax.ShapeDtypeStruct((local_diam, columns, MODES), F32)
+            ),
             compiler_params=LIMIT,
         )(core_arg, *operands)
 

time: 81.9 us -> 81.6 us (level)
  Pallas kernels: 12.7 us -> 14.1 us
  waiting for transfers between devices: 4.79 us -> 3.79 us
  transfers between devices with their start and end apart: 9 -> 9, of which waited for: 6 -> 6; matrix products, arithmetic and copies ran while one was open for 1% -> 2% of each run, Pallas kernels for 8% -> 8%
where the time goes in v8:
time: 81.6 us; the launch traced here: 81.1 us
  blocking collectives  43.9 us (54%)
  starting transfers between devices  16.7 us (20%)
  Pallas kernels  14.1 us (17%)
  waiting for transfers between devices  3.79 us (5%)
  matrix products  1.44 us (2%)
  local copies, waits for them, and re-layouts  0.82 us (1%)
    all_to_all x5, blocking collectives, exchange(): return lax.all_to_all(slots, 'rows', 0, 0, tiled=True)  43.9 us
    ppermute x8, starting transfers between devices, other_core(): return lax.ppermute(value, 'diam', SWAP)  10.1 us
    all_to_all x1, starting transfers between devices, exchange(): return lax.all_to_all(slots, 'rows', 0, 0, tiled=True)  6.68 us
    pallas_call x2, Pallas kernels, blades(): pl.pallas_call(functools.partial(blades_kernel, crossed), name='blades',...  4.69 us
    pallas_call x1, Pallas kernels, chunk_plan(): pl.pallas_call(regroup_kernel, name='regroup', in_specs=[SMEM, HBM], out_...  3.21 us
    ppermute x8, waiting for transfers between devices, other_core(): return lax.ppermute(value, 'diam', SWAP)  2.71 us
    pallas_call x8, Pallas kernels, product(): pl.pallas_call(functools.partial(product_kernel, source), name='product',...  2.7 us
    pallas_call x1, Pallas kernels, chunk_plan(): pl.pallas_call(functools.partial(load_kernel, columns), name='load', in_s...  2.66 us
  transfers between devices with their start and end apart: 9, of which 6 were waited for; matrix products, arithmetic and copies ran while one was open for 2% of the time, Pallas kernels for 8%

profile of v8, /device:TPU:1, one launch (start us, length us, event | category | flops | bytes accessed | tf_op | source)
XLA Modules:
  0.0 81.1 jit_solution(1521702285350214828)
XLA Ops:
  0.0 2.7 %load.1 = (bf16[4,32,1024]{2,1,0:T(8,128)(2,1)S(1)}, bf16[4,32,1024]{2,1,0:T(8,128)(2,1)S(1)}, bf16[4,200,1024]{2,1,0:T(8,128)(2,1)S(1)}, bf16[4,200,1024]{2,1,0:T(8,128)(2,1)S(1)}) custom-call(s32[1]{0:T(128)} %bitcast.core_ref, s32[16]{0:T(128)} %harm_hbm.1, bf16[1024,512]{1,0:T(8,128)(2,1)} %loads_hbm.1, bf16[8,200,1024]{2,1,0:T(8,128)(2,1)} %bitcast.10), custom_call_target="tpu_custom_call" | custom-call | tf_op jit(solution)/shard_map/load/pallas_call | solution.py:269
  2.7 0.6 convolution_convert_fusion
  3.4 0.6 convolution_convert_fusion.1.mine_ref
  4.0 0.5 collective-permute-done.recv_ref
  4.5 0.7 assemble.1
  5.3 6.7 %all-to-all-start = ((bf16[8,56,128]{2,1,0:T(8,128)(2,1)}), bf16[8,56,128]{2,1,0:T(8,128)(2,1)S(1)}, u32[]{:S(2)}, u32[]{:S(2)}) async-start(bf16[8,56,128]{2,1,0:T(8,128)(2,1)} %assemble.1), calls=%async_computation | async-start | bytes 229376 | tf_op jit(solution)/shard_map/all_to_all | solution.py:261
  12.0 3.2 %regroup.1 = (bf16[2,4,200,200]{3,2,1,0:T(8,128)(2,1)S(1)}, bf16[2,4,200,200]{3,2,1,0:T(8,128)(2,1)S(1)}) custom-call(s32[1]{0:T(128)} %bitcast.core_ref, f32[400,1600]{1,0:T(8,128)} %bitcast.15), custom_call_target="tpu_custom_call" | custom-call | flops 1280000 | bytes 5120000 | tf_op jit(solution)/shard_map/regroup/pallas_call | solution.py:303
  15.2 0.7 collective-permute-start.1
  16.1 0.8 dynamic_slice.7
  17.0 1.1 %all-to-all-done = bf16[8,56,128]{2,1,0:T(8,128)(2,1)S(1)} async-done(((bf16[8,56,128]{2,1,0:T(8,128)(2,1)}), bf16[8,56,128]{2,1,0:T(8,128)(2,1)S(1)}, u32[]{:S(2)}, u32[]{:S(2)}) %all-to-all-start) | async-done | bytes 114720 | tf_op jit(solution)/shard_map/all_to_all | solution.py:261
  18.1 1.8 %collective-permute-start.2 = (bf16[56,128]{1,0:T(8,128)(2,1)S(1)}, bf16[56,128]{1,0:T(8,128)(2,1)S(1)}, u32[]{:S(2)}, u32[]{:S(2)}) collective-permute-start(bf16[56,128]{1,0:T(8,128)(2,1)S(1)} %divide_convert_fusion.4.amp_ref), channel_id=1, source_target_pairs={{0,1},{1,0},{2,3},{3,2},{4,5},{5,4},{6,7},{7,6},{8,9},{9,8},{10,11... | collective-permute-start | bytes 43016 | tf_op jit(solution)/shard_map/ppermute | solution.py:258
  20.0 0.3 product.8.rest_0_
  20.3 0.5 collective-permute-done.2.amp_ref
  20.8 0.4 product.9
  21.2 9.1 %all_to_all.30 = bf16[8,56,128]{2,1,0:T(8,128)(2,1)S(1)} all-to-all(bf16[8,56,128]{2,1,0:T(8,128)(2,1)S(1)} %product.9), channel_id=1, replica_groups=mesh['grp'=2,'rows'=8,'diam'=2] {'rows'}, dimensions={0} | all-to-all | bytes 229376 | tf_op jit(solution)/shard_map/all_to_all | solution.py:261
  30.3 1.7 %collective-permute-start.3 = (bf16[56,128]{1,0:T(8,128)(2,1)S(1)}, bf16[56,128]{1,0:T(8,128)(2,1)S(1)}, u32[]{:S(2)}, u32[]{:S(2)}) collective-permute-start(bf16[56,128]{1,0:T(8,128)(2,1)S(1)} %divide_convert_fusion.3.amp_ref), channel_id=1, source_target_pairs={{0,1},{1,0},{2,3},{3,2},{4,5},{5,4},{6,7},{7,6},{8,9},{9,8},{10,11... | collective-permute-start | bytes 43016 | tf_op jit(solution)/shard_map/ppermute | solution.py:258
  32.4 0.5 collective-permute-done.3.amp_ref
  32.9 0.4 product.11
  33.3 8.5 %all_to_all.31 = bf16[8,56,128]{2,1,0:T(8,128)(2,1)S(1)} all-to-all(bf16[8,56,128]{2,1,0:T(8,128)(2,1)S(1)} %product.11), channel_id=1, replica_groups=mesh['grp'=2,'rows'=8,'diam'=2] {'rows'}, dimensions={0} | all-to-all | bytes 229376 | tf_op jit(solution)/shard_map/all_to_all | solution.py:261
  41.8 1.7 %collective-permute-start.4 = (bf16[56,128]{1,0:T(8,128)(2,1)S(1)}, bf16[56,128]{1,0:T(8,128)(2,1)S(1)}, u32[]{:S(2)}, u32[]{:S(2)}) collective-permute-start(bf16[56,128]{1,0:T(8,128)(2,1)S(1)} %divide_convert_fusion.2.amp_ref), channel_id=1, source_target_pairs={{0,1},{1,0},{2,3},{3,2},{4,5},{5,4},{6,7},{7,6},{8,9},{9,8},{10,11... | collective-permute-start | bytes 43016 | tf_op jit(solution)/shard_map/ppermute | solution.py:258
  43.8 0.5 collective-permute-done.4.amp_ref
  44.3 0.4 product.13
  44.7 8.6 %all_to_all.32 = bf16[8,56,128]{2,1,0:T(8,128)(2,1)S(1)} all-to-all(bf16[8,56,128]{2,1,0:T(8,128)(2,1)S(1)} %product.13), channel_id=1, replica_groups=mesh['grp'=2,'rows'=8,'diam'=2] {'rows'}, dimensions={0} | all-to-all | bytes 229376 | tf_op jit(solution)/shard_map/all_to_all | solution.py:261
  53.4 1.7 %collective-permute-start.5 = (bf16[56,128]{1,0:T(8,128)(2,1)S(1)}, bf16[56,128]{1,0:T(8,128)(2,1)S(1)}, u32[]{:S(2)}, u32[]{:S(2)}) collective-permute-start(bf16[56,128]{1,0:T(8,128)(2,1)S(1)} %divide_convert_fusion.1.amp_ref), channel_id=1, source_target_pairs={{0,1},{1,0},{2,3},{3,2},{4,5},{5,4},{6,7},{7,6},{8,9},{9,8},{10,11... | collective-permute-start | bytes 43016 | tf_op jit(solution)/shard_map/ppermute | solution.py:258
  55.3 0.5 collective-permute-done.5.amp_ref
  55.9 0.3 collective-permute-start.6
  56.2 0.4 product.15
  56.6 8.7 %all_to_all.33 = bf16[8,56,128]{2,1,0:T(8,128)(2,1)S(1)} all-to-all(bf16[8,56,128]{2,1,0:T(8,128)(2,1)S(1)} %product.15), channel_id=1, replica_groups=mesh['grp'=2,'rows'=8,'diam'=2] {'rows'}, dimensions={0} | all-to-all | bytes 229376 | tf_op jit(solution)/shard_map/all_to_all | solution.py:261
  65.3 9.0 %all_to_all.34.amp_ref = bf16[8,56,128]{2,1,0:T(8,128)(2,1)S(1)} all-to-all(bf16[8,56,128]{2,1,0:T(8,128)(2,1)S(1)} %broadcast_in_dim.33), channel_id=1, replica_groups=mesh['grp'=2,'rows'=8,'diam'=2] {'rows'}, dimensions={0} | all-to-all | bytes 229376 | tf_op jit(solution)/shard_map/all_to_all | solution.py:261
  74.3 2.0 %collective-permute-start.7 = (bf16[8,56,128]{2,1,0:T(8,128)(2,1)S(1)}, bf16[8,56,128]{2,1,0:T(8,128)(2,1)S(1)}, u32[]{:S(2)}, u32[]{:S(2)}) collective-permute-start(bf16[8,56,128]{2,1,0:T(8,128)(2,1)S(1)} %all_to_all.34.amp_ref), channel_id=1, source_target_pairs={{0,1},{1,0},{2,3},{3,2},{4,5},{5,4},{6,7},{7,6},{8,9},{9,8},{10,11... | collective-permute-start | bytes 344072 | tf_op jit(solution)/shard_map/ppermute | solution.py:258
  76.4 1.9 %blades.2.rest_0_ = f32[256,1024]{1,0:T(8,128)S(1)} custom-call(s32[1]{0:T(128)} %bitcast.core_ref, f32[8,16]{1,0:T(8,128)S(1)} %constant_dynamic-slice_fusion.table_ref, bf16[8,56,128]{2,1,0:T(8,128)(2,1)S(1)} %all_to_all.34.amp_ref, bf16[8,200,1024]{2,1,0:T(8,128)(2,1)S(1)} %bitcast.12, bf16[8,200,1024]{2,1,0:T(8,128)(2,1)S(1)} %collective-permute-done.6.recv_ref), custom_call_target="tpu_custom_call" | custom-call | flops 838860800 | bytes 3276800 | tf_op jit(solution)/shard_map/blades/pallas_call | solution.py:361
  78.3 2.7 %blades.3 = bf16[8,32,1024]{2,1,0:T(8,128)(2,1)} custom-call(s32[1]{0:T(128)} %bitcast.core_ref, f32[8,16]{1,0:T(8,128)S(1)} %constant_dynamic-slice_fusion.table_ref, bf16[8,56,128]{2,1,0:T(8,128)(2,1)S(1)} %collective-permute-done.7.amp_ref, bf16[8,200,1024]{2,1,0:T(8,128)(2,1)S(1)} %bitcast.13, bf16[8,200,1024]{2,1,0:T(8,128)(2,1)S(1)} %collective-permute-done.6.recv_ref, ...), custom_call_target="tpu_custom_call" | custom-call | flops 838860800 | bytes 3276800 | tf_op jit(solution)/shard_map/blades/pallas_call | solution.py:361
  (28 shorter events, 1.5 us)
Async XLA Ops:
  3.3 1.3 %collective-permute-start = (bf16[4,32,200]{2,1,0:T(8,128)(2,1)S(1)}, bf16[4,32,200]{2,1,0:T(8,128)(2,1)S(1)}, u32[]{:S(2)}, u32[]{:S(2)}) collective-permute-start(bf16[4,32,200]{2,1,0:T(8,128)(2,1)S(1)} %convolution_convert_fusion), channel_id=1, source_target_pairs={{0,1},{1,0},{2,3},{3,2},{4,5},{5,4},{6,7},{7,6},{8,9},{9,8},{10,11... | collective-permute-start | bytes 153608 | tf_op jit(solution)/shard_map/ppermute | solution.py:258
  4.0 11.9 %copy-start.1 = (s32[16]{0:T(128)S(1)}, s32[16]{0:T(128)}, u32[]{:S(2)}) copy-start(s32[16]{0:T(128)} %param.11) | copy-start | bytes 196
  5.3 12.8 %all-to-all-start = ((bf16[8,56,128]{2,1,0:T(8,128)(2,1)}), bf16[8,56,128]{2,1,0:T(8,128)(2,1)S(1)}, u32[]{:S(2)}, u32[]{:S(2)}) async-start(bf16[8,56,128]{2,1,0:T(8,128)(2,1)} %assemble.1), calls=%async_computation | async-start | bytes 229376 | tf_op jit(solution)/shard_map/all_to_all | solution.py:261
  15.2 4.8 %collective-permute-start.1 = (bf16[2,4,200,200]{3,2,1,0:T(8,128)(2,1)S(1)}, bf16[2,4,200,200]{3,2,1,0:T(8,128)(2,1)S(1)}, u32[]{:S(2)}, u32[]{:S(2)}) collective-permute-start(bf16[2,4,200,200]{3,2,1,0:T(8,128)(2,1)S(1)} %get-tuple-element.44), channel_id=1, source_target_pairs={{0,1},{1,0},{2,3},{3,2},{4,5},{5,4},{6,7},{7,6},{8,9},{9,8},{10,11... | collective-permute-start | bytes 1920008 | tf_op jit(solution)/shard_map/ppermute | solution.py:258
  18.1 2.7 %collective-permute-start.2 = (bf16[56,128]{1,0:T(8,128)(2,1)S(1)}, bf16[56,128]{1,0:T(8,128)(2,1)S(1)}, u32[]{:S(2)}, u32[]{:S(2)}) collective-permute-start(bf16[56,128]{1,0:T(8,128)(2,1)S(1)} %divide_convert_fusion.4.amp_ref), channel_id=1, source_target_pairs={{0,1},{1,0},{2,3},{3,2},{4,5},{5,4},{6,7},{7,6},{8,9},{9,8},{10,11... | collective-permute-start | bytes 43016 | tf_op jit(solution)/shard_map/ppermute | solution.py:258
  30.3 2.6 %collective-permute-start.3 = (bf16[56,128]{1,0:T(8,128)(2,1)S(1)}, bf16[56,128]{1,0:T(8,128)(2,1)S(1)}, u32[]{:S(2)}, u32[]{:S(2)}) collective-permute-start(bf16[56,128]{1,0:T(8,128)(2,1)S(1)} %divide_convert_fusion.3.amp_ref), channel_id=1, source_target_pairs={{0,1},{1,0},{2,3},{3,2},{4,5},{5,4},{6,7},{7,6},{8,9},{9,8},{10,11... | collective-permute-start | bytes 43016 | tf_op jit(solution)/shard_map/ppermute | solution.py:258
  41.8 2.5 %collective-permute-start.4 = (bf16[56,128]{1,0:T(8,128)(2,1)S(1)}, bf16[56,128]{1,0:T(8,128)(2,1)S(1)}, u32[]{:S(2)}, u32[]{:S(2)}) collective-permute-start(bf16[56,128]{1,0:T(8,128)(2,1)S(1)} %divide_convert_fusion.2.amp_ref), channel_id=1, source_target_pairs={{0,1},{1,0},{2,3},{3,2},{4,5},{5,4},{6,7},{7,6},{8,9},{9,8},{10,11... | collective-permute-start | bytes 43016 | tf_op jit(solution)/shard_map/ppermute | solution.py:258
  44.3 11.6 %copy-start = (bf16[1024,1600]{0,1:T(8,128)(2,1)S(1)}, bf16[1024,1600]{0,1:T(8,128)(2,1)}, u32[]{:S(2)}) copy-start(bf16[1024,1600]{0,1:T(8,128)(2,1)} %param.6) | copy-start | bytes 9830404
  53.4 2.5 %collective-permute-start.5 = (bf16[56,128]{1,0:T(8,128)(2,1)S(1)}, bf16[56,128]{1,0:T(8,128)(2,1)S(1)}, u32[]{:S(2)}, u32[]{:S(2)}) collective-permute-start(bf16[56,128]{1,0:T(8,128)(2,1)S(1)} %divide_convert_fusion.1.amp_ref), channel_id=1, source_target_pairs={{0,1},{1,0},{2,3},{3,2},{4,5},{5,4},{6,7},{7,6},{8,9},{9,8},{10,11... | collective-permute-start | bytes 43016 | tf_op jit(solution)/shard_map/ppermute | solution.py:258
  55.9 20.5 %collective-permute-start.6 = (bf16[8,200,1024]{2,1,0:T(8,128)(2,1)S(1)}, bf16[8,200,1024]{2,1,0:T(8,128)(2,1)S(1)}, u32[]{:S(2)}, u32[]{:S(2)}) collective-permute-start(bf16[8,200,1024]{2,1,0:T(8,128)(2,1)S(1)} %bitcast.11), channel_id=1, source_target_pairs={{0,1},{1,0},{2,3},{3,2},{4,5},{5,4},{6,7},{7,6},{8,9},{9,8},{10,11... | collective-permute-start | bytes 9830408 | tf_op jit(solution)/shard_map/ppermute | solution.py:258
  74.3 4.0 %collective-permute-start.7 = (bf16[8,56,128]{2,1,0:T(8,128)(2,1)S(1)}, bf16[8,56,128]{2,1,0:T(8,128)(2,1)S(1)}, u32[]{:S(2)}, u32[]{:S(2)}) collective-permute-start(bf16[8,56,128]{2,1,0:T(8,128)(2,1)S(1)} %all_to_all.34.amp_ref), channel_id=1, source_target_pairs={{0,1},{1,0},{2,3},{3,2},{4,5},{5,4},{6,7},{7,6},{8,9},{9,8},{10,11... | collective-permute-start | bytes 344072 | tf_op jit(solution)/shard_map/ppermute | solution.py:258

commit v9 on v7

--- a/solution.py
+++ b/solution.py
@@ -90,11 +90,6 @@
     return blades
 
 
-def by_parity(arr, parity):
-    pairs = arr.reshape((arr.shape[0] // 2, 2) + arr.shape[1:])
-    return jnp.where(parity == 0, pairs[:, 0], pairs[:, 1])
-
-
 VMEM = pl.BlockSpec(memory_space=pltpu.VMEM)
 SMEM = pl.BlockSpec(memory_space=pltpu.SMEM)
 HBM = pl.BlockSpec(memory_space=pltpu.HBM)
@@ -110,58 +105,79 @@
     return jnp.where(core == 0, even, odd)
 
 
-def load_kernel(columns, core_ref, harm_hbm, loads_hbm, phi_hbm, combined_ref, phi_ref, harm_ref, loads_ref, sems):
-    local_diam = phi_ref.shape[0]
+def load_kernel(columns, core_ref, harm_hbm, loads_hbm, phi_hbm, send_ref, mine_ref, phi_send_ref, phi_mine_ref, harm_ref, loads_ref, sems):
+    core = core_ref[0]
+    pairs = phi_mine_ref.shape[0]
     harm_copy = pltpu.make_async_copy(harm_hbm, harm_ref, sems.at[0])
     harm_copy.start()
     load_copy = pltpu.make_async_copy(loads_hbm, loads_ref, sems.at[1])
     load_copy.start()
-    phi_copy = pltpu.make_async_copy(phi_hbm, phi_ref, sems.at[2])
-    phi_copy.start()
+    copies = [
+        pltpu.make_async_copy(phi_hbm.at[:, 1 - core], phi_send_ref, sems.at[2]),
+        pltpu.make_async_copy(phi_hbm.at[:, core], phi_mine_ref, sems.at[3]),
+    ]
+    for copy in copies:
+        copy.start()
     harm_copy.wait()
     wide = loads_ref.shape[1]
-    first_diam = core_ref[0] * local_diam
     col = lax.broadcasted_iota(jnp.int32, (8, wide), 1)
-    key = jnp.zeros((8, wide), jnp.int32)
+    key = jnp.full((8, wide), -1, jnp.int32)
     for k in range(NHARM):
+        diam = harm_ref[k] - 2 * pairs * core
+        place = pick((diam & 1) - core, pairs, 0) + (diam >> 1)
+        place = jnp.where((diam >= 0) & (diam < 2 * pairs), place, 2 * pairs)
         inside = (col >= k * columns) & (col < (k + 1) * columns)
-        key = jnp.where(inside, (harm_ref[k] - first_diam - k) * columns + col, key)
-    shape = (local_diam * columns, wide)
+        key = jnp.where(inside, (place - k) * columns + col, key)
+    shape = (2 * pairs * columns, wide)
     row = lax.broadcasted_iota(jnp.int32, shape, 0)
     spread = jnp.where(row == jnp.broadcast_to(key[0:1], shape), 1.0, 0.0).astype(BF16)
     load_copy.wait()
     combined = lax.dot_general(
         spread, loads_ref[...], (((1,), (1,)), ((), ())), preferred_element_type=F32
-    )
-    combined_ref[...] = combined.astype(BF16).reshape(combined_ref.shape)
-    phi_copy.wait()
-
-
-def assemble_kernel(core_ref, part_ref, recv_ref, out_ref):
+    ).astype(BF16)
+    send_ref[...] = combined[: pairs * columns].reshape(send_ref.shape)
+    mine_ref[...] = combined[pairs * columns :].reshape(mine_ref.shape)
+    for copy in copies:
+        copy.wait()
+
+
+def assemble_kernel(core_ref, mine_ref, recv_ref, out_ref):
     core = core_ref[0]
     pairs = recv_ref.shape[0]
-    for k in range(pairs):
-        out_ref[core * pairs + k] = part_ref[2 * k + core]
-        out_ref[(1 - core) * pairs + k] = recv_ref[k]
+    for half, ref in ((core, mine_ref), (1 - core, recv_ref)):
+        for k in range(pairs):
+            out_ref[half * pairs + k] = ref[k]
 
 
 def regroup_kernel(core_ref, stiff_hbm, keep_ref, send_ref, stiff_ref, sems):
     core = core_ref[0]
-    chunks = [slice(0, MODES), slice(MODES, 2 * MODES)]
-    copies = [
-        pltpu.make_async_copy(stiff_hbm.at[rows], stiff_ref.at[rows], sems.at[chunk])
-        for chunk, rows in enumerate(chunks)
-    ]
-    for copy in copies:
-        copy.start()
-    for chunk, rows in enumerate(chunks):
-        copies[chunk].wait()
-        stiff = stiff_ref[rows].astype(BF16)
-        for k in range(keep_ref.shape[1]):
-            even = stiff[:, 2 * k * MODES : (2 * k + 1) * MODES]
-            odd = stiff[:, (2 * k + 1) * MODES : (2 * k + 2) * MODES]
-            keep_ref[pick(core, chunk, 1 - chunk), k] = pick(core, even, odd)
-            send_ref[pick(core, 1 - chunk, chunk), k] = pick(core, odd, even)
+    pieces = [(chunk, first, last) for chunk in range(2) for first, last in ((0, 112), (112, MODES))]
+    copies = []
+    for at, (chunk, first, last) in enumerate(pieces):
+        rows = pl.ds(chunk * MODES + first, last - first)
+        copies.append(
+            pltpu.make_async_copy(stiff_hbm.at[rows], stiff_ref.at[rows], sems.at[at])
+        )
+        copies[at].start()
+
+    def split(parity, refs, chunk, first, last):
+        stiff = stiff_ref[chunk * MODES + first : chunk * MODES + last].astype(BF16)
+        for k in range(2 * keep_ref.shape[1]):
+            odd = k % 2
+            owner = parity if odd == parity else 1 - parity
+            at = chunk if owner == 0 else 1 - chunk
+            refs[odd][at, k // 2, first:last] = stiff[:, k * MODES : (k + 1) * MODES]
+
+    for at, piece in enumerate(pieces):
+        copies[at].wait()
+
+        @pl.when(core == 0)
+        def _():
+            split(0, (keep_ref, send_ref), *piece)
+
+        @pl.when(core == 1)
+        def _():
+            split(1, (send_ref, keep_ref), *piece)
 
 
 def product_kernel(source, core_ref, amp_ref, keep_ref, recv_ref, *rest):
@@ -177,25 +193,53 @@
             out_ref[at] = value.astype(out_ref.dtype)
 
 
-def blades_kernel(crossed, core_ref, table_ref, amp_ref, own_ref, recv_ref, *rest):
-    *prev_ref, out_ref, weights_ref = rest
-    core = core_ref[0]
+def parity_weights(odd, core, table_ref, amp_ref, weights_ref):
     local_diam, columns, _ = amp_ref.shape
     pairs = local_diam // 2
-    odd = 1 - core if crossed else core
-    total = prev_ref[0][...] if crossed else 0.0
-    for at_half, (half, phi_ref) in enumerate(((core, own_ref), (1 - core, recv_ref))):
+    for at_half, half in enumerate((core, 1 - core)):
         for k in range(pairs):
             at = half * pairs + k
-            place = at_half * pairs + k
             amp = amp_ref[at].astype(F32)
             for s in range(local_diam):
                 value = table_ref[s, 2 * at + odd] * amp
-                weights_ref[place, s * columns : (s + 1) * columns] = value.astype(BF16)
+                weights_ref[at_half * pairs + k, s * columns : (s + 1) * columns] = value.astype(BF16)
+
+
+def parity_product(odd, weights_ref, own_ref, recv_ref, total, lanes):
+    pairs = own_ref.shape[0] // 2
+    for at_half, phi_ref in enumerate((own_ref, recv_ref)):
+        for k in range(pairs):
             total = total + jnp.dot(
-                weights_ref[place], phi_ref[2 * k + odd], preferred_element_type=F32
+                weights_ref[at_half * pairs + k],
+                phi_ref[2 * k + odd, :, lanes],
+                preferred_element_type=F32,
             )
-    out_ref[...] = total.astype(out_ref.dtype).reshape(out_ref.shape)
+    return total
+
+
+def same_kernel(core_ref, table_ref, amp_ref, own_ref, recv_ref, out_ref, weights_ref):
+    core = core_ref[0]
+    parity_weights(core, core, table_ref, amp_ref, weights_ref)
+    out_ref[...] = parity_product(core, weights_ref, own_ref, recv_ref, 0.0, slice(None))
+
+
+def crossed_kernel(core_ref, table_ref, amp_ref, own_ref, recv_ref, prev_ref, out_hbm, weights_ref, out_ref, sems):
+    core = core_ref[0]
+    parity_weights(1 - core, core, table_ref, amp_ref, weights_ref)
+    tiles = sems.shape[0]
+    wide = out_ref.shape[2] // tiles
+    copies = []
+    for tile in range(tiles):
+        lanes = slice(tile * wide, (tile + 1) * wide)
+        total = prev_ref[:, lanes]
+        total = parity_product(1 - core, weights_ref, own_ref, recv_ref, total, lanes)
+        out_ref[:, :, lanes] = total.astype(BF16).reshape(out_ref.shape[:2] + (wide,))
+        copies.append(
+            pltpu.make_async_copy(out_ref.at[:, :, lanes], out_hbm.at[:, :, lanes], sems.at[tile])
+        )
+        copies[tile].start()
+    for copy in copies:
+        copy.wait()
 
 
 def chunk_plan(phi, loads, harm_diam, mistuning, dyn_diag, blade_order):
@@ -218,27 +262,27 @@
         return jnp.sum(got.astype(F32), axis=0)
 
     shapes = phi.T.reshape(local_diam, MODES, rows_dev)
-    combined, shapes_near = pl.pallas_call(
+    half_combined = jax.ShapeDtypeStruct((pairs, columns, rows_dev), BF16)
+    half_shapes = jax.ShapeDtypeStruct((pairs, MODES, rows_dev), BF16)
+    combined_send, combined_mine, shapes_send, shapes_mine = pl.pallas_call(
         functools.partial(load_kernel, columns),
         name="load",
         in_specs=[SMEM, HBM, HBM, HBM],
-        out_specs=[VMEM, VMEM],
-        out_shape=[
-            jax.ShapeDtypeStruct((local_diam, columns, rows_dev), BF16),
-            jax.ShapeDtypeStruct(shapes.shape, BF16),
-        ],
+        out_specs=[VMEM] * 4,
+        out_shape=[half_combined, half_combined, half_shapes, half_shapes],
         scratch_shapes=[
             pltpu.SMEM(harm_diam.shape, jnp.int32),
             pltpu.VMEM(loads.shape, BF16),
-            pltpu.SemaphoreType.DMA((3,)),
+            pltpu.SemaphoreType.DMA((4,)),
         ],
         compiler_params=LIMIT,
-    )(core_arg, *in_hbm(harm_diam, loads, shapes))
-    force_part = jnp.einsum(
-        "hcr,hmr->hcm", combined, shapes_near, preferred_element_type=F32
-    ).astype(BF16)
+    )(core_arg, *in_hbm(harm_diam, loads, shapes.reshape(pairs, 2, MODES, rows_dev)))
+
+    def force_part(combined, near):
+        return jnp.einsum("hcr,hmr->hcm", combined, near, preferred_element_type=F32).astype(BF16)
+
+    force_recv = other_core(force_part(combined_send, shapes_send))
     slots_shape = (local_diam, columns, MODES)
-    force_recv = other_core(by_parity(force_part, 1 - core))
     force_slots = pl.pallas_call(
         assemble_kernel,
         name="assemble",
@@ -246,7 +290,7 @@
         out_specs=VMEM,
         out_shape=jax.ShapeDtypeStruct(slots_shape, BF16),
         compiler_params=LIMIT,
-    )(core_arg, force_part, force_recv)
+    )(core_arg, force_part(combined_mine, shapes_mine), force_recv)
     force_slots, stiff, order, dyn_diag = lax.optimization_barrier(
         (force_slots, mistuning.T, blade_order, dyn_diag)
     )
@@ -261,7 +305,7 @@
         out_shape=[group, group],
         scratch_shapes=[
             pltpu.VMEM(stiff.shape, F32),
-            pltpu.SemaphoreType.DMA((2,)),
+            pltpu.SemaphoreType.DMA((4,)),
         ],
         compiler_params=WIDE,
         cost_estimate=pl.CostEstimate(
@@ -298,26 +342,32 @@
     same = exchange(jnp.broadcast_to(amp.astype(BF16)[None], slots_shape))
     crossed = other_core(same)
 
-    def blades(crossed, amps, out_shape, *prev):
-        return pl.pallas_call(
-            functools.partial(blades_kernel, crossed),
-            name="blades",
-            in_specs=[SMEM, SMEM] + [VMEM] * (3 + len(prev)),
-            out_specs=VMEM,
-            out_shape=out_shape,
-            scratch_shapes=[pltpu.VMEM((local_diam, local_diam * columns, MODES), BF16)],
-            compiler_params=WIDE,
-            cost_estimate=pl.CostEstimate(
-                flops=2 * local_diam * columns * phi.size,
-                bytes_accessed=2 * phi.size,
-                transcendentals=0,
-            ),
-        )(core_arg, table, amps, shapes_sent, shapes_received, *prev)
-
-    part = blades(False, same, jax.ShapeDtypeStruct((local_diam * columns, rows_dev), F32))
+    half_cost = pl.CostEstimate(
+        flops=2 * local_diam * columns * phi.size, bytes_accessed=2 * phi.size, transcendentals=0
+    )
+    weights = pltpu.VMEM((local_diam, local_diam * columns, MODES), BF16)
+    part = pl.pallas_call(
+        same_kernel,
+        name="blades_same",
+        in_specs=[SMEM, SMEM] + [VMEM] * 3,
+        out_specs=VMEM,
+        out_shape=jax.ShapeDtypeStruct((local_diam * columns, rows_dev), F32),
+        scratch_shapes=[weights],
+        compiler_params=WIDE,
+        cost_estimate=half_cost,
+    )(core_arg, table, same, shapes_sent, shapes_received)
     part, crossed = lax.optimization_barrier((part, crossed))
-    out_shape = jax.ShapeDtypeStruct((local_diam, columns, rows_dev), BF16)
-    return blades(True, crossed, out_shape, part)
+    out_shape = (local_diam, columns, rows_dev)
+    return pl.pallas_call(
+        crossed_kernel,
+        name="blades_crossed",
+        in_specs=[SMEM, SMEM] + [VMEM] * 4,
+        out_specs=HBM,
+        out_shape=jax.ShapeDtypeStruct(out_shape, BF16),
+        scratch_shapes=[weights, pltpu.VMEM(out_shape, BF16), pltpu.SemaphoreType.DMA((4,))],
+        compiler_params=WIDE,
+        cost_estimate=half_cost,
+    )(core_arg, table, crossed, shapes_sent, shapes_received, part)
 
 
 def solution(mesh):

time: 81.9 us -> 81 us (0.989)
  Pallas kernels: 12.7 us -> 11.5 us
    all_to_all x1, waiting for transfers between devices: 1.27 us -> 2.46 us  [exchange(): return lax.all_to_all(slots, 'rows', 0, 0, tiled=True)]
    pallas_call x1, Pallas kernels: 3.21 us -> 2.02 us  [chunk_plan(): pl.pallas_call(regroup_kernel, name='regroup', in_specs=[SMEM, HBM], out_...]
  transfers between devices with their start and end apart: 9 -> 9, of which waited for: 6 -> 6; matrix products, arithmetic and copies ran while one was open for 1% -> 2% of each run, Pallas kernels for 8% -> 6%
where the time goes in v9:
time: 81 us; the launch traced here: 80.5 us
  blocking collectives  44 us (54%)
  starting transfers between devices  17.1 us (21%)
  Pallas kernels  11.5 us (14%)
  waiting for transfers between devices  5.35 us (7%)
  matrix products  1.44 us (2%)
  local copies, waits for them, and re-layouts  0.81 us (1%)
    all_to_all x5, blocking collectives, exchange(): return lax.all_to_all(slots, 'rows', 0, 0, tiled=True)  44 us
    ppermute x8, starting transfers between devices, other_core(): return lax.ppermute(value, 'diam', SWAP)  10.4 us
    all_to_all x1, starting transfers between devices, exchange(): return lax.all_to_all(slots, 'rows', 0, 0, tiled=True)  6.68 us
    ppermute x8, waiting for transfers between devices, other_core(): return lax.ppermute(value, 'diam', SWAP)  2.88 us
    pallas_call x1, Pallas kernels, chunk_plan(): pl.pallas_call(crossed_kernel, name='blades_crossed', in_specs=[SMEM, SME...  2.63 us
    all_to_all x1, waiting for transfers between devices, exchange(): return lax.all_to_all(slots, 'rows', 0, 0, tiled=True)  2.46 us
    pallas_call x1, Pallas kernels, chunk_plan(): pl.pallas_call(functools.partial(load_kernel, columns), name='load', in_s...  2.28 us
    pallas_call x8, Pallas kernels, product(): pl.pallas_call(functools.partial(product_kernel, source), name='product',...  2.03 us
  transfers between devices with their start and end apart: 9, of which 6 were waited for; matrix products, arithmetic and copies ran while one was open for 2% of the time, Pallas kernels for 6%

profile of v9, /device:TPU:1, one launch (start us, length us, event | category | flops | bytes accessed | tf_op | source)
XLA Modules:
  0.0 80.5 jit_solution(12236466282431602447)
XLA Ops:
  0.0 2.3 %load.1 = (bf16[4,32,1024]{2,1,0:T(8,128)(2,1)S(1)}, bf16[4,32,1024]{2,1,0:T(8,128)(2,1)S(1)}, bf16[4,200,1024]{2,1,0:T(8,128)(2,1)S(1)}, bf16[4,200,1024]{2,1,0:T(8,128)(2,1)S(1)}) custom-call(s32[1]{0:T(128)} %bitcast.core_ref, s32[16]{0:T(128)} %harm_hbm.1, bf16[1024,512]{1,0:T(8,128)(2,1)} %loads_hbm.1, bf16[4,2,200,1024]{3,2,1,0:T(8,128)(2,1)} %bitcast.13), custom_call_target="tpu_custom_call" | custom-call | tf_op jit(solution)/shard_map/load/pallas_call | solution.py:267
  2.3 0.6 convolution_convert_fusion
  3.0 0.6 convolution_convert_fusion.1.mine_ref
  3.6 0.5 collective-permute-done.recv_ref
  4.2 0.7 assemble.1
  4.8 6.7 %all-to-all-start = ((bf16[8,32,200]{2,1,0:T(8,128)(2,1)}), bf16[8,32,200]{2,1,0:T(8,128)(2,1)S(1)}, u32[]{:S(2)}, u32[]{:S(2)}) async-start(bf16[8,32,200]{2,1,0:T(8,128)(2,1)} %assemble.1), calls=%async_computation | async-start | bytes 262144 | tf_op jit(solution)/shard_map/all_to_all | solution.py:259
  11.5 2.0 %regroup.1 = (bf16[2,4,200,200]{3,2,1,0:T(8,128)(2,1)S(1)}, bf16[2,4,200,200]{3,2,1,0:T(8,128)(2,1)S(1)}) custom-call(s32[1]{0:T(128)} %bitcast.core_ref, f32[400,1600]{1,0:T(8,128)} %bitcast.17), custom_call_target="tpu_custom_call" | custom-call | flops 1280000 | bytes 5120000 | tf_op jit(solution)/shard_map/regroup/pallas_call | solution.py:300
  13.5 0.7 collective-permute-start.1
  14.5 0.8 dynamic_slice.7
  15.3 2.5 %all-to-all-done = bf16[8,32,200]{2,1,0:T(8,128)(2,1)S(1)} async-done(((bf16[8,32,200]{2,1,0:T(8,128)(2,1)}), bf16[8,32,200]{2,1,0:T(8,128)(2,1)S(1)}, u32[]{:S(2)}, u32[]{:S(2)}) %all-to-all-start) | async-done | bytes 102432 | tf_op jit(solution)/shard_map/all_to_all | solution.py:259
  17.8 1.8 %collective-permute-start.2 = (bf16[32,200]{1,0:T(8,128)(2,1)S(1)}, bf16[32,200]{1,0:T(8,128)(2,1)S(1)}, u32[]{:S(2)}, u32[]{:S(2)}) collective-permute-start(bf16[32,200]{1,0:T(8,128)(2,1)S(1)} %divide_convert_fusion.4.amp_ref), channel_id=1, source_target_pairs={{0,1},{1,0},{2,3},{3,2},{4,5},{5,4},{6,7},{7,6},{8,9},{9,8},{10,11... | collective-permute-start | bytes 38408 | tf_op jit(solution)/shard_map/ppermute | solution.py:256
  19.6 0.3 product.8.rest_0_
  19.9 0.6 collective-permute-done.2.amp_ref
  20.7 8.6 %all_to_all.30 = bf16[8,32,200]{2,1,0:T(8,128)(2,1)S(1)} all-to-all(bf16[8,32,200]{2,1,0:T(8,128)(2,1)S(1)} %product.9), channel_id=1, replica_groups=mesh['grp'=2,'rows'=8,'diam'=2] {'rows'}, dimensions={0} | all-to-all | bytes 204800 | tf_op jit(solution)/shard_map/all_to_all | solution.py:259
  29.3 1.8 %collective-permute-start.3 = (bf16[32,200]{1,0:T(8,128)(2,1)S(1)}, bf16[32,200]{1,0:T(8,128)(2,1)S(1)}, u32[]{:S(2)}, u32[]{:S(2)}) collective-permute-start(bf16[32,200]{1,0:T(8,128)(2,1)S(1)} %divide_convert_fusion.3.amp_ref), channel_id=1, source_target_pairs={{0,1},{1,0},{2,3},{3,2},{4,5},{5,4},{6,7},{7,6},{8,9},{9,8},{10,11... | collective-permute-start | bytes 38408 | tf_op jit(solution)/shard_map/ppermute | solution.py:256
  31.1 0.3 product.10.rest_0_
  31.4 0.6 collective-permute-done.3.amp_ref
  32.0 0.3 product.11
  32.2 8.6 %all_to_all.31 = bf16[8,32,200]{2,1,0:T(8,128)(2,1)S(1)} all-to-all(bf16[8,32,200]{2,1,0:T(8,128)(2,1)S(1)} %product.11), channel_id=1, replica_groups=mesh['grp'=2,'rows'=8,'diam'=2] {'rows'}, dimensions={0} | all-to-all | bytes 204800 | tf_op jit(solution)/shard_map/all_to_all | solution.py:259
  40.9 1.8 %collective-permute-start.4 = (bf16[32,200]{1,0:T(8,128)(2,1)S(1)}, bf16[32,200]{1,0:T(8,128)(2,1)S(1)}, u32[]{:S(2)}, u32[]{:S(2)}) collective-permute-start(bf16[32,200]{1,0:T(8,128)(2,1)S(1)} %divide_convert_fusion.2.amp_ref), channel_id=1, source_target_pairs={{0,1},{1,0},{2,3},{3,2},{4,5},{5,4},{6,7},{7,6},{8,9},{9,8},{10,11... | collective-permute-start | bytes 38408 | tf_op jit(solution)/shard_map/ppermute | solution.py:256
  42.7 0.3 product.12.rest_0_
  42.9 0.6 collective-permute-done.4.amp_ref
  43.5 0.3 product.13
  43.8 8.7 %all_to_all.32 = bf16[8,32,200]{2,1,0:T(8,128)(2,1)S(1)} all-to-all(bf16[8,32,200]{2,1,0:T(8,128)(2,1)S(1)} %product.13), channel_id=1, replica_groups=mesh['grp'=2,'rows'=8,'diam'=2] {'rows'}, dimensions={0} | all-to-all | bytes 204800 | tf_op jit(solution)/shard_map/all_to_all | solution.py:259
  52.5 1.8 %collective-permute-start.5 = (bf16[32,200]{1,0:T(8,128)(2,1)S(1)}, bf16[32,200]{1,0:T(8,128)(2,1)S(1)}, u32[]{:S(2)}, u32[]{:S(2)}) collective-permute-start(bf16[32,200]{1,0:T(8,128)(2,1)S(1)} %divide_convert_fusion.1.amp_ref), channel_id=1, source_target_pairs={{0,1},{1,0},{2,3},{3,2},{4,5},{5,4},{6,7},{7,6},{8,9},{9,8},{10,11... | collective-permute-start | bytes 38408 | tf_op jit(solution)/shard_map/ppermute | solution.py:256
  54.6 0.6 collective-permute-done.5.amp_ref
  55.2 0.3 collective-permute-start.6
  55.8 8.8 %all_to_all.33 = bf16[8,32,200]{2,1,0:T(8,128)(2,1)S(1)} all-to-all(bf16[8,32,200]{2,1,0:T(8,128)(2,1)S(1)} %product.15), channel_id=1, replica_groups=mesh['grp'=2,'rows'=8,'diam'=2] {'rows'}, dimensions={0} | all-to-all | bytes 204800 | tf_op jit(solution)/shard_map/all_to_all | solution.py:259
  64.6 9.3 %all_to_all.34.amp_ref = bf16[8,32,200]{2,1,0:T(8,128)(2,1)S(1)} all-to-all(bf16[8,32,200]{2,1,0:T(8,128)(2,1)S(1)} %broadcast_in_dim.33), channel_id=1, replica_groups=mesh['grp'=2,'rows'=8,'diam'=2] {'rows'}, dimensions={0} | all-to-all | bytes 204800 | tf_op jit(solution)/shard_map/all_to_all | solution.py:259
  74.0 2.1 %collective-permute-start.7 = (bf16[8,32,200]{2,1,0:T(8,128)(2,1)S(1)}, bf16[8,32,200]{2,1,0:T(8,128)(2,1)S(1)}, u32[]{:S(2)}, u32[]{:S(2)}) collective-permute-start(bf16[8,32,200]{2,1,0:T(8,128)(2,1)S(1)} %all_to_all.34.amp_ref), channel_id=1, source_target_pairs={{0,1},{1,0},{2,3},{3,2},{4,5},{5,4},{6,7},{7,6},{8,9},{9,8},{10,11... | collective-permute-start | bytes 307208 | tf_op jit(solution)/shard_map/ppermute | solution.py:256
  76.0 1.9 %blades_same.1.prev_ref = f32[256,1024]{1,0:T(8,128)S(1)} custom-call(s32[1]{0:T(128)} %bitcast.core_ref, f32[8,16]{1,0:T(8,128)S(1)} %constant_dynamic-slice_fusion.table_ref, bf16[8,32,200]{2,1,0:T(8,128)(2,1)S(1)} %all_to_all.34.amp_ref, bf16[8,200,1024]{2,1,0:T(8,128)(2,1)S(1)} %bitcast.15, bf16[8,200,1024]{2,1,0:T(8,128)(2,1)S(1)} %collective-permute-done.6.recv_ref), custom_call_target="tpu_custom_call" | custom-call | flops 838860800 | bytes 3276800 | tf_op jit(solution)/shard_map/blades_same/pallas_call | solution.py:349
  77.9 2.6 %blades_crossed.1 = bf16[8,32,1024]{2,1,0:T(8,128)(2,1)} custom-call(s32[1]{0:T(128)} %bitcast.core_ref, f32[8,16]{1,0:T(8,128)S(1)} %constant_dynamic-slice_fusion.table_ref, bf16[8,32,200]{2,1,0:T(8,128)(2,1)S(1)} %collective-permute-done.7.amp_ref, bf16[8,200,1024]{2,1,0:T(8,128)(2,1)S(1)} %bitcast.16, ...), custom_call_target="tpu_custom_call" | custom-call | flops 838860800 | bytes 3276800 | tf_op jit(solution)/shard_map/blades_crossed/pallas_call | solution.py:361
  (27 shorter events, 1.3 us)
Async XLA Ops:
  2.9 1.3 %collective-permute-start = (bf16[4,32,200]{2,1,0:T(8,128)(2,1)S(1)}, bf16[4,32,200]{2,1,0:T(8,128)(2,1)S(1)}, u32[]{:S(2)}, u32[]{:S(2)}) collective-permute-start(bf16[4,32,200]{2,1,0:T(8,128)(2,1)S(1)} %convolution_convert_fusion), channel_id=1, source_target_pairs={{0,1},{1,0},{2,3},{3,2},{4,5},{5,4},{6,7},{7,6},{8,9},{9,8},{10,11... | collective-permute-start | bytes 153608 | tf_op jit(solution)/shard_map/ppermute | solution.py:256
  3.6 10.7 %copy-start.1 = (s32[16]{0:T(128)S(1)}, s32[16]{0:T(128)}, u32[]{:S(2)}) copy-start(s32[16]{0:T(128)} %param.11) | copy-start | bytes 196
  4.8 12.9 %all-to-all-start = ((bf16[8,32,200]{2,1,0:T(8,128)(2,1)}), bf16[8,32,200]{2,1,0:T(8,128)(2,1)S(1)}, u32[]{:S(2)}, u32[]{:S(2)}) async-start(bf16[8,32,200]{2,1,0:T(8,128)(2,1)} %assemble.1), calls=%async_computation | async-start | bytes 262144 | tf_op jit(solution)/shard_map/all_to_all | solution.py:259
  13.5 6.1 %collective-permute-start.1 = (bf16[2,4,200,200]{3,2,1,0:T(8,128)(2,1)S(1)}, bf16[2,4,200,200]{3,2,1,0:T(8,128)(2,1)S(1)}, u32[]{:S(2)}, u32[]{:S(2)}) collective-permute-start(bf16[2,4,200,200]{3,2,1,0:T(8,128)(2,1)S(1)} %get-tuple-element.44), channel_id=1, source_target_pairs={{0,1},{1,0},{2,3},{3,2},{4,5},{5,4},{6,7},{7,6},{8,9},{9,8},{10,11... | collective-permute-start | bytes 1920008 | tf_op jit(solution)/shard_map/ppermute | solution.py:256
  17.8 2.7 %collective-permute-start.2 = (bf16[32,200]{1,0:T(8,128)(2,1)S(1)}, bf16[32,200]{1,0:T(8,128)(2,1)S(1)}, u32[]{:S(2)}, u32[]{:S(2)}) collective-permute-start(bf16[32,200]{1,0:T(8,128)(2,1)S(1)} %divide_convert_fusion.4.amp_ref), channel_id=1, source_target_pairs={{0,1},{1,0},{2,3},{3,2},{4,5},{5,4},{6,7},{7,6},{8,9},{9,8},{10,11... | collective-permute-start | bytes 38408 | tf_op jit(solution)/shard_map/ppermute | solution.py:256
  29.3 2.6 %collective-permute-start.3 = (bf16[32,200]{1,0:T(8,128)(2,1)S(1)}, bf16[32,200]{1,0:T(8,128)(2,1)S(1)}, u32[]{:S(2)}, u32[]{:S(2)}) collective-permute-start(bf16[32,200]{1,0:T(8,128)(2,1)S(1)} %divide_convert_fusion.3.amp_ref), channel_id=1, source_target_pairs={{0,1},{1,0},{2,3},{3,2},{4,5},{5,4},{6,7},{7,6},{8,9},{9,8},{10,11... | collective-permute-start | bytes 38408 | tf_op jit(solution)/shard_map/ppermute | solution.py:256
  40.9 2.6 %collective-permute-start.4 = (bf16[32,200]{1,0:T(8,128)(2,1)S(1)}, bf16[32,200]{1,0:T(8,128)(2,1)S(1)}, u32[]{:S(2)}, u32[]{:S(2)}) collective-permute-start(bf16[32,200]{1,0:T(8,128)(2,1)S(1)} %divide_convert_fusion.2.amp_ref), channel_id=1, source_target_pairs={{0,1},{1,0},{2,3},{3,2},{4,5},{5,4},{6,7},{7,6},{8,9},{9,8},{10,11... | collective-permute-start | bytes 38408 | tf_op jit(solution)/shard_map/ppermute | solution.py:256
  43.5 11.7 %copy-start = (bf16[1024,1600]{0,1:T(8,128)(2,1)S(1)}, bf16[1024,1600]{0,1:T(8,128)(2,1)}, u32[]{:S(2)}) copy-start(bf16[1024,1600]{0,1:T(8,128)(2,1)} %param.6) | copy-start | bytes 9830404
  52.5 2.6 %collective-permute-start.5 = (bf16[32,200]{1,0:T(8,128)(2,1)S(1)}, bf16[32,200]{1,0:T(8,128)(2,1)S(1)}, u32[]{:S(2)}, u32[]{:S(2)}) collective-permute-start(bf16[32,200]{1,0:T(8,128)(2,1)S(1)} %divide_convert_fusion.1.amp_ref), channel_id=1, source_target_pairs={{0,1},{1,0},{2,3},{3,2},{4,5},{5,4},{6,7},{7,6},{8,9},{9,8},{10,11... | collective-permute-start | bytes 38408 | tf_op jit(solution)/shard_map/ppermute | solution.py:256
  55.2 20.8 %collective-permute-start.6 = (bf16[8,200,1024]{2,1,0:T(8,128)(2,1)S(1)}, bf16[8,200,1024]{2,1,0:T(8,128)(2,1)S(1)}, u32[]{:S(2)}, u32[]{:S(2)}) collective-permute-start(bf16[8,200,1024]{2,1,0:T(8,128)(2,1)S(1)} %bitcast.14), channel_id=1, source_target_pairs={{0,1},{1,0},{2,3},{3,2},{4,5},{5,4},{6,7},{7,6},{8,9},{9,8},{10,11... | collective-permute-start | bytes 9830408 | tf_op jit(solution)/shard_map/ppermute | solution.py:256
  74.0 3.9 %collective-permute-start.7 = (bf16[8,32,200]{2,1,0:T(8,128)(2,1)S(1)}, bf16[8,32,200]{2,1,0:T(8,128)(2,1)S(1)}, u32[]{:S(2)}, u32[]{:S(2)}) collective-permute-start(bf16[8,32,200]{2,1,0:T(8,128)(2,1)S(1)} %all_to_all.34.amp_ref), channel_id=1, source_target_pairs={{0,1},{1,0},{2,3},{3,2},{4,5},{5,4},{6,7},{7,6},{8,9},{9,8},{10,11... | collective-permute-start | bytes 307208 | tf_op jit(solution)/shard_map/ppermute | solution.py:256

commit v10 on v9

--- a/solution.py
+++ b/solution.py
@@ -201,7 +201,7 @@
             at = half * pairs + k
             amp = amp_ref[at].astype(F32)
             for s in range(local_diam):
-                value = table_ref[s, 2 * at + odd] * amp
+                value = table_ref[2 * at + odd, s : s + 1] * amp
                 weights_ref[at_half * pairs + k, s * columns : (s + 1) * columns] = value.astype(BF16)
 
 
@@ -314,6 +314,7 @@
     )(core_arg, *in_hbm(stiff))
     recv = other_core(sent)
     table = lax.dynamic_slice_in_dim(cyclic_rows(order), first_diam, local_diam, 0)
+    table = jnp.broadcast_to(table.T[:, :, None], (NBLADE, local_diam, MODES))
     dyn_own = lax.dynamic_slice_in_dim(dyn_diag, own_diam * MODES, MODES, 0)[None, :]
     force_got, keep, table, dyn_own = lax.optimization_barrier((force_got, keep, table, dyn_own))
 
@@ -349,7 +350,7 @@
     part = pl.pallas_call(
         same_kernel,
         name="blades_same",
-        in_specs=[SMEM, SMEM] + [VMEM] * 3,
+        in_specs=[SMEM] + [VMEM] * 4,
         out_specs=VMEM,
         out_shape=jax.ShapeDtypeStruct((local_diam * columns, rows_dev), F32),
         scratch_shapes=[weights],
@@ -361,7 +362,7 @@
     return pl.pallas_call(
         crossed_kernel,
         name="blades_crossed",
-        in_specs=[SMEM, SMEM] + [VMEM] * 4,
+        in_specs=[SMEM] + [VMEM] * 5,
         out_specs=HBM,
         out_shape=jax.ShapeDtypeStruct(out_shape, BF16),
         scratch_shapes=[weights, pltpu.VMEM(out_shape, BF16), pltpu.SemaphoreType.DMA((4,))],

time: 81 us -> 79.9 us (0.986)
  Pallas kernels: 11.5 us -> 10.3 us
    pallas_call x2, Pallas kernels: 4.48 us -> 3.27 us  [the longest x1 2.02 us: chunk_plan(): pl.pallas_call(crossed_kernel, name='blades_crossed', in_specs=[SMEM] + [...]
where the time goes in v10:
time: 79.9 us; the launch traced here: 79.4 us
  blocking collectives  44 us (55%)
  starting transfers between devices  17.1 us (21%)
  Pallas kernels  10.3 us (13%)
  waiting for transfers between devices  5.28 us (7%)
  matrix products  1.44 us (2%)
  local copies, waits for them, and re-layouts  0.97 us (1%)
    all_to_all x5, blocking collectives, exchange(): return lax.all_to_all(slots, 'rows', 0, 0, tiled=True)  44 us
    ppermute x8, starting transfers between devices, other_core(): return lax.ppermute(value, 'diam', SWAP)  10.4 us
    all_to_all x1, starting transfers between devices, exchange(): return lax.all_to_all(slots, 'rows', 0, 0, tiled=True)  6.68 us
    ppermute x8, waiting for transfers between devices, other_core(): return lax.ppermute(value, 'diam', SWAP)  2.89 us
    all_to_all x1, waiting for transfers between devices, exchange(): return lax.all_to_all(slots, 'rows', 0, 0, tiled=True)  2.39 us
    pallas_call x1, Pallas kernels, chunk_plan(): pl.pallas_call(functools.partial(load_kernel, columns), name='load', in_s...  2.28 us
    pallas_call x1, Pallas kernels, chunk_plan(): pl.pallas_call(crossed_kernel, name='blades_crossed', in_specs=[SMEM] + [...  2.02 us
    pallas_call x8, Pallas kernels, product(): pl.pallas_call(functools.partial(product_kernel, source), name='product',...  2.02 us
  transfers between devices with their start and end apart: 9, of which 6 were waited for; matrix products, arithmetic and copies ran while one was open for 2% of the time, Pallas kernels for 6%

profile of v10, /device:TPU:1, one launch (start us, length us, event | category | flops | bytes accessed | tf_op | source)
XLA Modules:
  0.0 79.4 jit_solution(4866288804483566464)
XLA Ops:
  0.0 2.3 %load.1 = (bf16[4,32,1024]{2,1,0:T(8,128)(2,1)S(1)}, bf16[4,32,1024]{2,1,0:T(8,128)(2,1)S(1)}, bf16[4,200,1024]{2,1,0:T(8,128)(2,1)S(1)}, bf16[4,200,1024]{2,1,0:T(8,128)(2,1)S(1)}) custom-call(s32[1]{0:T(128)} %bitcast.core_ref, s32[16]{0:T(128)} %harm_hbm.1, bf16[1024,512]{1,0:T(8,128)(2,1)} %loads_hbm.1, bf16[4,2,200,1024]{3,2,1,0:T(8,128)(2,1)} %bitcast.15), custom_call_target="tpu_custom_call" | custom-call | tf_op jit(solution)/shard_map/load/pallas_call | solution.py:267
  2.3 0.6 convolution_convert_fusion
  3.0 0.6 convolution_convert_fusion.1.mine_ref
  3.6 0.5 collective-permute-done.recv_ref
  4.2 0.7 assemble.1
  4.8 6.7 %all-to-all-start = ((bf16[8,32,200]{2,1,0:T(8,128)(2,1)}), bf16[8,32,200]{2,1,0:T(8,128)(2,1)S(1)}, u32[]{:S(2)}, u32[]{:S(2)}) async-start(bf16[8,32,200]{2,1,0:T(8,128)(2,1)} %assemble.1), calls=%async_computation | async-start | bytes 262144 | tf_op jit(solution)/shard_map/all_to_all | solution.py:259
  11.5 2.0 %regroup.1 = (bf16[2,4,200,200]{3,2,1,0:T(8,128)(2,1)S(1)}, bf16[2,4,200,200]{3,2,1,0:T(8,128)(2,1)S(1)}) custom-call(s32[1]{0:T(128)} %bitcast.core_ref, f32[400,1600]{1,0:T(8,128)} %bitcast.19), custom_call_target="tpu_custom_call" | custom-call | flops 1280000 | bytes 5120000 | tf_op jit(solution)/shard_map/regroup/pallas_call | solution.py:300
  13.5 0.7 collective-permute-start.1
  14.5 0.8 dynamic_slice.7
  15.3 2.4 %all-to-all-done = bf16[8,32,200]{2,1,0:T(8,128)(2,1)S(1)} async-done(((bf16[8,32,200]{2,1,0:T(8,128)(2,1)}), bf16[8,32,200]{2,1,0:T(8,128)(2,1)S(1)}, u32[]{:S(2)}, u32[]{:S(2)}) %all-to-all-start) | async-done | bytes 102432 | tf_op jit(solution)/shard_map/all_to_all | solution.py:259
  17.9 1.8 %collective-permute-start.2 = (bf16[32,200]{1,0:T(8,128)(2,1)S(1)}, bf16[32,200]{1,0:T(8,128)(2,1)S(1)}, u32[]{:S(2)}, u32[]{:S(2)}) collective-permute-start(bf16[32,200]{1,0:T(8,128)(2,1)S(1)} %divide_convert_fusion.4.amp_ref), channel_id=1, source_target_pairs={{0,1},{1,0},{2,3},{3,2},{4,5},{5,4},{6,7},{7,6},{8,9},{9,8},{10,11... | collective-permute-start | bytes 38408 | tf_op jit(solution)/shard_map/ppermute | solution.py:256
  19.9 0.6 collective-permute-done.2.amp_ref
  20.5 0.3 product.9
  20.8 8.6 %all_to_all.30 = bf16[8,32,200]{2,1,0:T(8,128)(2,1)S(1)} all-to-all(bf16[8,32,200]{2,1,0:T(8,128)(2,1)S(1)} %product.9), channel_id=1, replica_groups=mesh['grp'=2,'rows'=8,'diam'=2] {'rows'}, dimensions={0} | all-to-all | bytes 204800 | tf_op jit(solution)/shard_map/all_to_all | solution.py:259
  29.4 1.8 %collective-permute-start.3 = (bf16[32,200]{1,0:T(8,128)(2,1)S(1)}, bf16[32,200]{1,0:T(8,128)(2,1)S(1)}, u32[]{:S(2)}, u32[]{:S(2)}) collective-permute-start(bf16[32,200]{1,0:T(8,128)(2,1)S(1)} %divide_convert_fusion.3.amp_ref), channel_id=1, source_target_pairs={{0,1},{1,0},{2,3},{3,2},{4,5},{5,4},{6,7},{7,6},{8,9},{9,8},{10,11... | collective-permute-start | bytes 38408 | tf_op jit(solution)/shard_map/ppermute | solution.py:256
  31.5 0.6 collective-permute-done.3.amp_ref
  32.1 0.3 product.11
  32.3 8.6 %all_to_all.31 = bf16[8,32,200]{2,1,0:T(8,128)(2,1)S(1)} all-to-all(bf16[8,32,200]{2,1,0:T(8,128)(2,1)S(1)} %product.11), channel_id=1, replica_groups=mesh['grp'=2,'rows'=8,'diam'=2] {'rows'}, dimensions={0} | all-to-all | bytes 204800 | tf_op jit(solution)/shard_map/all_to_all | solution.py:259
  41.0 1.8 %collective-permute-start.4 = (bf16[32,200]{1,0:T(8,128)(2,1)S(1)}, bf16[32,200]{1,0:T(8,128)(2,1)S(1)}, u32[]{:S(2)}, u32[]{:S(2)}) collective-permute-start(bf16[32,200]{1,0:T(8,128)(2,1)S(1)} %divide_convert_fusion.2.amp_ref), channel_id=1, source_target_pairs={{0,1},{1,0},{2,3},{3,2},{4,5},{5,4},{6,7},{7,6},{8,9},{9,8},{10,11... | collective-permute-start | bytes 38408 | tf_op jit(solution)/shard_map/ppermute | solution.py:256
  43.0 0.6 collective-permute-done.4.amp_ref
  43.6 0.3 product.13
  43.9 8.7 %all_to_all.32 = bf16[8,32,200]{2,1,0:T(8,128)(2,1)S(1)} all-to-all(bf16[8,32,200]{2,1,0:T(8,128)(2,1)S(1)} %product.13), channel_id=1, replica_groups=mesh['grp'=2,'rows'=8,'diam'=2] {'rows'}, dimensions={0} | all-to-all | bytes 204800 | tf_op jit(solution)/shard_map/all_to_all | solution.py:259
  52.6 1.8 %collective-permute-start.5 = (bf16[32,200]{1,0:T(8,128)(2,1)S(1)}, bf16[32,200]{1,0:T(8,128)(2,1)S(1)}, u32[]{:S(2)}, u32[]{:S(2)}) collective-permute-start(bf16[32,200]{1,0:T(8,128)(2,1)S(1)} %divide_convert_fusion.1.amp_ref), channel_id=1, source_target_pairs={{0,1},{1,0},{2,3},{3,2},{4,5},{5,4},{6,7},{7,6},{8,9},{9,8},{10,11... | collective-permute-start | bytes 38408 | tf_op jit(solution)/shard_map/ppermute | solution.py:256
  54.4 0.3 product.14.rest_0_
  54.7 0.6 collective-permute-done.5.amp_ref
  55.3 0.3 collective-permute-start.6
  55.6 0.3 product.15
  55.9 8.8 %all_to_all.33 = bf16[8,32,200]{2,1,0:T(8,128)(2,1)S(1)} all-to-all(bf16[8,32,200]{2,1,0:T(8,128)(2,1)S(1)} %product.15), channel_id=1, replica_groups=mesh['grp'=2,'rows'=8,'diam'=2] {'rows'}, dimensions={0} | all-to-all | bytes 204800 | tf_op jit(solution)/shard_map/all_to_all | solution.py:259
  64.7 9.3 %all_to_all.34.amp_ref = bf16[8,32,200]{2,1,0:T(8,128)(2,1)S(1)} all-to-all(bf16[8,32,200]{2,1,0:T(8,128)(2,1)S(1)} %broadcast_in_dim.40), channel_id=1, replica_groups=mesh['grp'=2,'rows'=8,'diam'=2] {'rows'}, dimensions={0} | all-to-all | bytes 204800 | tf_op jit(solution)/shard_map/all_to_all | solution.py:259
  74.1 2.1 %collective-permute-start.7 = (bf16[8,32,200]{2,1,0:T(8,128)(2,1)S(1)}, bf16[8,32,200]{2,1,0:T(8,128)(2,1)S(1)}, u32[]{:S(2)}, u32[]{:S(2)}) collective-permute-start(bf16[8,32,200]{2,1,0:T(8,128)(2,1)S(1)} %all_to_all.34.amp_ref), channel_id=1, source_target_pairs={{0,1},{1,0},{2,3},{3,2},{4,5},{5,4},{6,7},{7,6},{8,9},{9,8},{10,11... | collective-permute-start | bytes 307208 | tf_op jit(solution)/shard_map/ppermute | solution.py:256
  76.1 1.3 %blades_same.1.prev_ref = f32[256,1024]{1,0:T(8,128)S(1)} custom-call(s32[1]{0:T(128)} %bitcast.core_ref, f32[16,8,200]{2,1,0:T(8,128)S(1)} %broadcast_in_dim.38.table_ref, bf16[8,32,200]{2,1,0:T(8,128)(2,1)S(1)} %all_to_all.34.amp_ref, bf16[8,200,1024]{2,1,0:T(8,128)(2,1)S(1)} %bitcast.17, bf16[8,200,1024]{2,1,0:T(8,128)(2,1)S(1)} %collective-permute-done.6.recv_ref), custom_call_target="tpu_custom_call" | custom-call | flops 838860800 | bytes 3276800 | tf_op jit(solution)/shard_map/blades_same/pallas_call | solution.py:350
  77.4 2.0 %blades_crossed.1 = bf16[8,32,1024]{2,1,0:T(8,128)(2,1)} custom-call(s32[1]{0:T(128)} %bitcast.core_ref, f32[16,8,200]{2,1,0:T(8,128)S(1)} %broadcast_in_dim.38.table_ref, bf16[8,32,200]{2,1,0:T(8,128)(2,1)S(1)} %collective-permute-done.7.amp_ref, bf16[8,200,1024]{2,1,0:T(8,128)(2,1)S(1)} %bitcast.18, ...), custom_call_target="tpu_custom_call" | custom-call | flops 838860800 | bytes 3276800 | tf_op jit(solution)/shard_map/blades_crossed/pallas_call | solution.py:362
  (29 shorter events, 1.5 us)
Async XLA Ops:
  2.9 1.3 %collective-permute-start = (bf16[4,32,200]{2,1,0:T(8,128)(2,1)S(1)}, bf16[4,32,200]{2,1,0:T(8,128)(2,1)S(1)}, u32[]{:S(2)}, u32[]{:S(2)}) collective-permute-start(bf16[4,32,200]{2,1,0:T(8,128)(2,1)S(1)} %convolution_convert_fusion), channel_id=1, source_target_pairs={{0,1},{1,0},{2,3},{3,2},{4,5},{5,4},{6,7},{7,6},{8,9},{9,8},{10,11... | collective-permute-start | bytes 153608 | tf_op jit(solution)/shard_map/ppermute | solution.py:256
  3.6 10.7 %copy-start.1 = (s32[16]{0:T(128)S(1)}, s32[16]{0:T(128)}, u32[]{:S(2)}) copy-start(s32[16]{0:T(128)} %param.11) | copy-start | bytes 196
  4.8 12.9 %all-to-all-start = ((bf16[8,32,200]{2,1,0:T(8,128)(2,1)}), bf16[8,32,200]{2,1,0:T(8,128)(2,1)S(1)}, u32[]{:S(2)}, u32[]{:S(2)}) async-start(bf16[8,32,200]{2,1,0:T(8,128)(2,1)} %assemble.1), calls=%async_computation | async-start | bytes 262144 | tf_op jit(solution)/shard_map/all_to_all | solution.py:259
  13.5 6.2 %collective-permute-start.1 = (bf16[2,4,200,200]{3,2,1,0:T(8,128)(2,1)S(1)}, bf16[2,4,200,200]{3,2,1,0:T(8,128)(2,1)S(1)}, u32[]{:S(2)}, u32[]{:S(2)}) collective-permute-start(bf16[2,4,200,200]{3,2,1,0:T(8,128)(2,1)S(1)} %get-tuple-element.44), channel_id=1, source_target_pairs={{0,1},{1,0},{2,3},{3,2},{4,5},{5,4},{6,7},{7,6},{8,9},{9,8},{10,11... | collective-permute-start | bytes 1920008 | tf_op jit(solution)/shard_map/ppermute | solution.py:256
  17.9 2.7 %collective-permute-start.2 = (bf16[32,200]{1,0:T(8,128)(2,1)S(1)}, bf16[32,200]{1,0:T(8,128)(2,1)S(1)}, u32[]{:S(2)}, u32[]{:S(2)}) collective-permute-start(bf16[32,200]{1,0:T(8,128)(2,1)S(1)} %divide_convert_fusion.4.amp_ref), channel_id=1, source_target_pairs={{0,1},{1,0},{2,3},{3,2},{4,5},{5,4},{6,7},{7,6},{8,9},{9,8},{10,11... | collective-permute-start | bytes 38408 | tf_op jit(solution)/shard_map/ppermute | solution.py:256
  29.4 2.6 %collective-permute-start.3 = (bf16[32,200]{1,0:T(8,128)(2,1)S(1)}, bf16[32,200]{1,0:T(8,128)(2,1)S(1)}, u32[]{:S(2)}, u32[]{:S(2)}) collective-permute-start(bf16[32,200]{1,0:T(8,128)(2,1)S(1)} %divide_convert_fusion.3.amp_ref), channel_id=1, source_target_pairs={{0,1},{1,0},{2,3},{3,2},{4,5},{5,4},{6,7},{7,6},{8,9},{9,8},{10,11... | collective-permute-start | bytes 38408 | tf_op jit(solution)/shard_map/ppermute | solution.py:256
  41.0 2.6 %collective-permute-start.4 = (bf16[32,200]{1,0:T(8,128)(2,1)S(1)}, bf16[32,200]{1,0:T(8,128)(2,1)S(1)}, u32[]{:S(2)}, u32[]{:S(2)}) collective-permute-start(bf16[32,200]{1,0:T(8,128)(2,1)S(1)} %divide_convert_fusion.2.amp_ref), channel_id=1, source_target_pairs={{0,1},{1,0},{2,3},{3,2},{4,5},{5,4},{6,7},{7,6},{8,9},{9,8},{10,11... | collective-permute-start | bytes 38408 | tf_op jit(solution)/shard_map/ppermute | solution.py:256
  43.6 11.7 %copy-start = (bf16[1024,1600]{0,1:T(8,128)(2,1)S(1)}, bf16[1024,1600]{0,1:T(8,128)(2,1)}, u32[]{:S(2)}) copy-start(bf16[1024,1600]{0,1:T(8,128)(2,1)} %param.6) | copy-start | bytes 9830404
  52.6 2.6 %collective-permute-start.5 = (bf16[32,200]{1,0:T(8,128)(2,1)S(1)}, bf16[32,200]{1,0:T(8,128)(2,1)S(1)}, u32[]{:S(2)}, u32[]{:S(2)}) collective-permute-start(bf16[32,200]{1,0:T(8,128)(2,1)S(1)} %divide_convert_fusion.1.amp_ref), channel_id=1, source_target_pairs={{0,1},{1,0},{2,3},{3,2},{4,5},{5,4},{6,7},{7,6},{8,9},{9,8},{10,11... | collective-permute-start | bytes 38408 | tf_op jit(solution)/shard_map/ppermute | solution.py:256
  55.3 20.8 %collective-permute-start.6 = (bf16[8,200,1024]{2,1,0:T(8,128)(2,1)S(1)}, bf16[8,200,1024]{2,1,0:T(8,128)(2,1)S(1)}, u32[]{:S(2)}, u32[]{:S(2)}) collective-permute-start(bf16[8,200,1024]{2,1,0:T(8,128)(2,1)S(1)} %bitcast.16), channel_id=1, source_target_pairs={{0,1},{1,0},{2,3},{3,2},{4,5},{5,4},{6,7},{7,6},{8,9},{9,8},{10,11... | collective-permute-start | bytes 9830408 | tf_op jit(solution)/shard_map/ppermute | solution.py:256
  74.1 3.3 %collective-permute-start.7 = (bf16[8,32,200]{2,1,0:T(8,128)(2,1)S(1)}, bf16[8,32,200]{2,1,0:T(8,128)(2,1)S(1)}, u32[]{:S(2)}, u32[]{:S(2)}) collective-permute-start(bf16[8,32,200]{2,1,0:T(8,128)(2,1)S(1)} %all_to_all.34.amp_ref), channel_id=1, source_target_pairs={{0,1},{1,0},{2,3},{3,2},{4,5},{5,4},{6,7},{7,6},{8,9},{9,8},{10,11... | collective-permute-start | bytes 307208 | tf_op jit(solution)/shard_map/ppermute | solution.py:256

commit v11 on v10

--- a/solution.py
+++ b/solution.py
@@ -13,6 +13,9 @@
 NHARM = 16
 ITERS = 4
 SWAP = [(0, 1), (1, 0)]
+LANES = 128
+HALF = 64
+PACKED = (56, LANES)
 F32 = jnp.float32
 BF16 = jnp.bfloat16
 
@@ -99,6 +102,34 @@
 
 def in_hbm(*values):
     return [pltpu.with_memory_space_constraint(value, pltpu.HBM) for value in values]
+
+
+def pack(value):
+    spare = jnp.zeros((value.shape[0], 2 * LANES - MODES), F32)
+    tail = jnp.concatenate([value[:, LANES:], spare], axis=1)
+    lane = lax.broadcasted_iota(jnp.int32, (8, LANES), 1)
+    middle = []
+    for row in (0, 8):
+        late = pltpu.roll(tail[row + 16 : row + 24], HALF, 1)
+        middle.append(jnp.where(lane < HALF, tail[row : row + 8], late))
+    last = jnp.zeros((8, LANES), F32)
+    for g in range(4):
+        moved = pltpu.roll(tail[8 * g : 8 * g + 8], HALF + 8 * g, 1)
+        last = jnp.where((lane >= 8 * g) & (lane < 8 * g + 8), moved, last)
+    return jnp.concatenate([value[:, :LANES], *middle, last])
+
+
+def unpack(packed):
+    lane = lax.broadcasted_iota(jnp.int32, (8, LANES), 1)
+    tail = []
+    for g in range(4):
+        row = 32 + 8 * (g % 2)
+        middle = packed[row : row + 8]
+        if g >= 2:
+            middle = pltpu.roll(middle, HALF, 1)
+        last = pltpu.roll(packed[48:56], HALF - 8 * g, 1)
+        tail.append(jnp.where(lane < HALF, middle, last))
+    return jnp.concatenate([packed[:32], jnp.concatenate(tail)], axis=1)[:, :MODES]
 
 
 def pick(core, even, odd):
@@ -146,7 +177,13 @@
     pairs = recv_ref.shape[0]
     for half, ref in ((core, mine_ref), (1 - core, recv_ref)):
         for k in range(pairs):
-            out_ref[half * pairs + k] = ref[k]
+            out_ref[half * pairs + k] = pack(ref[k].astype(F32)).astype(BF16)
+
+
+def pack_kernel(columns, row_ref, out_ref):
+    row = jnp.broadcast_to(row_ref[...], (columns, MODES))
+    out = pack(row)
+    out_ref[...] = jnp.where(out == 0.0, 1.0, out)
 
 
 def regroup_kernel(core_ref, stiff_hbm, keep_ref, send_ref, stiff_ref, sems):
@@ -184,22 +221,24 @@
     prev_ref, out_ref = rest if len(rest) == 2 else (None, rest[0])
     core = core_ref[0]
     slots = keep_ref.shape[1]
+    amp = unpack(amp_ref[...].astype(F32)).astype(BF16)
     for half, ref in ((core, keep_ref), (1 - core, recv_ref)):
         for k in range(slots):
             at = half * slots + k
-            value = jnp.dot(amp_ref[...], ref[source, k], preferred_element_type=F32)
+            value = pack(jnp.dot(amp, ref[source, k], preferred_element_type=F32))
             if prev_ref is not None:
                 value = value + prev_ref[at]
             out_ref[at] = value.astype(out_ref.dtype)
 
 
 def parity_weights(odd, core, table_ref, amp_ref, weights_ref):
-    local_diam, columns, _ = amp_ref.shape
+    local_diam = amp_ref.shape[0]
+    columns = weights_ref.shape[1] // local_diam
     pairs = local_diam // 2
     for at_half, half in enumerate((core, 1 - core)):
         for k in range(pairs):
             at = half * pairs + k
-            amp = amp_ref[at].astype(F32)
+            amp = unpack(amp_ref[at].astype(F32))
             for s in range(local_diam):
                 value = table_ref[2 * at + odd, s : s + 1] * amp
                 weights_ref[at_half * pairs + k, s * columns : (s + 1) * columns] = value.astype(BF16)
@@ -282,7 +321,7 @@
         return jnp.einsum("hcr,hmr->hcm", combined, near, preferred_element_type=F32).astype(BF16)
 
     force_recv = other_core(force_part(combined_send, shapes_send))
-    slots_shape = (local_diam, columns, MODES)
+    slots_shape = (local_diam,) + PACKED
     force_slots = pl.pallas_call(
         assemble_kernel,
         name="assemble",
@@ -315,7 +354,15 @@
     recv = other_core(sent)
     table = lax.dynamic_slice_in_dim(cyclic_rows(order), first_diam, local_diam, 0)
     table = jnp.broadcast_to(table.T[:, :, None], (NBLADE, local_diam, MODES))
-    dyn_own = lax.dynamic_slice_in_dim(dyn_diag, own_diam * MODES, MODES, 0)[None, :]
+    dyn_own = pl.pallas_call(
+        functools.partial(pack_kernel, columns),
+        name="pack",
+        in_specs=[VMEM],
+        out_specs=VMEM,
+        out_shape=jax.ShapeDtypeStruct(PACKED, F32),
+        compiler_params=LIMIT,
+        cost_estimate=pl.CostEstimate(flops=1, bytes_accessed=1, transcendentals=0),
+    )(lax.dynamic_slice_in_dim(dyn_diag, own_diam * MODES, MODES, 0)[None, :])
     force_got, keep, table, dyn_own = lax.optimization_barrier((force_got, keep, table, dyn_own))
 
     def product(source, *operands):

time: 79.9 us -> 79.3 us (level)
  Pallas kernels: 10.3 us -> 11.6 us
  blocking collectives: 44 us -> 43.2 us
    pallas_call x8, Pallas kernels: 2.02 us -> 3 us  [product(): pl.pallas_call(functools.partial(product_kernel, source), name='product',...]
  transfers between devices with their start and end apart: 9 -> 9, of which waited for: 6 -> 6; matrix products, arithmetic and copies ran while one was open for 2% -> 2% of each run, Pallas kernels for 6% -> 7%
where the time goes in v11:
time: 79.3 us; the launch traced here: 78.8 us
  blocking collectives  43.2 us (54%)
  starting transfers between devices  16.7 us (21%)
  Pallas kernels  11.6 us (15%)
  waiting for transfers between devices  4.59 us (6%)
  matrix products  1.44 us (2%)
  local copies, waits for them, and re-layouts  0.97 us (1%)
    all_to_all x5, blocking collectives, exchange(): return lax.all_to_all(slots, 'rows', 0, 0, tiled=True)  43.2 us
    ppermute x8, starting transfers between devices, other_core(): return lax.ppermute(value, 'diam', SWAP)  10 us
    all_to_all x1, starting transfers between devices, exchange(): return lax.all_to_all(slots, 'rows', 0, 0, tiled=True)  6.68 us
    pallas_call x8, Pallas kernels, product(): pl.pallas_call(functools.partial(product_kernel, source), name='product',...  3 us
    ppermute x8, waiting for transfers between devices, other_core(): return lax.ppermute(value, 'diam', SWAP)  2.39 us
    pallas_call x1, Pallas kernels, chunk_plan(): pl.pallas_call(functools.partial(load_kernel, columns), name='load', in_s...  2.28 us
    all_to_all x1, waiting for transfers between devices, exchange(): return lax.all_to_all(slots, 'rows', 0, 0, tiled=True)  2.2 us
    pallas_call x1, Pallas kernels, chunk_plan(): pl.pallas_call(crossed_kernel, name='blades_crossed', in_specs=[SMEM] + [...  2.1 us
  transfers between devices with their start and end apart: 9, of which 6 were waited for; matrix products, arithmetic and copies ran while one was open for 2% of the time, Pallas kernels for 7%

profile of v11, /device:TPU:1, one launch (start us, length us, event | category | flops | bytes accessed | tf_op | source)
XLA Modules:
  0.0 78.8 jit_solution(9605456131376857663)
XLA Ops:
  0.0 2.3 %load.1 = (bf16[4,32,1024]{2,1,0:T(8,128)(2,1)S(1)}, bf16[4,32,1024]{2,1,0:T(8,128)(2,1)S(1)}, bf16[4,200,1024]{2,1,0:T(8,128)(2,1)S(1)}, bf16[4,200,1024]{2,1,0:T(8,128)(2,1)S(1)}) custom-call(s32[1]{0:T(128)} %bitcast.core_ref, s32[16]{0:T(128)} %harm_hbm.1, bf16[1024,512]{1,0:T(8,128)(2,1)} %loads_hbm.1, bf16[4,2,200,1024]{3,2,1,0:T(8,128)(2,1)} %bitcast.14), custom_call_target="tpu_custom_call" | custom-call | tf_op jit(solution)/shard_map/load/pallas_call | solution.py:306
  2.3 0.6 convolution_convert_fusion
  3.0 0.6 convolution_convert_fusion.1.mine_ref
  3.6 0.5 collective-permute-done.recv_ref
  4.2 0.7 assemble.1
  4.9 6.7 %all-to-all-start = ((bf16[8,56,128]{2,1,0:T(8,128)(2,1)}), bf16[8,56,128]{2,1,0:T(8,128)(2,1)S(1)}, u32[]{:S(2)}, u32[]{:S(2)}) async-start(bf16[8,56,128]{2,1,0:T(8,128)(2,1)} %assemble.1), calls=%async_computation | async-start | bytes 229376 | tf_op jit(solution)/shard_map/all_to_all | solution.py:298
  11.6 2.0 %regroup.1 = (bf16[2,4,200,200]{3,2,1,0:T(8,128)(2,1)S(1)}, bf16[2,4,200,200]{3,2,1,0:T(8,128)(2,1)S(1)}) custom-call(s32[1]{0:T(128)} %bitcast.core_ref, f32[400,1600]{1,0:T(8,128)} %bitcast.19), custom_call_target="tpu_custom_call" | custom-call | flops 1280000 | bytes 5120000 | tf_op jit(solution)/shard_map/regroup/pallas_call | solution.py:339
  13.6 0.7 collective-permute-start.1
  14.5 0.8 dynamic_slice.7
  15.5 2.2 %all-to-all-done = bf16[8,56,128]{2,1,0:T(8,128)(2,1)S(1)} async-done(((bf16[8,56,128]{2,1,0:T(8,128)(2,1)}), bf16[8,56,128]{2,1,0:T(8,128)(2,1)S(1)}, u32[]{:S(2)}, u32[]{:S(2)}) %all-to-all-start) | async-done | bytes 114720 | tf_op jit(solution)/shard_map/all_to_all | solution.py:298
  17.8 1.8 %collective-permute-start.2 = (bf16[56,128]{1,0:T(8,128)(2,1)S(1)}, bf16[56,128]{1,0:T(8,128)(2,1)S(1)}, u32[]{:S(2)}, u32[]{:S(2)}) collective-permute-start(bf16[56,128]{1,0:T(8,128)(2,1)S(1)} %divide_convert_fusion.4.amp_ref), channel_id=1, source_target_pairs={{0,1},{1,0},{2,3},{3,2},{4,5},{5,4},{6,7},{7,6},{8,9},{9,8},{10,11... | collective-permute-start | bytes 43016 | tf_op jit(solution)/shard_map/ppermute | solution.py:295
  19.7 0.4 product.8.rest_0_
  20.0 0.5 collective-permute-done.2.amp_ref
  20.5 0.4 product.9
  20.9 8.5 %all_to_all.30 = bf16[8,56,128]{2,1,0:T(8,128)(2,1)S(1)} all-to-all(bf16[8,56,128]{2,1,0:T(8,128)(2,1)S(1)} %product.9), channel_id=1, replica_groups=mesh['grp'=2,'rows'=8,'diam'=2] {'rows'}, dimensions={0} | all-to-all | bytes 229376 | tf_op jit(solution)/shard_map/all_to_all | solution.py:298
  29.4 1.7 %collective-permute-start.3 = (bf16[56,128]{1,0:T(8,128)(2,1)S(1)}, bf16[56,128]{1,0:T(8,128)(2,1)S(1)}, u32[]{:S(2)}, u32[]{:S(2)}) collective-permute-start(bf16[56,128]{1,0:T(8,128)(2,1)S(1)} %divide_convert_fusion.3.amp_ref), channel_id=1, source_target_pairs={{0,1},{1,0},{2,3},{3,2},{4,5},{5,4},{6,7},{7,6},{8,9},{9,8},{10,11... | collective-permute-start | bytes 43016 | tf_op jit(solution)/shard_map/ppermute | solution.py:295
  31.1 0.4 product.10.rest_0_
  31.4 0.5 collective-permute-done.3.amp_ref
  31.9 0.4 product.11
  32.3 8.5 %all_to_all.31 = bf16[8,56,128]{2,1,0:T(8,128)(2,1)S(1)} all-to-all(bf16[8,56,128]{2,1,0:T(8,128)(2,1)S(1)} %product.11), channel_id=1, replica_groups=mesh['grp'=2,'rows'=8,'diam'=2] {'rows'}, dimensions={0} | all-to-all | bytes 229376 | tf_op jit(solution)/shard_map/all_to_all | solution.py:298
  40.8 1.7 %collective-permute-start.4 = (bf16[56,128]{1,0:T(8,128)(2,1)S(1)}, bf16[56,128]{1,0:T(8,128)(2,1)S(1)}, u32[]{:S(2)}, u32[]{:S(2)}) collective-permute-start(bf16[56,128]{1,0:T(8,128)(2,1)S(1)} %divide_convert_fusion.2.amp_ref), channel_id=1, source_target_pairs={{0,1},{1,0},{2,3},{3,2},{4,5},{5,4},{6,7},{7,6},{8,9},{9,8},{10,11... | collective-permute-start | bytes 43016 | tf_op jit(solution)/shard_map/ppermute | solution.py:295
  42.5 0.4 product.12.rest_0_
  42.8 0.5 collective-permute-done.4.amp_ref
  43.7 8.6 %all_to_all.32 = bf16[8,56,128]{2,1,0:T(8,128)(2,1)S(1)} all-to-all(bf16[8,56,128]{2,1,0:T(8,128)(2,1)S(1)} %product.13), channel_id=1, replica_groups=mesh['grp'=2,'rows'=8,'diam'=2] {'rows'}, dimensions={0} | all-to-all | bytes 229376 | tf_op jit(solution)/shard_map/all_to_all | solution.py:298
  52.3 1.7 %collective-permute-start.5 = (bf16[56,128]{1,0:T(8,128)(2,1)S(1)}, bf16[56,128]{1,0:T(8,128)(2,1)S(1)}, u32[]{:S(2)}, u32[]{:S(2)}) collective-permute-start(bf16[56,128]{1,0:T(8,128)(2,1)S(1)} %divide_convert_fusion.1.amp_ref), channel_id=1, source_target_pairs={{0,1},{1,0},{2,3},{3,2},{4,5},{5,4},{6,7},{7,6},{8,9},{9,8},{10,11... | collective-permute-start | bytes 43016 | tf_op jit(solution)/shard_map/ppermute | solution.py:295
  54.0 0.4 product.14.rest_0_
  54.4 0.5 collective-permute-done.5.amp_ref
  55.6 8.7 %all_to_all.33 = bf16[8,56,128]{2,1,0:T(8,128)(2,1)S(1)} all-to-all(bf16[8,56,128]{2,1,0:T(8,128)(2,1)S(1)} %product.15), channel_id=1, replica_groups=mesh['grp'=2,'rows'=8,'diam'=2] {'rows'}, dimensions={0} | all-to-all | bytes 229376 | tf_op jit(solution)/shard_map/all_to_all | solution.py:298
  64.3 9.0 %all_to_all.34.amp_ref = bf16[8,56,128]{2,1,0:T(8,128)(2,1)S(1)} all-to-all(bf16[8,56,128]{2,1,0:T(8,128)(2,1)S(1)} %broadcast_in_dim.40), channel_id=1, replica_groups=mesh['grp'=2,'rows'=8,'diam'=2] {'rows'}, dimensions={0} | all-to-all | bytes 229376 | tf_op jit(solution)/shard_map/all_to_all | solution.py:298
  73.3 2.0 %collective-permute-start.7 = (bf16[8,56,128]{2,1,0:T(8,128)(2,1)S(1)}, bf16[8,56,128]{2,1,0:T(8,128)(2,1)S(1)}, u32[]{:S(2)}, u32[]{:S(2)}) collective-permute-start(bf16[8,56,128]{2,1,0:T(8,128)(2,1)S(1)} %all_to_all.34.amp_ref), channel_id=1, source_target_pairs={{0,1},{1,0},{2,3},{3,2},{4,5},{5,4},{6,7},{7,6},{8,9},{9,8},{10,11... | collective-permute-start | bytes 344072 | tf_op jit(solution)/shard_map/ppermute | solution.py:295
  75.3 1.3 %blades_same.1.prev_ref = f32[256,1024]{1,0:T(8,128)S(1)} custom-call(s32[1]{0:T(128)} %bitcast.core_ref, f32[16,8,200]{2,1,0:T(8,128)S(1)} %broadcast_in_dim.38.table_ref, bf16[8,56,128]{2,1,0:T(8,128)(2,1)S(1)} %all_to_all.34.amp_ref, bf16[8,200,1024]{2,1,0:T(8,128)(2,1)S(1)} %bitcast.16, bf16[8,200,1024]{2,1,0:T(8,128)(2,1)S(1)} %collective-permute-done.6.recv_ref), custom_call_target="tpu_custom_call" | custom-call | flops 838860800 | bytes 3276800 | tf_op jit(solution)/shard_map/blades_same/pallas_call | solution.py:397
  76.7 2.1 %blades_crossed.1 = bf16[8,32,1024]{2,1,0:T(8,128)(2,1)} custom-call(s32[1]{0:T(128)} %bitcast.core_ref, f32[16,8,200]{2,1,0:T(8,128)S(1)} %broadcast_in_dim.38.table_ref, bf16[8,56,128]{2,1,0:T(8,128)(2,1)S(1)} %collective-permute-done.7.amp_ref, bf16[8,200,1024]{2,1,0:T(8,128)(2,1)S(1)} %bitcast.17, ...), custom_call_target="tpu_custom_call" | custom-call | flops 838860800 | bytes 3276800 | tf_op jit(solution)/shard_map/blades_crossed/pallas_call | solution.py:409
  (30 shorter events, 1.9 us)
Async XLA Ops:
  2.9 1.3 %collective-permute-start = (bf16[4,32,200]{2,1,0:T(8,128)(2,1)S(1)}, bf16[4,32,200]{2,1,0:T(8,128)(2,1)S(1)}, u32[]{:S(2)}, u32[]{:S(2)}) collective-permute-start(bf16[4,32,200]{2,1,0:T(8,128)(2,1)S(1)} %convolution_convert_fusion), channel_id=1, source_target_pairs={{0,1},{1,0},{2,3},{3,2},{4,5},{5,4},{6,7},{7,6},{8,9},{9,8},{10,11... | collective-permute-start | bytes 153608 | tf_op jit(solution)/shard_map/ppermute | solution.py:295
  3.6 10.7 %copy-start.1 = (s32[16]{0:T(128)S(1)}, s32[16]{0:T(128)}, u32[]{:S(2)}) copy-start(s32[16]{0:T(128)} %param.11) | copy-start | bytes 196
  4.9 12.8 %all-to-all-start = ((bf16[8,56,128]{2,1,0:T(8,128)(2,1)}), bf16[8,56,128]{2,1,0:T(8,128)(2,1)S(1)}, u32[]{:S(2)}, u32[]{:S(2)}) async-start(bf16[8,56,128]{2,1,0:T(8,128)(2,1)} %assemble.1), calls=%async_computation | async-start | bytes 229376 | tf_op jit(solution)/shard_map/all_to_all | solution.py:298
  13.6 6.0 %collective-permute-start.1 = (bf16[2,4,200,200]{3,2,1,0:T(8,128)(2,1)S(1)}, bf16[2,4,200,200]{3,2,1,0:T(8,128)(2,1)S(1)}, u32[]{:S(2)}, u32[]{:S(2)}) collective-permute-start(bf16[2,4,200,200]{3,2,1,0:T(8,128)(2,1)S(1)} %get-tuple-element.44), channel_id=1, source_target_pairs={{0,1},{1,0},{2,3},{3,2},{4,5},{5,4},{6,7},{7,6},{8,9},{9,8},{10,11... | collective-permute-start | bytes 1920008 | tf_op jit(solution)/shard_map/ppermute | solution.py:295
  17.8 2.7 %collective-permute-start.2 = (bf16[56,128]{1,0:T(8,128)(2,1)S(1)}, bf16[56,128]{1,0:T(8,128)(2,1)S(1)}, u32[]{:S(2)}, u32[]{:S(2)}) collective-permute-start(bf16[56,128]{1,0:T(8,128)(2,1)S(1)} %divide_convert_fusion.4.amp_ref), channel_id=1, source_target_pairs={{0,1},{1,0},{2,3},{3,2},{4,5},{5,4},{6,7},{7,6},{8,9},{9,8},{10,11... | collective-permute-start | bytes 43016 | tf_op jit(solution)/shard_map/ppermute | solution.py:295
  29.4 2.5 %collective-permute-start.3 = (bf16[56,128]{1,0:T(8,128)(2,1)S(1)}, bf16[56,128]{1,0:T(8,128)(2,1)S(1)}, u32[]{:S(2)}, u32[]{:S(2)}) collective-permute-start(bf16[56,128]{1,0:T(8,128)(2,1)S(1)} %divide_convert_fusion.3.amp_ref), channel_id=1, source_target_pairs={{0,1},{1,0},{2,3},{3,2},{4,5},{5,4},{6,7},{7,6},{8,9},{9,8},{10,11... | collective-permute-start | bytes 43016 | tf_op jit(solution)/shard_map/ppermute | solution.py:295
  40.8 2.5 %collective-permute-start.4 = (bf16[56,128]{1,0:T(8,128)(2,1)S(1)}, bf16[56,128]{1,0:T(8,128)(2,1)S(1)}, u32[]{:S(2)}, u32[]{:S(2)}) collective-permute-start(bf16[56,128]{1,0:T(8,128)(2,1)S(1)} %divide_convert_fusion.2.amp_ref), channel_id=1, source_target_pairs={{0,1},{1,0},{2,3},{3,2},{4,5},{5,4},{6,7},{7,6},{8,9},{9,8},{10,11... | collective-permute-start | bytes 43016 | tf_op jit(solution)/shard_map/ppermute | solution.py:295
  43.3 11.5 %copy-start = (bf16[1024,1600]{0,1:T(8,128)(2,1)S(1)}, bf16[1024,1600]{0,1:T(8,128)(2,1)}, u32[]{:S(2)}) copy-start(bf16[1024,1600]{0,1:T(8,128)(2,1)} %param.6) | copy-start | bytes 9830404
  52.3 2.5 %collective-permute-start.5 = (bf16[56,128]{1,0:T(8,128)(2,1)S(1)}, bf16[56,128]{1,0:T(8,128)(2,1)S(1)}, u32[]{:S(2)}, u32[]{:S(2)}) collective-permute-start(bf16[56,128]{1,0:T(8,128)(2,1)S(1)} %divide_convert_fusion.1.amp_ref), channel_id=1, source_target_pairs={{0,1},{1,0},{2,3},{3,2},{4,5},{5,4},{6,7},{7,6},{8,9},{9,8},{10,11... | collective-permute-start | bytes 43016 | tf_op jit(solution)/shard_map/ppermute | solution.py:295
  54.8 20.5 %collective-permute-start.6 = (bf16[8,200,1024]{2,1,0:T(8,128)(2,1)S(1)}, bf16[8,200,1024]{2,1,0:T(8,128)(2,1)S(1)}, u32[]{:S(2)}, u32[]{:S(2)}) collective-permute-start(bf16[8,200,1024]{2,1,0:T(8,128)(2,1)S(1)} %bitcast.15), channel_id=1, source_target_pairs={{0,1},{1,0},{2,3},{3,2},{4,5},{5,4},{6,7},{7,6},{8,9},{9,8},{10,11... | collective-permute-start | bytes 9830408 | tf_op jit(solution)/shard_map/ppermute | solution.py:295
  73.3 3.4 %collective-permute-start.7 = (bf16[8,56,128]{2,1,0:T(8,128)(2,1)S(1)}, bf16[8,56,128]{2,1,0:T(8,128)(2,1)S(1)}, u32[]{:S(2)}, u32[]{:S(2)}) collective-permute-start(bf16[8,56,128]{2,1,0:T(8,128)(2,1)S(1)} %all_to_all.34.amp_ref), channel_id=1, source_target_pairs={{0,1},{1,0},{2,3},{3,2},{4,5},{5,4},{6,7},{7,6},{8,9},{9,8},{10,11... | collective-permute-start | bytes 344072 | tf_op jit(solution)/shard_map/ppermute | solution.py:295

commit v12 on v11

--- a/solution.py
+++ b/solution.py
@@ -15,6 +15,7 @@
 SWAP = [(0, 1), (1, 0)]
 LANES = 128
 HALF = 64
+HUB = 2
 PACKED = (56, LANES)
 F32 = jnp.float32
 BF16 = jnp.bfloat16
@@ -177,7 +178,7 @@
     pairs = recv_ref.shape[0]
     for half, ref in ((core, mine_ref), (1 - core, recv_ref)):
         for k in range(pairs):
-            out_ref[half * pairs + k] = pack(ref[k].astype(F32)).astype(BF16)
+            out_ref[half * pairs + (k ^ HUB)] = pack(ref[k].astype(F32)).astype(BF16)
 
 
 def pack_kernel(columns, row_ref, out_ref):
@@ -224,7 +225,7 @@
     amp = unpack(amp_ref[...].astype(F32)).astype(BF16)
     for half, ref in ((core, keep_ref), (1 - core, recv_ref)):
         for k in range(slots):
-            at = half * slots + k
+            at = half * slots + (k ^ HUB)
             value = pack(jnp.dot(amp, ref[source, k], preferred_element_type=F32))
             if prev_ref is not None:
                 value = value + prev_ref[at]
@@ -238,7 +239,7 @@
     for at_half, half in enumerate((core, 1 - core)):
         for k in range(pairs):
             at = half * pairs + k
-            amp = unpack(amp_ref[at].astype(F32))
+            amp = unpack(amp_ref[half * pairs + (k ^ HUB)].astype(F32))
             for s in range(local_diam):
                 value = table_ref[2 * at + odd, s : s + 1] * amp
                 weights_ref[at_half * pairs + k, s * columns : (s + 1) * columns] = value.astype(BF16)
@@ -295,7 +296,8 @@
         return lax.ppermute(value, "diam", SWAP)
 
     def exchange(slots):
-        return lax.all_to_all(slots, "rows", 0, 0, tiled=True)
+        order = [row ^ HUB for row in range(slots.shape[0])]
+        return lax.all_to_all(slots, "rows", 0, 0, tiled=True, axis_index_groups=[order])
 
     def row_total(got):
         return jnp.sum(got.astype(F32), axis=0)

time: 79.3 us -> 73.8 us (0.931)
  blocking collectives: 43.2 us -> 37.4 us
  starting transfers between devices: 16.7 us -> 18.7 us
  waiting for transfers between devices: 4.59 us -> 2.97 us
    all_to_all x5, blocking collectives: 43.2 us -> 37.4 us  [exchange(): lax.all_to_all(slots, 'rows', 0, 0, tiled=True, axis_index_groups=[order])]
    ppermute x8, starting transfers between devices: 10 us -> 11.7 us  [other_core(): return lax.ppermute(value, 'diam', SWAP)]
    all_to_all x1, waiting for transfers between devices: 2.2 us -> 0.59 us  [exchange(): lax.all_to_all(slots, 'rows', 0, 0, tiled=True, axis_index_groups=[order])]
  transfers between devices with their start and end apart: 9 -> 9, of which waited for: 6 -> 6; matrix products, arithmetic and copies ran while one was open for 2% -> 3% of each run, Pallas kernels for 7% -> 7%
where the time goes in v12:
time: 73.8 us; the launch traced here: 73.4 us
  blocking collectives  37.4 us (51%)
  starting transfers between devices  18.7 us (25%)
  Pallas kernels  11.6 us (16%)
  waiting for transfers between devices  2.97 us (4%)
  matrix products  1.44 us (2%)
  local copies, waits for them, and re-layouts  0.97 us (1%)
    all_to_all x5, blocking collectives, exchange(): lax.all_to_all(slots, 'rows', 0, 0, tiled=True, axis_index_groups=[order])  37.4 us
    ppermute x8, starting transfers between devices, other_core(): return lax.ppermute(value, 'diam', SWAP)  11.7 us
    all_to_all x1, starting transfers between devices, exchange(): lax.all_to_all(slots, 'rows', 0, 0, tiled=True, axis_index_groups=[order])  6.96 us
    pallas_call x8, Pallas kernels, product(): pl.pallas_call(functools.partial(product_kernel, source), name='product',...  3 us
    ppermute x8, waiting for transfers between devices, other_core(): return lax.ppermute(value, 'diam', SWAP)  2.39 us
    pallas_call x1, Pallas kernels, chunk_plan(): pl.pallas_call(functools.partial(load_kernel, columns), name='load', in_s...  2.28 us
    pallas_call x1, Pallas kernels, chunk_plan(): pl.pallas_call(crossed_kernel, name='blades_crossed', in_specs=[SMEM] + [...  2.1 us
    pallas_call x1, Pallas kernels, chunk_plan(): pl.pallas_call(regroup_kernel, name='regroup', in_specs=[SMEM, HBM], out_...  2.02 us
  transfers between devices with their start and end apart: 9, of which 6 were waited for; matrix products, arithmetic and copies ran while one was open for 3% of the time, Pallas kernels for 7%

profile of v12, /device:TPU:1, one launch (start us, length us, event | category | flops | bytes accessed | tf_op | source)
XLA Modules:
  0.0 73.4 jit_solution(11345384006514595364)
XLA Ops:
  0.0 2.3 %load.1 = (bf16[4,32,1024]{2,1,0:T(8,128)(2,1)S(1)}, bf16[4,32,1024]{2,1,0:T(8,128)(2,1)S(1)}, bf16[4,200,1024]{2,1,0:T(8,128)(2,1)S(1)}, bf16[4,200,1024]{2,1,0:T(8,128)(2,1)S(1)}) custom-call(s32[1]{0:T(128)} %bitcast.core_ref, s32[16]{0:T(128)} %harm_hbm.1, bf16[1024,512]{1,0:T(8,128)(2,1)} %loads_hbm.1, bf16[4,2,200,1024]{3,2,1,0:T(8,128)(2,1)} %bitcast.14), custom_call_target="tpu_custom_call" | custom-call | tf_op jit(solution)/shard_map/load/pallas_call | solution.py:308
  2.3 0.6 convolution_convert_fusion
  3.0 0.6 convolution_convert_fusion.1.mine_ref
  3.6 0.5 collective-permute-done.recv_ref
  4.2 0.7 %assemble.1 = bf16[8,56,128]{2,1,0:T(8,128)(2,1)} custom-call(s32[1]{0:T(128)} %bitcast.core_ref, bf16[4,32,200]{2,1,0:T(8,128)(2,1)S(1)} %convolution_convert_fusion.1.mine_ref, bf16[4,32,200]{2,1,0:T(8,128)(2,1)S(1)} %collective-permute-done.recv_ref), custom_call_target="tpu_custom_call" | custom-call | tf_op jit(solution)/shard_map/assemble/pallas_call | solution.py:327
  4.9 7.0 %all-to-all-start = ((bf16[8,56,128]{2,1,0:T(8,128)(2,1)}), bf16[8,56,128]{2,1,0:T(8,128)(2,1)S(1)}, u32[]{:S(2)}, u32[]{:S(2)}) async-start(bf16[8,56,128]{2,1,0:T(8,128)(2,1)} %assemble.1), calls=%async_computation | async-start | bytes 229376 | tf_op jit(solution)/shard_map/all_to_all | solution.py:300
  11.9 2.0 %regroup.1 = (bf16[2,4,200,200]{3,2,1,0:T(8,128)(2,1)S(1)}, bf16[2,4,200,200]{3,2,1,0:T(8,128)(2,1)S(1)}) custom-call(s32[1]{0:T(128)} %bitcast.core_ref, f32[400,1600]{1,0:T(8,128)} %bitcast.19), custom_call_target="tpu_custom_call" | custom-call | flops 1280000 | bytes 5120000 | tf_op jit(solution)/shard_map/regroup/pallas_call | solution.py:341
  13.9 1.0 %collective-permute-start.1 = (bf16[2,4,200,200]{3,2,1,0:T(8,128)(2,1)S(1)}, bf16[2,4,200,200]{3,2,1,0:T(8,128)(2,1)S(1)}, u32[]{:S(2)}, u32[]{:S(2)}) collective-permute-start(bf16[2,4,200,200]{3,2,1,0:T(8,128)(2,1)S(1)} %get-tuple-element.44), channel_id=1, source_target_pairs={{0,1},{1,0},{2,3},{3,2},{4,5},{5,4},{6,7},{7,6},{8,9},{9,8},{10,11... | collective-permute-start | bytes 1920008 | tf_op jit(solution)/shard_map/ppermute | solution.py:296
  15.1 0.8 %dynamic_slice.7 = f32[200]{0:T(256)S(1)} dynamic-slice(f32[3200]{0:T(1024)} %param.10, s32[]{:T(128)S(6)} %select_n.32), dynamic_slice_sizes={200} | dynamic-slice | bytes 1604 | tf_op jit(solution)/shard_map/dynamic_slice | solution.py:367
  16.0 0.6 all-to-all-done
  16.8 1.8 %collective-permute-start.2 = (bf16[56,128]{1,0:T(8,128)(2,1)S(1)}, bf16[56,128]{1,0:T(8,128)(2,1)S(1)}, u32[]{:S(2)}, u32[]{:S(2)}) collective-permute-start(bf16[56,128]{1,0:T(8,128)(2,1)S(1)} %divide_convert_fusion.4.amp_ref), channel_id=1, source_target_pairs={{0,1},{1,0},{2,3},{3,2},{4,5},{5,4},{6,7},{7,6},{8,9},{9,8},{10,11... | collective-permute-start | bytes 43016 | tf_op jit(solution)/shard_map/ppermute | solution.py:296
  18.6 0.4 product.8.rest_0_
  19.0 0.5 collective-permute-done.2.amp_ref
  19.4 0.4 product.9
  19.8 7.5 %all_to_all.30 = bf16[8,56,128]{2,1,0:T(8,128)(2,1)S(1)} all-to-all(bf16[8,56,128]{2,1,0:T(8,128)(2,1)S(1)} %product.9), channel_id=1, replica_groups={{4,6,0,2,12,14,8,10},{5,7,1,3,13,15,9,11},{20,22,16,18,28,30,24,26},{21..., dimensions={0} | all-to-all | bytes 229376 | tf_op jit(solution)/shard_map/all_to_all | solution.py:300
  27.3 1.8 %collective-permute-start.3 = (bf16[56,128]{1,0:T(8,128)(2,1)S(1)}, bf16[56,128]{1,0:T(8,128)(2,1)S(1)}, u32[]{:S(2)}, u32[]{:S(2)}) collective-permute-start(bf16[56,128]{1,0:T(8,128)(2,1)S(1)} %divide_convert_fusion.3.amp_ref), channel_id=1, source_target_pairs={{0,1},{1,0},{2,3},{3,2},{4,5},{5,4},{6,7},{7,6},{8,9},{9,8},{10,11... | collective-permute-start | bytes 43016 | tf_op jit(solution)/shard_map/ppermute | solution.py:296
  29.1 0.4 product.10.rest_0_
  29.5 0.5 collective-permute-done.3.amp_ref
  30.3 7.5 %all_to_all.31 = bf16[8,56,128]{2,1,0:T(8,128)(2,1)S(1)} all-to-all(bf16[8,56,128]{2,1,0:T(8,128)(2,1)S(1)} %product.11), channel_id=1, replica_groups={{4,6,0,2,12,14,8,10},{5,7,1,3,13,15,9,11},{20,22,16,18,28,30,24,26},{21..., dimensions={0} | all-to-all | bytes 229376 | tf_op jit(solution)/shard_map/all_to_all | solution.py:300
  37.8 1.8 %collective-permute-start.4 = (bf16[56,128]{1,0:T(8,128)(2,1)S(1)}, bf16[56,128]{1,0:T(8,128)(2,1)S(1)}, u32[]{:S(2)}, u32[]{:S(2)}) collective-permute-start(bf16[56,128]{1,0:T(8,128)(2,1)S(1)} %divide_convert_fusion.2.amp_ref), channel_id=1, source_target_pairs={{0,1},{1,0},{2,3},{3,2},{4,5},{5,4},{6,7},{7,6},{8,9},{9,8},{10,11... | collective-permute-start | bytes 43016 | tf_op jit(solution)/shard_map/ppermute | solution.py:296
  39.7 0.4 product.12.rest_0_
  40.0 0.5 collective-permute-done.4.amp_ref
  40.9 7.6 %all_to_all.32 = bf16[8,56,128]{2,1,0:T(8,128)(2,1)S(1)} all-to-all(bf16[8,56,128]{2,1,0:T(8,128)(2,1)S(1)} %product.13), channel_id=1, replica_groups={{4,6,0,2,12,14,8,10},{5,7,1,3,13,15,9,11},{20,22,16,18,28,30,24,26},{21..., dimensions={0} | all-to-all | bytes 229376 | tf_op jit(solution)/shard_map/all_to_all | solution.py:300
  48.5 1.8 %collective-permute-start.5 = (bf16[56,128]{1,0:T(8,128)(2,1)S(1)}, bf16[56,128]{1,0:T(8,128)(2,1)S(1)}, u32[]{:S(2)}, u32[]{:S(2)}) collective-permute-start(bf16[56,128]{1,0:T(8,128)(2,1)S(1)} %divide_convert_fusion.1.amp_ref), channel_id=1, source_target_pairs={{0,1},{1,0},{2,3},{3,2},{4,5},{5,4},{6,7},{7,6},{8,9},{9,8},{10,11... | collective-permute-start | bytes 43016 | tf_op jit(solution)/shard_map/ppermute | solution.py:296
  50.3 0.4 product.14.rest_0_
  50.7 0.5 collective-permute-done.5.amp_ref
  51.5 0.4 product.15
  51.9 7.5 %all_to_all.33 = bf16[8,56,128]{2,1,0:T(8,128)(2,1)S(1)} all-to-all(bf16[8,56,128]{2,1,0:T(8,128)(2,1)S(1)} %product.15), channel_id=1, replica_groups={{4,6,0,2,12,14,8,10},{5,7,1,3,13,15,9,11},{20,22,16,18,28,30,24,26},{21..., dimensions={0} | all-to-all | bytes 229376 | tf_op jit(solution)/shard_map/all_to_all | solution.py:300
  59.4 7.4 %all_to_all.34.amp_ref = bf16[8,56,128]{2,1,0:T(8,128)(2,1)S(1)} all-to-all(bf16[8,56,128]{2,1,0:T(8,128)(2,1)S(1)} %broadcast_in_dim.40), channel_id=1, replica_groups={{4,6,0,2,12,14,8,10},{5,7,1,3,13,15,9,11},{20,22,16,18,28,30,24,26},{21..., dimensions={0} | all-to-all | bytes 229376 | tf_op jit(solution)/shard_map/all_to_all | solution.py:300
  66.8 3.0 %collective-permute-start.7 = (bf16[8,56,128]{2,1,0:T(8,128)(2,1)S(1)}, bf16[8,56,128]{2,1,0:T(8,128)(2,1)S(1)}, u32[]{:S(2)}, u32[]{:S(2)}) collective-permute-start(bf16[8,56,128]{2,1,0:T(8,128)(2,1)S(1)} %all_to_all.34.amp_ref), channel_id=1, source_target_pairs={{0,1},{1,0},{2,3},{3,2},{4,5},{5,4},{6,7},{7,6},{8,9},{9,8},{10,11... | collective-permute-start | bytes 344072 | tf_op jit(solution)/shard_map/ppermute | solution.py:296
  69.9 1.4 %blades_same.1.prev_ref = f32[256,1024]{1,0:T(8,128)S(1)} custom-call(s32[1]{0:T(128)} %bitcast.core_ref, f32[16,8,200]{2,1,0:T(8,128)S(1)} %broadcast_in_dim.38.table_ref, bf16[8,56,128]{2,1,0:T(8,128)(2,1)S(1)} %all_to_all.34.amp_ref, bf16[8,200,1024]{2,1,0:T(8,128)(2,1)S(1)} %bitcast.16, bf16[8,200,1024]{2,1,0:T(8,128)(2,1)S(1)} %collective-permute-done.6.recv_ref), custom_call_target="tpu_custom_call" | custom-call | flops 838860800 | bytes 3276800 | tf_op jit(solution)/shard_map/blades_same/pallas_call | solution.py:399
  71.3 2.1 %blades_crossed.1 = bf16[8,32,1024]{2,1,0:T(8,128)(2,1)} custom-call(s32[1]{0:T(128)} %bitcast.core_ref, f32[16,8,200]{2,1,0:T(8,128)S(1)} %broadcast_in_dim.38.table_ref, bf16[8,56,128]{2,1,0:T(8,128)(2,1)S(1)} %collective-permute-done.7.amp_ref, bf16[8,200,1024]{2,1,0:T(8,128)(2,1)S(1)} %bitcast.17, ...), custom_call_target="tpu_custom_call" | custom-call | flops 838860800 | bytes 3276800 | tf_op jit(solution)/shard_map/blades_crossed/pallas_call | solution.py:411
  (30 shorter events, 1.9 us)
Async XLA Ops:
  2.9 1.3 %collective-permute-start = (bf16[4,32,200]{2,1,0:T(8,128)(2,1)S(1)}, bf16[4,32,200]{2,1,0:T(8,128)(2,1)S(1)}, u32[]{:S(2)}, u32[]{:S(2)}) collective-permute-start(bf16[4,32,200]{2,1,0:T(8,128)(2,1)S(1)} %convolution_convert_fusion), channel_id=1, source_target_pairs={{0,1},{1,0},{2,3},{3,2},{4,5},{5,4},{6,7},{7,6},{8,9},{9,8},{10,11... | collective-permute-start | bytes 153608 | tf_op jit(solution)/shard_map/ppermute | solution.py:296
  3.6 11.3 %copy-start.1 = (s32[16]{0:T(128)S(1)}, s32[16]{0:T(128)}, u32[]{:S(2)}) copy-start(s32[16]{0:T(128)} %param.11) | copy-start | bytes 196
  4.9 11.7 %all-to-all-start = ((bf16[8,56,128]{2,1,0:T(8,128)(2,1)}), bf16[8,56,128]{2,1,0:T(8,128)(2,1)S(1)}, u32[]{:S(2)}, u32[]{:S(2)}) async-start(bf16[8,56,128]{2,1,0:T(8,128)(2,1)} %assemble.1), calls=%async_computation | async-start | bytes 229376 | tf_op jit(solution)/shard_map/all_to_all | solution.py:300
  13.9 4.7 %collective-permute-start.1 = (bf16[2,4,200,200]{3,2,1,0:T(8,128)(2,1)S(1)}, bf16[2,4,200,200]{3,2,1,0:T(8,128)(2,1)S(1)}, u32[]{:S(2)}, u32[]{:S(2)}) collective-permute-start(bf16[2,4,200,200]{3,2,1,0:T(8,128)(2,1)S(1)} %get-tuple-element.44), channel_id=1, source_target_pairs={{0,1},{1,0},{2,3},{3,2},{4,5},{5,4},{6,7},{7,6},{8,9},{9,8},{10,11... | collective-permute-start | bytes 1920008 | tf_op jit(solution)/shard_map/ppermute | solution.py:296
  16.8 2.7 %collective-permute-start.2 = (bf16[56,128]{1,0:T(8,128)(2,1)S(1)}, bf16[56,128]{1,0:T(8,128)(2,1)S(1)}, u32[]{:S(2)}, u32[]{:S(2)}) collective-permute-start(bf16[56,128]{1,0:T(8,128)(2,1)S(1)} %divide_convert_fusion.4.amp_ref), channel_id=1, source_target_pairs={{0,1},{1,0},{2,3},{3,2},{4,5},{5,4},{6,7},{7,6},{8,9},{9,8},{10,11... | collective-permute-start | bytes 43016 | tf_op jit(solution)/shard_map/ppermute | solution.py:296
  27.3 2.7 %collective-permute-start.3 = (bf16[56,128]{1,0:T(8,128)(2,1)S(1)}, bf16[56,128]{1,0:T(8,128)(2,1)S(1)}, u32[]{:S(2)}, u32[]{:S(2)}) collective-permute-start(bf16[56,128]{1,0:T(8,128)(2,1)S(1)} %divide_convert_fusion.3.amp_ref), channel_id=1, source_target_pairs={{0,1},{1,0},{2,3},{3,2},{4,5},{5,4},{6,7},{7,6},{8,9},{9,8},{10,11... | collective-permute-start | bytes 43016 | tf_op jit(solution)/shard_map/ppermute | solution.py:296
  37.8 2.7 %collective-permute-start.4 = (bf16[56,128]{1,0:T(8,128)(2,1)S(1)}, bf16[56,128]{1,0:T(8,128)(2,1)S(1)}, u32[]{:S(2)}, u32[]{:S(2)}) collective-permute-start(bf16[56,128]{1,0:T(8,128)(2,1)S(1)} %divide_convert_fusion.2.amp_ref), channel_id=1, source_target_pairs={{0,1},{1,0},{2,3},{3,2},{4,5},{5,4},{6,7},{7,6},{8,9},{9,8},{10,11... | collective-permute-start | bytes 43016 | tf_op jit(solution)/shard_map/ppermute | solution.py:296
  40.5 10.7 %copy-start = (bf16[1024,1600]{0,1:T(8,128)(2,1)S(1)}, bf16[1024,1600]{0,1:T(8,128)(2,1)}, u32[]{:S(2)}) copy-start(bf16[1024,1600]{0,1:T(8,128)(2,1)} %param.6) | copy-start | bytes 9830404
  48.5 2.7 %collective-permute-start.5 = (bf16[56,128]{1,0:T(8,128)(2,1)S(1)}, bf16[56,128]{1,0:T(8,128)(2,1)S(1)}, u32[]{:S(2)}, u32[]{:S(2)}) collective-permute-start(bf16[56,128]{1,0:T(8,128)(2,1)S(1)} %divide_convert_fusion.1.amp_ref), channel_id=1, source_target_pairs={{0,1},{1,0},{2,3},{3,2},{4,5},{5,4},{6,7},{7,6},{8,9},{9,8},{10,11... | collective-permute-start | bytes 43016 | tf_op jit(solution)/shard_map/ppermute | solution.py:296
  51.2 18.7 %collective-permute-start.6 = (bf16[8,200,1024]{2,1,0:T(8,128)(2,1)S(1)}, bf16[8,200,1024]{2,1,0:T(8,128)(2,1)S(1)}, u32[]{:S(2)}, u32[]{:S(2)}) collective-permute-start(bf16[8,200,1024]{2,1,0:T(8,128)(2,1)S(1)} %bitcast.15), channel_id=1, source_target_pairs={{0,1},{1,0},{2,3},{3,2},{4,5},{5,4},{6,7},{7,6},{8,9},{9,8},{10,11... | collective-permute-start | bytes 9830408 | tf_op jit(solution)/shard_map/ppermute | solution.py:296
  66.8 4.4 %collective-permute-start.7 = (bf16[8,56,128]{2,1,0:T(8,128)(2,1)S(1)}, bf16[8,56,128]{2,1,0:T(8,128)(2,1)S(1)}, u32[]{:S(2)}, u32[]{:S(2)}) collective-permute-start(bf16[8,56,128]{2,1,0:T(8,128)(2,1)S(1)} %all_to_all.34.amp_ref), channel_id=1, source_target_pairs={{0,1},{1,0},{2,3},{3,2},{4,5},{5,4},{6,7},{7,6},{8,9},{9,8},{10,11... | collective-permute-start | bytes 344072 | tf_op jit(solution)/shard_map/ppermute | solution.py:296

commit v13 on v11

--- a/solution.py
+++ b/solution.py
@@ -15,6 +15,7 @@
 SWAP = [(0, 1), (1, 0)]
 LANES = 128
 HALF = 64
+ORDER = [5, 4, 3, 2, 1, 0, 7, 6]
 PACKED = (56, LANES)
 F32 = jnp.float32
 BF16 = jnp.bfloat16
@@ -130,6 +131,10 @@
         last = pltpu.roll(packed[48:56], HALF - 8 * g, 1)
         tail.append(jnp.where(lane < HALF, middle, last))
     return jnp.concatenate([packed[:32], jnp.concatenate(tail)], axis=1)[:, :MODES]
+
+
+def slot_of(half, pairs, k):
+    return jnp.where(half == 0, ORDER.index(k), ORDER.index(pairs + k))
 
 
 def pick(core, even, odd):
@@ -177,7 +182,7 @@
     pairs = recv_ref.shape[0]
     for half, ref in ((core, mine_ref), (1 - core, recv_ref)):
         for k in range(pairs):
-            out_ref[half * pairs + k] = pack(ref[k].astype(F32)).astype(BF16)
+            out_ref[slot_of(half, pairs, k)] = pack(ref[k].astype(F32)).astype(BF16)
 
 
 def pack_kernel(columns, row_ref, out_ref):
@@ -224,7 +229,7 @@
     amp = unpack(amp_ref[...].astype(F32)).astype(BF16)
     for half, ref in ((core, keep_ref), (1 - core, recv_ref)):
         for k in range(slots):
-            at = half * slots + k
+            at = slot_of(half, slots, k)
             value = pack(jnp.dot(amp, ref[source, k], preferred_element_type=F32))
             if prev_ref is not None:
                 value = value + prev_ref[at]
@@ -238,7 +243,7 @@
     for at_half, half in enumerate((core, 1 - core)):
         for k in range(pairs):
             at = half * pairs + k
-            amp = unpack(amp_ref[at].astype(F32))
+            amp = unpack(amp_ref[slot_of(half, pairs, k)].astype(F32))
             for s in range(local_diam):
                 value = table_ref[2 * at + odd, s : s + 1] * amp
                 weights_ref[at_half * pairs + k, s * columns : (s + 1) * columns] = value.astype(BF16)
@@ -295,7 +300,7 @@
         return lax.ppermute(value, "diam", SWAP)
 
     def exchange(slots):
-        return lax.all_to_all(slots, "rows", 0, 0, tiled=True)
+        return lax.all_to_all(slots, "rows", 0, 0, tiled=True, axis_index_groups=[ORDER])
 
     def row_total(got):
         return jnp.sum(got.astype(F32), axis=0)

time: 79.3 us -> 72.3 us (0.912)
  blocking collectives: 43.2 us -> 36.8 us
  waiting for transfers between devices: 4.59 us -> 2.41 us
  starting transfers between devices: 16.7 us -> 18.3 us
    all_to_all x5, blocking collectives: 43.2 us -> 36.8 us  [exchange(): lax.all_to_all(slots, 'rows', 0, 0, tiled=True, axis_index_groups=[ORDER])]
    all_to_all x1, waiting for transfers between devices: 2.2 us -> 0.01 us  [exchange(): lax.all_to_all(slots, 'rows', 0, 0, tiled=True, axis_index_groups=[ORDER])]
    all_to_all x1, starting transfers between devices: 6.68 us -> 7.69 us  [exchange(): lax.all_to_all(slots, 'rows', 0, 0, tiled=True, axis_index_groups=[ORDER])]
  transfers between devices with their start and end apart: 9 -> 9, of which waited for: 6 -> 5; matrix products, arithmetic and copies ran while one was open for 2% -> 3% of each run, Pallas kernels for 7% -> 7%
where the time goes in v13:
time: 72.3 us; the launch traced here: 71.8 us
  blocking collectives  36.8 us (51%)
  starting transfers between devices  18.3 us (25%)
  Pallas kernels  11.6 us (16%)
  waiting for transfers between devices  2.41 us (3%)
  matrix products  1.44 us (2%)
  local copies, waits for them, and re-layouts  0.97 us (1%)
    all_to_all x5, blocking collectives, exchange(): lax.all_to_all(slots, 'rows', 0, 0, tiled=True, axis_index_groups=[ORDER])  36.8 us
    ppermute x8, starting transfers between devices, other_core(): return lax.ppermute(value, 'diam', SWAP)  10.6 us
    all_to_all x1, starting transfers between devices, exchange(): lax.all_to_all(slots, 'rows', 0, 0, tiled=True, axis_index_groups=[ORDER])  7.69 us
    pallas_call x8, Pallas kernels, product(): pl.pallas_call(functools.partial(product_kernel, source), name='product',...  3 us
    ppermute x8, waiting for transfers between devices, other_core(): return lax.ppermute(value, 'diam', SWAP)  2.4 us
    pallas_call x1, Pallas kernels, chunk_plan(): pl.pallas_call(functools.partial(load_kernel, columns), name='load', in_s...  2.28 us
    pallas_call x1, Pallas kernels, chunk_plan(): pl.pallas_call(crossed_kernel, name='blades_crossed', in_specs=[SMEM] + [...  2.12 us
    pallas_call x1, Pallas kernels, chunk_plan(): pl.pallas_call(regroup_kernel, name='regroup', in_specs=[SMEM, HBM], out_...  2.02 us
  transfers between devices with their start and end apart: 9, of which 5 were waited for; matrix products, arithmetic and copies ran while one was open for 3% of the time, Pallas kernels for 7%

profile of v13, /device:TPU:1, one launch (start us, length us, event | category | flops | bytes accessed | tf_op | source)
XLA Modules:
  0.0 71.8 jit_solution(18440961287605922052)
XLA Ops:
  0.0 2.3 %load.1 = (bf16[4,32,1024]{2,1,0:T(8,128)(2,1)S(1)}, bf16[4,32,1024]{2,1,0:T(8,128)(2,1)S(1)}, bf16[4,200,1024]{2,1,0:T(8,128)(2,1)S(1)}, bf16[4,200,1024]{2,1,0:T(8,128)(2,1)S(1)}) custom-call(s32[1]{0:T(128)} %bitcast.core_ref, s32[16]{0:T(128)} %harm_hbm.1, bf16[1024,512]{1,0:T(8,128)(2,1)} %loads_hbm.1, bf16[4,2,200,1024]{3,2,1,0:T(8,128)(2,1)} %bitcast.14), custom_call_target="tpu_custom_call" | custom-call | tf_op jit(solution)/shard_map/load/pallas_call | solution.py:311
  2.3 0.6 convolution_convert_fusion
  3.0 0.6 convolution_convert_fusion.1.mine_ref
  3.6 0.5 collective-permute-done.recv_ref
  4.2 0.7 %assemble.1 = bf16[8,56,128]{2,1,0:T(8,128)(2,1)} custom-call(s32[1]{0:T(128)} %bitcast.core_ref, bf16[4,32,200]{2,1,0:T(8,128)(2,1)S(1)} %convolution_convert_fusion.1.mine_ref, bf16[4,32,200]{2,1,0:T(8,128)(2,1)S(1)} %collective-permute-done.recv_ref), custom_call_target="tpu_custom_call" | custom-call | tf_op jit(solution)/shard_map/assemble/pallas_call | solution.py:330
  4.9 7.7 %all-to-all-start = ((bf16[8,56,128]{2,1,0:T(8,128)(2,1)}), bf16[8,56,128]{2,1,0:T(8,128)(2,1)S(1)}, u32[]{:S(2)}, u32[]{:S(2)}) async-start(bf16[8,56,128]{2,1,0:T(8,128)(2,1)} %assemble.1), calls=%async_computation | async-start | bytes 229376 | tf_op jit(solution)/shard_map/all_to_all | solution.py:303
  12.6 2.0 %regroup.1 = (bf16[2,4,200,200]{3,2,1,0:T(8,128)(2,1)S(1)}, bf16[2,4,200,200]{3,2,1,0:T(8,128)(2,1)S(1)}) custom-call(s32[1]{0:T(128)} %bitcast.core_ref, f32[400,1600]{1,0:T(8,128)} %bitcast.19), custom_call_target="tpu_custom_call" | custom-call | flops 1280000 | bytes 5120000 | tf_op jit(solution)/shard_map/regroup/pallas_call | solution.py:344
  14.6 0.7 collective-permute-start.1
  15.6 0.8 %dynamic_slice.7 = f32[200]{0:T(256)S(1)} dynamic-slice(f32[3200]{0:T(1024)} %param.10, s32[]{:T(128)S(6)} %select_n.32), dynamic_slice_sizes={200} | dynamic-slice | bytes 1604 | tf_op jit(solution)/shard_map/dynamic_slice | solution.py:370
  16.6 0.8 %collective-permute-start.2 = (bf16[56,128]{1,0:T(8,128)(2,1)S(1)}, bf16[56,128]{1,0:T(8,128)(2,1)S(1)}, u32[]{:S(2)}, u32[]{:S(2)}) collective-permute-start(bf16[56,128]{1,0:T(8,128)(2,1)S(1)} %divide_convert_fusion.4.amp_ref), channel_id=1, source_target_pairs={{0,1},{1,0},{2,3},{3,2},{4,5},{5,4},{6,7},{7,6},{8,9},{9,8},{10,11... | collective-permute-start | bytes 43016 | tf_op jit(solution)/shard_map/ppermute | solution.py:300
  17.4 0.4 product.8.rest_0_
  17.8 0.5 collective-permute-done.2.amp_ref
  18.2 0.4 product.9
  18.6 7.2 %all_to_all.30 = bf16[8,56,128]{2,1,0:T(8,128)(2,1)S(1)} all-to-all(bf16[8,56,128]{2,1,0:T(8,128)(2,1)S(1)} %product.9), channel_id=1, replica_groups={{10,8,6,4,2,0,14,12},{11,9,7,5,3,1,15,13},{26,24,22,20,18,16,30,28},{27..., dimensions={0} | all-to-all | bytes 229376 | tf_op jit(solution)/shard_map/all_to_all | solution.py:303
  25.8 1.9 %collective-permute-start.3 = (bf16[56,128]{1,0:T(8,128)(2,1)S(1)}, bf16[56,128]{1,0:T(8,128)(2,1)S(1)}, u32[]{:S(2)}, u32[]{:S(2)}) collective-permute-start(bf16[56,128]{1,0:T(8,128)(2,1)S(1)} %divide_convert_fusion.3.amp_ref), channel_id=1, source_target_pairs={{0,1},{1,0},{2,3},{3,2},{4,5},{5,4},{6,7},{7,6},{8,9},{9,8},{10,11... | collective-permute-start | bytes 43016 | tf_op jit(solution)/shard_map/ppermute | solution.py:300
  27.7 0.4 product.10.rest_0_
  28.1 0.5 collective-permute-done.3.amp_ref
  28.6 0.4 product.11
  28.9 7.4 %all_to_all.31 = bf16[8,56,128]{2,1,0:T(8,128)(2,1)S(1)} all-to-all(bf16[8,56,128]{2,1,0:T(8,128)(2,1)S(1)} %product.11), channel_id=1, replica_groups={{10,8,6,4,2,0,14,12},{11,9,7,5,3,1,15,13},{26,24,22,20,18,16,30,28},{27..., dimensions={0} | all-to-all | bytes 229376 | tf_op jit(solution)/shard_map/all_to_all | solution.py:303
  36.4 1.9 %collective-permute-start.4 = (bf16[56,128]{1,0:T(8,128)(2,1)S(1)}, bf16[56,128]{1,0:T(8,128)(2,1)S(1)}, u32[]{:S(2)}, u32[]{:S(2)}) collective-permute-start(bf16[56,128]{1,0:T(8,128)(2,1)S(1)} %divide_convert_fusion.2.amp_ref), channel_id=1, source_target_pairs={{0,1},{1,0},{2,3},{3,2},{4,5},{5,4},{6,7},{7,6},{8,9},{9,8},{10,11... | collective-permute-start | bytes 43016 | tf_op jit(solution)/shard_map/ppermute | solution.py:300
  38.3 0.4 product.12.rest_0_
  38.6 0.5 collective-permute-done.4.amp_ref
  39.1 0.4 product.13
  39.5 7.5 %all_to_all.32 = bf16[8,56,128]{2,1,0:T(8,128)(2,1)S(1)} all-to-all(bf16[8,56,128]{2,1,0:T(8,128)(2,1)S(1)} %product.13), channel_id=1, replica_groups={{10,8,6,4,2,0,14,12},{11,9,7,5,3,1,15,13},{26,24,22,20,18,16,30,28},{27..., dimensions={0} | all-to-all | bytes 229376 | tf_op jit(solution)/shard_map/all_to_all | solution.py:303
  47.0 1.9 %collective-permute-start.5 = (bf16[56,128]{1,0:T(8,128)(2,1)S(1)}, bf16[56,128]{1,0:T(8,128)(2,1)S(1)}, u32[]{:S(2)}, u32[]{:S(2)}) collective-permute-start(bf16[56,128]{1,0:T(8,128)(2,1)S(1)} %divide_convert_fusion.1.amp_ref), channel_id=1, source_target_pairs={{0,1},{1,0},{2,3},{3,2},{4,5},{5,4},{6,7},{7,6},{8,9},{9,8},{10,11... | collective-permute-start | bytes 43016 | tf_op jit(solution)/shard_map/ppermute | solution.py:300
  49.3 0.5 collective-permute-done.5.amp_ref
  50.1 0.4 product.15
  50.5 7.3 %all_to_all.33 = bf16[8,56,128]{2,1,0:T(8,128)(2,1)S(1)} all-to-all(bf16[8,56,128]{2,1,0:T(8,128)(2,1)S(1)} %product.15), channel_id=1, replica_groups={{10,8,6,4,2,0,14,12},{11,9,7,5,3,1,15,13},{26,24,22,20,18,16,30,28},{27..., dimensions={0} | all-to-all | bytes 229376 | tf_op jit(solution)/shard_map/all_to_all | solution.py:303
  57.9 7.4 %all_to_all.34.amp_ref = bf16[8,56,128]{2,1,0:T(8,128)(2,1)S(1)} all-to-all(bf16[8,56,128]{2,1,0:T(8,128)(2,1)S(1)} %broadcast_in_dim.40), channel_id=1, replica_groups={{10,8,6,4,2,0,14,12},{11,9,7,5,3,1,15,13},{26,24,22,20,18,16,30,28},{27..., dimensions={0} | all-to-all | bytes 229376 | tf_op jit(solution)/shard_map/all_to_all | solution.py:303
  65.3 3.0 %collective-permute-start.7 = (bf16[8,56,128]{2,1,0:T(8,128)(2,1)S(1)}, bf16[8,56,128]{2,1,0:T(8,128)(2,1)S(1)}, u32[]{:S(2)}, u32[]{:S(2)}) collective-permute-start(bf16[8,56,128]{2,1,0:T(8,128)(2,1)S(1)} %all_to_all.34.amp_ref), channel_id=1, source_target_pairs={{0,1},{1,0},{2,3},{3,2},{4,5},{5,4},{6,7},{7,6},{8,9},{9,8},{10,11... | collective-permute-start | bytes 344072 | tf_op jit(solution)/shard_map/ppermute | solution.py:300
  68.3 1.4 %blades_same.1.prev_ref = f32[256,1024]{1,0:T(8,128)S(1)} custom-call(s32[1]{0:T(128)} %bitcast.core_ref, f32[16,8,200]{2,1,0:T(8,128)S(1)} %broadcast_in_dim.38.table_ref, bf16[8,56,128]{2,1,0:T(8,128)(2,1)S(1)} %all_to_all.34.amp_ref, bf16[8,200,1024]{2,1,0:T(8,128)(2,1)S(1)} %bitcast.16, bf16[8,200,1024]{2,1,0:T(8,128)(2,1)S(1)} %collective-permute-done.6.recv_ref), custom_call_target="tpu_custom_call" | custom-call | flops 838860800 | bytes 3276800 | tf_op jit(solution)/shard_map/blades_same/pallas_call | solution.py:402
  69.7 2.1 %blades_crossed.1 = bf16[8,32,1024]{2,1,0:T(8,128)(2,1)} custom-call(s32[1]{0:T(128)} %bitcast.core_ref, f32[16,8,200]{2,1,0:T(8,128)S(1)} %broadcast_in_dim.38.table_ref, bf16[8,56,128]{2,1,0:T(8,128)(2,1)S(1)} %collective-permute-done.7.amp_ref, bf16[8,200,1024]{2,1,0:T(8,128)(2,1)S(1)} %bitcast.17, ...), custom_call_target="tpu_custom_call" | custom-call | flops 838860800 | bytes 3276800 | tf_op jit(solution)/shard_map/blades_crossed/pallas_call | solution.py:414
  (30 shorter events, 1.5 us)
Async XLA Ops:
  2.9 1.3 %collective-permute-start = (bf16[4,32,200]{2,1,0:T(8,128)(2,1)S(1)}, bf16[4,32,200]{2,1,0:T(8,128)(2,1)S(1)}, u32[]{:S(2)}, u32[]{:S(2)}) collective-permute-start(bf16[4,32,200]{2,1,0:T(8,128)(2,1)S(1)} %convolution_convert_fusion), channel_id=1, source_target_pairs={{0,1},{1,0},{2,3},{3,2},{4,5},{5,4},{6,7},{7,6},{8,9},{9,8},{10,11... | collective-permute-start | bytes 153608 | tf_op jit(solution)/shard_map/ppermute | solution.py:300
  3.6 11.7 %copy-start.1 = (s32[16]{0:T(128)S(1)}, s32[16]{0:T(128)}, u32[]{:S(2)}) copy-start(s32[16]{0:T(128)} %param.11) | copy-start | bytes 196
  4.9 11.6 %all-to-all-start = ((bf16[8,56,128]{2,1,0:T(8,128)(2,1)}), bf16[8,56,128]{2,1,0:T(8,128)(2,1)S(1)}, u32[]{:S(2)}, u32[]{:S(2)}) async-start(bf16[8,56,128]{2,1,0:T(8,128)(2,1)} %assemble.1), calls=%async_computation | async-start | bytes 229376 | tf_op jit(solution)/shard_map/all_to_all | solution.py:303
  14.6 2.8 %collective-permute-start.1 = (bf16[2,4,200,200]{3,2,1,0:T(8,128)(2,1)S(1)}, bf16[2,4,200,200]{3,2,1,0:T(8,128)(2,1)S(1)}, u32[]{:S(2)}, u32[]{:S(2)}) collective-permute-start(bf16[2,4,200,200]{3,2,1,0:T(8,128)(2,1)S(1)} %get-tuple-element.44), channel_id=1, source_target_pairs={{0,1},{1,0},{2,3},{3,2},{4,5},{5,4},{6,7},{7,6},{8,9},{9,8},{10,11... | collective-permute-start | bytes 1920008 | tf_op jit(solution)/shard_map/ppermute | solution.py:300
  16.6 1.6 %collective-permute-start.2 = (bf16[56,128]{1,0:T(8,128)(2,1)S(1)}, bf16[56,128]{1,0:T(8,128)(2,1)S(1)}, u32[]{:S(2)}, u32[]{:S(2)}) collective-permute-start(bf16[56,128]{1,0:T(8,128)(2,1)S(1)} %divide_convert_fusion.4.amp_ref), channel_id=1, source_target_pairs={{0,1},{1,0},{2,3},{3,2},{4,5},{5,4},{6,7},{7,6},{8,9},{9,8},{10,11... | collective-permute-start | bytes 43016 | tf_op jit(solution)/shard_map/ppermute | solution.py:300
  25.8 2.7 %collective-permute-start.3 = (bf16[56,128]{1,0:T(8,128)(2,1)S(1)}, bf16[56,128]{1,0:T(8,128)(2,1)S(1)}, u32[]{:S(2)}, u32[]{:S(2)}) collective-permute-start(bf16[56,128]{1,0:T(8,128)(2,1)S(1)} %divide_convert_fusion.3.amp_ref), channel_id=1, source_target_pairs={{0,1},{1,0},{2,3},{3,2},{4,5},{5,4},{6,7},{7,6},{8,9},{9,8},{10,11... | collective-permute-start | bytes 43016 | tf_op jit(solution)/shard_map/ppermute | solution.py:300
  36.4 2.7 %collective-permute-start.4 = (bf16[56,128]{1,0:T(8,128)(2,1)S(1)}, bf16[56,128]{1,0:T(8,128)(2,1)S(1)}, u32[]{:S(2)}, u32[]{:S(2)}) collective-permute-start(bf16[56,128]{1,0:T(8,128)(2,1)S(1)} %divide_convert_fusion.2.amp_ref), channel_id=1, source_target_pairs={{0,1},{1,0},{2,3},{3,2},{4,5},{5,4},{6,7},{7,6},{8,9},{9,8},{10,11... | collective-permute-start | bytes 43016 | tf_op jit(solution)/shard_map/ppermute | solution.py:300
  39.1 10.7 %copy-start = (bf16[1024,1600]{0,1:T(8,128)(2,1)S(1)}, bf16[1024,1600]{0,1:T(8,128)(2,1)}, u32[]{:S(2)}) copy-start(bf16[1024,1600]{0,1:T(8,128)(2,1)} %param.6) | copy-start | bytes 9830404
  47.0 2.7 %collective-permute-start.5 = (bf16[56,128]{1,0:T(8,128)(2,1)S(1)}, bf16[56,128]{1,0:T(8,128)(2,1)S(1)}, u32[]{:S(2)}, u32[]{:S(2)}) collective-permute-start(bf16[56,128]{1,0:T(8,128)(2,1)S(1)} %divide_convert_fusion.1.amp_ref), channel_id=1, source_target_pairs={{0,1},{1,0},{2,3},{3,2},{4,5},{5,4},{6,7},{7,6},{8,9},{9,8},{10,11... | collective-permute-start | bytes 43016 | tf_op jit(solution)/shard_map/ppermute | solution.py:300
  49.8 18.6 %collective-permute-start.6 = (bf16[8,200,1024]{2,1,0:T(8,128)(2,1)S(1)}, bf16[8,200,1024]{2,1,0:T(8,128)(2,1)S(1)}, u32[]{:S(2)}, u32[]{:S(2)}) collective-permute-start(bf16[8,200,1024]{2,1,0:T(8,128)(2,1)S(1)} %bitcast.15), channel_id=1, source_target_pairs={{0,1},{1,0},{2,3},{3,2},{4,5},{5,4},{6,7},{7,6},{8,9},{9,8},{10,11... | collective-permute-start | bytes 9830408 | tf_op jit(solution)/shard_map/ppermute | solution.py:300
  65.3 4.4 %collective-permute-start.7 = (bf16[8,56,128]{2,1,0:T(8,128)(2,1)S(1)}, bf16[8,56,128]{2,1,0:T(8,128)(2,1)S(1)}, u32[]{:S(2)}, u32[]{:S(2)}) collective-permute-start(bf16[8,56,128]{2,1,0:T(8,128)(2,1)S(1)} %all_to_all.34.amp_ref), channel_id=1, source_target_pairs={{0,1},{1,0},{2,3},{3,2},{4,5},{5,4},{6,7},{7,6},{8,9},{9,8},{10,11... | collective-permute-start | bytes 344072 | tf_op jit(solution)/shard_map/ppermute | solution.py:300

commit v14 on v13

--- a/solution.py
+++ b/solution.py
@@ -417,7 +417,7 @@
         in_specs=[SMEM] + [VMEM] * 5,
         out_specs=HBM,
         out_shape=jax.ShapeDtypeStruct(out_shape, BF16),
-        scratch_shapes=[weights, pltpu.VMEM(out_shape, BF16), pltpu.SemaphoreType.DMA((4,))],
+        scratch_shapes=[weights, pltpu.VMEM(out_shape, BF16), pltpu.SemaphoreType.DMA((2,))],
         compiler_params=WIDE,
         cost_estimate=half_cost,
     )(core_arg, table, crossed, shapes_sent, shapes_received, part)

time: 72.3 us -> 72.2 us (level)
  no operation moved by 1% of the time
where the time goes in v14:
time: 72.2 us; the launch traced here: 71.8 us
  blocking collectives  36.8 us (51%)
  starting transfers between devices  18.3 us (25%)
  Pallas kernels  11.6 us (16%)
  waiting for transfers between devices  2.41 us (3%)
  matrix products  1.44 us (2%)
  local copies, waits for them, and re-layouts  0.97 us (1%)
    all_to_all x5, blocking collectives, exchange(): lax.all_to_all(slots, 'rows', 0, 0, tiled=True, axis_index_groups=[ORDER])  36.8 us
    ppermute x8, starting transfers between devices, other_core(): return lax.ppermute(value, 'diam', SWAP)  10.6 us
    all_to_all x1, starting transfers between devices, exchange(): lax.all_to_all(slots, 'rows', 0, 0, tiled=True, axis_index_groups=[ORDER])  7.69 us
    pallas_call x8, Pallas kernels, product(): pl.pallas_call(functools.partial(product_kernel, source), name='product',...  3 us
    ppermute x8, waiting for transfers between devices, other_core(): return lax.ppermute(value, 'diam', SWAP)  2.4 us
    pallas_call x1, Pallas kernels, chunk_plan(): pl.pallas_call(functools.partial(load_kernel, columns), name='load', in_s...  2.28 us
    pallas_call x1, Pallas kernels, chunk_plan(): pl.pallas_call(crossed_kernel, name='blades_crossed', in_specs=[SMEM] + [...  2.09 us
    pallas_call x1, Pallas kernels, chunk_plan(): pl.pallas_call(regroup_kernel, name='regroup', in_specs=[SMEM, HBM], out_...  2.02 us
  transfers between devices with their start and end apart: 9, of which 5 were waited for; matrix products, arithmetic and copies ran while one was open for 3% of the time, Pallas kernels for 7%

profile of v14, /device:TPU:1, one launch (start us, length us, event | category | flops | bytes accessed | tf_op | source)
XLA Modules:
  0.0 71.8 jit_solution(5933648538234213074)
XLA Ops:
  0.0 2.3 %load.1 = (bf16[4,32,1024]{2,1,0:T(8,128)(2,1)S(1)}, bf16[4,32,1024]{2,1,0:T(8,128)(2,1)S(1)}, bf16[4,200,1024]{2,1,0:T(8,128)(2,1)S(1)}, bf16[4,200,1024]{2,1,0:T(8,128)(2,1)S(1)}) custom-call(s32[1]{0:T(128)} %bitcast.core_ref, s32[16]{0:T(128)} %harm_hbm.1, bf16[1024,512]{1,0:T(8,128)(2,1)} %loads_hbm.1, bf16[4,2,200,1024]{3,2,1,0:T(8,128)(2,1)} %bitcast.14), custom_call_target="tpu_custom_call" | custom-call | tf_op jit(solution)/shard_map/load/pallas_call | solution.py:311
  2.3 0.6 convolution_convert_fusion
  3.0 0.6 convolution_convert_fusion.1.mine_ref
  3.6 0.5 collective-permute-done.recv_ref
  4.2 0.7 %assemble.1 = bf16[8,56,128]{2,1,0:T(8,128)(2,1)} custom-call(s32[1]{0:T(128)} %bitcast.core_ref, bf16[4,32,200]{2,1,0:T(8,128)(2,1)S(1)} %convolution_convert_fusion.1.mine_ref, bf16[4,32,200]{2,1,0:T(8,128)(2,1)S(1)} %collective-permute-done.recv_ref), custom_call_target="tpu_custom_call" | custom-call | tf_op jit(solution)/shard_map/assemble/pallas_call | solution.py:330
  4.9 7.7 %all-to-all-start = ((bf16[8,56,128]{2,1,0:T(8,128)(2,1)}), bf16[8,56,128]{2,1,0:T(8,128)(2,1)S(1)}, u32[]{:S(2)}, u32[]{:S(2)}) async-start(bf16[8,56,128]{2,1,0:T(8,128)(2,1)} %assemble.1), calls=%async_computation | async-start | bytes 229376 | tf_op jit(solution)/shard_map/all_to_all | solution.py:303
  12.6 2.0 %regroup.1 = (bf16[2,4,200,200]{3,2,1,0:T(8,128)(2,1)S(1)}, bf16[2,4,200,200]{3,2,1,0:T(8,128)(2,1)S(1)}) custom-call(s32[1]{0:T(128)} %bitcast.core_ref, f32[400,1600]{1,0:T(8,128)} %bitcast.19), custom_call_target="tpu_custom_call" | custom-call | flops 1280000 | bytes 5120000 | tf_op jit(solution)/shard_map/regroup/pallas_call | solution.py:344
  14.6 0.7 collective-permute-start.1
  15.6 0.8 %dynamic_slice.7 = f32[200]{0:T(256)S(1)} dynamic-slice(f32[3200]{0:T(1024)} %param.10, s32[]{:T(128)S(6)} %select_n.32), dynamic_slice_sizes={200} | dynamic-slice | bytes 1604 | tf_op jit(solution)/shard_map/dynamic_slice | solution.py:370
  16.6 0.8 %collective-permute-start.2 = (bf16[56,128]{1,0:T(8,128)(2,1)S(1)}, bf16[56,128]{1,0:T(8,128)(2,1)S(1)}, u32[]{:S(2)}, u32[]{:S(2)}) collective-permute-start(bf16[56,128]{1,0:T(8,128)(2,1)S(1)} %divide_convert_fusion.4.amp_ref), channel_id=1, source_target_pairs={{0,1},{1,0},{2,3},{3,2},{4,5},{5,4},{6,7},{7,6},{8,9},{9,8},{10,11... | collective-permute-start | bytes 43016 | tf_op jit(solution)/shard_map/ppermute | solution.py:300
  17.4 0.4 product.8.rest_0_
  17.8 0.5 collective-permute-done.2.amp_ref
  18.2 0.4 product.9
  18.6 7.2 %all_to_all.30 = bf16[8,56,128]{2,1,0:T(8,128)(2,1)S(1)} all-to-all(bf16[8,56,128]{2,1,0:T(8,128)(2,1)S(1)} %product.9), channel_id=1, replica_groups={{10,8,6,4,2,0,14,12},{11,9,7,5,3,1,15,13},{26,24,22,20,18,16,30,28},{27..., dimensions={0} | all-to-all | bytes 229376 | tf_op jit(solution)/shard_map/all_to_all | solution.py:303
  25.8 1.9 %collective-permute-start.3 = (bf16[56,128]{1,0:T(8,128)(2,1)S(1)}, bf16[56,128]{1,0:T(8,128)(2,1)S(1)}, u32[]{:S(2)}, u32[]{:S(2)}) collective-permute-start(bf16[56,128]{1,0:T(8,128)(2,1)S(1)} %divide_convert_fusion.3.amp_ref), channel_id=1, source_target_pairs={{0,1},{1,0},{2,3},{3,2},{4,5},{5,4},{6,7},{7,6},{8,9},{9,8},{10,11... | collective-permute-start | bytes 43016 | tf_op jit(solution)/shard_map/ppermute | solution.py:300
  27.7 0.4 product.10.rest_0_
  28.1 0.5 collective-permute-done.3.amp_ref
  28.6 0.4 product.11
  28.9 7.4 %all_to_all.31 = bf16[8,56,128]{2,1,0:T(8,128)(2,1)S(1)} all-to-all(bf16[8,56,128]{2,1,0:T(8,128)(2,1)S(1)} %product.11), channel_id=1, replica_groups={{10,8,6,4,2,0,14,12},{11,9,7,5,3,1,15,13},{26,24,22,20,18,16,30,28},{27..., dimensions={0} | all-to-all | bytes 229376 | tf_op jit(solution)/shard_map/all_to_all | solution.py:303
  36.4 1.9 %collective-permute-start.4 = (bf16[56,128]{1,0:T(8,128)(2,1)S(1)}, bf16[56,128]{1,0:T(8,128)(2,1)S(1)}, u32[]{:S(2)}, u32[]{:S(2)}) collective-permute-start(bf16[56,128]{1,0:T(8,128)(2,1)S(1)} %divide_convert_fusion.2.amp_ref), channel_id=1, source_target_pairs={{0,1},{1,0},{2,3},{3,2},{4,5},{5,4},{6,7},{7,6},{8,9},{9,8},{10,11... | collective-permute-start | bytes 43016 | tf_op jit(solution)/shard_map/ppermute | solution.py:300
  38.3 0.4 product.12.rest_0_
  38.6 0.5 collective-permute-done.4.amp_ref
  39.1 0.4 product.13
  39.5 7.5 %all_to_all.32 = bf16[8,56,128]{2,1,0:T(8,128)(2,1)S(1)} all-to-all(bf16[8,56,128]{2,1,0:T(8,128)(2,1)S(1)} %product.13), channel_id=1, replica_groups={{10,8,6,4,2,0,14,12},{11,9,7,5,3,1,15,13},{26,24,22,20,18,16,30,28},{27..., dimensions={0} | all-to-all | bytes 229376 | tf_op jit(solution)/shard_map/all_to_all | solution.py:303
  47.0 1.9 %collective-permute-start.5 = (bf16[56,128]{1,0:T(8,128)(2,1)S(1)}, bf16[56,128]{1,0:T(8,128)(2,1)S(1)}, u32[]{:S(2)}, u32[]{:S(2)}) collective-permute-start(bf16[56,128]{1,0:T(8,128)(2,1)S(1)} %divide_convert_fusion.1.amp_ref), channel_id=1, source_target_pairs={{0,1},{1,0},{2,3},{3,2},{4,5},{5,4},{6,7},{7,6},{8,9},{9,8},{10,11... | collective-permute-start | bytes 43016 | tf_op jit(solution)/shard_map/ppermute | solution.py:300
  49.3 0.5 collective-permute-done.5.amp_ref
  50.1 0.4 product.15
  50.5 7.3 %all_to_all.33 = bf16[8,56,128]{2,1,0:T(8,128)(2,1)S(1)} all-to-all(bf16[8,56,128]{2,1,0:T(8,128)(2,1)S(1)} %product.15), channel_id=1, replica_groups={{10,8,6,4,2,0,14,12},{11,9,7,5,3,1,15,13},{26,24,22,20,18,16,30,28},{27..., dimensions={0} | all-to-all | bytes 229376 | tf_op jit(solution)/shard_map/all_to_all | solution.py:303
  57.9 7.4 %all_to_all.34.amp_ref = bf16[8,56,128]{2,1,0:T(8,128)(2,1)S(1)} all-to-all(bf16[8,56,128]{2,1,0:T(8,128)(2,1)S(1)} %broadcast_in_dim.40), channel_id=1, replica_groups={{10,8,6,4,2,0,14,12},{11,9,7,5,3,1,15,13},{26,24,22,20,18,16,30,28},{27..., dimensions={0} | all-to-all | bytes 229376 | tf_op jit(solution)/shard_map/all_to_all | solution.py:303
  65.3 3.0 %collective-permute-start.7 = (bf16[8,56,128]{2,1,0:T(8,128)(2,1)S(1)}, bf16[8,56,128]{2,1,0:T(8,128)(2,1)S(1)}, u32[]{:S(2)}, u32[]{:S(2)}) collective-permute-start(bf16[8,56,128]{2,1,0:T(8,128)(2,1)S(1)} %all_to_all.34.amp_ref), channel_id=1, source_target_pairs={{0,1},{1,0},{2,3},{3,2},{4,5},{5,4},{6,7},{7,6},{8,9},{9,8},{10,11... | collective-permute-start | bytes 344072 | tf_op jit(solution)/shard_map/ppermute | solution.py:300
  68.3 1.4 %blades_same.1.prev_ref = f32[256,1024]{1,0:T(8,128)S(1)} custom-call(s32[1]{0:T(128)} %bitcast.core_ref, f32[16,8,200]{2,1,0:T(8,128)S(1)} %broadcast_in_dim.38.table_ref, bf16[8,56,128]{2,1,0:T(8,128)(2,1)S(1)} %all_to_all.34.amp_ref, bf16[8,200,1024]{2,1,0:T(8,128)(2,1)S(1)} %bitcast.16, bf16[8,200,1024]{2,1,0:T(8,128)(2,1)S(1)} %collective-permute-done.6.recv_ref), custom_call_target="tpu_custom_call" | custom-call | flops 838860800 | bytes 3276800 | tf_op jit(solution)/shard_map/blades_same/pallas_call | solution.py:402
  69.7 2.1 %blades_crossed.1 = bf16[8,32,1024]{2,1,0:T(8,128)(2,1)} custom-call(s32[1]{0:T(128)} %bitcast.core_ref, f32[16,8,200]{2,1,0:T(8,128)S(1)} %broadcast_in_dim.38.table_ref, bf16[8,56,128]{2,1,0:T(8,128)(2,1)S(1)} %collective-permute-done.7.amp_ref, bf16[8,200,1024]{2,1,0:T(8,128)(2,1)S(1)} %bitcast.17, ...), custom_call_target="tpu_custom_call" | custom-call | flops 838860800 | bytes 3276800 | tf_op jit(solution)/shard_map/blades_crossed/pallas_call | solution.py:414
  (30 shorter events, 1.5 us)
Async XLA Ops:
  2.9 1.3 %collective-permute-start = (bf16[4,32,200]{2,1,0:T(8,128)(2,1)S(1)}, bf16[4,32,200]{2,1,0:T(8,128)(2,1)S(1)}, u32[]{:S(2)}, u32[]{:S(2)}) collective-permute-start(bf16[4,32,200]{2,1,0:T(8,128)(2,1)S(1)} %convolution_convert_fusion), channel_id=1, source_target_pairs={{0,1},{1,0},{2,3},{3,2},{4,5},{5,4},{6,7},{7,6},{8,9},{9,8},{10,11... | collective-permute-start | bytes 153608 | tf_op jit(solution)/shard_map/ppermute | solution.py:300
  3.6 11.7 %copy-start.1 = (s32[16]{0:T(128)S(1)}, s32[16]{0:T(128)}, u32[]{:S(2)}) copy-start(s32[16]{0:T(128)} %param.11) | copy-start | bytes 196
  4.9 11.6 %all-to-all-start = ((bf16[8,56,128]{2,1,0:T(8,128)(2,1)}), bf16[8,56,128]{2,1,0:T(8,128)(2,1)S(1)}, u32[]{:S(2)}, u32[]{:S(2)}) async-start(bf16[8,56,128]{2,1,0:T(8,128)(2,1)} %assemble.1), calls=%async_computation | async-start | bytes 229376 | tf_op jit(solution)/shard_map/all_to_all | solution.py:303
  14.6 2.8 %collective-permute-start.1 = (bf16[2,4,200,200]{3,2,1,0:T(8,128)(2,1)S(1)}, bf16[2,4,200,200]{3,2,1,0:T(8,128)(2,1)S(1)}, u32[]{:S(2)}, u32[]{:S(2)}) collective-permute-start(bf16[2,4,200,200]{3,2,1,0:T(8,128)(2,1)S(1)} %get-tuple-element.44), channel_id=1, source_target_pairs={{0,1},{1,0},{2,3},{3,2},{4,5},{5,4},{6,7},{7,6},{8,9},{9,8},{10,11... | collective-permute-start | bytes 1920008 | tf_op jit(solution)/shard_map/ppermute | solution.py:300
  16.6 1.6 %collective-permute-start.2 = (bf16[56,128]{1,0:T(8,128)(2,1)S(1)}, bf16[56,128]{1,0:T(8,128)(2,1)S(1)}, u32[]{:S(2)}, u32[]{:S(2)}) collective-permute-start(bf16[56,128]{1,0:T(8,128)(2,1)S(1)} %divide_convert_fusion.4.amp_ref), channel_id=1, source_target_pairs={{0,1},{1,0},{2,3},{3,2},{4,5},{5,4},{6,7},{7,6},{8,9},{9,8},{10,11... | collective-permute-start | bytes 43016 | tf_op jit(solution)/shard_map/ppermute | solution.py:300
  25.8 2.7 %collective-permute-start.3 = (bf16[56,128]{1,0:T(8,128)(2,1)S(1)}, bf16[56,128]{1,0:T(8,128)(2,1)S(1)}, u32[]{:S(2)}, u32[]{:S(2)}) collective-permute-start(bf16[56,128]{1,0:T(8,128)(2,1)S(1)} %divide_convert_fusion.3.amp_ref), channel_id=1, source_target_pairs={{0,1},{1,0},{2,3},{3,2},{4,5},{5,4},{6,7},{7,6},{8,9},{9,8},{10,11... | collective-permute-start | bytes 43016 | tf_op jit(solution)/shard_map/ppermute | solution.py:300
  36.4 2.7 %collective-permute-start.4 = (bf16[56,128]{1,0:T(8,128)(2,1)S(1)}, bf16[56,128]{1,0:T(8,128)(2,1)S(1)}, u32[]{:S(2)}, u32[]{:S(2)}) collective-permute-start(bf16[56,128]{1,0:T(8,128)(2,1)S(1)} %divide_convert_fusion.2.amp_ref), channel_id=1, source_target_pairs={{0,1},{1,0},{2,3},{3,2},{4,5},{5,4},{6,7},{7,6},{8,9},{9,8},{10,11... | collective-permute-start | bytes 43016 | tf_op jit(solution)/shard_map/ppermute | solution.py:300
  39.1 10.7 %copy-start = (bf16[1024,1600]{0,1:T(8,128)(2,1)S(1)}, bf16[1024,1600]{0,1:T(8,128)(2,1)}, u32[]{:S(2)}) copy-start(bf16[1024,1600]{0,1:T(8,128)(2,1)} %param.6) | copy-start | bytes 9830404
  47.0 2.7 %collective-permute-start.5 = (bf16[56,128]{1,0:T(8,128)(2,1)S(1)}, bf16[56,128]{1,0:T(8,128)(2,1)S(1)}, u32[]{:S(2)}, u32[]{:S(2)}) collective-permute-start(bf16[56,128]{1,0:T(8,128)(2,1)S(1)} %divide_convert_fusion.1.amp_ref), channel_id=1, source_target_pairs={{0,1},{1,0},{2,3},{3,2},{4,5},{5,4},{6,7},{7,6},{8,9},{9,8},{10,11... | collective-permute-start | bytes 43016 | tf_op jit(solution)/shard_map/ppermute | solution.py:300
  49.8 18.6 %collective-permute-start.6 = (bf16[8,200,1024]{2,1,0:T(8,128)(2,1)S(1)}, bf16[8,200,1024]{2,1,0:T(8,128)(2,1)S(1)}, u32[]{:S(2)}, u32[]{:S(2)}) collective-permute-start(bf16[8,200,1024]{2,1,0:T(8,128)(2,1)S(1)} %bitcast.15), channel_id=1, source_target_pairs={{0,1},{1,0},{2,3},{3,2},{4,5},{5,4},{6,7},{7,6},{8,9},{9,8},{10,11... | collective-permute-start | bytes 9830408 | tf_op jit(solution)/shard_map/ppermute | solution.py:300
  65.3 4.4 %collective-permute-start.7 = (bf16[8,56,128]{2,1,0:T(8,128)(2,1)S(1)}, bf16[8,56,128]{2,1,0:T(8,128)(2,1)S(1)}, u32[]{:S(2)}, u32[]{:S(2)}) collective-permute-start(bf16[8,56,128]{2,1,0:T(8,128)(2,1)S(1)} %all_to_all.34.amp_ref), channel_id=1, source_target_pairs={{0,1},{1,0},{2,3},{3,2},{4,5},{5,4},{6,7},{7,6},{8,9},{9,8},{10,11... | collective-permute-start | bytes 344072 | tf_op jit(solution)/shard_map/ppermute | solution.py:300
